TPU v7x, 32 devices: a whole 2x2x4 slice. The times are simulated.
32 devices in a mesh: pipe: 4 (over x, core), dp: 8 (over z, y).
Axes of the slice: x: 2, y: 2, z: 4, core: 2. Of those that a mesh axis runs over, the one named last changes fastest.
Arguments:
- inputs: bfloat16 [2, 2, 256, 1024], P(None, None, 'dp'), may hold values from -6 to 6
- cotangent: bfloat16 [2, 2, 256, 1024], P(None, None, 'dp'), may hold values from -0.375 to 0.375
- reduce_weight: bfloat16 [2, 4, 1024, 256], P(None, 'pipe'), may hold values from -0.1875 to 0.1875
- expand_weight: bfloat16 [2, 4, 1024, 256], P(None, 'pipe'), may hold values from -0.375 to 0.375
Outputs:
- gradients: float32 [4, 2, 1024, 256], P('pipe', None, 'dp')
All inputs are finite; a program needn't handle non-finite values.
Results may differ from a plain program's by a relative error of at most 0.023.
Values may be sent and summed in bfloat16 or wider, within the bound.
No kernel may reach another device: no remote copies, remote signals or barrier semaphores. Data moves between devices by JAX's collectives and lax.ppermute only.
A program may use at most 64 MiB of HBM per device.

v0:
```python
import functools

import jax
import jax.numpy as jnp
from jax import lax
from jax.experimental import pallas as pl
from jax.experimental.pallas import tpu as pltpu
from jax.sharding import PartitionSpec as P


EPSILON = 1e-06
AXES = ("pipe", "dp")
HBM = pl.BlockSpec(memory_space=pltpu.HBM)
ANY = pl.BlockSpec(memory_space=pl.ANY)
VMEM = pl.BlockSpec(memory_space=pltpu.VMEM)
PARAMS = pltpu.CompilerParams(vmem_limit_bytes=16 << 20)


def contract(first_op, second_op, first_dim, second_dim):
    return lax.dot_general(
        first_op,
        second_op,
        (((first_dim,), (second_dim,)), ((), ())),
        preferred_element_type=jnp.float32,
    )


def smooth_slope(values):
    sigma = jax.nn.sigmoid(values)
    return sigma * (1.0 + values * (1.0 - sigma))


def norm_of(widened):
    return lax.rsqrt(jnp.mean(widened * widened, axis=-1, keepdims=True) + EPSILON)


def where_am_i(step):
    position = lax.axis_index("pipe")
    stage, core = lax.div(position, 2), lax.rem(position, 2)
    way = jnp.where(stage == step, 0, 1)
    return stage, core, way


def bring_all(sources, outs, sems):
    copies = [
        pltpu.make_async_copy(source, out, sems.at[at])
        for at, (source, out) in enumerate(zip(sources, outs))
    ]
    for copy in copies:
        copy.start()
    return copies


def load_body(step, reduce_all, expand_all, *refs):
    _, core, way = where_am_i(step)
    sources, outs = [reduce_all.at[way], expand_all.at[way]], refs[:-1]
    if step == 0:
        sources.append(refs[0].at[way, core])
        outs = outs[1:]
    for copy in bring_all(sources, outs, refs[-1]):
        copy.wait()


def load(step, own, *more):
    channels, inner = own[0].shape[1:]
    mat = jax.ShapeDtypeStruct((channels, inner), jnp.bfloat16)
    outs = [mat, mat] + [jax.ShapeDtypeStruct(a.shape[2:], a.dtype) for a in more]
    return pl.pallas_call(
        functools.partial(load_body, step),
        out_shape=outs,
        in_specs=[HBM] * (2 + len(more)),
        out_specs=[VMEM] * len(outs),
        scratch_shapes=[pltpu.SemaphoreType.DMA((len(outs),))],
        compiler_params=PARAMS,
    )(*own, *more)


def meanwhile_body(step, mirrored, expand_own, expand_other, inputs, cotangent, leave, *refs):
    outs, sems = refs[:-1], refs[-1]
    stage, core, way = where_am_i(step)
    ending, back_active = outs[:2]
    sources = [cotangent.at[way, core]]
    if mirrored:
        sources += [cotangent.at[1, core], inputs.at[1, core]]
    copies = bring_all(sources, [outs[0]] + list(outs[2:]), sems)
    copies[0].wait()

    @pl.when(way == core)
    def _():
        back_active[...] = jnp.dot(
            ending[...], expand_other[...], preferred_element_type=jnp.float32
        )

    @pl.when(way != core)
    def _():
        back_active[...] = jnp.dot(ending[...], expand_own[...], preferred_element_type=jnp.float32)

    for copy in copies[1:]:
        copy.wait()
    if mirrored:
        rows = outs[3]

        @pl.when(stage != 0)
        def _():
            rows[...] = leave[...]

        widened = rows[...].astype(jnp.float32)
        rows[...] = jax.nn.silu(widened * norm_of(widened)).astype(jnp.bfloat16)


def weight_copies(own, other, held, sems, core, way):
    copies = []
    for order in range(2):
        is_own = lax.rem(way + order, 2) == core
        for kind in range(2):
            mine = pltpu.make_async_copy(own[kind].at[way], held[kind].at[order], sems.at[kind, order])
            theirs = pltpu.make_async_copy(
                other[kind].at[way], held[kind].at[order], sems.at[kind, order]
            )
            copies.append((is_own, mine, theirs))
    return copies


def start_all(copies):
    for is_own, mine, theirs in copies:
        pl.when(is_own)(mine.start)
        pl.when(jnp.logical_not(is_own))(theirs.start)


def stage_body(step, forward, backward, last, near, *refs):
    refs = list(refs)
    _, core, way = where_am_i(step)
    own, other = (refs.pop(0), refs.pop(0)), (refs.pop(0), refs.pop(0))
    enter = refs.pop(0) if forward else None
    upstream_in = refs.pop(0) if backward else None
    first_active = refs.pop(0) if forward and backward else None
    if not forward:
        trunks, inners = refs.pop(0), refs.pop(0)
    if forward:
        flows = refs.pop(0)
    if forward and not backward:
        leave = refs.pop(0)
    if backward:
        upstreams, back_inners = refs.pop(0), refs.pop(0)
    if backward and not last:
        back_leave = refs.pop(0)
    if forward:
        trunks, inners = refs.pop(0), refs.pop(0)
    channels = trunks.shape[2]

    def run(reduce_mats, expand_mats, wait):
        if forward:
            rows = enter[...]
            for order in range(2):
                slot = lax.rem(order + core, 2)
                widened = rows.astype(jnp.float32)
                normed = widened * norm_of(widened)
                lifted = jax.nn.silu(normed).astype(jnp.bfloat16)
                trunks[order] = rows
                flows[slot, :, :channels] = lifted
                wait(0, order)
                inner_sum = jnp.dot(
                    lifted, reduce_mats[order][...], preferred_element_type=jnp.float32
                )
                active = jax.nn.silu(inner_sum).astype(jnp.bfloat16)
                inners[order] = inner_sum
                flows[slot, :, channels:] = active
                wait(1, order)
                rows = (widened + contract(active, expand_mats[order][...], 1, 1)).astype(jnp.bfloat16)
            if not backward:
                leave[...] = rows
        if backward:
            upstream = upstream_in[...]
            for order in (1, 0):
                slot = lax.rem(order + core, 2)
                upstreams[slot] = upstream
                if not forward:
                    wait(1, order)
                if forward and order:
                    back_active = first_active[...]
                else:
                    back_active = jnp.dot(
                        upstream, expand_mats[order][...], preferred_element_type=jnp.float32
                    )
                back_inner = (back_active * smooth_slope(inners[order])).astype(jnp.bfloat16)
                back_inners[slot] = back_inner
                if not forward:
                    wait(0, order)
                if last and order == 0:
                    break
                back_lifted = contract(back_inner, reduce_mats[order][...], 1, 1)
                widened = trunks[order].astype(jnp.float32)
                norm_scale = norm_of(widened)
                back_normed = back_lifted * smooth_slope(widened * norm_scale)
                projection = jnp.mean(back_normed * widened, axis=-1, keepdims=True)
                upstream = (
                    upstream.astype(jnp.float32)
                    + norm_scale * back_normed
                    - widened * norm_scale**3 * projection
                ).astype(jnp.bfloat16)
            if not last:
                back_leave[...] = upstream

    if near:
        idle = lambda kind, order: None

        @pl.when(way == core)
        def _():
            run((own[0], other[0]), (own[1], other[1]), idle)

        @pl.when(way != core)
        def _():
            run((other[0], own[0]), (other[1], own[1]), idle)

    else:
        held = (refs.pop(0), refs.pop(0))
        copies = weight_copies(own, other, held, refs.pop(0), core, way)
        start_all(copies if forward else copies[2:] + copies[:2])
        run(
            [held[0].at[order] for order in range(2)],
            [held[1].at[order] for order in range(2)],
            lambda kind, order: copies[2 * order + kind][1].wait(),
        )


def run_stage(weights, step, forward, backward, near, rows, sizes, *arrays):
    channels, inner = sizes
    last = backward and step == 0 and not forward
    shape = lambda dtype, *dims: jax.ShapeDtypeStruct(dims, dtype)
    line = shape(jnp.bfloat16, rows, channels)
    kept = [((2, rows, channels), jnp.bfloat16), ((2, rows, inner), jnp.float32)]
    outs, scratch = [], []
    if forward:
        outs.append(shape(jnp.bfloat16, 2, rows, channels + inner))
    if forward and not backward:
        outs.append(line)
    if backward:
        outs.append(shape(jnp.bfloat16, 2, rows, channels))
        outs.append(shape(jnp.bfloat16, 2, rows, inner))
    if backward and not last:
        outs.append(line)
    if forward and not backward:
        outs += [jax.ShapeDtypeStruct(*one) for one in kept]
    if forward and backward:
        scratch += [pltpu.VMEM(*one) for one in kept]
    if not near:
        scratch += [pltpu.VMEM((2, channels, inner), jnp.bfloat16)] * 2
        scratch += [pltpu.SemaphoreType.DMA((2, 2))]
    passes = 4 * (int(forward) + int(backward))
    return pl.pallas_call(
        functools.partial(stage_body, step, forward, backward, last, near),
        out_shape=outs,
        in_specs=[VMEM if near else ANY] * 4 + [VMEM] * len(arrays),
        out_specs=[VMEM] * len(outs),
        scratch_shapes=scratch,
        compiler_params=PARAMS,
        cost_estimate=pl.CostEstimate(
            flops=2 * passes * rows * channels * inner,
            bytes_accessed=8 * channels * inner,
            transcendentals=passes * rows * channels,
        ),
    )(*weights, *arrays)


def parity(value, mask):
    total, bit = 0, 0
    while mask >> bit:
        if mask >> bit & 1:
            total = total + lax.rem(lax.div(value, 1 << bit), 2)
        bit += 1
    return lax.rem(total, 2)


def halving_plan(size, turn):
    order = [1 << bit for bit in range(size.bit_length() - 1)]
    if turn and len(order) > 1:
        order[:2] = order[1::-1]
    table = [0] * size
    for chunk in range(size):
        place = 0
        for mask in order:
            place = 2 * place + int(chunk & mask != 0)
        table[place] = chunk
    return order, order, table


def side_of(plans, at):
    core, shard = lax.rem(lax.axis_index("pipe"), 2), lax.axis_index("dp")
    return jnp.where(core == 0, parity(shard, plans[0][1][at]), parity(shard, plans[1][1][at]))


def gradient_body(plans, pick_left, pick_right, count, *refs):
    arrays, (send, keep, left, right, full) = refs[:count], refs[count:]
    stage, core, _ = where_am_i(0)
    rows = left.shape[0] // 4
    chunk = send.shape[1]
    for target, pick in ((left, pick_left), (right, pick_right)):
        near, away = pick(arrays)
        for step, part in enumerate(near):

            @pl.when(stage == step)
            def _():
                target[:rows] = part[...]

        for at, part in enumerate(away):
            target[(at + 1) * rows : (at + 2) * rows] = part[...]
    full[...] = contract(left[...], right[...], 0, 0)
    side = side_of(plans, 0)
    half = send.shape[0]
    flip = [plan[2][half] for plan in plans]
    for at in range(half):
        spots = []
        for target_side in (1 - side, side):
            first = plans[0][2][at] ^ (flip[0] * target_side)
            second = plans[1][2][at] ^ (flip[1] * target_side)
            spots.append(pl.multiple_of(jnp.where(core == 0, first, second) * chunk, chunk))
        send[at] = full[pl.ds(spots[0], chunk)].astype(jnp.bfloat16)
        keep[at] = full[pl.ds(spots[1], chunk)]


def halve_body(plans, at, keep_in, came, send, keep):
    half = keep.shape[0]
    side = side_of(plans, at)
    for spot in range(half):
        mine, theirs = side * half + spot, (1 - side) * half + spot
        send[spot] = (keep_in[theirs] + came[theirs].astype(jnp.float32)).astype(jnp.bfloat16)
        keep[spot] = keep_in[mine] + came[mine].astype(jnp.float32)


def bit_of(value, bit):
    return lax.rem(lax.div(value, 1 << bit), 2)


def first_sides():
    core, shard = lax.rem(lax.axis_index("pipe"), 2), lax.axis_index("dp")
    low, high = bit_of(shard, 0), bit_of(shard, 1)
    return core, jnp.where(core == 0, low, high), jnp.where(core == 0, high, low)


def split_columns(wide, keep, send, chunk):
    core, side, _ = first_sides()
    for place in range(wide.shape[1] // (2 * chunk)):
        for target, at in ((keep, side), (send, 1 - side)):
            block = jnp.where(core == 0, 2 * place + at, place // 2 * 4 + 2 * at + place % 2)
            source = pl.ds(pl.multiple_of(block * chunk, chunk), chunk)
            target[:, place * chunk : (place + 1) * chunk] = wide[:, source]


def gather_rows(target, near, away):
    stage, _, _ = where_am_i(0)
    rows = target.shape[0] // 4
    for step, part in enumerate(near):

        @pl.when(stage == step)
        def _():
            target[:rows] = part[...]

    for at, part in enumerate(away):
        target[(at + 1) * rows : (at + 2) * rows] = part[...]


def early_body(stages, chunk, *refs):
    arrays, (keep_left, keep_right, send, wide) = refs[: stages + 3], refs[stages + 3 :]
    channels = wide.shape[1]
    flows, (side, far, cross) = arrays[:stages], arrays[stages:]
    for target, columns in ((wide, slice(0, channels)), (keep_right, slice(channels, None))):
        near = [flow.at[0, :, columns] for flow in flows]
        gather_rows(target, near, [side.at[:, columns], far.at[:, columns], cross.at[:, columns]])
    split_columns(wide, keep_left, send, chunk)
    send[:, channels // 2 :] = keep_right[...]


def late_body(stages, chunk, *refs):
    arrays, outs = refs[: stages + 3], refs[stages + 3 :]
    side, far, cross = arrays[stages:]
    gather_rows(outs[-1], [back.at[0] for back in arrays[:stages]], [side, far, cross])
    if chunk:
        split_columns(outs[2], outs[0], outs[1], chunk)


def half_gradient_body(left, left_came, right, right_came, send, keep, full):
    full[...] = contract(left[...], right[...], 0, 0) + contract(left_came[...], right_came[...], 0, 0)
    _, _, side = first_sides()
    chunk = send.shape[1]
    for place in range(send.shape[0]):
        theirs = pl.ds(pl.multiple_of((2 * place + 1 - side) * chunk, chunk), chunk)
        mine = pl.ds(pl.multiple_of((2 * place + side) * chunk, chunk), chunk)
        send[place] = full[theirs].astype(jnp.bfloat16)
        keep[place] = full[mine]


def next_body(bit, keep_in, came, send, keep):
    side = bit_of(lax.axis_index("dp"), bit)
    for place in range(keep.shape[0]):
        theirs, mine = 2 * place + 1 - side, 2 * place + side
        send[place] = (keep_in[theirs] + came[theirs].astype(jnp.float32)).astype(jnp.bfloat16)
        keep[place] = keep_in[mine] + came[mine].astype(jnp.float32)


def finish_body(keep_reduce, came_reduce, keep_expand, came_expand, out):
    out[0, 0] = keep_reduce[0] + came_reduce[0].astype(jnp.float32)
    out[0, 1] = keep_expand[0] + came_expand[0].astype(jnp.float32)


def shards(inputs, cotangent, reduce_weight, expand_weight):
    stages = lax.axis_size("pipe") // 2
    replicas = lax.axis_size("dp")
    stage, core, _ = where_am_i(0)
    channels, inner = reduce_weight.shape[2:]
    rows = inputs.shape[1] * inputs.shape[2] // 2
    sizes = (channels, inner)
    entering = inputs.reshape(2, 2, rows, channels)
    ending = cotangent.reshape(2, 2, rows, channels)
    own = [reduce_weight[:, 0], expand_weight[:, 0]]

    core_pairs = [(p, p ^ 1) for p in range(2 * stages)]
    mirror_pairs = [(p, 2 * (stages - 1 - p // 2) + p % 2) for p in range(2 * stages)]

    def hop(shard, step):
        pairs = []
        for c in range(2):
            pairs.append((2 * step + c, 2 * step + 2 + c))
            pairs.append((2 * (stages - 1 - step) + c, 2 * (stages - 2 - step) + c))
        return lax.ppermute(shard, "pipe", pairs)

    def swap_cores(shard):
        return lax.ppermute(shard, "pipe", core_pairs)

    def mirror(shard):
        return lax.ppermute(shard, "pipe", mirror_pairs)

    def pick(parts, at):
        chosen = parts[0]
        for step in range(1, stages):
            chosen = jnp.where(at == step, parts[step], chosen)
        return chosen

    in_hbm = lambda array: pltpu.with_memory_space_constraint(array, pltpu.HBM)
    own, entering, ending = [in_hbm(one) for one in own], in_hbm(entering), in_hbm(ending)
    *near, enter = load(0, own, entering)
    near += [swap_cores(weight) for weight in near]
    turn = list(load(stages - 1, own))
    turn += [swap_cores(weight) for weight in turn]
    if stages > 2:
        weights = own + [swap_cores(weight) for weight in own]
    flows, trunks, inners = [], [], []
    for step in range(stages - 1):
        flow, leave, trunk, inner_sum = run_stage(
            weights if step else near, step, True, False, step == 0, rows, sizes, enter
        )
        flows.append(flow)
        trunks.append(trunk)
        inners.append(inner_sum)
        enter = hop(leave, step)
    mirrored = stages == 2
    line = jax.ShapeDtypeStruct((rows, channels), jnp.bfloat16)
    outs = [line, jax.ShapeDtypeStruct((rows, inner), jnp.float32)] + [line, line] * mirrored
    ending, first_active, *known = pl.pallas_call(
        functools.partial(meanwhile_body, stages - 1, mirrored),
        out_shape=outs,
        in_specs=[VMEM, VMEM, HBM, HBM, VMEM],
        out_specs=[VMEM] * len(outs),
        scratch_shapes=[pltpu.SemaphoreType.DMA((3,))],
        compiler_params=PARAMS,
    )(turn[1], turn[3], entering, ending, leave)
    flow, upstreams, back_inners, leave = run_stage(
        turn, stages - 1, True, True, True, rows, sizes, enter, ending, first_active
    )
    flows.append(flow)
    upstreams, back_inners = [upstreams], [back_inners]
    upstream = hop(leave, 0)
    away = stages - 1 - stage
    side_flow = swap_cores(pick(flows, stage)[1])
    near_core = lambda first, second: jnp.where(core == 0, first, second)
    going = pick(flows, away)
    if mirrored:
        lifted = near_core(going[1, :, :channels], going[0, :, :channels])
        going = jnp.concatenate([lifted, going[0, :, channels:], going[1, :, channels:]], axis=1)
    far_flow = mirror(going)
    if mirrored:
        lifted, actives = far_flow[:, :channels], far_flow[:, channels:]
        far_flow = jnp.concatenate([near_core(known[1], lifted), actives[:, :inner]], axis=1)
        cross_flow = jnp.concatenate([near_core(lifted, known[1]), actives[:, inner:]], axis=1)
    else:
        far_flow, cross_flow = far_flow[0], far_flow[1]
    cross_flow = swap_cores(cross_flow)
    for step in range(stages - 2, -1, -1):
        outs = run_stage(
            weights if step else near,
            step,
            False,
            True,
            step == 0,
            rows,
            sizes,
            upstream,
            trunks[step],
            inners[step],
        )
        upstreams.insert(0, outs[0])
        back_inners.insert(0, outs[1])
        if step:
            upstream = hop(outs[2], stages - 1 - step)
    going = pick(upstreams, away)
    far_up = mirror(near_core(going[0], going[1]) if mirrored else going)
    far_inner = mirror(pick(back_inners, away))
    side_up = swap_cores(pick(upstreams, stage)[1])
    side_inner = swap_cores(pick(back_inners, stage)[1])
    if mirrored:
        top = jnp.where(stage == 0, leave, known[0])
        far_up, cross_up = near_core(far_up, top), near_core(top, far_up)
    else:
        far_up, cross_up = far_up[0], far_up[1]
    cross_up = swap_cores(cross_up)
    cross_inner = swap_cores(far_inner[1])
    far_inner = far_inner[0]

    chunk = channels // replicas
    fore = flows + [side_flow, far_flow, cross_flow]
    ups = upstreams + [side_up, far_up, cross_up]
    backs = back_inners + [side_inner, far_inner, cross_inner]
    halve = halve_rows if chunk % 128 == 0 and replicas >= 4 else halve_sums
    parts = halve(stages, replicas, chunk, sizes, rows, fore, ups, backs)
    return pl.pallas_call(
        finish_body,
        out_shape=jax.ShapeDtypeStruct((1, 2, chunk, inner), jnp.float32),
        in_specs=[VMEM] * 4,
        out_specs=VMEM,
        compiler_params=PARAMS,
    )(*parts)


def sums(count, chunk, inner):
    return [
        jax.ShapeDtypeStruct((count, chunk, inner), jnp.bfloat16),
        jax.ShapeDtypeStruct((count, chunk, inner), jnp.float32),
    ]


def exchange(shard, stages, replicas, first, second):
    pairs = []
    for p in range(2 * stages):
        for q in range(replicas):
            pairs.append((p * replicas + q, p * replicas + (q ^ (second if p % 2 else first))))
    return lax.ppermute(shard, AXES, pairs)


def halve_rows(stages, replicas, chunk, sizes, rows, fore, ups, backs):
    channels, inner = sizes
    shape = lambda *dims: jax.ShapeDtypeStruct(dims, jnp.bfloat16)
    half = shape(4 * rows, channels // 2)
    narrow = shape(4 * rows, inner)
    left, right, send = pl.pallas_call(
        functools.partial(early_body, stages, chunk),
        out_shape=[half, narrow, shape(4 * rows, channels // 2 + inner)],
        in_specs=[VMEM] * len(fore),
        out_specs=[VMEM] * 3,
        scratch_shapes=[pltpu.VMEM((4 * rows, channels), jnp.bfloat16)],
        compiler_params=PARAMS,
    )(*fore)
    came = exchange(send, stages, replicas, 1, 2)
    came_left, came_right = came[:, : channels // 2], came[:, channels // 2 :]
    back = pl.pallas_call(
        functools.partial(late_body, stages, 0),
        out_shape=narrow,
        in_specs=[VMEM] * len(backs),
        out_specs=VMEM,
        compiler_params=PARAMS,
    )(*backs)
    came_back = exchange(back, stages, replicas, 1, 2)
    up, up_send = pl.pallas_call(
        functools.partial(late_body, stages, chunk),
        out_shape=[half, half],
        in_specs=[VMEM] * len(ups),
        out_specs=[VMEM] * 2,
        scratch_shapes=[pltpu.VMEM((4 * rows, channels), jnp.bfloat16)],
        compiler_params=PARAMS,
    )(*ups)
    came_up = exchange(up_send, stages, replicas, 1, 2)
    parts = []
    for operands in ((left, came_left, back, came_back), (up, came_up, right, came_right)):
        count = replicas // 4
        send, keep = pl.pallas_call(
            half_gradient_body,
            out_shape=sums(count, chunk, inner),
            in_specs=[VMEM] * 4,
            out_specs=[VMEM] * 2,
            scratch_shapes=[pltpu.VMEM((channels // 2, inner), jnp.float32)],
            compiler_params=PARAMS,
        )(*operands)
        came = exchange(send, stages, replicas, 2, 1)
        for bit in range(2, replicas.bit_length() - 1):
            count //= 2
            send, keep = pl.pallas_call(
                functools.partial(next_body, bit),
                out_shape=sums(count, chunk, inner),
                in_specs=[VMEM] * 2,
                out_specs=[VMEM] * 2,
                compiler_params=PARAMS,
            )(keep, came)
            came = exchange(send, stages, replicas, 1 << bit, 1 << bit)
        parts += [keep, came]
    return parts


def halve_sums(stages, replicas, chunk, sizes, rows, fore, ups, backs):
    channels, inner = sizes
    wide, narrow = slice(0, channels), slice(channels, channels + inner)

    def of_flows(columns):
        def pick_parts(arrays):
            near = [flow.at[0, :, columns] for flow in arrays[:stages]]
            side, far, cross = arrays[stages : stages + 3]
            return near, [side.at[:, columns], far.at[:, columns], cross.at[:, columns]]

        return pick_parts

    def of_backs(arrays):
        near = [back.at[0] for back in arrays[stages + 3 : 2 * stages + 3]]
        side, far, cross = arrays[2 * stages + 3 : 2 * stages + 6]
        return near, [side, far, cross]

    plans = [halving_plan(replicas, turn) for turn in range(2)]
    streams = []
    for pick_left, pick_right, late, plan in (
        (of_backs, of_flows(narrow), ups, plans),
        (of_flows(wide), of_backs, backs, plans[::-1]),
    ):
        arrays = fore + late
        send, keep = pl.pallas_call(
            functools.partial(gradient_body, plan, pick_left, pick_right, len(arrays)),
            out_shape=sums(replicas // 2, chunk, inner),
            in_specs=[VMEM] * len(arrays),
            out_specs=[VMEM] * 2,
            scratch_shapes=[
                pltpu.VMEM((4 * rows, channels), jnp.bfloat16),
                pltpu.VMEM((4 * rows, inner), jnp.bfloat16),
                pltpu.VMEM((channels, inner), jnp.float32),
            ],
            compiler_params=PARAMS,
        )(*arrays)
        streams.append((plan, send, keep))
    for at in range(replicas.bit_length() - 1):
        half = replicas >> (at + 2)
        arrived = []
        for plan, send, keep in streams:
            pairs = []
            for p in range(2 * stages):
                for q in range(replicas):
                    pairs.append((p * replicas + q, p * replicas + (q ^ plan[p % 2][0][at])))
            arrived.append((plan, keep, lax.ppermute(send, AXES, pairs)))
        if half == 0:
            break
        streams = []
        for plan, keep, came in arrived:
            send, keep = pl.pallas_call(
                functools.partial(halve_body, plan, at + 1),
                out_shape=sums(half, chunk, inner),
                in_specs=[VMEM] * 2,
                out_specs=[VMEM] * 2,
                compiler_params=PARAMS,
            )(keep, came)
            streams.append((plan, send, keep))
    (_, keep_expand, came_expand), (_, keep_reduce, came_reduce) = arrived
    return keep_reduce, came_reduce, keep_expand, came_expand


def solution(mesh):
    return jax.shard_map(
        shards,
        mesh=mesh,
        in_specs=(
            P(None, None, "dp", None),
            P(None, None, "dp", None),
            P(None, "pipe", None, None),
            P(None, "pipe", None, None),
        ),
        out_specs=P("pipe", None, "dp", None),
        check_vma=False,
    )
```

profile of v0, /device:TPU:0, one launch (start us, length us, event | category | flops | bytes accessed | tf_op | source)
XLA Modules:
  0.0 47.5 jit_solution(16258043185196603980)
XLA Ops:
  0.0 1.2 %shard_map.46 = (bf16[1024,256]{1,0:T(8,128)(2,1)S(1)}, bf16[1024,256]{1,0:T(8,128)(2,1)S(1)}, bf16[32,1024]{1,0:T(8,128)(2,1)S(1)}) custom-call(bf16[2,1024,256]{2,1,0:T(8,128)(2,1)} %bitcast.20, bf16[2,1024,256]{2,1,0:T(8,128)(2,1)} %bitcast.22, bf16[2,2,32,1024]{3,2,1,0:T(8,128)(2,1)} %inputs.1), custom_call_target="tpu_custom_call" | custom-call | tf_op jit(solution)/shard_map/pallas_call | solution.py:68
  1.2 0.6 %collective-permute-start = (bf16[1024,256]{1,0:T(8,128)(2,1)S(1)}, bf16[1024,256]{1,0:T(8,128)(2,1)S(1)}, u32[]{:S(2)}, u32[]{:S(2)}) collective-permute-start(bf16[1024,256]{1,0:T(8,128)(2,1)S(1)} %get-tuple-element.37.refs_0_), channel_id=1, source_target_pairs={{0,8},{8,0},{16,24},{24,16},{1,9},{9,1},{17,25},{25,17},{2,10},{10... | collective-permute-start | bytes 1572872 | tf_op jit(solution)/shard_map/ppermute | solution.py:427
  1.8 0.1 collective-permute-start.1
  1.9 2.0 %shard_map.48 = (bf16[1024,256]{1,0:T(8,128)(2,1)}, bf16[1024,256]{1,0:T(8,128)(2,1)S(1)}) custom-call(bf16[2,1024,256]{2,1,0:T(8,128)(2,1)} %bitcast.21, bf16[2,1024,256]{2,1,0:T(8,128)(2,1)} %bitcast.23), custom_call_target="tpu_custom_call" | custom-call | tf_op jit(solution)/shard_map/pallas_call | solution.py:68
  3.9 0.5 %collective-permute-start.3 = (bf16[1024,256]{1,0:T(8,128)(2,1)S(1)}, bf16[1024,256]{1,0:T(8,128)(2,1)S(1)}, u32[]{:S(2)}, u32[]{:S(2)}) collective-permute-start(bf16[1024,256]{1,0:T(8,128)(2,1)S(1)} %get-tuple-element.42.expand_own.refs_1_), channel_id=1, source_target_pairs={{0,8},{8,0},{16,24},{24,16},{1,9},{9,1},{17,25},{25,17},{2,10},{10... | collective-permute-start | bytes 1572872 | tf_op jit(solution)/shard_map/ppermute | solution.py:427
  4.4 0.1 collective-permute-start.2
  4.5 0.0 collective-permute-done.refs_2_
  4.5 0.0 collective-permute-done.1.refs_3_
  4.5 1.8 %shard_map.47 = (bf16[2,32,1280]{2,1,0:T(8,128)(2,1)S(1)}, bf16[32,1024]{1,0:T(8,128)(2,1)}, bf16[2,32,1024]{2,1,0:T(8,128)(2,1)S(1)}, f32[2,32,256]{2,1,0:T(8,128)S(1)}) custom-call(bf16[1024,256]{1,0:T(8,128)(2,1)S(1)} %get-tuple-element.37.refs_0_, bf16[1024,256]{1,0:T(8,128)(2,1)S(1)} %get-tuple-element.38.refs_1_, ...), custom_call_target="tpu_custom_call" | custom-call | flops 67108864 | bytes 2097152 | tf_op jit(solution)/shard_map/pallas_call | solution.py:250
  6.3 2.9 %collective-permute-start.4 = (bf16[32,1024]{1,0:T(8,128)(2,1)}, bf16[32,1024]{1,0:T(8,128)(2,1)}, u32[]{:S(2)}, u32[]{:S(2)}) collective-permute-start(bf16[32,1024]{1,0:T(8,128)(2,1)} %get-tuple-element.43.leave), channel_id=1, source_target_pairs={{0,16},{16,0},{8,24},{24,8},{1,17},{17,1},{9,25},{25,9},{2,18},{18... | collective-permute-start | bytes 196616 | tf_op jit(solution)/shard_map/ppermute | solution.py:424
  9.2 2.1 %shard_map.49 = (bf16[32,1024]{1,0:T(8,128)(2,1)S(1)}, f32[32,256]{1,0:T(8,128)S(1)}, bf16[32,1024]{1,0:T(8,128)(2,1)S(1)}, bf16[32,1024]{1,0:T(8,128)(2,1)S(1)}) custom-call(bf16[1024,256]{1,0:T(8,128)(2,1)S(1)} %get-tuple-element.42.expand_own.refs_1_, bf16[1024,256]{1,0:T(8,128)(2,1)S(1)} %collective-permute-done.3.expand_other.refs_3_, ...), custom_call_target="tpu_custom_call" | custom-call | tf_op jit(solution)/shard_map/pallas_call | solution.py:458
  11.3 0.0 collective-permute-done.2.refs_2_
  11.3 0.6 %collective-permute-done.4.refs_4_ = bf16[32,1024]{1,0:T(8,128)(2,1)} collective-permute-done((bf16[32,1024]{1,0:T(8,128)(2,1)}, bf16[32,1024]{1,0:T(8,128)(2,1)}, u32[]{:S(2)}, u32[]{:S(2)}) %collective-permute-start.4) | collective-permute-done | bytes 65568 | tf_op jit(solution)/shard_map/ppermute | solution.py:424
  11.8 3.0 %shard_map.50 = (bf16[2,32,1280]{2,1,0:T(8,128)(2,1)S(1)}, bf16[2,32,1024]{2,1,0:T(8,128)(2,1)S(1)}, bf16[2,32,256]{2,1,0:T(8,128)(2,1)S(1)}, bf16[32,1024]{1,0:T(8,128)(2,1)S(1)}) custom-call(bf16[1024,256]{1,0:T(8,128)(2,1)} %get-tuple-element.41.refs_0_, bf16[1024,256]{1,0:T(8,128)(2,1)S(1)} %get-tuple-element.42.expand_own.refs_1_, ...), custom_call_target="tpu_custom_call" | custom-call | flops 134217728 | bytes 2097152 | tf_op jit(solution)/shard_map/pallas_call | solution.py:250
  14.9 2.0 %collective-permute-start.9 = (bf16[32,1024]{1,0:T(8,128)(2,1)S(1)}, bf16[32,1024]{1,0:T(8,128)(2,1)S(1)}, u32[]{:S(2)}, u32[]{:S(2)}) collective-permute-start(bf16[32,1024]{1,0:T(8,128)(2,1)S(1)} %get-tuple-element.50), channel_id=1, source_target_pairs={{0,16},{16,0},{8,24},{24,8},{1,17},{17,1},{9,25},{25,9},{2,18},{18... | collective-permute-start | bytes 196616 | tf_op jit(solution)/shard_map/ppermute | solution.py:424
  16.9 0.2 collective-permute-start.6
  17.1 0.1 collective-permute-start.5
  17.2 2.7 %collective-permute-done.9.refs_4_ = bf16[32,1024]{1,0:T(8,128)(2,1)S(1)} collective-permute-done((bf16[32,1024]{1,0:T(8,128)(2,1)S(1)}, bf16[32,1024]{1,0:T(8,128)(2,1)S(1)}, u32[]{:S(2)}, u32[]{:S(2)}) %collective-permute-start.9) | collective-permute-done | bytes 65568 | tf_op jit(solution)/shard_map/ppermute | solution.py:424
  19.9 0.9 %shard_map.52 = (bf16[2,32,1024]{2,1,0:T(8,128)(2,1)S(1)}, bf16[2,32,256]{2,1,0:T(8,128)(2,1)S(1)}) custom-call(bf16[1024,256]{1,0:T(8,128)(2,1)S(1)} %get-tuple-element.37.refs_0_, bf16[1024,256]{1,0:T(8,128)(2,1)S(1)} %get-tuple-element.38.refs_1_, bf16[1024,256]{1,0:T(8,128)(2,1)S(1)} %collective-permute-done.refs_2_, ...), custom_call_target="tpu_custom_call" | custom-call | flops 67108864 | bytes 2097152 | tf_op jit(solution)/shard_map/pallas_call | solution.py:250
  20.9 1.3 %collective-permute-start.17 = (bf16[32,1024]{1,0:T(8,128)(2,1)S(1)}, bf16[32,1024]{1,0:T(8,128)(2,1)S(1)}, u32[]{:S(2)}, u32[]{:S(2)}) collective-permute-start(bf16[32,1024]{1,0:T(8,128)(2,1)S(1)} %fusion.1), channel_id=1, source_target_pairs={{0,16},{8,24},{16,0},{24,8},{1,17},{9,25},{17,1},{25,9},{2,18},{10... | collective-permute-start | bytes 196616 | tf_op jit(solution)/shard_map/ppermute | solution.py:430
  22.2 0.8 %collective-permute-start.11 = (bf16[2,32,256]{2,1,0:T(8,128)(2,1)S(1)}, bf16[2,32,256]{2,1,0:T(8,128)(2,1)S(1)}, u32[]{:S(2)}, u32[]{:S(2)}) collective-permute-start(bf16[2,32,256]{2,1,0:T(8,128)(2,1)S(1)} %broadcast_select_fusion.7), channel_id=1, source_target_pairs={{0,16},{8,24},{16,0},{24,8},{1,17},{9,25},{17,1},{25,9},{2,18},{10... | collective-permute-start | bytes 98312 | tf_op jit(solution)/shard_map/ppermute | solution.py:430
  23.0 0.3 collective-permute-start.7
  23.3 1.9 %collective-permute-done.17 = bf16[32,1024]{1,0:T(8,128)(2,1)S(1)} collective-permute-done((bf16[32,1024]{1,0:T(8,128)(2,1)S(1)}, bf16[32,1024]{1,0:T(8,128)(2,1)S(1)}, u32[]{:S(2)}, u32[]{:S(2)}) %collective-permute-start.17) | collective-permute-done | bytes 65568 | tf_op jit(solution)/shard_map/ppermute | solution.py:430
  25.2 0.1 collective-permute-start.18
  25.3 0.0 collective-permute-done.5.refs_2_
  25.3 0.5 %collective-permute-start.10 = (bf16[32,256]{1,0:T(8,128)(2,1)S(1)}, bf16[32,256]{1,0:T(8,128)(2,1)S(1)}, u32[]{:S(2)}, u32[]{:S(2)}) collective-permute-start(bf16[32,256]{1,0:T(8,128)(2,1)S(1)} %fusion.4), channel_id=1, source_target_pairs={{0,8},{8,0},{16,24},{24,16},{1,9},{9,1},{17,25},{25,17},{2,10},{10... | collective-permute-start | bytes 49160 | tf_op jit(solution)/shard_map/ppermute | solution.py:427
  25.9 0.1 shard_map.51
  26.0 1.7 %collective-permute-start.8 = (bf16[128,768]{1,0:T(8,128)(2,1)S(1)}, bf16[128,768]{1,0:T(8,128)(2,1)S(1)}, u32[]{:S(2)}, u32[]{:S(2)}) collective-permute-start(bf16[128,768]{1,0:T(8,128)(2,1)S(1)} %get-tuple-element.49), channel_id=1, source_target_pairs={{0,1},{1,0},{2,3},{3,2},{4,5},{5,4},{6,7},{7,6},{8,10},{9,11},{10,... | collective-permute-start | bytes 589832 | tf_op jit(solution)/shard_map/ppermute | solution.py:545
  27.7 0.1 shard_map.56
  27.8 0.5 %collective-permute-start.19 = (bf16[128,512]{1,0:T(8,128)(2,1)S(1)}, bf16[128,512]{1,0:T(8,128)(2,1)S(1)}, u32[]{:S(2)}, u32[]{:S(2)}) collective-permute-start(bf16[128,512]{1,0:T(8,128)(2,1)S(1)} %get-tuple-element.63), channel_id=1, source_target_pairs={{0,1},{1,0},{2,3},{3,2},{4,5},{5,4},{6,7},{7,6},{8,10},{9,11},{10,... | collective-permute-start | bytes 393224 | tf_op jit(solution)/shard_map/ppermute | solution.py:545
  28.3 0.0 collective-permute-start.12
  28.4 0.0 collective-permute-done.10.refs_2_
  28.4 1.2 %collective-permute-done.12.refs_4_ = bf16[32,256]{1,0:T(8,128)(2,1)S(1)} collective-permute-done((bf16[32,256]{1,0:T(8,128)(2,1)S(1)}, bf16[32,256]{1,0:T(8,128)(2,1)S(1)}, u32[]{:S(2)}, u32[]{:S(2)}) %collective-permute-start.12) | collective-permute-done | bytes 16416 | tf_op jit(solution)/shard_map/ppermute | solution.py:427
  29.5 1.6 %collective-permute-start.13 = (bf16[128,256]{1,0:T(8,128)(2,1)S(1)}, bf16[128,256]{1,0:T(8,128)(2,1)S(1)}, u32[]{:S(2)}, u32[]{:S(2)}) collective-permute-start(bf16[128,256]{1,0:T(8,128)(2,1)S(1)} %shard_map.53.right), channel_id=1, source_target_pairs={{0,1},{1,0},{2,3},{3,2},{4,5},{5,4},{6,7},{7,6},{8,10},{9,11},{10,... | collective-permute-start | bytes 196616 | tf_op jit(solution)/shard_map/ppermute | solution.py:545
  31.1 0.6 %collective-permute-done.8 = bf16[128,768]{1,0:T(8,128)(2,1)S(1)} collective-permute-done((bf16[128,768]{1,0:T(8,128)(2,1)S(1)}, bf16[128,768]{1,0:T(8,128)(2,1)S(1)}, u32[]{:S(2)}, u32[]{:S(2)}) %collective-permute-start.8) | collective-permute-done | bytes 196640 | tf_op jit(solution)/shard_map/ppermute | solution.py:545
  31.7 1.4 %collective-permute-done.19.left_came = bf16[128,512]{1,0:T(8,128)(2,1)S(1)} collective-permute-done((bf16[128,512]{1,0:T(8,128)(2,1)S(1)}, bf16[128,512]{1,0:T(8,128)(2,1)S(1)}, u32[]{:S(2)}, u32[]{:S(2)}) %collective-permute-start.19) | collective-permute-done | bytes 131104 | tf_op jit(solution)/shard_map/ppermute | solution.py:545
  33.1 0.4 shard_map.57
  33.5 1.8 %collective-permute-start.20 = (bf16[2,128,256]{2,1,0:T(8,128)(2,1)S(1)}, bf16[2,128,256]{2,1,0:T(8,128)(2,1)S(1)}, u32[]{:S(2)}, u32[]{:S(2)}) collective-permute-start(bf16[2,128,256]{2,1,0:T(8,128)(2,1)S(1)} %get-tuple-element.66), channel_id=1, source_target_pairs={{0,2},{1,3},{2,0},{3,1},{4,6},{5,7},{6,4},{7,5},{8,9},{9,8},{10,11... | collective-permute-start | bytes 393224 | tf_op jit(solution)/shard_map/ppermute | solution.py:545
  35.3 0.0 collective-permute-done.13.right_came
  35.3 0.4 shard_map.54
  35.7 0.4 collective-permute-start.14
  36.1 2.4 %collective-permute-done.20.came = bf16[2,128,256]{2,1,0:T(8,128)(2,1)S(1)} collective-permute-done((bf16[2,128,256]{2,1,0:T(8,128)(2,1)S(1)}, bf16[2,128,256]{2,1,0:T(8,128)(2,1)S(1)}, u32[]{:S(2)}, u32[]{:S(2)}) %collective-permute-start.20) | collective-permute-done | bytes 131104 | tf_op jit(solution)/shard_map/ppermute | solution.py:545
  38.6 2.8 %collective-permute-start.21 = (bf16[1,128,256]{2,1,0:T(8,128)(2,1)S(1)}, bf16[1,128,256]{2,1,0:T(8,128)(2,1)S(1)}, u32[]{:S(2)}, u32[]{:S(2)}) collective-permute-start(bf16[1,128,256]{2,1,0:T(8,128)(2,1)S(1)} %get-tuple-element.68), channel_id=1, source_target_pairs={{0,4},{1,5},{2,6},{3,7},{4,0},{5,1},{6,2},{7,3},{8,12},{9,13},{10,... | collective-permute-start | bytes 196616 | tf_op jit(solution)/shard_map/ppermute | solution.py:545
  41.4 0.1 collective-permute-done.14.came
  41.5 2.6 %collective-permute-start.15 = (bf16[1,128,256]{2,1,0:T(8,128)(2,1)S(1)}, bf16[1,128,256]{2,1,0:T(8,128)(2,1)S(1)}, u32[]{:S(2)}, u32[]{:S(2)}) collective-permute-start(bf16[1,128,256]{2,1,0:T(8,128)(2,1)S(1)} %get-tuple-element.58), channel_id=1, source_target_pairs={{0,4},{1,5},{2,6},{3,7},{4,0},{5,1},{6,2},{7,3},{8,12},{9,13},{10,... | collective-permute-start | bytes 196616 | tf_op jit(solution)/shard_map/ppermute | solution.py:545
  44.1 1.4 %collective-permute-done.21.came_expand = bf16[1,128,256]{2,1,0:T(8,128)(2,1)S(1)} collective-permute-done((bf16[1,128,256]{2,1,0:T(8,128)(2,1)S(1)}, bf16[1,128,256]{2,1,0:T(8,128)(2,1)S(1)}, u32[]{:S(2)}, u32[]{:S(2)}) %collective-permute-start.21) | collective-permute-done | bytes 65568 | tf_op jit(solution)/shard_map/ppermute | solution.py:545
  45.5 1.2 %collective-permute-done.15.came_reduce = bf16[1,128,256]{2,1,0:T(8,128)(2,1)S(1)} collective-permute-done((bf16[1,128,256]{2,1,0:T(8,128)(2,1)S(1)}, bf16[1,128,256]{2,1,0:T(8,128)(2,1)S(1)}, u32[]{:S(2)}, u32[]{:S(2)}) %collective-permute-start.15) | collective-permute-done | bytes 65568 | tf_op jit(solution)/shard_map/ppermute | solution.py:545
  46.7 0.7 %shard_map.59 = f32[1,2,128,256]{3,2,1,0:T(8,128)} custom-call(f32[1,128,256]{2,1,0:T(8,128)S(1)} %get-tuple-element.57.keep_reduce, bf16[1,128,256]{2,1,0:T(8,128)(2,1)S(1)} %collective-permute-done.15.came_reduce, f32[1,128,256]{2,1,0:T(8,128)S(1)} %get-tuple-element.67.keep_expand, bf16[1,128,256]{2,1,0:T(8,128)(2,1)S(1)} %collective-permute-done.21.came_expand), custom_call_target="tpu_custom_call" | custom-call | tf_op jit(solution)/shard_map/pallas_call | solution.py:524
  (28 shorter events, 0.2 us)
Async XLA Ops:
  1.2 3.2 %collective-permute-start = (bf16[1024,256]{1,0:T(8,128)(2,1)S(1)}, bf16[1024,256]{1,0:T(8,128)(2,1)S(1)}, u32[]{:S(2)}, u32[]{:S(2)}) collective-permute-start(bf16[1024,256]{1,0:T(8,128)(2,1)S(1)} %get-tuple-element.37.refs_0_), channel_id=1, source_target_pairs={{0,8},{8,0},{16,24},{24,16},{1,9},{9,1},{17,25},{25,17},{2,10},{10... | collective-permute-start | bytes 1572872 | tf_op jit(solution)/shard_map/ppermute | solution.py:427
  1.8 2.7 %collective-permute-start.1 = (bf16[1024,256]{1,0:T(8,128)(2,1)S(1)}, bf16[1024,256]{1,0:T(8,128)(2,1)S(1)}, u32[]{:S(2)}, u32[]{:S(2)}) collective-permute-start(bf16[1024,256]{1,0:T(8,128)(2,1)S(1)} %get-tuple-element.38.refs_1_), channel_id=1, source_target_pairs={{0,8},{8,0},{16,24},{24,16},{1,9},{9,1},{17,25},{25,17},{2,10},{10... | collective-permute-start | bytes 1572872 | tf_op jit(solution)/shard_map/ppermute | solution.py:427
  3.9 5.3 %collective-permute-start.3 = (bf16[1024,256]{1,0:T(8,128)(2,1)S(1)}, bf16[1024,256]{1,0:T(8,128)(2,1)S(1)}, u32[]{:S(2)}, u32[]{:S(2)}) collective-permute-start(bf16[1024,256]{1,0:T(8,128)(2,1)S(1)} %get-tuple-element.42.expand_own.refs_1_), channel_id=1, source_target_pairs={{0,8},{8,0},{16,24},{24,16},{1,9},{9,1},{17,25},{25,17},{2,10},{10... | collective-permute-start | bytes 1572872 | tf_op jit(solution)/shard_map/ppermute | solution.py:427
  4.4 6.9 %collective-permute-start.2 = (bf16[1024,256]{1,0:T(8,128)(2,1)}, bf16[1024,256]{1,0:T(8,128)(2,1)}, u32[]{:S(2)}, u32[]{:S(2)}) collective-permute-start(bf16[1024,256]{1,0:T(8,128)(2,1)} %get-tuple-element.41.refs_0_), channel_id=1, source_target_pairs={{0,8},{8,0},{16,24},{24,16},{1,9},{9,1},{17,25},{25,17},{2,10},{10... | collective-permute-start | bytes 1572872 | tf_op jit(solution)/shard_map/ppermute | solution.py:427
  6.3 5.6 %collective-permute-start.4 = (bf16[32,1024]{1,0:T(8,128)(2,1)}, bf16[32,1024]{1,0:T(8,128)(2,1)}, u32[]{:S(2)}, u32[]{:S(2)}) collective-permute-start(bf16[32,1024]{1,0:T(8,128)(2,1)} %get-tuple-element.43.leave), channel_id=1, source_target_pairs={{0,16},{16,0},{8,24},{24,8},{1,17},{17,1},{9,25},{25,9},{2,18},{18... | collective-permute-start | bytes 196616 | tf_op jit(solution)/shard_map/ppermute | solution.py:424
  14.9 5.0 %collective-permute-start.9 = (bf16[32,1024]{1,0:T(8,128)(2,1)S(1)}, bf16[32,1024]{1,0:T(8,128)(2,1)S(1)}, u32[]{:S(2)}, u32[]{:S(2)}) collective-permute-start(bf16[32,1024]{1,0:T(8,128)(2,1)S(1)} %get-tuple-element.50), channel_id=1, source_target_pairs={{0,16},{16,0},{8,24},{24,8},{1,17},{17,1},{9,25},{25,9},{2,18},{18... | collective-permute-start | bytes 196616 | tf_op jit(solution)/shard_map/ppermute | solution.py:424
  16.9 6.0 %collective-permute-start.6 = (bf16[32,1536]{1,0:T(8,128)(2,1)S(1)}, bf16[32,1536]{1,0:T(8,128)(2,1)S(1)}, u32[]{:S(2)}, u32[]{:S(2)}) collective-permute-start(bf16[32,1536]{1,0:T(8,128)(2,1)S(1)} %pad_maximum_fusion), channel_id=1, source_target_pairs={{0,16},{8,24},{16,0},{24,8},{1,17},{9,25},{17,1},{25,9},{2,18},{10... | collective-permute-start | bytes 294920 | tf_op jit(solution)/shard_map/ppermute | solution.py:430
  17.1 8.2 %collective-permute-start.5 = (bf16[32,1280]{1,0:T(8,128)(2,1)S(1)}, bf16[32,1280]{1,0:T(8,128)(2,1)S(1)}, u32[]{:S(2)}, u32[]{:S(2)}) collective-permute-start(bf16[32,1280]{1,0:T(8,128)(2,1)S(1)} %fusion), channel_id=1, source_target_pairs={{0,8},{8,0},{16,24},{24,16},{1,9},{9,1},{17,25},{25,17},{2,10},{10... | collective-permute-start | bytes 245768 | tf_op jit(solution)/shard_map/ppermute | solution.py:427
  20.9 4.3 %collective-permute-start.17 = (bf16[32,1024]{1,0:T(8,128)(2,1)S(1)}, bf16[32,1024]{1,0:T(8,128)(2,1)S(1)}, u32[]{:S(2)}, u32[]{:S(2)}) collective-permute-start(bf16[32,1024]{1,0:T(8,128)(2,1)S(1)} %fusion.1), channel_id=1, source_target_pairs={{0,16},{8,24},{16,0},{24,8},{1,17},{9,25},{17,1},{25,9},{2,18},{10... | collective-permute-start | bytes 196616 | tf_op jit(solution)/shard_map/ppermute | solution.py:430
  22.2 5.5 %collective-permute-start.16 = (bf16[32,1024]{1,0:T(8,128)(2,1)S(1)}, bf16[32,1024]{1,0:T(8,128)(2,1)S(1)}, u32[]{:S(2)}, u32[]{:S(2)}) collective-permute-start(bf16[32,1024]{1,0:T(8,128)(2,1)S(1)} %fusion.2), channel_id=1, source_target_pairs={{0,8},{8,0},{16,24},{24,16},{1,9},{9,1},{17,25},{25,17},{2,10},{10... | collective-permute-start | bytes 196616 | tf_op jit(solution)/shard_map/ppermute | solution.py:427
  22.2 6.2 %collective-permute-start.11 = (bf16[2,32,256]{2,1,0:T(8,128)(2,1)S(1)}, bf16[2,32,256]{2,1,0:T(8,128)(2,1)S(1)}, u32[]{:S(2)}, u32[]{:S(2)}) collective-permute-start(bf16[2,32,256]{2,1,0:T(8,128)(2,1)S(1)} %broadcast_select_fusion.7), channel_id=1, source_target_pairs={{0,16},{8,24},{16,0},{24,8},{1,17},{9,25},{17,1},{25,9},{2,18},{10... | collective-permute-start | bytes 98312 | tf_op jit(solution)/shard_map/ppermute | solution.py:430
  23.0 2.9 %collective-permute-start.7 = (bf16[32,1280]{1,0:T(8,128)(2,1)S(1)}, bf16[32,1280]{1,0:T(8,128)(2,1)S(1)}, u32[]{:S(2)}, u32[]{:S(2)}) collective-permute-start(bf16[32,1280]{1,0:T(8,128)(2,1)S(1)} %pad_maximum_fusion.2), channel_id=1, source_target_pairs={{0,8},{8,0},{16,24},{24,16},{1,9},{9,1},{17,25},{25,17},{2,10},{10... | collective-permute-start | bytes 245768 | tf_op jit(solution)/shard_map/ppermute | solution.py:427
  25.2 2.5 %collective-permute-start.18 = (bf16[32,1024]{1,0:T(8,128)(2,1)S(1)}, bf16[32,1024]{1,0:T(8,128)(2,1)S(1)}, u32[]{:S(2)}, u32[]{:S(2)}) collective-permute-start(bf16[32,1024]{1,0:T(8,128)(2,1)S(1)} %get-tuple-element.69), channel_id=1, source_target_pairs={{0,8},{8,0},{16,24},{24,16},{1,9},{9,1},{17,25},{25,17},{2,10},{10... | collective-permute-start | bytes 196616 | tf_op jit(solution)/shard_map/ppermute | solution.py:427
  25.3 3.0 %collective-permute-start.10 = (bf16[32,256]{1,0:T(8,128)(2,1)S(1)}, bf16[32,256]{1,0:T(8,128)(2,1)S(1)}, u32[]{:S(2)}, u32[]{:S(2)}) collective-permute-start(bf16[32,256]{1,0:T(8,128)(2,1)S(1)} %fusion.4), channel_id=1, source_target_pairs={{0,8},{8,0},{16,24},{24,16},{1,9},{9,1},{17,25},{25,17},{2,10},{10... | collective-permute-start | bytes 49160 | tf_op jit(solution)/shard_map/ppermute | solution.py:427
  26.0 5.7 %collective-permute-start.8 = (bf16[128,768]{1,0:T(8,128)(2,1)S(1)}, bf16[128,768]{1,0:T(8,128)(2,1)S(1)}, u32[]{:S(2)}, u32[]{:S(2)}) collective-permute-start(bf16[128,768]{1,0:T(8,128)(2,1)S(1)} %get-tuple-element.49), channel_id=1, source_target_pairs={{0,1},{1,0},{2,3},{3,2},{4,5},{5,4},{6,7},{7,6},{8,10},{9,11},{10,... | collective-permute-start | bytes 589832 | tf_op jit(solution)/shard_map/ppermute | solution.py:545
  27.8 5.3 %collective-permute-start.19 = (bf16[128,512]{1,0:T(8,128)(2,1)S(1)}, bf16[128,512]{1,0:T(8,128)(2,1)S(1)}, u32[]{:S(2)}, u32[]{:S(2)}) collective-permute-start(bf16[128,512]{1,0:T(8,128)(2,1)S(1)} %get-tuple-element.63), channel_id=1, source_target_pairs={{0,1},{1,0},{2,3},{3,2},{4,5},{5,4},{6,7},{7,6},{8,10},{9,11},{10,... | collective-permute-start | bytes 393224 | tf_op jit(solution)/shard_map/ppermute | solution.py:545
  28.3 1.2 %collective-permute-start.12 = (bf16[32,256]{1,0:T(8,128)(2,1)S(1)}, bf16[32,256]{1,0:T(8,128)(2,1)S(1)}, u32[]{:S(2)}, u32[]{:S(2)}) collective-permute-start(bf16[32,256]{1,0:T(8,128)(2,1)S(1)} %get-tuple-element.77), channel_id=1, source_target_pairs={{0,8},{8,0},{16,24},{24,16},{1,9},{9,1},{17,25},{25,17},{2,10},{10... | collective-permute-start | bytes 49160 | tf_op jit(solution)/shard_map/ppermute | solution.py:427
  29.5 5.8 %collective-permute-start.13 = (bf16[128,256]{1,0:T(8,128)(2,1)S(1)}, bf16[128,256]{1,0:T(8,128)(2,1)S(1)}, u32[]{:S(2)}, u32[]{:S(2)}) collective-permute-start(bf16[128,256]{1,0:T(8,128)(2,1)S(1)} %shard_map.53.right), channel_id=1, source_target_pairs={{0,1},{1,0},{2,3},{3,2},{4,5},{5,4},{6,7},{7,6},{8,10},{9,11},{10,... | collective-permute-start | bytes 196616 | tf_op jit(solution)/shard_map/ppermute | solution.py:545
  33.5 5.0 %collective-permute-start.20 = (bf16[2,128,256]{2,1,0:T(8,128)(2,1)S(1)}, bf16[2,128,256]{2,1,0:T(8,128)(2,1)S(1)}, u32[]{:S(2)}, u32[]{:S(2)}) collective-permute-start(bf16[2,128,256]{2,1,0:T(8,128)(2,1)S(1)} %get-tuple-element.66), channel_id=1, source_target_pairs={{0,2},{1,3},{2,0},{3,1},{4,6},{5,7},{6,4},{7,5},{8,9},{9,8},{10,11... | collective-permute-start | bytes 393224 | tf_op jit(solution)/shard_map/ppermute | solution.py:545
  35.7 5.7 %collective-permute-start.14 = (bf16[2,128,256]{2,1,0:T(8,128)(2,1)S(1)}, bf16[2,128,256]{2,1,0:T(8,128)(2,1)S(1)}, u32[]{:S(2)}, u32[]{:S(2)}) collective-permute-start(bf16[2,128,256]{2,1,0:T(8,128)(2,1)S(1)} %get-tuple-element.56), channel_id=1, source_target_pairs={{0,2},{1,3},{2,0},{3,1},{4,6},{5,7},{6,4},{7,5},{8,9},{9,8},{10,11... | collective-permute-start | bytes 393224 | tf_op jit(solution)/shard_map/ppermute | solution.py:545
  38.6 6.9 %collective-permute-start.21 = (bf16[1,128,256]{2,1,0:T(8,128)(2,1)S(1)}, bf16[1,128,256]{2,1,0:T(8,128)(2,1)S(1)}, u32[]{:S(2)}, u32[]{:S(2)}) collective-permute-start(bf16[1,128,256]{2,1,0:T(8,128)(2,1)S(1)} %get-tuple-element.68), channel_id=1, source_target_pairs={{0,4},{1,5},{2,6},{3,7},{4,0},{5,1},{6,2},{7,3},{8,12},{9,13},{10,... | collective-permute-start | bytes 196616 | tf_op jit(solution)/shard_map/ppermute | solution.py:545
  41.5 5.2 %collective-permute-start.15 = (bf16[1,128,256]{2,1,0:T(8,128)(2,1)S(1)}, bf16[1,128,256]{2,1,0:T(8,128)(2,1)S(1)}, u32[]{:S(2)}, u32[]{:S(2)}) collective-permute-start(bf16[1,128,256]{2,1,0:T(8,128)(2,1)S(1)} %get-tuple-element.58), channel_id=1, source_target_pairs={{0,4},{1,5},{2,6},{3,7},{4,0},{5,1},{6,2},{7,3},{8,12},{9,13},{10,... | collective-permute-start | bytes 196616 | tf_op jit(solution)/shard_map/ppermute | solution.py:545
where the time goes:
time: 47.7 us; the launch traced here: 47.5 us
  starting transfers between devices  20.7 us (43%)
  waiting for transfers between devices  13.6 us (29%)
  Pallas kernels  12.8 us (27%)
    ppermute x7, starting transfers between devices, exchange(): return lax.ppermute(shard, AXES, pairs)  11.3 us
    ppermute x7, waiting for transfers between devices, exchange(): return lax.ppermute(shard, AXES, pairs)  7.21 us
    pallas_call x3, Pallas kernels, run_stage(): pl.pallas_call(functools.partial(stage_body, step, forward, backward, las...  5.71 us
    ppermute x2, starting transfers between devices, hop(): return lax.ppermute(shard, 'pipe', pairs)  4.91 us
    ppermute x2, waiting for transfers between devices, hop(): return lax.ppermute(shard, 'pipe', pairs)  3.27 us
    pallas_call x2, Pallas kernels, load(): pl.pallas_call(functools.partial(load_body, step), out_shape=outs, in_spe...  3.24 us
    ppermute x3, starting transfers between devices, mirror(): return lax.ppermute(shard, 'pipe', mirror_pairs)  2.25 us
    ppermute x10, starting transfers between devices, swap_cores(): return lax.ppermute(shard, 'pipe', core_pairs)  2.2 us
  transfers between devices with their start and end apart: 22, of which 10 were waited for; matrix products, arithmetic and copies ran while one was open for 0% of the time, Pallas kernels for 16%

commit v1 on v0

--- a/solution.py
+++ b/solution.py
@@ -429,10 +429,15 @@
     def mirror(shard):
         return lax.ppermute(shard, "pipe", mirror_pairs)
 
-    def pick(parts, at):
+    at_stage = [stage == step for step in range(stages)]
+    first_core = core == 0
+    at_stage, first_core, entering = lax.optimization_barrier((at_stage, first_core, entering))
+
+    def pick(parts, mirrored_stage=False):
+        tests = at_stage[::-1] if mirrored_stage else at_stage
         chosen = parts[0]
-        for step in range(1, stages):
-            chosen = jnp.where(at == step, parts[step], chosen)
+        for test, part in zip(tests[1:], parts[1:]):
+            chosen = jnp.where(test, part, chosen)
         return chosen
 
     in_hbm = lambda array: pltpu.with_memory_space_constraint(array, pltpu.HBM)
@@ -469,10 +474,9 @@
     flows.append(flow)
     upstreams, back_inners = [upstreams], [back_inners]
     upstream = hop(leave, 0)
-    away = stages - 1 - stage
-    side_flow = swap_cores(pick(flows, stage)[1])
-    near_core = lambda first, second: jnp.where(core == 0, first, second)
-    going = pick(flows, away)
+    side_flow = swap_cores(pick(flows)[1])
+    near_core = lambda first, second: jnp.where(first_core, first, second)
+    going = pick(flows, True)
     if mirrored:
         lifted = near_core(going[1, :, :channels], going[0, :, :channels])
         going = jnp.concatenate([lifted, going[0, :, channels:], going[1, :, channels:]], axis=1)
@@ -501,13 +505,13 @@
         back_inners.insert(0, outs[1])
         if step:
             upstream = hop(outs[2], stages - 1 - step)
-    going = pick(upstreams, away)
+    going = pick(upstreams, True)
     far_up = mirror(near_core(going[0], going[1]) if mirrored else going)
-    far_inner = mirror(pick(back_inners, away))
-    side_up = swap_cores(pick(upstreams, stage)[1])
-    side_inner = swap_cores(pick(back_inners, stage)[1])
+    far_inner = mirror(pick(back_inners, True))
+    side_up = swap_cores(pick(upstreams)[1])
+    side_inner = swap_cores(pick(back_inners)[1])
     if mirrored:
-        top = jnp.where(stage == 0, leave, known[0])
+        top = jnp.where(at_stage[0], leave, known[0])
         far_up, cross_up = near_core(far_up, top), near_core(top, far_up)
     else:
         far_up, cross_up = far_up[0], far_up[1]
@@ -578,7 +582,8 @@
     )(*ups)
     came_up = exchange(up_send, stages, replicas, 1, 2)
     parts = []
-    for operands in ((left, came_left, back, came_back), (up, came_up, right, came_right)):
+    streams = ((left, came_left, back, came_back), (up, came_up, right, came_right))
+    for operands in streams:
         count = replicas // 4
         send, keep = pl.pallas_call(
             half_gradient_body,

time: 47.7 us -> 46.9 us (0.983)
  Pallas kernels: 12.8 us -> 9.29 us
  waiting for transfers between devices: 13.6 us -> 16.3 us
    ppermute x3, waiting for transfers between devices: 1.91 us -> 3.86 us  [mirror(): return lax.ppermute(shard, 'pipe', mirror_pairs)]
    pallas_call x3, Pallas kernels: 5.71 us -> 3.85 us  [run_stage(): pl.pallas_call(functools.partial(stage_body, step, forward, backward, las...]
    pallas_call x1, Pallas kernels: 2.07 us -> 1.2 us  [shards(): pl.pallas_call(functools.partial(meanwhile_body, stages - 1, mirrored), o...]
    pallas_call x2, Pallas kernels: 3.24 us -> 2.44 us  [load(): pl.pallas_call(functools.partial(load_body, step), out_shape=outs, in_spe...]
    ppermute x7, starting transfers between devices: 11.3 us -> 10.6 us  [exchange(): return lax.ppermute(shard, AXES, pairs)]
    ppermute x3, starting transfers between devices: 2.25 us -> 2.93 us  [mirror(): return lax.ppermute(shard, 'pipe', mirror_pairs)]
  transfers between devices with their start and end apart: 22 -> 22, of which waited for: 10 -> 11; matrix products, arithmetic and copies ran while one was open for 0% -> 0% of each run, Pallas kernels for 16% -> 12%
where the time goes in v1:
time: 46.9 us; the launch traced here: 46.7 us
  starting transfers between devices  20.7 us (44%)
  waiting for transfers between devices  16.3 us (35%)
  Pallas kernels  9.29 us (20%)
    ppermute x7, starting transfers between devices, exchange(): return lax.ppermute(shard, AXES, pairs)  10.6 us
    ppermute x7, waiting for transfers between devices, exchange(): return lax.ppermute(shard, AXES, pairs)  7.59 us
    ppermute x2, starting transfers between devices, hop(): return lax.ppermute(shard, 'pipe', pairs)  4.81 us
    ppermute x3, waiting for transfers between devices, mirror(): return lax.ppermute(shard, 'pipe', mirror_pairs)  3.86 us
    pallas_call x3, Pallas kernels, run_stage(): pl.pallas_call(functools.partial(stage_body, step, forward, backward, las...  3.85 us
    ppermute x2, waiting for transfers between devices, hop(): return lax.ppermute(shard, 'pipe', pairs)  3.23 us
    ppermute x3, starting transfers between devices, mirror(): return lax.ppermute(shard, 'pipe', mirror_pairs)  2.93 us
    pallas_call x2, Pallas kernels, load(): pl.pallas_call(functools.partial(load_body, step), out_shape=outs, in_spe...  2.44 us
  transfers between devices with their start and end apart: 22, of which 11 were waited for; matrix products, arithmetic and copies ran while one was open for 0% of the time, Pallas kernels for 12%

profile of v1, /device:TPU:0, one launch (start us, length us, event | category | flops | bytes accessed | tf_op | source)
XLA Modules:
  0.0 46.7 jit_solution(10834021635844044755)
XLA Ops:
  0.0 1.2 %shard_map.46 = (bf16[1024,256]{1,0:T(8,128)(2,1)S(1)}, bf16[1024,256]{1,0:T(8,128)(2,1)S(1)}, bf16[32,1024]{1,0:T(8,128)(2,1)S(1)}) custom-call(bf16[2,1024,256]{2,1,0:T(8,128)(2,1)} %bitcast.20, bf16[2,1024,256]{2,1,0:T(8,128)(2,1)} %bitcast.22, bf16[2,2,32,1024]{3,2,1,0:T(8,128)(2,1)} %inputs), custom_call_target="tpu_custom_call" | custom-call | tf_op jit(solution)/shard_map/pallas_call | solution.py:68
  1.2 0.6 %collective-permute-start = (bf16[1024,256]{1,0:T(8,128)(2,1)S(1)}, bf16[1024,256]{1,0:T(8,128)(2,1)S(1)}, u32[]{:S(2)}, u32[]{:S(2)}) collective-permute-start(bf16[1024,256]{1,0:T(8,128)(2,1)S(1)} %get-tuple-element.42.refs_0_), channel_id=1, source_target_pairs={{0,8},{8,0},{16,24},{24,16},{1,9},{9,1},{17,25},{25,17},{2,10},{10... | collective-permute-start | bytes 1572872 | tf_op jit(solution)/shard_map/ppermute | solution.py:427
  1.8 0.1 collective-permute-start.1
  1.9 1.2 %shard_map.48 = (bf16[1024,256]{1,0:T(8,128)(2,1)S(1)}, bf16[1024,256]{1,0:T(8,128)(2,1)S(1)}) custom-call(bf16[2,1024,256]{2,1,0:T(8,128)(2,1)} %bitcast.21, bf16[2,1024,256]{2,1,0:T(8,128)(2,1)} %bitcast.23), custom_call_target="tpu_custom_call" | custom-call | tf_op jit(solution)/shard_map/pallas_call | solution.py:68
  3.1 0.5 %collective-permute-start.3 = (bf16[1024,256]{1,0:T(8,128)(2,1)S(1)}, bf16[1024,256]{1,0:T(8,128)(2,1)S(1)}, u32[]{:S(2)}, u32[]{:S(2)}) collective-permute-start(bf16[1024,256]{1,0:T(8,128)(2,1)S(1)} %get-tuple-element.47.expand_own.refs_1_), channel_id=1, source_target_pairs={{0,8},{8,0},{16,24},{24,16},{1,9},{9,1},{17,25},{25,17},{2,10},{10... | collective-permute-start | bytes 1572872 | tf_op jit(solution)/shard_map/ppermute | solution.py:427
  3.6 0.1 collective-permute-start.2
  3.7 0.4 collective-permute-done.1.refs_3_
  4.1 1.2 %shard_map.47 = (bf16[2,32,1280]{2,1,0:T(8,128)(2,1)S(1)}, bf16[32,1024]{1,0:T(8,128)(2,1)S(1)}, bf16[2,32,1024]{2,1,0:T(8,128)(2,1)S(1)}, f32[2,32,256]{2,1,0:T(8,128)S(1)}) custom-call(bf16[1024,256]{1,0:T(8,128)(2,1)S(1)} %get-tuple-element.42.refs_0_, bf16[1024,256]{1,0:T(8,128)(2,1)S(1)} %get-tuple-element.43.refs_1_, ...), custom_call_target="tpu_custom_call" | custom-call | flops 67108864 | bytes 2097152 | tf_op jit(solution)/shard_map/pallas_call | solution.py:250
  5.2 2.9 %collective-permute-start.4 = (bf16[32,1024]{1,0:T(8,128)(2,1)S(1)}, bf16[32,1024]{1,0:T(8,128)(2,1)S(1)}, u32[]{:S(2)}, u32[]{:S(2)}) collective-permute-start(bf16[32,1024]{1,0:T(8,128)(2,1)S(1)} %get-tuple-element.48.leave), channel_id=1, source_target_pairs={{0,16},{16,0},{8,24},{24,8},{1,17},{17,1},{9,25},{25,9},{2,18},{18... | collective-permute-start | bytes 196616 | tf_op jit(solution)/shard_map/ppermute | solution.py:424
  8.1 1.2 %shard_map.49 = (bf16[32,1024]{1,0:T(8,128)(2,1)S(1)}, f32[32,256]{1,0:T(8,128)S(1)}, bf16[32,1024]{1,0:T(8,128)(2,1)S(1)}, bf16[32,1024]{1,0:T(8,128)(2,1)S(1)}) custom-call(bf16[1024,256]{1,0:T(8,128)(2,1)S(1)} %get-tuple-element.47.expand_own.refs_1_, bf16[1024,256]{1,0:T(8,128)(2,1)S(1)} %collective-permute-done.3.expand_other.refs_3_, ...), custom_call_target="tpu_custom_call" | custom-call | tf_op jit(solution)/shard_map/pallas_call | solution.py:463
  9.3 1.2 %collective-permute-done.4.refs_4_ = bf16[32,1024]{1,0:T(8,128)(2,1)S(1)} collective-permute-done((bf16[32,1024]{1,0:T(8,128)(2,1)S(1)}, bf16[32,1024]{1,0:T(8,128)(2,1)S(1)}, u32[]{:S(2)}, u32[]{:S(2)}) %collective-permute-start.4) | collective-permute-done | bytes 65568 | tf_op jit(solution)/shard_map/ppermute | solution.py:424
  10.5 1.8 %shard_map.50 = (bf16[2,32,1280]{2,1,0:T(8,128)(2,1)S(1)}, bf16[2,32,1024]{2,1,0:T(8,128)(2,1)S(1)}, bf16[2,32,256]{2,1,0:T(8,128)(2,1)S(1)}, bf16[32,1024]{1,0:T(8,128)(2,1)S(1)}) custom-call(bf16[1024,256]{1,0:T(8,128)(2,1)S(1)} %get-tuple-element.46.refs_0_, bf16[1024,256]{1,0:T(8,128)(2,1)S(1)} %get-tuple-element.47.expand_own.refs_1_, ...), custom_call_target="tpu_custom_call" | custom-call | flops 134217728 | bytes 2097152 | tf_op jit(solution)/shard_map/pallas_call | solution.py:250
  12.3 1.9 %collective-permute-start.9 = (bf16[32,1024]{1,0:T(8,128)(2,1)S(1)}, bf16[32,1024]{1,0:T(8,128)(2,1)S(1)}, u32[]{:S(2)}, u32[]{:S(2)}) collective-permute-start(bf16[32,1024]{1,0:T(8,128)(2,1)S(1)} %get-tuple-element.58), channel_id=1, source_target_pairs={{0,16},{16,0},{8,24},{24,8},{1,17},{17,1},{9,25},{25,9},{2,18},{18... | collective-permute-start | bytes 196616 | tf_op jit(solution)/shard_map/ppermute | solution.py:424
  14.3 0.1 collective-permute-start.5
  14.5 0.2 collective-permute-start.6
  14.7 2.1 %collective-permute-done.9.refs_4_ = bf16[32,1024]{1,0:T(8,128)(2,1)S(1)} collective-permute-done((bf16[32,1024]{1,0:T(8,128)(2,1)S(1)}, bf16[32,1024]{1,0:T(8,128)(2,1)S(1)}, u32[]{:S(2)}, u32[]{:S(2)}) %collective-permute-start.9) | collective-permute-done | bytes 65568 | tf_op jit(solution)/shard_map/ppermute | solution.py:424
  16.7 0.9 %shard_map.52 = (bf16[2,32,1024]{2,1,0:T(8,128)(2,1)S(1)}, bf16[2,32,256]{2,1,0:T(8,128)(2,1)S(1)}) custom-call(bf16[1024,256]{1,0:T(8,128)(2,1)S(1)} %get-tuple-element.42.refs_0_, bf16[1024,256]{1,0:T(8,128)(2,1)S(1)} %get-tuple-element.43.refs_1_, bf16[1024,256]{1,0:T(8,128)(2,1)S(1)} %collective-permute-done.refs_2_, ...), custom_call_target="tpu_custom_call" | custom-call | flops 67108864 | bytes 2097152 | tf_op jit(solution)/shard_map/pallas_call | solution.py:250
  17.7 2.5 %collective-permute-start.11 = (bf16[2,32,256]{2,1,0:T(8,128)(2,1)S(1)}, bf16[2,32,256]{2,1,0:T(8,128)(2,1)S(1)}, u32[]{:S(2)}, u32[]{:S(2)}) collective-permute-start(bf16[2,32,256]{2,1,0:T(8,128)(2,1)S(1)} %broadcast_select_fusion.7), channel_id=1, source_target_pairs={{0,16},{8,24},{16,0},{24,8},{1,17},{9,25},{17,1},{25,9},{2,18},{10... | collective-permute-start | bytes 98312 | tf_op jit(solution)/shard_map/ppermute | solution.py:430
  20.2 0.2 collective-permute-start.17
  20.4 0.0 collective-permute-done.6
  20.4 0.5 %collective-permute-start.7 = (bf16[32,1280]{1,0:T(8,128)(2,1)S(1)}, bf16[32,1280]{1,0:T(8,128)(2,1)S(1)}, u32[]{:S(2)}, u32[]{:S(2)}) collective-permute-start(bf16[32,1280]{1,0:T(8,128)(2,1)S(1)} %pad_maximum_fusion.2), channel_id=1, source_target_pairs={{0,8},{8,0},{16,24},{24,16},{1,9},{9,1},{17,25},{25,17},{2,10},{10... | collective-permute-start | bytes 245768 | tf_op jit(solution)/shard_map/ppermute | solution.py:427
  20.9 3.9 %collective-permute-done.17 = bf16[32,1024]{1,0:T(8,128)(2,1)S(1)} collective-permute-done((bf16[32,1024]{1,0:T(8,128)(2,1)S(1)}, bf16[32,1024]{1,0:T(8,128)(2,1)S(1)}, u32[]{:S(2)}, u32[]{:S(2)}) %collective-permute-start.17) | collective-permute-done | bytes 65568 | tf_op jit(solution)/shard_map/ppermute | solution.py:430
  24.8 0.1 collective-permute-start.18
  24.9 0.5 %collective-permute-start.10 = (bf16[32,256]{1,0:T(8,128)(2,1)S(1)}, bf16[32,256]{1,0:T(8,128)(2,1)S(1)}, u32[]{:S(2)}, u32[]{:S(2)}) collective-permute-start(bf16[32,256]{1,0:T(8,128)(2,1)S(1)} %fusion.4), channel_id=1, source_target_pairs={{0,8},{8,0},{16,24},{24,16},{1,9},{9,1},{17,25},{25,17},{2,10},{10... | collective-permute-start | bytes 49160 | tf_op jit(solution)/shard_map/ppermute | solution.py:427
  25.5 0.0 collective-permute-done.7.refs_4_
  25.5 0.1 shard_map.51
  25.6 1.3 %collective-permute-start.8 = (bf16[128,768]{1,0:T(8,128)(2,1)S(1)}, bf16[128,768]{1,0:T(8,128)(2,1)S(1)}, u32[]{:S(2)}, u32[]{:S(2)}) collective-permute-start(bf16[128,768]{1,0:T(8,128)(2,1)S(1)} %get-tuple-element.57), channel_id=1, source_target_pairs={{0,1},{1,0},{2,3},{3,2},{4,5},{5,4},{6,7},{7,6},{8,10},{9,11},{10,... | collective-permute-start | bytes 589832 | tf_op jit(solution)/shard_map/ppermute | solution.py:549
  26.9 0.0 collective-permute-done.16.refs_2_
  26.9 0.0 collective-permute-done.18.refs_4_
  26.9 0.1 shard_map.56
  27.0 0.8 %collective-permute-start.19 = (bf16[128,512]{1,0:T(8,128)(2,1)S(1)}, bf16[128,512]{1,0:T(8,128)(2,1)S(1)}, u32[]{:S(2)}, u32[]{:S(2)}) collective-permute-start(bf16[128,512]{1,0:T(8,128)(2,1)S(1)} %get-tuple-element.71), channel_id=1, source_target_pairs={{0,1},{1,0},{2,3},{3,2},{4,5},{5,4},{6,7},{7,6},{8,10},{9,11},{10,... | collective-permute-start | bytes 393224 | tf_op jit(solution)/shard_map/ppermute | solution.py:549
  27.9 0.0 collective-permute-done.10.refs_2_
  27.9 1.2 %collective-permute-done.12.refs_4_ = bf16[32,256]{1,0:T(8,128)(2,1)S(1)} collective-permute-done((bf16[32,256]{1,0:T(8,128)(2,1)S(1)}, bf16[32,256]{1,0:T(8,128)(2,1)S(1)}, u32[]{:S(2)}, u32[]{:S(2)}) %collective-permute-start.12) | collective-permute-done | bytes 16416 | tf_op jit(solution)/shard_map/ppermute | solution.py:427
  29.1 1.3 %collective-permute-start.13 = (bf16[128,256]{1,0:T(8,128)(2,1)S(1)}, bf16[128,256]{1,0:T(8,128)(2,1)S(1)}, u32[]{:S(2)}, u32[]{:S(2)}) collective-permute-start(bf16[128,256]{1,0:T(8,128)(2,1)S(1)} %shard_map.53.right), channel_id=1, source_target_pairs={{0,1},{1,0},{2,3},{3,2},{4,5},{5,4},{6,7},{7,6},{8,10},{9,11},{10,... | collective-permute-start | bytes 196616 | tf_op jit(solution)/shard_map/ppermute | solution.py:549
  30.3 1.0 %collective-permute-done.8 = bf16[128,768]{1,0:T(8,128)(2,1)S(1)} collective-permute-done((bf16[128,768]{1,0:T(8,128)(2,1)S(1)}, bf16[128,768]{1,0:T(8,128)(2,1)S(1)}, u32[]{:S(2)}, u32[]{:S(2)}) %collective-permute-start.8) | collective-permute-done | bytes 196640 | tf_op jit(solution)/shard_map/ppermute | solution.py:549
  31.3 1.4 %collective-permute-done.19.left_came = bf16[128,512]{1,0:T(8,128)(2,1)S(1)} collective-permute-done((bf16[128,512]{1,0:T(8,128)(2,1)S(1)}, bf16[128,512]{1,0:T(8,128)(2,1)S(1)}, u32[]{:S(2)}, u32[]{:S(2)}) %collective-permute-start.19) | collective-permute-done | bytes 131104 | tf_op jit(solution)/shard_map/ppermute | solution.py:549
  32.7 0.4 shard_map.57
  33.1 1.4 %collective-permute-start.20 = (bf16[2,128,256]{2,1,0:T(8,128)(2,1)S(1)}, bf16[2,128,256]{2,1,0:T(8,128)(2,1)S(1)}, u32[]{:S(2)}, u32[]{:S(2)}) collective-permute-start(bf16[2,128,256]{2,1,0:T(8,128)(2,1)S(1)} %get-tuple-element.74), channel_id=1, source_target_pairs={{0,2},{1,3},{2,0},{3,1},{4,6},{5,7},{6,4},{7,5},{8,9},{9,8},{10,11... | collective-permute-start | bytes 393224 | tf_op jit(solution)/shard_map/ppermute | solution.py:549
  34.6 0.0 collective-permute-done.13.right_came
  34.6 0.4 shard_map.54
  35.0 0.8 %collective-permute-start.14 = (bf16[2,128,256]{2,1,0:T(8,128)(2,1)S(1)}, bf16[2,128,256]{2,1,0:T(8,128)(2,1)S(1)}, u32[]{:S(2)}, u32[]{:S(2)}) collective-permute-start(bf16[2,128,256]{2,1,0:T(8,128)(2,1)S(1)} %get-tuple-element.64), channel_id=1, source_target_pairs={{0,2},{1,3},{2,0},{3,1},{4,6},{5,7},{6,4},{7,5},{8,9},{9,8},{10,11... | collective-permute-start | bytes 393224 | tf_op jit(solution)/shard_map/ppermute | solution.py:549
  35.7 2.4 %collective-permute-done.20.came = bf16[2,128,256]{2,1,0:T(8,128)(2,1)S(1)} collective-permute-done((bf16[2,128,256]{2,1,0:T(8,128)(2,1)S(1)}, bf16[2,128,256]{2,1,0:T(8,128)(2,1)S(1)}, u32[]{:S(2)}, u32[]{:S(2)}) %collective-permute-start.20) | collective-permute-done | bytes 131104 | tf_op jit(solution)/shard_map/ppermute | solution.py:549
  38.2 2.4 %collective-permute-start.21 = (bf16[1,128,256]{2,1,0:T(8,128)(2,1)S(1)}, bf16[1,128,256]{2,1,0:T(8,128)(2,1)S(1)}, u32[]{:S(2)}, u32[]{:S(2)}) collective-permute-start(bf16[1,128,256]{2,1,0:T(8,128)(2,1)S(1)} %get-tuple-element.76), channel_id=1, source_target_pairs={{0,4},{1,5},{2,6},{3,7},{4,0},{5,1},{6,2},{7,3},{8,12},{9,13},{10,... | collective-permute-start | bytes 196616 | tf_op jit(solution)/shard_map/ppermute | solution.py:549
  40.6 0.1 collective-permute-done.14.came
  40.8 2.6 %collective-permute-start.15 = (bf16[1,128,256]{2,1,0:T(8,128)(2,1)S(1)}, bf16[1,128,256]{2,1,0:T(8,128)(2,1)S(1)}, u32[]{:S(2)}, u32[]{:S(2)}) collective-permute-start(bf16[1,128,256]{2,1,0:T(8,128)(2,1)S(1)} %get-tuple-element.66), channel_id=1, source_target_pairs={{0,4},{1,5},{2,6},{3,7},{4,0},{5,1},{6,2},{7,3},{8,12},{9,13},{10,... | collective-permute-start | bytes 196616 | tf_op jit(solution)/shard_map/ppermute | solution.py:549
  43.3 1.5 %collective-permute-done.21.came_expand = bf16[1,128,256]{2,1,0:T(8,128)(2,1)S(1)} collective-permute-done((bf16[1,128,256]{2,1,0:T(8,128)(2,1)S(1)}, bf16[1,128,256]{2,1,0:T(8,128)(2,1)S(1)}, u32[]{:S(2)}, u32[]{:S(2)}) %collective-permute-start.21) | collective-permute-done | bytes 65568 | tf_op jit(solution)/shard_map/ppermute | solution.py:549
  44.8 1.1 %collective-permute-done.15.came_reduce = bf16[1,128,256]{2,1,0:T(8,128)(2,1)S(1)} collective-permute-done((bf16[1,128,256]{2,1,0:T(8,128)(2,1)S(1)}, bf16[1,128,256]{2,1,0:T(8,128)(2,1)S(1)}, u32[]{:S(2)}, u32[]{:S(2)}) %collective-permute-start.15) | collective-permute-done | bytes 65568 | tf_op jit(solution)/shard_map/ppermute | solution.py:549
  46.0 0.7 %shard_map.59 = f32[1,2,128,256]{3,2,1,0:T(8,128)} custom-call(f32[1,128,256]{2,1,0:T(8,128)S(1)} %get-tuple-element.65.keep_reduce, bf16[1,128,256]{2,1,0:T(8,128)(2,1)S(1)} %collective-permute-done.15.came_reduce, f32[1,128,256]{2,1,0:T(8,128)S(1)} %get-tuple-element.75.keep_expand, bf16[1,128,256]{2,1,0:T(8,128)(2,1)S(1)} %collective-permute-done.21.came_expand), custom_call_target="tpu_custom_call" | custom-call | tf_op jit(solution)/shard_map/pallas_call | solution.py:528
  (28 shorter events, 0.2 us)
Async XLA Ops:
  1.2 2.4 %collective-permute-start = (bf16[1024,256]{1,0:T(8,128)(2,1)S(1)}, bf16[1024,256]{1,0:T(8,128)(2,1)S(1)}, u32[]{:S(2)}, u32[]{:S(2)}) collective-permute-start(bf16[1024,256]{1,0:T(8,128)(2,1)S(1)} %get-tuple-element.42.refs_0_), channel_id=1, source_target_pairs={{0,8},{8,0},{16,24},{24,16},{1,9},{9,1},{17,25},{25,17},{2,10},{10... | collective-permute-start | bytes 1572872 | tf_op jit(solution)/shard_map/ppermute | solution.py:427
  1.8 2.3 %collective-permute-start.1 = (bf16[1024,256]{1,0:T(8,128)(2,1)S(1)}, bf16[1024,256]{1,0:T(8,128)(2,1)S(1)}, u32[]{:S(2)}, u32[]{:S(2)}) collective-permute-start(bf16[1024,256]{1,0:T(8,128)(2,1)S(1)} %get-tuple-element.43.refs_1_), channel_id=1, source_target_pairs={{0,8},{8,0},{16,24},{24,16},{1,9},{9,1},{17,25},{25,17},{2,10},{10... | collective-permute-start | bytes 1572872 | tf_op jit(solution)/shard_map/ppermute | solution.py:427
  3.1 5.0 %collective-permute-start.3 = (bf16[1024,256]{1,0:T(8,128)(2,1)S(1)}, bf16[1024,256]{1,0:T(8,128)(2,1)S(1)}, u32[]{:S(2)}, u32[]{:S(2)}) collective-permute-start(bf16[1024,256]{1,0:T(8,128)(2,1)S(1)} %get-tuple-element.47.expand_own.refs_1_), channel_id=1, source_target_pairs={{0,8},{8,0},{16,24},{24,16},{1,9},{9,1},{17,25},{25,17},{2,10},{10... | collective-permute-start | bytes 1572872 | tf_op jit(solution)/shard_map/ppermute | solution.py:427
  3.6 5.7 %collective-permute-start.2 = (bf16[1024,256]{1,0:T(8,128)(2,1)S(1)}, bf16[1024,256]{1,0:T(8,128)(2,1)S(1)}, u32[]{:S(2)}, u32[]{:S(2)}) collective-permute-start(bf16[1024,256]{1,0:T(8,128)(2,1)S(1)} %get-tuple-element.46.refs_0_), channel_id=1, source_target_pairs={{0,8},{8,0},{16,24},{24,16},{1,9},{9,1},{17,25},{25,17},{2,10},{10... | collective-permute-start | bytes 1572872 | tf_op jit(solution)/shard_map/ppermute | solution.py:427
  5.2 5.3 %collective-permute-start.4 = (bf16[32,1024]{1,0:T(8,128)(2,1)S(1)}, bf16[32,1024]{1,0:T(8,128)(2,1)S(1)}, u32[]{:S(2)}, u32[]{:S(2)}) collective-permute-start(bf16[32,1024]{1,0:T(8,128)(2,1)S(1)} %get-tuple-element.48.leave), channel_id=1, source_target_pairs={{0,16},{16,0},{8,24},{24,8},{1,17},{17,1},{9,25},{25,9},{2,18},{18... | collective-permute-start | bytes 196616 | tf_op jit(solution)/shard_map/ppermute | solution.py:424
  12.3 4.4 %collective-permute-start.9 = (bf16[32,1024]{1,0:T(8,128)(2,1)S(1)}, bf16[32,1024]{1,0:T(8,128)(2,1)S(1)}, u32[]{:S(2)}, u32[]{:S(2)}) collective-permute-start(bf16[32,1024]{1,0:T(8,128)(2,1)S(1)} %get-tuple-element.58), channel_id=1, source_target_pairs={{0,16},{16,0},{8,24},{24,8},{1,17},{17,1},{9,25},{25,9},{2,18},{18... | collective-permute-start | bytes 196616 | tf_op jit(solution)/shard_map/ppermute | solution.py:424
  14.3 10.6 %collective-permute-start.5 = (bf16[32,1280]{1,0:T(8,128)(2,1)S(1)}, bf16[32,1280]{1,0:T(8,128)(2,1)S(1)}, u32[]{:S(2)}, u32[]{:S(2)}) collective-permute-start(bf16[32,1280]{1,0:T(8,128)(2,1)S(1)} %fusion), channel_id=1, source_target_pairs={{0,8},{8,0},{16,24},{24,16},{1,9},{9,1},{17,25},{25,17},{2,10},{10... | collective-permute-start | bytes 245768 | tf_op jit(solution)/shard_map/ppermute | solution.py:427
  14.5 5.9 %collective-permute-start.6 = (bf16[32,1536]{1,0:T(8,128)(2,1)S(1)}, bf16[32,1536]{1,0:T(8,128)(2,1)S(1)}, u32[]{:S(2)}, u32[]{:S(2)}) collective-permute-start(bf16[32,1536]{1,0:T(8,128)(2,1)S(1)} %pad_maximum_fusion), channel_id=1, source_target_pairs={{0,16},{8,24},{16,0},{24,8},{1,17},{9,25},{17,1},{25,9},{2,18},{10... | collective-permute-start | bytes 294920 | tf_op jit(solution)/shard_map/ppermute | solution.py:430
  17.7 10.2 %collective-permute-start.11 = (bf16[2,32,256]{2,1,0:T(8,128)(2,1)S(1)}, bf16[2,32,256]{2,1,0:T(8,128)(2,1)S(1)}, u32[]{:S(2)}, u32[]{:S(2)}) collective-permute-start(bf16[2,32,256]{2,1,0:T(8,128)(2,1)S(1)} %broadcast_select_fusion.7), channel_id=1, source_target_pairs={{0,16},{8,24},{16,0},{24,8},{1,17},{9,25},{17,1},{25,9},{2,18},{10... | collective-permute-start | bytes 98312 | tf_op jit(solution)/shard_map/ppermute | solution.py:430
  20.2 6.7 %collective-permute-start.16 = (bf16[32,1024]{1,0:T(8,128)(2,1)S(1)}, bf16[32,1024]{1,0:T(8,128)(2,1)S(1)}, u32[]{:S(2)}, u32[]{:S(2)}) collective-permute-start(bf16[32,1024]{1,0:T(8,128)(2,1)S(1)} %fusion.2), channel_id=1, source_target_pairs={{0,8},{8,0},{16,24},{24,16},{1,9},{9,1},{17,25},{25,17},{2,10},{10... | collective-permute-start | bytes 196616 | tf_op jit(solution)/shard_map/ppermute | solution.py:427
  20.2 4.6 %collective-permute-start.17 = (bf16[32,1024]{1,0:T(8,128)(2,1)S(1)}, bf16[32,1024]{1,0:T(8,128)(2,1)S(1)}, u32[]{:S(2)}, u32[]{:S(2)}) collective-permute-start(bf16[32,1024]{1,0:T(8,128)(2,1)S(1)} %fusion.1), channel_id=1, source_target_pairs={{0,16},{8,24},{16,0},{24,8},{1,17},{9,25},{17,1},{25,9},{2,18},{10... | collective-permute-start | bytes 196616 | tf_op jit(solution)/shard_map/ppermute | solution.py:430
  20.4 5.0 %collective-permute-start.7 = (bf16[32,1280]{1,0:T(8,128)(2,1)S(1)}, bf16[32,1280]{1,0:T(8,128)(2,1)S(1)}, u32[]{:S(2)}, u32[]{:S(2)}) collective-permute-start(bf16[32,1280]{1,0:T(8,128)(2,1)S(1)} %pad_maximum_fusion.2), channel_id=1, source_target_pairs={{0,8},{8,0},{16,24},{24,16},{1,9},{9,1},{17,25},{25,17},{2,10},{10... | collective-permute-start | bytes 245768 | tf_op jit(solution)/shard_map/ppermute | solution.py:427
  24.8 2.1 %collective-permute-start.18 = (bf16[32,1024]{1,0:T(8,128)(2,1)S(1)}, bf16[32,1024]{1,0:T(8,128)(2,1)S(1)}, u32[]{:S(2)}, u32[]{:S(2)}) collective-permute-start(bf16[32,1024]{1,0:T(8,128)(2,1)S(1)} %get-tuple-element.77), channel_id=1, source_target_pairs={{0,8},{8,0},{16,24},{24,16},{1,9},{9,1},{17,25},{25,17},{2,10},{10... | collective-permute-start | bytes 196616 | tf_op jit(solution)/shard_map/ppermute | solution.py:427
  24.9 2.9 %collective-permute-start.10 = (bf16[32,256]{1,0:T(8,128)(2,1)S(1)}, bf16[32,256]{1,0:T(8,128)(2,1)S(1)}, u32[]{:S(2)}, u32[]{:S(2)}) collective-permute-start(bf16[32,256]{1,0:T(8,128)(2,1)S(1)} %fusion.4), channel_id=1, source_target_pairs={{0,8},{8,0},{16,24},{24,16},{1,9},{9,1},{17,25},{25,17},{2,10},{10... | collective-permute-start | bytes 49160 | tf_op jit(solution)/shard_map/ppermute | solution.py:427
  25.6 5.7 %collective-permute-start.8 = (bf16[128,768]{1,0:T(8,128)(2,1)S(1)}, bf16[128,768]{1,0:T(8,128)(2,1)S(1)}, u32[]{:S(2)}, u32[]{:S(2)}) collective-permute-start(bf16[128,768]{1,0:T(8,128)(2,1)S(1)} %get-tuple-element.57), channel_id=1, source_target_pairs={{0,1},{1,0},{2,3},{3,2},{4,5},{5,4},{6,7},{7,6},{8,10},{9,11},{10,... | collective-permute-start | bytes 589832 | tf_op jit(solution)/shard_map/ppermute | solution.py:549
  27.0 5.7 %collective-permute-start.19 = (bf16[128,512]{1,0:T(8,128)(2,1)S(1)}, bf16[128,512]{1,0:T(8,128)(2,1)S(1)}, u32[]{:S(2)}, u32[]{:S(2)}) collective-permute-start(bf16[128,512]{1,0:T(8,128)(2,1)S(1)} %get-tuple-element.71), channel_id=1, source_target_pairs={{0,1},{1,0},{2,3},{3,2},{4,5},{5,4},{6,7},{7,6},{8,10},{9,11},{10,... | collective-permute-start | bytes 393224 | tf_op jit(solution)/shard_map/ppermute | solution.py:549
  27.9 1.2 %collective-permute-start.12 = (bf16[32,256]{1,0:T(8,128)(2,1)S(1)}, bf16[32,256]{1,0:T(8,128)(2,1)S(1)}, u32[]{:S(2)}, u32[]{:S(2)}) collective-permute-start(bf16[32,256]{1,0:T(8,128)(2,1)S(1)} %get-tuple-element.85), channel_id=1, source_target_pairs={{0,8},{8,0},{16,24},{24,16},{1,9},{9,1},{17,25},{25,17},{2,10},{10... | collective-permute-start | bytes 49160 | tf_op jit(solution)/shard_map/ppermute | solution.py:427
  29.1 5.5 %collective-permute-start.13 = (bf16[128,256]{1,0:T(8,128)(2,1)S(1)}, bf16[128,256]{1,0:T(8,128)(2,1)S(1)}, u32[]{:S(2)}, u32[]{:S(2)}) collective-permute-start(bf16[128,256]{1,0:T(8,128)(2,1)S(1)} %shard_map.53.right), channel_id=1, source_target_pairs={{0,1},{1,0},{2,3},{3,2},{4,5},{5,4},{6,7},{7,6},{8,10},{9,11},{10,... | collective-permute-start | bytes 196616 | tf_op jit(solution)/shard_map/ppermute | solution.py:549
  33.1 5.0 %collective-permute-start.20 = (bf16[2,128,256]{2,1,0:T(8,128)(2,1)S(1)}, bf16[2,128,256]{2,1,0:T(8,128)(2,1)S(1)}, u32[]{:S(2)}, u32[]{:S(2)}) collective-permute-start(bf16[2,128,256]{2,1,0:T(8,128)(2,1)S(1)} %get-tuple-element.74), channel_id=1, source_target_pairs={{0,2},{1,3},{2,0},{3,1},{4,6},{5,7},{6,4},{7,5},{8,9},{9,8},{10,11... | collective-permute-start | bytes 393224 | tf_op jit(solution)/shard_map/ppermute | solution.py:549
  35.0 5.7 %collective-permute-start.14 = (bf16[2,128,256]{2,1,0:T(8,128)(2,1)S(1)}, bf16[2,128,256]{2,1,0:T(8,128)(2,1)S(1)}, u32[]{:S(2)}, u32[]{:S(2)}) collective-permute-start(bf16[2,128,256]{2,1,0:T(8,128)(2,1)S(1)} %get-tuple-element.64), channel_id=1, source_target_pairs={{0,2},{1,3},{2,0},{3,1},{4,6},{5,7},{6,4},{7,5},{8,9},{9,8},{10,11... | collective-permute-start | bytes 393224 | tf_op jit(solution)/shard_map/ppermute | solution.py:549
  38.2 6.6 %collective-permute-start.21 = (bf16[1,128,256]{2,1,0:T(8,128)(2,1)S(1)}, bf16[1,128,256]{2,1,0:T(8,128)(2,1)S(1)}, u32[]{:S(2)}, u32[]{:S(2)}) collective-permute-start(bf16[1,128,256]{2,1,0:T(8,128)(2,1)S(1)} %get-tuple-element.76), channel_id=1, source_target_pairs={{0,4},{1,5},{2,6},{3,7},{4,0},{5,1},{6,2},{7,3},{8,12},{9,13},{10,... | collective-permute-start | bytes 196616 | tf_op jit(solution)/shard_map/ppermute | solution.py:549
  40.8 5.2 %collective-permute-start.15 = (bf16[1,128,256]{2,1,0:T(8,128)(2,1)S(1)}, bf16[1,128,256]{2,1,0:T(8,128)(2,1)S(1)}, u32[]{:S(2)}, u32[]{:S(2)}) collective-permute-start(bf16[1,128,256]{2,1,0:T(8,128)(2,1)S(1)} %get-tuple-element.66), channel_id=1, source_target_pairs={{0,4},{1,5},{2,6},{3,7},{4,0},{5,1},{6,2},{7,3},{8,12},{9,13},{10,... | collective-permute-start | bytes 196616 | tf_op jit(solution)/shard_map/ppermute | solution.py:549

commit v2 on v1

--- a/solution.py
+++ b/solution.py
@@ -359,27 +359,40 @@
         target[(at + 1) * rows : (at + 2) * rows] = part[...]
 
 
-def early_body(stages, chunk, *refs):
-    arrays, (keep_left, keep_right, send, wide) = refs[: stages + 3], refs[stages + 3 :]
+def flow_rows(arrays, stages, columns):
+    near = [flow.at[0, :, columns] for flow in arrays[:stages]]
+    return near, [part.at[:, columns] for part in arrays[stages : stages + 3]]
+
+
+def back_rows(arrays, stages):
+    return [back.at[0] for back in arrays[:stages]], arrays[stages : stages + 3]
+
+
+def early_body(stages, channels, *refs):
+    gather_rows(refs[-1], *flow_rows(refs, stages, slice(channels, None)))
+
+
+def late_up_body(stages, chunk, *refs):
+    keep, send, wide = refs[stages + 3 :]
+    gather_rows(wide, *back_rows(refs, stages))
+    split_columns(wide, keep, send, chunk)
+
+
+def late_inner_body(stages, chunk, *refs):
+    left, right, send, wide = refs[2 * stages + 6 :]
     channels = wide.shape[1]
-    flows, (side, far, cross) = arrays[:stages], arrays[stages:]
-    for target, columns in ((wide, slice(0, channels)), (keep_right, slice(channels, None))):
-        near = [flow.at[0, :, columns] for flow in flows]
-        gather_rows(target, near, [side.at[:, columns], far.at[:, columns], cross.at[:, columns]])
-    split_columns(wide, keep_left, send, chunk)
-    send[:, channels // 2 :] = keep_right[...]
-
-
-def late_body(stages, chunk, *refs):
-    arrays, outs = refs[: stages + 3], refs[stages + 3 :]
-    side, far, cross = arrays[stages:]
-    gather_rows(outs[-1], [back.at[0] for back in arrays[:stages]], [side, far, cross])
-    if chunk:
-        split_columns(outs[2], outs[0], outs[1], chunk)
-
-
-def half_gradient_body(left, left_came, right, right_came, send, keep, full):
-    full[...] = contract(left[...], right[...], 0, 0) + contract(left_came[...], right_came[...], 0, 0)
+    gather_rows(wide, *flow_rows(refs, stages, slice(0, channels)))
+    split_columns(wide, left, send, chunk)
+    gather_rows(right, *back_rows(refs[stages + 3 :], stages))
+    send[:, channels // 2 :] = right[...]
+
+
+def half_gradient_body(left, right, *refs):
+    came, (send, keep, full) = refs[:-3], refs[-3:]
+    columns = left.shape[1]
+    if len(came) == 1:
+        came = (came[0].at[:, :columns], came[0].at[:, columns:])
+    full[...] = contract(left[...], right[...], 0, 0) + contract(came[0][...], came[1][...], 0, 0)
     _, _, side = first_sides()
     chunk = send.shape[1]
     for place in range(send.shape[0]):
@@ -554,26 +567,16 @@
     shape = lambda *dims: jax.ShapeDtypeStruct(dims, jnp.bfloat16)
     half = shape(4 * rows, channels // 2)
     narrow = shape(4 * rows, inner)
-    left, right, send = pl.pallas_call(
-        functools.partial(early_body, stages, chunk),
-        out_shape=[half, narrow, shape(4 * rows, channels // 2 + inner)],
+    active = pl.pallas_call(
+        functools.partial(early_body, stages, channels),
+        out_shape=narrow,
         in_specs=[VMEM] * len(fore),
-        out_specs=[VMEM] * 3,
-        scratch_shapes=[pltpu.VMEM((4 * rows, channels), jnp.bfloat16)],
+        out_specs=VMEM,
         compiler_params=PARAMS,
     )(*fore)
-    came = exchange(send, stages, replicas, 1, 2)
-    came_left, came_right = came[:, : channels // 2], came[:, channels // 2 :]
-    back = pl.pallas_call(
-        functools.partial(late_body, stages, 0),
-        out_shape=narrow,
-        in_specs=[VMEM] * len(backs),
-        out_specs=VMEM,
-        compiler_params=PARAMS,
-    )(*backs)
-    came_back = exchange(back, stages, replicas, 1, 2)
+    came_active = exchange(active, stages, replicas, 1, 2)
     up, up_send = pl.pallas_call(
-        functools.partial(late_body, stages, chunk),
+        functools.partial(late_up_body, stages, chunk),
         out_shape=[half, half],
         in_specs=[VMEM] * len(ups),
         out_specs=[VMEM] * 2,
@@ -581,14 +584,23 @@
         compiler_params=PARAMS,
     )(*ups)
     came_up = exchange(up_send, stages, replicas, 1, 2)
+    lifted, back, send = pl.pallas_call(
+        functools.partial(late_inner_body, stages, chunk),
+        out_shape=[half, narrow, shape(4 * rows, channels // 2 + inner)],
+        in_specs=[VMEM] * (len(fore) + len(backs)),
+        out_specs=[VMEM] * 3,
+        scratch_shapes=[pltpu.VMEM((4 * rows, channels), jnp.bfloat16)],
+        compiler_params=PARAMS,
+    )(*fore, *backs)
+    came_inner = exchange(send, stages, replicas, 1, 2)
     parts = []
-    streams = ((left, came_left, back, came_back), (up, came_up, right, came_right))
+    streams = ((lifted, back, came_inner), (up, active, came_up, came_active))
     for operands in streams:
         count = replicas // 4
         send, keep = pl.pallas_call(
             half_gradient_body,
             out_shape=sums(count, chunk, inner),
-            in_specs=[VMEM] * 4,
+            in_specs=[VMEM] * len(operands),
             out_specs=[VMEM] * 2,
             scratch_shapes=[pltpu.VMEM((channels // 2, inner), jnp.float32)],
             compiler_params=PARAMS,

time: 46.9 us -> 50 us (1.066)
  starting transfers between devices: 20.7 us -> 22.3 us
  waiting for transfers between devices: 16.3 us -> 17.8 us
    ppermute x7, waiting for transfers between devices: 7.59 us -> 9.39 us  [exchange(): return lax.ppermute(shard, AXES, pairs)]
    ppermute x3, starting transfers between devices: 2.93 us -> 4.7 us  [mirror(): return lax.ppermute(shard, 'pipe', mirror_pairs)]
    ppermute x10, waiting for transfers between devices: 1.59 us -> 1.08 us  [swap_cores(): return lax.ppermute(shard, 'pipe', core_pairs)]
  transfers between devices with their start and end apart: 22 -> 22, of which waited for: 11 -> 11; matrix products, arithmetic and copies ran while one was open for 0% -> 0% of each run, Pallas kernels for 12% -> 11%
where the time goes in v2:
time: 50 us; the launch traced here: 49.8 us
  starting transfers between devices  22.3 us (45%)
  waiting for transfers between devices  17.8 us (36%)
  Pallas kernels  9.28 us (19%)
    ppermute x7, starting transfers between devices, exchange(): return lax.ppermute(shard, AXES, pairs)  10.7 us
    ppermute x7, waiting for transfers between devices, exchange(): return lax.ppermute(shard, AXES, pairs)  9.39 us
    ppermute x2, starting transfers between devices, hop(): return lax.ppermute(shard, 'pipe', pairs)  4.81 us
    ppermute x3, starting transfers between devices, mirror(): return lax.ppermute(shard, 'pipe', mirror_pairs)  4.7 us
    ppermute x3, waiting for transfers between devices, mirror(): return lax.ppermute(shard, 'pipe', mirror_pairs)  4.09 us
    pallas_call x3, Pallas kernels, run_stage(): pl.pallas_call(functools.partial(stage_body, step, forward, backward, las...  3.85 us
    ppermute x2, waiting for transfers between devices, hop(): return lax.ppermute(shard, 'pipe', pairs)  3.23 us
    pallas_call x2, Pallas kernels, load(): pl.pallas_call(functools.partial(load_body, step), out_shape=outs, in_spe...  2.44 us
  transfers between devices with their start and end apart: 22, of which 11 were waited for; matrix products, arithmetic and copies ran while one was open for 0% of the time, Pallas kernels for 11%

profile of v2, /device:TPU:0, one launch (start us, length us, event | category | flops | bytes accessed | tf_op | source)
XLA Modules:
  0.0 49.8 jit_solution(17904797938535523217)
XLA Ops:
  0.0 1.2 %shard_map.46 = (bf16[1024,256]{1,0:T(8,128)(2,1)S(1)}, bf16[1024,256]{1,0:T(8,128)(2,1)S(1)}, bf16[32,1024]{1,0:T(8,128)(2,1)S(1)}) custom-call(bf16[2,1024,256]{2,1,0:T(8,128)(2,1)} %bitcast.20, bf16[2,1024,256]{2,1,0:T(8,128)(2,1)} %bitcast.22, bf16[2,2,32,1024]{3,2,1,0:T(8,128)(2,1)} %inputs), custom_call_target="tpu_custom_call" | custom-call | tf_op jit(solution)/shard_map/pallas_call | solution.py:68
  1.2 0.6 %collective-permute-start = (bf16[1024,256]{1,0:T(8,128)(2,1)S(1)}, bf16[1024,256]{1,0:T(8,128)(2,1)S(1)}, u32[]{:S(2)}, u32[]{:S(2)}) collective-permute-start(bf16[1024,256]{1,0:T(8,128)(2,1)S(1)} %get-tuple-element.42.refs_0_), channel_id=1, source_target_pairs={{0,8},{8,0},{16,24},{24,16},{1,9},{9,1},{17,25},{25,17},{2,10},{10... | collective-permute-start | bytes 1572872 | tf_op jit(solution)/shard_map/ppermute | solution.py:440
  1.8 0.1 collective-permute-start.1
  1.9 1.2 %shard_map.48 = (bf16[1024,256]{1,0:T(8,128)(2,1)S(1)}, bf16[1024,256]{1,0:T(8,128)(2,1)S(1)}) custom-call(bf16[2,1024,256]{2,1,0:T(8,128)(2,1)} %bitcast.21, bf16[2,1024,256]{2,1,0:T(8,128)(2,1)} %bitcast.23), custom_call_target="tpu_custom_call" | custom-call | tf_op jit(solution)/shard_map/pallas_call | solution.py:68
  3.1 0.5 collective-permute-start.3
  3.6 0.1 collective-permute-start.2
  3.7 0.0 collective-permute-done.refs_2_
  3.7 0.4 collective-permute-done.1.refs_3_
  4.1 1.2 %shard_map.47 = (bf16[2,32,1280]{2,1,0:T(8,128)(2,1)S(1)}, bf16[32,1024]{1,0:T(8,128)(2,1)S(1)}, bf16[2,32,1024]{2,1,0:T(8,128)(2,1)S(1)}, f32[2,32,256]{2,1,0:T(8,128)S(1)}) custom-call(bf16[1024,256]{1,0:T(8,128)(2,1)S(1)} %get-tuple-element.42.refs_0_, bf16[1024,256]{1,0:T(8,128)(2,1)S(1)} %get-tuple-element.43.refs_1_, ...), custom_call_target="tpu_custom_call" | custom-call | flops 67108864 | bytes 2097152 | tf_op jit(solution)/shard_map/pallas_call | solution.py:250
  5.2 2.9 %collective-permute-start.4 = (bf16[32,1024]{1,0:T(8,128)(2,1)S(1)}, bf16[32,1024]{1,0:T(8,128)(2,1)S(1)}, u32[]{:S(2)}, u32[]{:S(2)}) collective-permute-start(bf16[32,1024]{1,0:T(8,128)(2,1)S(1)} %get-tuple-element.48.leave), channel_id=1, source_target_pairs={{0,16},{16,0},{8,24},{24,8},{1,17},{17,1},{9,25},{25,9},{2,18},{18... | collective-permute-start | bytes 196616 | tf_op jit(solution)/shard_map/ppermute | solution.py:437
  8.1 1.2 %shard_map.49 = (bf16[32,1024]{1,0:T(8,128)(2,1)S(1)}, f32[32,256]{1,0:T(8,128)S(1)}, bf16[32,1024]{1,0:T(8,128)(2,1)S(1)}, bf16[32,1024]{1,0:T(8,128)(2,1)S(1)}) custom-call(bf16[1024,256]{1,0:T(8,128)(2,1)S(1)} %get-tuple-element.47.expand_own.refs_1_, bf16[1024,256]{1,0:T(8,128)(2,1)S(1)} %collective-permute-done.3.expand_other.refs_3_, ...), custom_call_target="tpu_custom_call" | custom-call | tf_op jit(solution)/shard_map/pallas_call | solution.py:476
  9.3 1.2 %collective-permute-done.4.refs_4_ = bf16[32,1024]{1,0:T(8,128)(2,1)S(1)} collective-permute-done((bf16[32,1024]{1,0:T(8,128)(2,1)S(1)}, bf16[32,1024]{1,0:T(8,128)(2,1)S(1)}, u32[]{:S(2)}, u32[]{:S(2)}) %collective-permute-start.4) | collective-permute-done | bytes 65568 | tf_op jit(solution)/shard_map/ppermute | solution.py:437
  10.5 1.8 %shard_map.50 = (bf16[2,32,1280]{2,1,0:T(8,128)(2,1)S(1)}, bf16[2,32,1024]{2,1,0:T(8,128)(2,1)S(1)}, bf16[2,32,256]{2,1,0:T(8,128)(2,1)S(1)}, bf16[32,1024]{1,0:T(8,128)(2,1)S(1)}) custom-call(bf16[1024,256]{1,0:T(8,128)(2,1)S(1)} %get-tuple-element.46.refs_0_, bf16[1024,256]{1,0:T(8,128)(2,1)S(1)} %get-tuple-element.47.expand_own.refs_1_, ...), custom_call_target="tpu_custom_call" | custom-call | flops 134217728 | bytes 2097152 | tf_op jit(solution)/shard_map/pallas_call | solution.py:250
  12.3 1.9 %collective-permute-start.8 = (bf16[32,1024]{1,0:T(8,128)(2,1)S(1)}, bf16[32,1024]{1,0:T(8,128)(2,1)S(1)}, u32[]{:S(2)}, u32[]{:S(2)}) collective-permute-start(bf16[32,1024]{1,0:T(8,128)(2,1)S(1)} %get-tuple-element.56), channel_id=1, source_target_pairs={{0,16},{16,0},{8,24},{24,8},{1,17},{17,1},{9,25},{25,9},{2,18},{18... | collective-permute-start | bytes 196616 | tf_op jit(solution)/shard_map/ppermute | solution.py:437
  14.3 0.1 collective-permute-start.5
  14.5 0.2 collective-permute-start.6
  14.7 2.1 %collective-permute-done.8.refs_4_ = bf16[32,1024]{1,0:T(8,128)(2,1)S(1)} collective-permute-done((bf16[32,1024]{1,0:T(8,128)(2,1)S(1)}, bf16[32,1024]{1,0:T(8,128)(2,1)S(1)}, u32[]{:S(2)}, u32[]{:S(2)}) %collective-permute-start.8) | collective-permute-done | bytes 65568 | tf_op jit(solution)/shard_map/ppermute | solution.py:437
  16.7 0.9 %shard_map.51 = (bf16[2,32,1024]{2,1,0:T(8,128)(2,1)S(1)}, bf16[2,32,256]{2,1,0:T(8,128)(2,1)S(1)}) custom-call(bf16[1024,256]{1,0:T(8,128)(2,1)S(1)} %get-tuple-element.42.refs_0_, bf16[1024,256]{1,0:T(8,128)(2,1)S(1)} %get-tuple-element.43.refs_1_, bf16[1024,256]{1,0:T(8,128)(2,1)S(1)} %collective-permute-done.refs_2_, ...), custom_call_target="tpu_custom_call" | custom-call | flops 67108864 | bytes 2097152 | tf_op jit(solution)/shard_map/pallas_call | solution.py:250
  17.7 0.1 collective-permute-start.9
  17.7 2.5 %collective-permute-start.10 = (bf16[2,32,256]{2,1,0:T(8,128)(2,1)S(1)}, bf16[2,32,256]{2,1,0:T(8,128)(2,1)S(1)}, u32[]{:S(2)}, u32[]{:S(2)}) collective-permute-start(bf16[2,32,256]{2,1,0:T(8,128)(2,1)S(1)} %broadcast_select_fusion.7), channel_id=1, source_target_pairs={{0,16},{8,24},{16,0},{24,8},{1,17},{9,25},{17,1},{25,9},{2,18},{10... | collective-permute-start | bytes 98312 | tf_op jit(solution)/shard_map/ppermute | solution.py:443
  20.3 0.2 collective-permute-start.15
  20.5 1.8 %collective-permute-done.10 = bf16[2,32,256]{2,1,0:T(8,128)(2,1)S(1)} collective-permute-done((bf16[2,32,256]{2,1,0:T(8,128)(2,1)S(1)}, bf16[2,32,256]{2,1,0:T(8,128)(2,1)S(1)}, u32[]{:S(2)}, u32[]{:S(2)}) %collective-permute-start.10) | collective-permute-done | bytes 32800 | tf_op jit(solution)/shard_map/ppermute | solution.py:443
  22.3 1.9 %collective-permute-start.16 = (bf16[32,1024]{1,0:T(8,128)(2,1)S(1)}, bf16[32,1024]{1,0:T(8,128)(2,1)S(1)}, u32[]{:S(2)}, u32[]{:S(2)}) collective-permute-start(bf16[32,1024]{1,0:T(8,128)(2,1)S(1)} %fusion.1), channel_id=1, source_target_pairs={{0,16},{8,24},{16,0},{24,8},{1,17},{9,25},{17,1},{25,9},{2,18},{10... | collective-permute-start | bytes 196616 | tf_op jit(solution)/shard_map/ppermute | solution.py:443
  24.3 2.3 %collective-permute-done.16 = bf16[32,1024]{1,0:T(8,128)(2,1)S(1)} collective-permute-done((bf16[32,1024]{1,0:T(8,128)(2,1)S(1)}, bf16[32,1024]{1,0:T(8,128)(2,1)S(1)}, u32[]{:S(2)}, u32[]{:S(2)}) %collective-permute-start.16) | collective-permute-done | bytes 65568 | tf_op jit(solution)/shard_map/ppermute | solution.py:443
  26.6 0.6 %collective-permute-start.17 = (bf16[32,1024]{1,0:T(8,128)(2,1)S(1)}, bf16[32,1024]{1,0:T(8,128)(2,1)S(1)}, u32[]{:S(2)}, u32[]{:S(2)}) collective-permute-start(bf16[32,1024]{1,0:T(8,128)(2,1)S(1)} %get-tuple-element.77), channel_id=1, source_target_pairs={{0,8},{8,0},{16,24},{24,16},{1,9},{9,1},{17,25},{25,17},{2,10},{10... | collective-permute-start | bytes 196616 | tf_op jit(solution)/shard_map/ppermute | solution.py:440
  27.2 0.0 collective-permute-done.5.refs_2_
  27.2 0.7 %collective-permute-done.7.refs_4_ = bf16[32,1280]{1,0:T(8,128)(2,1)S(1)} collective-permute-done((bf16[32,1280]{1,0:T(8,128)(2,1)S(1)}, bf16[32,1280]{1,0:T(8,128)(2,1)S(1)}, u32[]{:S(2)}, u32[]{:S(2)}) %collective-permute-start.7) | collective-permute-done | bytes 81952 | tf_op jit(solution)/shard_map/ppermute | solution.py:440
  27.8 0.1 shard_map.52
  27.9 1.4 %collective-permute-start.12 = (bf16[128,768]{1,0:T(8,128)(2,1)S(1)}, bf16[128,768]{1,0:T(8,128)(2,1)S(1)}, u32[]{:S(2)}, u32[]{:S(2)}) collective-permute-start(bf16[128,768]{1,0:T(8,128)(2,1)S(1)} %get-tuple-element.63), channel_id=1, source_target_pairs={{0,1},{1,0},{2,3},{3,2},{4,5},{5,4},{6,7},{7,6},{8,10},{9,11},{10,... | collective-permute-start | bytes 589832 | tf_op jit(solution)/shard_map/ppermute | solution.py:562
  29.3 0.0 collective-permute-done.15.refs_2_
  29.3 0.0 collective-permute-done.17.refs_4_
  29.3 0.1 shard_map.55
  29.4 0.8 %collective-permute-start.18 = (bf16[128,512]{1,0:T(8,128)(2,1)S(1)}, bf16[128,512]{1,0:T(8,128)(2,1)S(1)}, u32[]{:S(2)}, u32[]{:S(2)}) collective-permute-start(bf16[128,512]{1,0:T(8,128)(2,1)S(1)} %get-tuple-element.72), channel_id=1, source_target_pairs={{0,1},{1,0},{2,3},{3,2},{4,5},{5,4},{6,7},{7,6},{8,10},{9,11},{10,... | collective-permute-start | bytes 393224 | tf_op jit(solution)/shard_map/ppermute | solution.py:562
  30.2 1.3 %collective-permute-start.19 = (bf16[128,256]{1,0:T(8,128)(2,1)S(1)}, bf16[128,256]{1,0:T(8,128)(2,1)S(1)}, u32[]{:S(2)}, u32[]{:S(2)}) collective-permute-start(bf16[128,256]{1,0:T(8,128)(2,1)S(1)} %shard_map.56.right), channel_id=1, source_target_pairs={{0,1},{1,0},{2,3},{3,2},{4,5},{5,4},{6,7},{7,6},{8,10},{9,11},{10,... | collective-permute-start | bytes 196616 | tf_op jit(solution)/shard_map/ppermute | solution.py:562
  31.5 4.3 %collective-permute-done.19.refs_1_ = bf16[128,256]{1,0:T(8,128)(2,1)S(1)} collective-permute-done((bf16[128,256]{1,0:T(8,128)(2,1)S(1)}, bf16[128,256]{1,0:T(8,128)(2,1)S(1)}, u32[]{:S(2)}, u32[]{:S(2)}) %collective-permute-start.19) | collective-permute-done | bytes 65568 | tf_op jit(solution)/shard_map/ppermute | solution.py:562
  35.8 0.0 collective-permute-done.18.refs_0_
  35.8 0.4 shard_map.57
  36.2 1.4 %collective-permute-start.20 = (bf16[2,128,256]{2,1,0:T(8,128)(2,1)S(1)}, bf16[2,128,256]{2,1,0:T(8,128)(2,1)S(1)}, u32[]{:S(2)}, u32[]{:S(2)}) collective-permute-start(bf16[2,128,256]{2,1,0:T(8,128)(2,1)S(1)} %get-tuple-element.74), channel_id=1, source_target_pairs={{0,2},{1,3},{2,0},{3,1},{4,6},{5,7},{6,4},{7,5},{8,9},{9,8},{10,11... | collective-permute-start | bytes 393224 | tf_op jit(solution)/shard_map/ppermute | solution.py:562
  37.6 0.0 collective-permute-done.12.refs_0_
  37.6 0.4 shard_map.53
  38.0 0.7 %collective-permute-start.13 = (bf16[2,128,256]{2,1,0:T(8,128)(2,1)S(1)}, bf16[2,128,256]{2,1,0:T(8,128)(2,1)S(1)}, u32[]{:S(2)}, u32[]{:S(2)}) collective-permute-start(bf16[2,128,256]{2,1,0:T(8,128)(2,1)S(1)} %get-tuple-element.65), channel_id=1, source_target_pairs={{0,2},{1,3},{2,0},{3,1},{4,6},{5,7},{6,4},{7,5},{8,9},{9,8},{10,11... | collective-permute-start | bytes 393224 | tf_op jit(solution)/shard_map/ppermute | solution.py:562
  38.8 2.5 %collective-permute-done.20.came = bf16[2,128,256]{2,1,0:T(8,128)(2,1)S(1)} collective-permute-done((bf16[2,128,256]{2,1,0:T(8,128)(2,1)S(1)}, bf16[2,128,256]{2,1,0:T(8,128)(2,1)S(1)}, u32[]{:S(2)}, u32[]{:S(2)}) %collective-permute-start.20) | collective-permute-done | bytes 131104 | tf_op jit(solution)/shard_map/ppermute | solution.py:562
  41.2 2.4 %collective-permute-start.21 = (bf16[1,128,256]{2,1,0:T(8,128)(2,1)S(1)}, bf16[1,128,256]{2,1,0:T(8,128)(2,1)S(1)}, u32[]{:S(2)}, u32[]{:S(2)}) collective-permute-start(bf16[1,128,256]{2,1,0:T(8,128)(2,1)S(1)} %get-tuple-element.76), channel_id=1, source_target_pairs={{0,4},{1,5},{2,6},{3,7},{4,0},{5,1},{6,2},{7,3},{8,12},{9,13},{10,... | collective-permute-start | bytes 196616 | tf_op jit(solution)/shard_map/ppermute | solution.py:562
  43.7 0.1 collective-permute-done.13.came
  43.8 2.7 %collective-permute-start.14 = (bf16[1,128,256]{2,1,0:T(8,128)(2,1)S(1)}, bf16[1,128,256]{2,1,0:T(8,128)(2,1)S(1)}, u32[]{:S(2)}, u32[]{:S(2)}) collective-permute-start(bf16[1,128,256]{2,1,0:T(8,128)(2,1)S(1)} %get-tuple-element.67), channel_id=1, source_target_pairs={{0,4},{1,5},{2,6},{3,7},{4,0},{5,1},{6,2},{7,3},{8,12},{9,13},{10,... | collective-permute-start | bytes 196616 | tf_op jit(solution)/shard_map/ppermute | solution.py:562
  46.5 1.5 %collective-permute-done.21.came_expand = bf16[1,128,256]{2,1,0:T(8,128)(2,1)S(1)} collective-permute-done((bf16[1,128,256]{2,1,0:T(8,128)(2,1)S(1)}, bf16[1,128,256]{2,1,0:T(8,128)(2,1)S(1)}, u32[]{:S(2)}, u32[]{:S(2)}) %collective-permute-start.21) | collective-permute-done | bytes 65568 | tf_op jit(solution)/shard_map/ppermute | solution.py:562
  48.0 1.1 %collective-permute-done.14.came_reduce = bf16[1,128,256]{2,1,0:T(8,128)(2,1)S(1)} collective-permute-done((bf16[1,128,256]{2,1,0:T(8,128)(2,1)S(1)}, bf16[1,128,256]{2,1,0:T(8,128)(2,1)S(1)}, u32[]{:S(2)}, u32[]{:S(2)}) %collective-permute-start.14) | collective-permute-done | bytes 65568 | tf_op jit(solution)/shard_map/ppermute | solution.py:562
  49.0 0.7 %shard_map.59 = f32[1,2,128,256]{3,2,1,0:T(8,128)} custom-call(f32[1,128,256]{2,1,0:T(8,128)S(1)} %get-tuple-element.66.keep_reduce, bf16[1,128,256]{2,1,0:T(8,128)(2,1)S(1)} %collective-permute-done.14.came_reduce, f32[1,128,256]{2,1,0:T(8,128)S(1)} %get-tuple-element.75.keep_expand, bf16[1,128,256]{2,1,0:T(8,128)(2,1)S(1)} %collective-permute-done.21.came_expand), custom_call_target="tpu_custom_call" | custom-call | tf_op jit(solution)/shard_map/pallas_call | solution.py:541
  (26 shorter events, 0.2 us)
Async XLA Ops:
  1.2 2.4 %collective-permute-start = (bf16[1024,256]{1,0:T(8,128)(2,1)S(1)}, bf16[1024,256]{1,0:T(8,128)(2,1)S(1)}, u32[]{:S(2)}, u32[]{:S(2)}) collective-permute-start(bf16[1024,256]{1,0:T(8,128)(2,1)S(1)} %get-tuple-element.42.refs_0_), channel_id=1, source_target_pairs={{0,8},{8,0},{16,24},{24,16},{1,9},{9,1},{17,25},{25,17},{2,10},{10... | collective-permute-start | bytes 1572872 | tf_op jit(solution)/shard_map/ppermute | solution.py:440
  1.8 2.3 %collective-permute-start.1 = (bf16[1024,256]{1,0:T(8,128)(2,1)S(1)}, bf16[1024,256]{1,0:T(8,128)(2,1)S(1)}, u32[]{:S(2)}, u32[]{:S(2)}) collective-permute-start(bf16[1024,256]{1,0:T(8,128)(2,1)S(1)} %get-tuple-element.43.refs_1_), channel_id=1, source_target_pairs={{0,8},{8,0},{16,24},{24,16},{1,9},{9,1},{17,25},{25,17},{2,10},{10... | collective-permute-start | bytes 1572872 | tf_op jit(solution)/shard_map/ppermute | solution.py:440
  3.1 5.0 %collective-permute-start.3 = (bf16[1024,256]{1,0:T(8,128)(2,1)S(1)}, bf16[1024,256]{1,0:T(8,128)(2,1)S(1)}, u32[]{:S(2)}, u32[]{:S(2)}) collective-permute-start(bf16[1024,256]{1,0:T(8,128)(2,1)S(1)} %get-tuple-element.47.expand_own.refs_1_), channel_id=1, source_target_pairs={{0,8},{8,0},{16,24},{24,16},{1,9},{9,1},{17,25},{25,17},{2,10},{10... | collective-permute-start | bytes 1572872 | tf_op jit(solution)/shard_map/ppermute | solution.py:440
  3.6 5.7 %collective-permute-start.2 = (bf16[1024,256]{1,0:T(8,128)(2,1)S(1)}, bf16[1024,256]{1,0:T(8,128)(2,1)S(1)}, u32[]{:S(2)}, u32[]{:S(2)}) collective-permute-start(bf16[1024,256]{1,0:T(8,128)(2,1)S(1)} %get-tuple-element.46.refs_0_), channel_id=1, source_target_pairs={{0,8},{8,0},{16,24},{24,16},{1,9},{9,1},{17,25},{25,17},{2,10},{10... | collective-permute-start | bytes 1572872 | tf_op jit(solution)/shard_map/ppermute | solution.py:440
  5.2 5.3 %collective-permute-start.4 = (bf16[32,1024]{1,0:T(8,128)(2,1)S(1)}, bf16[32,1024]{1,0:T(8,128)(2,1)S(1)}, u32[]{:S(2)}, u32[]{:S(2)}) collective-permute-start(bf16[32,1024]{1,0:T(8,128)(2,1)S(1)} %get-tuple-element.48.leave), channel_id=1, source_target_pairs={{0,16},{16,0},{8,24},{24,8},{1,17},{17,1},{9,25},{25,9},{2,18},{18... | collective-permute-start | bytes 196616 | tf_op jit(solution)/shard_map/ppermute | solution.py:437
  12.3 4.4 %collective-permute-start.8 = (bf16[32,1024]{1,0:T(8,128)(2,1)S(1)}, bf16[32,1024]{1,0:T(8,128)(2,1)S(1)}, u32[]{:S(2)}, u32[]{:S(2)}) collective-permute-start(bf16[32,1024]{1,0:T(8,128)(2,1)S(1)} %get-tuple-element.56), channel_id=1, source_target_pairs={{0,16},{16,0},{8,24},{24,8},{1,17},{17,1},{9,25},{25,9},{2,18},{18... | collective-permute-start | bytes 196616 | tf_op jit(solution)/shard_map/ppermute | solution.py:437
  14.3 12.9 %collective-permute-start.5 = (bf16[32,1280]{1,0:T(8,128)(2,1)S(1)}, bf16[32,1280]{1,0:T(8,128)(2,1)S(1)}, u32[]{:S(2)}, u32[]{:S(2)}) collective-permute-start(bf16[32,1280]{1,0:T(8,128)(2,1)S(1)} %fusion), channel_id=1, source_target_pairs={{0,8},{8,0},{16,24},{24,16},{1,9},{9,1},{17,25},{25,17},{2,10},{10... | collective-permute-start | bytes 245768 | tf_op jit(solution)/shard_map/ppermute | solution.py:440
  14.5 9.8 %collective-permute-start.6 = (bf16[32,1536]{1,0:T(8,128)(2,1)S(1)}, bf16[32,1536]{1,0:T(8,128)(2,1)S(1)}, u32[]{:S(2)}, u32[]{:S(2)}) collective-permute-start(bf16[32,1536]{1,0:T(8,128)(2,1)S(1)} %pad_maximum_fusion), channel_id=1, source_target_pairs={{0,16},{8,24},{16,0},{24,8},{1,17},{9,25},{17,1},{25,9},{2,18},{10... | collective-permute-start | bytes 294920 | tf_op jit(solution)/shard_map/ppermute | solution.py:443
  17.7 8.9 %collective-permute-start.9 = (bf16[32,256]{1,0:T(8,128)(2,1)S(1)}, bf16[32,256]{1,0:T(8,128)(2,1)S(1)}, u32[]{:S(2)}, u32[]{:S(2)}) collective-permute-start(bf16[32,256]{1,0:T(8,128)(2,1)S(1)} %fusion.4), channel_id=1, source_target_pairs={{0,8},{8,0},{16,24},{24,16},{1,9},{9,1},{17,25},{25,17},{2,10},{10... | collective-permute-start | bytes 49160 | tf_op jit(solution)/shard_map/ppermute | solution.py:440
  17.7 4.5 %collective-permute-start.10 = (bf16[2,32,256]{2,1,0:T(8,128)(2,1)S(1)}, bf16[2,32,256]{2,1,0:T(8,128)(2,1)S(1)}, u32[]{:S(2)}, u32[]{:S(2)}) collective-permute-start(bf16[2,32,256]{2,1,0:T(8,128)(2,1)S(1)} %broadcast_select_fusion.7), channel_id=1, source_target_pairs={{0,16},{8,24},{16,0},{24,8},{1,17},{9,25},{17,1},{25,9},{2,18},{10... | collective-permute-start | bytes 98312 | tf_op jit(solution)/shard_map/ppermute | solution.py:443
  20.3 9.0 %collective-permute-start.15 = (bf16[32,1024]{1,0:T(8,128)(2,1)S(1)}, bf16[32,1024]{1,0:T(8,128)(2,1)S(1)}, u32[]{:S(2)}, u32[]{:S(2)}) collective-permute-start(bf16[32,1024]{1,0:T(8,128)(2,1)S(1)} %fusion.2), channel_id=1, source_target_pairs={{0,8},{8,0},{16,24},{24,16},{1,9},{9,1},{17,25},{25,17},{2,10},{10... | collective-permute-start | bytes 196616 | tf_op jit(solution)/shard_map/ppermute | solution.py:440
  22.3 4.3 %collective-permute-start.16 = (bf16[32,1024]{1,0:T(8,128)(2,1)S(1)}, bf16[32,1024]{1,0:T(8,128)(2,1)S(1)}, u32[]{:S(2)}, u32[]{:S(2)}) collective-permute-start(bf16[32,1024]{1,0:T(8,128)(2,1)S(1)} %fusion.1), channel_id=1, source_target_pairs={{0,16},{8,24},{16,0},{24,8},{1,17},{9,25},{17,1},{25,9},{2,18},{10... | collective-permute-start | bytes 196616 | tf_op jit(solution)/shard_map/ppermute | solution.py:443
  24.2 2.9 %collective-permute-start.11 = (bf16[32,256]{1,0:T(8,128)(2,1)S(1)}, bf16[32,256]{1,0:T(8,128)(2,1)S(1)}, u32[]{:S(2)}, u32[]{:S(2)}) collective-permute-start(bf16[32,256]{1,0:T(8,128)(2,1)S(1)} %get-tuple-element.85), channel_id=1, source_target_pairs={{0,8},{8,0},{16,24},{24,16},{1,9},{9,1},{17,25},{25,17},{2,10},{10... | collective-permute-start | bytes 49160 | tf_op jit(solution)/shard_map/ppermute | solution.py:440
  26.5 1.3 %collective-permute-start.7 = (bf16[32,1280]{1,0:T(8,128)(2,1)S(1)}, bf16[32,1280]{1,0:T(8,128)(2,1)S(1)}, u32[]{:S(2)}, u32[]{:S(2)}) collective-permute-start(bf16[32,1280]{1,0:T(8,128)(2,1)S(1)} %pad_maximum_fusion.2), channel_id=1, source_target_pairs={{0,8},{8,0},{16,24},{24,16},{1,9},{9,1},{17,25},{25,17},{2,10},{10... | collective-permute-start | bytes 245768 | tf_op jit(solution)/shard_map/ppermute | solution.py:440
  26.6 2.7 %collective-permute-start.17 = (bf16[32,1024]{1,0:T(8,128)(2,1)S(1)}, bf16[32,1024]{1,0:T(8,128)(2,1)S(1)}, u32[]{:S(2)}, u32[]{:S(2)}) collective-permute-start(bf16[32,1024]{1,0:T(8,128)(2,1)S(1)} %get-tuple-element.77), channel_id=1, source_target_pairs={{0,8},{8,0},{16,24},{24,16},{1,9},{9,1},{17,25},{25,17},{2,10},{10... | collective-permute-start | bytes 196616 | tf_op jit(solution)/shard_map/ppermute | solution.py:440
  27.9 9.7 %collective-permute-start.12 = (bf16[128,768]{1,0:T(8,128)(2,1)S(1)}, bf16[128,768]{1,0:T(8,128)(2,1)S(1)}, u32[]{:S(2)}, u32[]{:S(2)}) collective-permute-start(bf16[128,768]{1,0:T(8,128)(2,1)S(1)} %get-tuple-element.63), channel_id=1, source_target_pairs={{0,1},{1,0},{2,3},{3,2},{4,5},{5,4},{6,7},{7,6},{8,10},{9,11},{10,... | collective-permute-start | bytes 589832 | tf_op jit(solution)/shard_map/ppermute | solution.py:562
  29.4 6.4 %collective-permute-start.18 = (bf16[128,512]{1,0:T(8,128)(2,1)S(1)}, bf16[128,512]{1,0:T(8,128)(2,1)S(1)}, u32[]{:S(2)}, u32[]{:S(2)}) collective-permute-start(bf16[128,512]{1,0:T(8,128)(2,1)S(1)} %get-tuple-element.72), channel_id=1, source_target_pairs={{0,1},{1,0},{2,3},{3,2},{4,5},{5,4},{6,7},{7,6},{8,10},{9,11},{10,... | collective-permute-start | bytes 393224 | tf_op jit(solution)/shard_map/ppermute | solution.py:562
  30.2 5.6 %collective-permute-start.19 = (bf16[128,256]{1,0:T(8,128)(2,1)S(1)}, bf16[128,256]{1,0:T(8,128)(2,1)S(1)}, u32[]{:S(2)}, u32[]{:S(2)}) collective-permute-start(bf16[128,256]{1,0:T(8,128)(2,1)S(1)} %shard_map.56.right), channel_id=1, source_target_pairs={{0,1},{1,0},{2,3},{3,2},{4,5},{5,4},{6,7},{7,6},{8,10},{9,11},{10,... | collective-permute-start | bytes 196616 | tf_op jit(solution)/shard_map/ppermute | solution.py:562
  36.2 5.0 %collective-permute-start.20 = (bf16[2,128,256]{2,1,0:T(8,128)(2,1)S(1)}, bf16[2,128,256]{2,1,0:T(8,128)(2,1)S(1)}, u32[]{:S(2)}, u32[]{:S(2)}) collective-permute-start(bf16[2,128,256]{2,1,0:T(8,128)(2,1)S(1)} %get-tuple-element.74), channel_id=1, source_target_pairs={{0,2},{1,3},{2,0},{3,1},{4,6},{5,7},{6,4},{7,5},{8,9},{9,8},{10,11... | collective-permute-start | bytes 393224 | tf_op jit(solution)/shard_map/ppermute | solution.py:562
  38.0 5.7 %collective-permute-start.13 = (bf16[2,128,256]{2,1,0:T(8,128)(2,1)S(1)}, bf16[2,128,256]{2,1,0:T(8,128)(2,1)S(1)}, u32[]{:S(2)}, u32[]{:S(2)}) collective-permute-start(bf16[2,128,256]{2,1,0:T(8,128)(2,1)S(1)} %get-tuple-element.65), channel_id=1, source_target_pairs={{0,2},{1,3},{2,0},{3,1},{4,6},{5,7},{6,4},{7,5},{8,9},{9,8},{10,11... | collective-permute-start | bytes 393224 | tf_op jit(solution)/shard_map/ppermute | solution.py:562
  41.2 6.7 %collective-permute-start.21 = (bf16[1,128,256]{2,1,0:T(8,128)(2,1)S(1)}, bf16[1,128,256]{2,1,0:T(8,128)(2,1)S(1)}, u32[]{:S(2)}, u32[]{:S(2)}) collective-permute-start(bf16[1,128,256]{2,1,0:T(8,128)(2,1)S(1)} %get-tuple-element.76), channel_id=1, source_target_pairs={{0,4},{1,5},{2,6},{3,7},{4,0},{5,1},{6,2},{7,3},{8,12},{9,13},{10,... | collective-permute-start | bytes 196616 | tf_op jit(solution)/shard_map/ppermute | solution.py:562
  43.8 5.2 %collective-permute-start.14 = (bf16[1,128,256]{2,1,0:T(8,128)(2,1)S(1)}, bf16[1,128,256]{2,1,0:T(8,128)(2,1)S(1)}, u32[]{:S(2)}, u32[]{:S(2)}) collective-permute-start(bf16[1,128,256]{2,1,0:T(8,128)(2,1)S(1)} %get-tuple-element.67), channel_id=1, source_target_pairs={{0,4},{1,5},{2,6},{3,7},{4,0},{5,1},{6,2},{7,3},{8,12},{9,13},{10,... | collective-permute-start | bytes 196616 | tf_op jit(solution)/shard_map/ppermute | solution.py:562

commit v3 on v2

--- a/solution.py
+++ b/solution.py
@@ -368,31 +368,25 @@
     return [back.at[0] for back in arrays[:stages]], arrays[stages : stages + 3]
 
 
-def early_body(stages, channels, *refs):
-    gather_rows(refs[-1], *flow_rows(refs, stages, slice(channels, None)))
-
-
-def late_up_body(stages, chunk, *refs):
-    keep, send, wide = refs[stages + 3 :]
-    gather_rows(wide, *back_rows(refs, stages))
-    split_columns(wide, keep, send, chunk)
-
-
-def late_inner_body(stages, chunk, *refs):
+def late_body(stages, chunk, up, *refs):
     left, right, send, wide = refs[2 * stages + 6 :]
     channels = wide.shape[1]
-    gather_rows(wide, *flow_rows(refs, stages, slice(0, channels)))
+    backs = back_rows(refs[stages + 3 :], stages)
+    if up:
+        gather_rows(wide, *backs)
+        gather_rows(right, *flow_rows(refs, stages, slice(channels, None)))
+    else:
+        gather_rows(wide, *flow_rows(refs, stages, slice(0, channels)))
+        gather_rows(right, *backs)
     split_columns(wide, left, send, chunk)
-    gather_rows(right, *back_rows(refs[stages + 3 :], stages))
     send[:, channels // 2 :] = right[...]
 
 
-def half_gradient_body(left, right, *refs):
-    came, (send, keep, full) = refs[:-3], refs[-3:]
+def half_gradient_body(left, right, came, send, keep, full):
     columns = left.shape[1]
-    if len(came) == 1:
-        came = (came[0].at[:, :columns], came[0].at[:, columns:])
-    full[...] = contract(left[...], right[...], 0, 0) + contract(came[0][...], came[1][...], 0, 0)
+    full[...] = contract(left[...], right[...], 0, 0) + contract(
+        came[:, :columns], came[:, columns:], 0, 0
+    )
     _, _, side = first_sides()
     chunk = send.shape[1]
     for place in range(send.shape[0]):
@@ -529,8 +523,8 @@
     else:
         far_up, cross_up = far_up[0], far_up[1]
     cross_up = swap_cores(cross_up)
-    cross_inner = swap_cores(far_inner[1])
-    far_inner = far_inner[0]
+    far_inner, cross_inner = far_inner[0], far_inner[1]
+    cross_inner = swap_cores(cross_inner)
 
     chunk = channels // replicas
     fore = flows + [side_flow, far_flow, cross_flow]
@@ -567,44 +561,26 @@
     shape = lambda *dims: jax.ShapeDtypeStruct(dims, jnp.bfloat16)
     half = shape(4 * rows, channels // 2)
     narrow = shape(4 * rows, inner)
-    active = pl.pallas_call(
-        functools.partial(early_body, stages, channels),
-        out_shape=narrow,
-        in_specs=[VMEM] * len(fore),
-        out_specs=VMEM,
-        compiler_params=PARAMS,
-    )(*fore)
-    came_active = exchange(active, stages, replicas, 1, 2)
-    up, up_send = pl.pallas_call(
-        functools.partial(late_up_body, stages, chunk),
-        out_shape=[half, half],
-        in_specs=[VMEM] * len(ups),
-        out_specs=[VMEM] * 2,
-        scratch_shapes=[pltpu.VMEM((4 * rows, channels), jnp.bfloat16)],
-        compiler_params=PARAMS,
-    )(*ups)
-    came_up = exchange(up_send, stages, replicas, 1, 2)
-    lifted, back, send = pl.pallas_call(
-        functools.partial(late_inner_body, stages, chunk),
-        out_shape=[half, narrow, shape(4 * rows, channels // 2 + inner)],
-        in_specs=[VMEM] * (len(fore) + len(backs)),
-        out_specs=[VMEM] * 3,
-        scratch_shapes=[pltpu.VMEM((4 * rows, channels), jnp.bfloat16)],
-        compiler_params=PARAMS,
-    )(*fore, *backs)
-    came_inner = exchange(send, stages, replicas, 1, 2)
     parts = []
-    streams = ((lifted, back, came_inner), (up, active, came_up, came_active))
-    for operands in streams:
+    for name, late in (("inner", backs), ("up", ups)):
+        left, right, send = pl.pallas_call(
+            functools.partial(late_body, stages, chunk, name == "up"),
+            out_shape=[half, narrow, shape(4 * rows, channels // 2 + inner)],
+            in_specs=[VMEM] * (len(fore) + len(late)),
+            out_specs=[VMEM] * 3,
+            scratch_shapes=[pltpu.VMEM((4 * rows, channels), jnp.bfloat16)],
+            compiler_params=PARAMS,
+        )(*fore, *late)
+        came = exchange(send, stages, replicas, 1, 2)
         count = replicas // 4
         send, keep = pl.pallas_call(
             half_gradient_body,
             out_shape=sums(count, chunk, inner),
-            in_specs=[VMEM] * len(operands),
+            in_specs=[VMEM] * 3,
             out_specs=[VMEM] * 2,
             scratch_shapes=[pltpu.VMEM((channels // 2, inner), jnp.float32)],
             compiler_params=PARAMS,
-        )(*operands)
+        )(left, right, came)
         came = exchange(send, stages, replicas, 2, 1)
         for bit in range(2, replicas.bit_length() - 1):
             count //= 2

time: 50 us -> 48.1 us (0.962)
  waiting for transfers between devices: 17.8 us -> 16.8 us
  starting transfers between devices: 22.3 us -> 21.5 us
    ppermute x7 -> x6, waiting for transfers between devices: 9.39 us -> 8.36 us  [exchange(): return lax.ppermute(shard, AXES, pairs)]
    ppermute x7 -> x6, starting transfers between devices: 10.7 us -> 9.89 us  [exchange(): return lax.ppermute(shard, AXES, pairs)]
  transfers between devices with their start and end apart: 22 -> 21, of which waited for: 11 -> 12; matrix products, arithmetic and copies ran while one was open for 0% -> 0% of each run, Pallas kernels for 11% -> 12%
where the time goes in v3:
time: 48.1 us; the launch traced here: 47.9 us
  starting transfers between devices  21.5 us (45%)
  waiting for transfers between devices  16.8 us (35%)
  Pallas kernels  9.29 us (19%)
    ppermute x6, starting transfers between devices, exchange(): return lax.ppermute(shard, AXES, pairs)  9.89 us
    ppermute x6, waiting for transfers between devices, exchange(): return lax.ppermute(shard, AXES, pairs)  8.36 us
    ppermute x2, starting transfers between devices, hop(): return lax.ppermute(shard, 'pipe', pairs)  4.81 us
    ppermute x3, starting transfers between devices, mirror(): return lax.ppermute(shard, 'pipe', mirror_pairs)  4.7 us
    ppermute x3, waiting for transfers between devices, mirror(): return lax.ppermute(shard, 'pipe', mirror_pairs)  4.09 us
    pallas_call x3, Pallas kernels, run_stage(): pl.pallas_call(functools.partial(stage_body, step, forward, backward, las...  3.85 us
    ppermute x2, waiting for transfers between devices, hop(): return lax.ppermute(shard, 'pipe', pairs)  3.23 us
    pallas_call x2, Pallas kernels, load(): pl.pallas_call(functools.partial(load_body, step), out_shape=outs, in_spe...  2.44 us
  transfers between devices with their start and end apart: 21, of which 12 were waited for; matrix products, arithmetic and copies ran while one was open for 0% of the time, Pallas kernels for 12%

profile of v3, /device:TPU:0, one launch (start us, length us, event | category | flops | bytes accessed | tf_op | source)
XLA Modules:
  0.0 47.9 jit_solution(8570470580924850671)
XLA Ops:
  0.0 1.2 %shard_map.46 = (bf16[1024,256]{1,0:T(8,128)(2,1)S(1)}, bf16[1024,256]{1,0:T(8,128)(2,1)S(1)}, bf16[32,1024]{1,0:T(8,128)(2,1)S(1)}) custom-call(bf16[2,1024,256]{2,1,0:T(8,128)(2,1)} %bitcast.20, bf16[2,1024,256]{2,1,0:T(8,128)(2,1)} %bitcast.22, bf16[2,2,32,1024]{3,2,1,0:T(8,128)(2,1)} %inputs), custom_call_target="tpu_custom_call" | custom-call | tf_op jit(solution)/shard_map/pallas_call | solution.py:68
  1.2 0.6 %collective-permute-start = (bf16[1024,256]{1,0:T(8,128)(2,1)S(1)}, bf16[1024,256]{1,0:T(8,128)(2,1)S(1)}, u32[]{:S(2)}, u32[]{:S(2)}) collective-permute-start(bf16[1024,256]{1,0:T(8,128)(2,1)S(1)} %get-tuple-element.43.refs_0_), channel_id=1, source_target_pairs={{0,8},{8,0},{16,24},{24,16},{1,9},{9,1},{17,25},{25,17},{2,10},{10... | collective-permute-start | bytes 1572872 | tf_op jit(solution)/shard_map/ppermute | solution.py:434
  1.8 0.1 collective-permute-start.1
  1.9 1.2 %shard_map.48 = (bf16[1024,256]{1,0:T(8,128)(2,1)S(1)}, bf16[1024,256]{1,0:T(8,128)(2,1)S(1)}) custom-call(bf16[2,1024,256]{2,1,0:T(8,128)(2,1)} %bitcast.21, bf16[2,1024,256]{2,1,0:T(8,128)(2,1)} %bitcast.23), custom_call_target="tpu_custom_call" | custom-call | tf_op jit(solution)/shard_map/pallas_call | solution.py:68
  3.1 0.5 %collective-permute-start.3 = (bf16[1024,256]{1,0:T(8,128)(2,1)S(1)}, bf16[1024,256]{1,0:T(8,128)(2,1)S(1)}, u32[]{:S(2)}, u32[]{:S(2)}) collective-permute-start(bf16[1024,256]{1,0:T(8,128)(2,1)S(1)} %get-tuple-element.48.expand_own.refs_1_), channel_id=1, source_target_pairs={{0,8},{8,0},{16,24},{24,16},{1,9},{9,1},{17,25},{25,17},{2,10},{10... | collective-permute-start | bytes 1572872 | tf_op jit(solution)/shard_map/ppermute | solution.py:434
  3.6 0.1 collective-permute-start.2
  3.7 0.0 collective-permute-done.refs_2_
  3.7 0.4 collective-permute-done.1.refs_3_
  4.1 1.2 %shard_map.47 = (bf16[2,32,1280]{2,1,0:T(8,128)(2,1)S(1)}, bf16[32,1024]{1,0:T(8,128)(2,1)S(1)}, bf16[2,32,1024]{2,1,0:T(8,128)(2,1)S(1)}, f32[2,32,256]{2,1,0:T(8,128)S(1)}) custom-call(bf16[1024,256]{1,0:T(8,128)(2,1)S(1)} %get-tuple-element.43.refs_0_, bf16[1024,256]{1,0:T(8,128)(2,1)S(1)} %get-tuple-element.44.refs_1_, ...), custom_call_target="tpu_custom_call" | custom-call | flops 67108864 | bytes 2097152 | tf_op jit(solution)/shard_map/pallas_call | solution.py:250
  5.2 2.9 %collective-permute-start.4 = (bf16[32,1024]{1,0:T(8,128)(2,1)S(1)}, bf16[32,1024]{1,0:T(8,128)(2,1)S(1)}, u32[]{:S(2)}, u32[]{:S(2)}) collective-permute-start(bf16[32,1024]{1,0:T(8,128)(2,1)S(1)} %get-tuple-element.49.leave), channel_id=1, source_target_pairs={{0,16},{16,0},{8,24},{24,8},{1,17},{17,1},{9,25},{25,9},{2,18},{18... | collective-permute-start | bytes 196616 | tf_op jit(solution)/shard_map/ppermute | solution.py:431
  8.1 0.0 collective-permute-done.3.expand_other.refs_3_
  8.1 1.2 %shard_map.49 = (bf16[32,1024]{1,0:T(8,128)(2,1)S(1)}, f32[32,256]{1,0:T(8,128)S(1)}, bf16[32,1024]{1,0:T(8,128)(2,1)S(1)}, bf16[32,1024]{1,0:T(8,128)(2,1)S(1)}) custom-call(bf16[1024,256]{1,0:T(8,128)(2,1)S(1)} %get-tuple-element.48.expand_own.refs_1_, bf16[1024,256]{1,0:T(8,128)(2,1)S(1)} %collective-permute-done.3.expand_other.refs_3_, ...), custom_call_target="tpu_custom_call" | custom-call | tf_op jit(solution)/shard_map/pallas_call | solution.py:470
  9.3 0.0 collective-permute-done.2.refs_2_
  9.3 1.2 %collective-permute-done.4.refs_4_ = bf16[32,1024]{1,0:T(8,128)(2,1)S(1)} collective-permute-done((bf16[32,1024]{1,0:T(8,128)(2,1)S(1)}, bf16[32,1024]{1,0:T(8,128)(2,1)S(1)}, u32[]{:S(2)}, u32[]{:S(2)}) %collective-permute-start.4) | collective-permute-done | bytes 65568 | tf_op jit(solution)/shard_map/ppermute | solution.py:431
  10.5 1.8 %shard_map.50 = (bf16[2,32,1280]{2,1,0:T(8,128)(2,1)S(1)}, bf16[2,32,1024]{2,1,0:T(8,128)(2,1)S(1)}, bf16[2,32,256]{2,1,0:T(8,128)(2,1)S(1)}, bf16[32,1024]{1,0:T(8,128)(2,1)S(1)}) custom-call(bf16[1024,256]{1,0:T(8,128)(2,1)S(1)} %get-tuple-element.47.refs_0_, bf16[1024,256]{1,0:T(8,128)(2,1)S(1)} %get-tuple-element.48.expand_own.refs_1_, ...), custom_call_target="tpu_custom_call" | custom-call | flops 134217728 | bytes 2097152 | tf_op jit(solution)/shard_map/pallas_call | solution.py:250
  12.3 1.9 %collective-permute-start.8 = (bf16[32,1024]{1,0:T(8,128)(2,1)S(1)}, bf16[32,1024]{1,0:T(8,128)(2,1)S(1)}, u32[]{:S(2)}, u32[]{:S(2)}) collective-permute-start(bf16[32,1024]{1,0:T(8,128)(2,1)S(1)} %get-tuple-element.57), channel_id=1, source_target_pairs={{0,16},{16,0},{8,24},{24,8},{1,17},{17,1},{9,25},{25,9},{2,18},{18... | collective-permute-start | bytes 196616 | tf_op jit(solution)/shard_map/ppermute | solution.py:431
  14.3 0.1 collective-permute-start.5
  14.5 0.2 collective-permute-start.6
  14.7 2.1 %collective-permute-done.8.refs_4_ = bf16[32,1024]{1,0:T(8,128)(2,1)S(1)} collective-permute-done((bf16[32,1024]{1,0:T(8,128)(2,1)S(1)}, bf16[32,1024]{1,0:T(8,128)(2,1)S(1)}, u32[]{:S(2)}, u32[]{:S(2)}) %collective-permute-start.8) | collective-permute-done | bytes 65568 | tf_op jit(solution)/shard_map/ppermute | solution.py:431
  16.7 0.9 %shard_map.51 = (bf16[2,32,1024]{2,1,0:T(8,128)(2,1)S(1)}, bf16[2,32,256]{2,1,0:T(8,128)(2,1)S(1)}) custom-call(bf16[1024,256]{1,0:T(8,128)(2,1)S(1)} %get-tuple-element.43.refs_0_, bf16[1024,256]{1,0:T(8,128)(2,1)S(1)} %get-tuple-element.44.refs_1_, bf16[1024,256]{1,0:T(8,128)(2,1)S(1)} %collective-permute-done.refs_2_, ...), custom_call_target="tpu_custom_call" | custom-call | flops 67108864 | bytes 2097152 | tf_op jit(solution)/shard_map/pallas_call | solution.py:250
  17.7 0.1 collective-permute-start.9
  17.7 2.5 %collective-permute-start.10 = (bf16[2,32,256]{2,1,0:T(8,128)(2,1)S(1)}, bf16[2,32,256]{2,1,0:T(8,128)(2,1)S(1)}, u32[]{:S(2)}, u32[]{:S(2)}) collective-permute-start(bf16[2,32,256]{2,1,0:T(8,128)(2,1)S(1)} %broadcast_select_fusion.7), channel_id=1, source_target_pairs={{0,16},{8,24},{16,0},{24,8},{1,17},{9,25},{17,1},{25,9},{2,18},{10... | collective-permute-start | bytes 98312 | tf_op jit(solution)/shard_map/ppermute | solution.py:437
  20.3 0.2 collective-permute-start.15
  20.5 1.8 %collective-permute-done.10 = bf16[2,32,256]{2,1,0:T(8,128)(2,1)S(1)} collective-permute-done((bf16[2,32,256]{2,1,0:T(8,128)(2,1)S(1)}, bf16[2,32,256]{2,1,0:T(8,128)(2,1)S(1)}, u32[]{:S(2)}, u32[]{:S(2)}) %collective-permute-start.10) | collective-permute-done | bytes 32800 | tf_op jit(solution)/shard_map/ppermute | solution.py:437
  22.3 1.9 %collective-permute-start.16 = (bf16[32,1024]{1,0:T(8,128)(2,1)S(1)}, bf16[32,1024]{1,0:T(8,128)(2,1)S(1)}, u32[]{:S(2)}, u32[]{:S(2)}) collective-permute-start(bf16[32,1024]{1,0:T(8,128)(2,1)S(1)} %fusion.1), channel_id=1, source_target_pairs={{0,16},{8,24},{16,0},{24,8},{1,17},{9,25},{17,1},{25,9},{2,18},{10... | collective-permute-start | bytes 196616 | tf_op jit(solution)/shard_map/ppermute | solution.py:437
  24.3 2.3 %collective-permute-done.16 = bf16[32,1024]{1,0:T(8,128)(2,1)S(1)} collective-permute-done((bf16[32,1024]{1,0:T(8,128)(2,1)S(1)}, bf16[32,1024]{1,0:T(8,128)(2,1)S(1)}, u32[]{:S(2)}, u32[]{:S(2)}) %collective-permute-start.16) | collective-permute-done | bytes 65568 | tf_op jit(solution)/shard_map/ppermute | solution.py:437
  26.6 0.6 %collective-permute-start.17 = (bf16[32,1024]{1,0:T(8,128)(2,1)S(1)}, bf16[32,1024]{1,0:T(8,128)(2,1)S(1)}, u32[]{:S(2)}, u32[]{:S(2)}) collective-permute-start(bf16[32,1024]{1,0:T(8,128)(2,1)S(1)} %get-tuple-element.79), channel_id=1, source_target_pairs={{0,8},{8,0},{16,24},{24,16},{1,9},{9,1},{17,25},{25,17},{2,10},{10... | collective-permute-start | bytes 196616 | tf_op jit(solution)/shard_map/ppermute | solution.py:434
  27.2 0.0 collective-permute-done.5.refs_2_
  27.2 0.7 %collective-permute-done.7.refs_4_ = bf16[32,1280]{1,0:T(8,128)(2,1)S(1)} collective-permute-done((bf16[32,1280]{1,0:T(8,128)(2,1)S(1)}, bf16[32,1280]{1,0:T(8,128)(2,1)S(1)}, u32[]{:S(2)}, u32[]{:S(2)}) %collective-permute-start.7) | collective-permute-done | bytes 81952 | tf_op jit(solution)/shard_map/ppermute | solution.py:434
  27.8 0.1 shard_map.52
  27.9 1.4 %collective-permute-start.12 = (bf16[128,768]{1,0:T(8,128)(2,1)S(1)}, bf16[128,768]{1,0:T(8,128)(2,1)S(1)}, u32[]{:S(2)}, u32[]{:S(2)}) collective-permute-start(bf16[128,768]{1,0:T(8,128)(2,1)S(1)} %get-tuple-element.64), channel_id=1, source_target_pairs={{0,1},{1,0},{2,3},{3,2},{4,5},{5,4},{6,7},{7,6},{8,10},{9,11},{10,... | collective-permute-start | bytes 589832 | tf_op jit(solution)/shard_map/ppermute | solution.py:556
  29.3 0.0 collective-permute-done.15.refs_7_
  29.3 0.0 collective-permute-done.17.refs_9_
  29.3 0.1 shard_map.55
  29.4 0.8 %collective-permute-start.18 = (bf16[128,768]{1,0:T(8,128)(2,1)S(1)}, bf16[128,768]{1,0:T(8,128)(2,1)S(1)}, u32[]{:S(2)}, u32[]{:S(2)}) collective-permute-start(bf16[128,768]{1,0:T(8,128)(2,1)S(1)} %get-tuple-element.74), channel_id=1, source_target_pairs={{0,1},{1,0},{2,3},{3,2},{4,5},{5,4},{6,7},{7,6},{8,10},{9,11},{10,... | collective-permute-start | bytes 589832 | tf_op jit(solution)/shard_map/ppermute | solution.py:556
  30.2 3.5 %collective-permute-done.12.came = bf16[128,768]{1,0:T(8,128)(2,1)S(1)} collective-permute-done((bf16[128,768]{1,0:T(8,128)(2,1)S(1)}, bf16[128,768]{1,0:T(8,128)(2,1)S(1)}, u32[]{:S(2)}, u32[]{:S(2)}) %collective-permute-start.12) | collective-permute-done | bytes 196640 | tf_op jit(solution)/shard_map/ppermute | solution.py:556
  33.7 0.4 shard_map.53
  34.1 1.4 %collective-permute-start.13 = (bf16[2,128,256]{2,1,0:T(8,128)(2,1)S(1)}, bf16[2,128,256]{2,1,0:T(8,128)(2,1)S(1)}, u32[]{:S(2)}, u32[]{:S(2)}) collective-permute-start(bf16[2,128,256]{2,1,0:T(8,128)(2,1)S(1)} %get-tuple-element.66), channel_id=1, source_target_pairs={{0,2},{1,3},{2,0},{3,1},{4,6},{5,7},{6,4},{7,5},{8,9},{9,8},{10,11... | collective-permute-start | bytes 393224 | tf_op jit(solution)/shard_map/ppermute | solution.py:556
  35.5 0.3 collective-permute-done.18.came
  35.8 0.4 shard_map.56
  36.2 1.4 %collective-permute-start.19 = (bf16[2,128,256]{2,1,0:T(8,128)(2,1)S(1)}, bf16[2,128,256]{2,1,0:T(8,128)(2,1)S(1)}, u32[]{:S(2)}, u32[]{:S(2)}) collective-permute-start(bf16[2,128,256]{2,1,0:T(8,128)(2,1)S(1)} %get-tuple-element.76), channel_id=1, source_target_pairs={{0,2},{1,3},{2,0},{3,1},{4,6},{5,7},{6,4},{7,5},{8,9},{9,8},{10,11... | collective-permute-start | bytes 393224 | tf_op jit(solution)/shard_map/ppermute | solution.py:556
  37.6 1.5 %collective-permute-done.13.came = bf16[2,128,256]{2,1,0:T(8,128)(2,1)S(1)} collective-permute-done((bf16[2,128,256]{2,1,0:T(8,128)(2,1)S(1)}, bf16[2,128,256]{2,1,0:T(8,128)(2,1)S(1)}, u32[]{:S(2)}, u32[]{:S(2)}) %collective-permute-start.13) | collective-permute-done | bytes 131104 | tf_op jit(solution)/shard_map/ppermute | solution.py:556
  39.1 2.4 %collective-permute-start.14 = (bf16[1,128,256]{2,1,0:T(8,128)(2,1)S(1)}, bf16[1,128,256]{2,1,0:T(8,128)(2,1)S(1)}, u32[]{:S(2)}, u32[]{:S(2)}) collective-permute-start(bf16[1,128,256]{2,1,0:T(8,128)(2,1)S(1)} %get-tuple-element.68), channel_id=1, source_target_pairs={{0,4},{1,5},{2,6},{3,7},{4,0},{5,1},{6,2},{7,3},{8,12},{9,13},{10,... | collective-permute-start | bytes 196616 | tf_op jit(solution)/shard_map/ppermute | solution.py:556
  41.6 0.3 collective-permute-done.19.came
  42.0 2.4 %collective-permute-start.20 = (bf16[1,128,256]{2,1,0:T(8,128)(2,1)S(1)}, bf16[1,128,256]{2,1,0:T(8,128)(2,1)S(1)}, u32[]{:S(2)}, u32[]{:S(2)}) collective-permute-start(bf16[1,128,256]{2,1,0:T(8,128)(2,1)S(1)} %get-tuple-element.78), channel_id=1, source_target_pairs={{0,4},{1,5},{2,6},{3,7},{4,0},{5,1},{6,2},{7,3},{8,12},{9,13},{10,... | collective-permute-start | bytes 196616 | tf_op jit(solution)/shard_map/ppermute | solution.py:556
  44.4 1.5 %collective-permute-done.14.came_reduce = bf16[1,128,256]{2,1,0:T(8,128)(2,1)S(1)} collective-permute-done((bf16[1,128,256]{2,1,0:T(8,128)(2,1)S(1)}, bf16[1,128,256]{2,1,0:T(8,128)(2,1)S(1)}, u32[]{:S(2)}, u32[]{:S(2)}) %collective-permute-start.14) | collective-permute-done | bytes 65568 | tf_op jit(solution)/shard_map/ppermute | solution.py:556
  45.9 1.3 %collective-permute-done.20.came_expand = bf16[1,128,256]{2,1,0:T(8,128)(2,1)S(1)} collective-permute-done((bf16[1,128,256]{2,1,0:T(8,128)(2,1)S(1)}, bf16[1,128,256]{2,1,0:T(8,128)(2,1)S(1)}, u32[]{:S(2)}, u32[]{:S(2)}) %collective-permute-start.20) | collective-permute-done | bytes 65568 | tf_op jit(solution)/shard_map/ppermute | solution.py:556
  47.2 0.7 %shard_map.58 = f32[1,2,128,256]{3,2,1,0:T(8,128)} custom-call(f32[1,128,256]{2,1,0:T(8,128)S(1)} %get-tuple-element.67.keep_reduce, bf16[1,128,256]{2,1,0:T(8,128)(2,1)S(1)} %collective-permute-done.14.came_reduce, f32[1,128,256]{2,1,0:T(8,128)S(1)} %get-tuple-element.77.keep_expand, bf16[1,128,256]{2,1,0:T(8,128)(2,1)S(1)} %collective-permute-done.20.came_expand), custom_call_target="tpu_custom_call" | custom-call | tf_op jit(solution)/shard_map/pallas_call | solution.py:535
  (23 shorter events, 0.2 us)
Async XLA Ops:
  1.2 2.4 %collective-permute-start = (bf16[1024,256]{1,0:T(8,128)(2,1)S(1)}, bf16[1024,256]{1,0:T(8,128)(2,1)S(1)}, u32[]{:S(2)}, u32[]{:S(2)}) collective-permute-start(bf16[1024,256]{1,0:T(8,128)(2,1)S(1)} %get-tuple-element.43.refs_0_), channel_id=1, source_target_pairs={{0,8},{8,0},{16,24},{24,16},{1,9},{9,1},{17,25},{25,17},{2,10},{10... | collective-permute-start | bytes 1572872 | tf_op jit(solution)/shard_map/ppermute | solution.py:434
  1.8 2.3 %collective-permute-start.1 = (bf16[1024,256]{1,0:T(8,128)(2,1)S(1)}, bf16[1024,256]{1,0:T(8,128)(2,1)S(1)}, u32[]{:S(2)}, u32[]{:S(2)}) collective-permute-start(bf16[1024,256]{1,0:T(8,128)(2,1)S(1)} %get-tuple-element.44.refs_1_), channel_id=1, source_target_pairs={{0,8},{8,0},{16,24},{24,16},{1,9},{9,1},{17,25},{25,17},{2,10},{10... | collective-permute-start | bytes 1572872 | tf_op jit(solution)/shard_map/ppermute | solution.py:434
  3.1 5.0 %collective-permute-start.3 = (bf16[1024,256]{1,0:T(8,128)(2,1)S(1)}, bf16[1024,256]{1,0:T(8,128)(2,1)S(1)}, u32[]{:S(2)}, u32[]{:S(2)}) collective-permute-start(bf16[1024,256]{1,0:T(8,128)(2,1)S(1)} %get-tuple-element.48.expand_own.refs_1_), channel_id=1, source_target_pairs={{0,8},{8,0},{16,24},{24,16},{1,9},{9,1},{17,25},{25,17},{2,10},{10... | collective-permute-start | bytes 1572872 | tf_op jit(solution)/shard_map/ppermute | solution.py:434
  3.6 5.7 %collective-permute-start.2 = (bf16[1024,256]{1,0:T(8,128)(2,1)S(1)}, bf16[1024,256]{1,0:T(8,128)(2,1)S(1)}, u32[]{:S(2)}, u32[]{:S(2)}) collective-permute-start(bf16[1024,256]{1,0:T(8,128)(2,1)S(1)} %get-tuple-element.47.refs_0_), channel_id=1, source_target_pairs={{0,8},{8,0},{16,24},{24,16},{1,9},{9,1},{17,25},{25,17},{2,10},{10... | collective-permute-start | bytes 1572872 | tf_op jit(solution)/shard_map/ppermute | solution.py:434
  5.2 5.3 %collective-permute-start.4 = (bf16[32,1024]{1,0:T(8,128)(2,1)S(1)}, bf16[32,1024]{1,0:T(8,128)(2,1)S(1)}, u32[]{:S(2)}, u32[]{:S(2)}) collective-permute-start(bf16[32,1024]{1,0:T(8,128)(2,1)S(1)} %get-tuple-element.49.leave), channel_id=1, source_target_pairs={{0,16},{16,0},{8,24},{24,8},{1,17},{17,1},{9,25},{25,9},{2,18},{18... | collective-permute-start | bytes 196616 | tf_op jit(solution)/shard_map/ppermute | solution.py:431
  12.3 4.4 %collective-permute-start.8 = (bf16[32,1024]{1,0:T(8,128)(2,1)S(1)}, bf16[32,1024]{1,0:T(8,128)(2,1)S(1)}, u32[]{:S(2)}, u32[]{:S(2)}) collective-permute-start(bf16[32,1024]{1,0:T(8,128)(2,1)S(1)} %get-tuple-element.57), channel_id=1, source_target_pairs={{0,16},{16,0},{8,24},{24,8},{1,17},{17,1},{9,25},{25,9},{2,18},{18... | collective-permute-start | bytes 196616 | tf_op jit(solution)/shard_map/ppermute | solution.py:431
  14.3 12.9 %collective-permute-start.5 = (bf16[32,1280]{1,0:T(8,128)(2,1)S(1)}, bf16[32,1280]{1,0:T(8,128)(2,1)S(1)}, u32[]{:S(2)}, u32[]{:S(2)}) collective-permute-start(bf16[32,1280]{1,0:T(8,128)(2,1)S(1)} %fusion), channel_id=1, source_target_pairs={{0,8},{8,0},{16,24},{24,16},{1,9},{9,1},{17,25},{25,17},{2,10},{10... | collective-permute-start | bytes 245768 | tf_op jit(solution)/shard_map/ppermute | solution.py:434
  14.5 9.8 %collective-permute-start.6 = (bf16[32,1536]{1,0:T(8,128)(2,1)S(1)}, bf16[32,1536]{1,0:T(8,128)(2,1)S(1)}, u32[]{:S(2)}, u32[]{:S(2)}) collective-permute-start(bf16[32,1536]{1,0:T(8,128)(2,1)S(1)} %pad_maximum_fusion), channel_id=1, source_target_pairs={{0,16},{8,24},{16,0},{24,8},{1,17},{9,25},{17,1},{25,9},{2,18},{10... | collective-permute-start | bytes 294920 | tf_op jit(solution)/shard_map/ppermute | solution.py:437
  17.7 8.9 %collective-permute-start.9 = (bf16[32,256]{1,0:T(8,128)(2,1)S(1)}, bf16[32,256]{1,0:T(8,128)(2,1)S(1)}, u32[]{:S(2)}, u32[]{:S(2)}) collective-permute-start(bf16[32,256]{1,0:T(8,128)(2,1)S(1)} %fusion.4), channel_id=1, source_target_pairs={{0,8},{8,0},{16,24},{24,16},{1,9},{9,1},{17,25},{25,17},{2,10},{10... | collective-permute-start | bytes 49160 | tf_op jit(solution)/shard_map/ppermute | solution.py:434
  17.7 4.5 %collective-permute-start.10 = (bf16[2,32,256]{2,1,0:T(8,128)(2,1)S(1)}, bf16[2,32,256]{2,1,0:T(8,128)(2,1)S(1)}, u32[]{:S(2)}, u32[]{:S(2)}) collective-permute-start(bf16[2,32,256]{2,1,0:T(8,128)(2,1)S(1)} %broadcast_select_fusion.7), channel_id=1, source_target_pairs={{0,16},{8,24},{16,0},{24,8},{1,17},{9,25},{17,1},{25,9},{2,18},{10... | collective-permute-start | bytes 98312 | tf_op jit(solution)/shard_map/ppermute | solution.py:437
  20.3 9.0 %collective-permute-start.15 = (bf16[32,1024]{1,0:T(8,128)(2,1)S(1)}, bf16[32,1024]{1,0:T(8,128)(2,1)S(1)}, u32[]{:S(2)}, u32[]{:S(2)}) collective-permute-start(bf16[32,1024]{1,0:T(8,128)(2,1)S(1)} %fusion.2), channel_id=1, source_target_pairs={{0,8},{8,0},{16,24},{24,16},{1,9},{9,1},{17,25},{25,17},{2,10},{10... | collective-permute-start | bytes 196616 | tf_op jit(solution)/shard_map/ppermute | solution.py:434
  22.3 4.3 %collective-permute-start.16 = (bf16[32,1024]{1,0:T(8,128)(2,1)S(1)}, bf16[32,1024]{1,0:T(8,128)(2,1)S(1)}, u32[]{:S(2)}, u32[]{:S(2)}) collective-permute-start(bf16[32,1024]{1,0:T(8,128)(2,1)S(1)} %fusion.1), channel_id=1, source_target_pairs={{0,16},{8,24},{16,0},{24,8},{1,17},{9,25},{17,1},{25,9},{2,18},{10... | collective-permute-start | bytes 196616 | tf_op jit(solution)/shard_map/ppermute | solution.py:437
  24.2 2.9 %collective-permute-start.11 = (bf16[32,256]{1,0:T(8,128)(2,1)S(1)}, bf16[32,256]{1,0:T(8,128)(2,1)S(1)}, u32[]{:S(2)}, u32[]{:S(2)}) collective-permute-start(bf16[32,256]{1,0:T(8,128)(2,1)S(1)} %get-tuple-element.87), channel_id=1, source_target_pairs={{0,8},{8,0},{16,24},{24,16},{1,9},{9,1},{17,25},{25,17},{2,10},{10... | collective-permute-start | bytes 49160 | tf_op jit(solution)/shard_map/ppermute | solution.py:434
  26.5 1.3 %collective-permute-start.7 = (bf16[32,1280]{1,0:T(8,128)(2,1)S(1)}, bf16[32,1280]{1,0:T(8,128)(2,1)S(1)}, u32[]{:S(2)}, u32[]{:S(2)}) collective-permute-start(bf16[32,1280]{1,0:T(8,128)(2,1)S(1)} %pad_maximum_fusion.2), channel_id=1, source_target_pairs={{0,8},{8,0},{16,24},{24,16},{1,9},{9,1},{17,25},{25,17},{2,10},{10... | collective-permute-start | bytes 245768 | tf_op jit(solution)/shard_map/ppermute | solution.py:434
  26.6 2.7 %collective-permute-start.17 = (bf16[32,1024]{1,0:T(8,128)(2,1)S(1)}, bf16[32,1024]{1,0:T(8,128)(2,1)S(1)}, u32[]{:S(2)}, u32[]{:S(2)}) collective-permute-start(bf16[32,1024]{1,0:T(8,128)(2,1)S(1)} %get-tuple-element.79), channel_id=1, source_target_pairs={{0,8},{8,0},{16,24},{24,16},{1,9},{9,1},{17,25},{25,17},{2,10},{10... | collective-permute-start | bytes 196616 | tf_op jit(solution)/shard_map/ppermute | solution.py:434
  27.9 5.7 %collective-permute-start.12 = (bf16[128,768]{1,0:T(8,128)(2,1)S(1)}, bf16[128,768]{1,0:T(8,128)(2,1)S(1)}, u32[]{:S(2)}, u32[]{:S(2)}) collective-permute-start(bf16[128,768]{1,0:T(8,128)(2,1)S(1)} %get-tuple-element.64), channel_id=1, source_target_pairs={{0,1},{1,0},{2,3},{3,2},{4,5},{5,4},{6,7},{7,6},{8,10},{9,11},{10,... | collective-permute-start | bytes 589832 | tf_op jit(solution)/shard_map/ppermute | solution.py:556
  29.4 6.4 %collective-permute-start.18 = (bf16[128,768]{1,0:T(8,128)(2,1)S(1)}, bf16[128,768]{1,0:T(8,128)(2,1)S(1)}, u32[]{:S(2)}, u32[]{:S(2)}) collective-permute-start(bf16[128,768]{1,0:T(8,128)(2,1)S(1)} %get-tuple-element.74), channel_id=1, source_target_pairs={{0,1},{1,0},{2,3},{3,2},{4,5},{5,4},{6,7},{7,6},{8,10},{9,11},{10,... | collective-permute-start | bytes 589832 | tf_op jit(solution)/shard_map/ppermute | solution.py:556
  34.1 5.0 %collective-permute-start.13 = (bf16[2,128,256]{2,1,0:T(8,128)(2,1)S(1)}, bf16[2,128,256]{2,1,0:T(8,128)(2,1)S(1)}, u32[]{:S(2)}, u32[]{:S(2)}) collective-permute-start(bf16[2,128,256]{2,1,0:T(8,128)(2,1)S(1)} %get-tuple-element.66), channel_id=1, source_target_pairs={{0,2},{1,3},{2,0},{3,1},{4,6},{5,7},{6,4},{7,5},{8,9},{9,8},{10,11... | collective-permute-start | bytes 393224 | tf_op jit(solution)/shard_map/ppermute | solution.py:556
  36.2 5.7 %collective-permute-start.19 = (bf16[2,128,256]{2,1,0:T(8,128)(2,1)S(1)}, bf16[2,128,256]{2,1,0:T(8,128)(2,1)S(1)}, u32[]{:S(2)}, u32[]{:S(2)}) collective-permute-start(bf16[2,128,256]{2,1,0:T(8,128)(2,1)S(1)} %get-tuple-element.76), channel_id=1, source_target_pairs={{0,2},{1,3},{2,0},{3,1},{4,6},{5,7},{6,4},{7,5},{8,9},{9,8},{10,11... | collective-permute-start | bytes 393224 | tf_op jit(solution)/shard_map/ppermute | solution.py:556
  39.1 6.7 %collective-permute-start.14 = (bf16[1,128,256]{2,1,0:T(8,128)(2,1)S(1)}, bf16[1,128,256]{2,1,0:T(8,128)(2,1)S(1)}, u32[]{:S(2)}, u32[]{:S(2)}) collective-permute-start(bf16[1,128,256]{2,1,0:T(8,128)(2,1)S(1)} %get-tuple-element.68), channel_id=1, source_target_pairs={{0,4},{1,5},{2,6},{3,7},{4,0},{5,1},{6,2},{7,3},{8,12},{9,13},{10,... | collective-permute-start | bytes 196616 | tf_op jit(solution)/shard_map/ppermute | solution.py:556
  42.0 5.2 %collective-permute-start.20 = (bf16[1,128,256]{2,1,0:T(8,128)(2,1)S(1)}, bf16[1,128,256]{2,1,0:T(8,128)(2,1)S(1)}, u32[]{:S(2)}, u32[]{:S(2)}) collective-permute-start(bf16[1,128,256]{2,1,0:T(8,128)(2,1)S(1)} %get-tuple-element.78), channel_id=1, source_target_pairs={{0,4},{1,5},{2,6},{3,7},{4,0},{5,1},{6,2},{7,3},{8,12},{9,13},{10,... | collective-permute-start | bytes 196616 | tf_op jit(solution)/shard_map/ppermute | solution.py:556

commit v4 on v3

--- a/solution.py
+++ b/solution.py
@@ -41,11 +41,18 @@
     return stage, core, way
 
 
+PIECES = 4
+
+
 def bring_all(sources, outs, sems):
-    copies = [
-        pltpu.make_async_copy(source, out, sems.at[at])
-        for at, (source, out) in enumerate(zip(sources, outs))
-    ]
+    copies = []
+    for at, (source, out) in enumerate(zip(sources, outs)):
+        size = out.shape[0] // PIECES
+        for piece in range(PIECES):
+            part = pl.ds(piece * size, size)
+            copies.append(
+                pltpu.make_async_copy(source.at[part], out.at[part], sems.at[at, piece])
+            )
     for copy in copies:
         copy.start()
     return copies
@@ -70,7 +77,7 @@
         out_shape=outs,
         in_specs=[HBM] * (2 + len(more)),
         out_specs=[VMEM] * len(outs),
-        scratch_shapes=[pltpu.SemaphoreType.DMA((len(outs),))],
+        scratch_shapes=[pltpu.SemaphoreType.DMA((len(outs), PIECES))],
         compiler_params=PARAMS,
     )(*own, *more)
 
@@ -83,7 +90,8 @@
     if mirrored:
         sources += [cotangent.at[1, core], inputs.at[1, core]]
     copies = bring_all(sources, [outs[0]] + list(outs[2:]), sems)
-    copies[0].wait()
+    for copy in copies[:PIECES]:
+        copy.wait()
 
     @pl.when(way == core)
     def _():
@@ -95,7 +103,7 @@
     def _():
         back_active[...] = jnp.dot(ending[...], expand_own[...], preferred_element_type=jnp.float32)
 
-    for copy in copies[1:]:
+    for copy in copies[PIECES:]:
         copy.wait()
     if mirrored:
         rows = outs[3]
@@ -472,7 +480,7 @@
         out_shape=outs,
         in_specs=[VMEM, VMEM, HBM, HBM, VMEM],
         out_specs=[VMEM] * len(outs),
-        scratch_shapes=[pltpu.SemaphoreType.DMA((3,))],
+        scratch_shapes=[pltpu.SemaphoreType.DMA((3, PIECES))],
         compiler_params=PARAMS,
     )(turn[1], turn[3], entering, ending, leave)
     flow, upstreams, back_inners, leave = run_stage(

time: 48.1 us -> 48.3 us (level)
  no operation moved by 1% of the time
where the time goes in v4:
time: 48.3 us; the launch traced here: 48.1 us
  starting transfers between devices  21.5 us (45%)
  waiting for transfers between devices  16.6 us (34%)
  Pallas kernels  9.61 us (20%)
    ppermute x6, starting transfers between devices, exchange(): return lax.ppermute(shard, AXES, pairs)  9.89 us
    ppermute x6, waiting for transfers between devices, exchange(): return lax.ppermute(shard, AXES, pairs)  8.36 us
    ppermute x2, starting transfers between devices, hop(): return lax.ppermute(shard, 'pipe', pairs)  4.81 us
    ppermute x3, starting transfers between devices, mirror(): return lax.ppermute(shard, 'pipe', mirror_pairs)  4.7 us
    ppermute x3, waiting for transfers between devices, mirror(): return lax.ppermute(shard, 'pipe', mirror_pairs)  4.09 us
    pallas_call x3, Pallas kernels, run_stage(): pl.pallas_call(functools.partial(stage_body, step, forward, backward, las...  3.86 us
    ppermute x2, waiting for transfers between devices, hop(): return lax.ppermute(shard, 'pipe', pairs)  3.21 us
    pallas_call x2, Pallas kernels, load(): pl.pallas_call(functools.partial(load_body, step), out_shape=outs, in_spe...  2.74 us
  transfers between devices with their start and end apart: 21, of which 12 were waited for; matrix products, arithmetic and copies ran while one was open for 0% of the time, Pallas kernels for 12%

profile of v4, /device:TPU:0, one launch (start us, length us, event | category | flops | bytes accessed | tf_op | source)
XLA Modules:
  0.0 48.1 jit_solution(11943452952583533187)
XLA Ops:
  0.0 1.4 %shard_map.46 = (bf16[1024,256]{1,0:T(8,128)(2,1)S(1)}, bf16[1024,256]{1,0:T(8,128)(2,1)S(1)}, bf16[32,1024]{1,0:T(8,128)(2,1)S(1)}) custom-call(bf16[2,1024,256]{2,1,0:T(8,128)(2,1)} %bitcast.20, bf16[2,1024,256]{2,1,0:T(8,128)(2,1)} %bitcast.22, bf16[2,2,32,1024]{3,2,1,0:T(8,128)(2,1)} %inputs), custom_call_target="tpu_custom_call" | custom-call | tf_op jit(solution)/shard_map/pallas_call | solution.py:75
  1.4 0.6 %collective-permute-start = (bf16[1024,256]{1,0:T(8,128)(2,1)S(1)}, bf16[1024,256]{1,0:T(8,128)(2,1)S(1)}, u32[]{:S(2)}, u32[]{:S(2)}) collective-permute-start(bf16[1024,256]{1,0:T(8,128)(2,1)S(1)} %get-tuple-element.43.refs_0_), channel_id=1, source_target_pairs={{0,8},{8,0},{16,24},{24,16},{1,9},{9,1},{17,25},{25,17},{2,10},{10... | collective-permute-start | bytes 1572872 | tf_op jit(solution)/shard_map/ppermute | solution.py:442
  2.0 0.1 collective-permute-start.1
  2.0 1.3 %shard_map.48 = (bf16[1024,256]{1,0:T(8,128)(2,1)S(1)}, bf16[1024,256]{1,0:T(8,128)(2,1)S(1)}) custom-call(bf16[2,1024,256]{2,1,0:T(8,128)(2,1)} %bitcast.21, bf16[2,1024,256]{2,1,0:T(8,128)(2,1)} %bitcast.23), custom_call_target="tpu_custom_call" | custom-call | tf_op jit(solution)/shard_map/pallas_call | solution.py:75
  3.4 0.5 %collective-permute-start.3 = (bf16[1024,256]{1,0:T(8,128)(2,1)S(1)}, bf16[1024,256]{1,0:T(8,128)(2,1)S(1)}, u32[]{:S(2)}, u32[]{:S(2)}) collective-permute-start(bf16[1024,256]{1,0:T(8,128)(2,1)S(1)} %get-tuple-element.48.expand_own.refs_1_), channel_id=1, source_target_pairs={{0,8},{8,0},{16,24},{24,16},{1,9},{9,1},{17,25},{25,17},{2,10},{10... | collective-permute-start | bytes 1572872 | tf_op jit(solution)/shard_map/ppermute | solution.py:442
  3.9 0.1 collective-permute-start.2
  4.0 0.3 collective-permute-done.1.refs_3_
  4.2 1.2 %shard_map.47 = (bf16[2,32,1280]{2,1,0:T(8,128)(2,1)S(1)}, bf16[32,1024]{1,0:T(8,128)(2,1)S(1)}, bf16[2,32,1024]{2,1,0:T(8,128)(2,1)S(1)}, f32[2,32,256]{2,1,0:T(8,128)S(1)}) custom-call(bf16[1024,256]{1,0:T(8,128)(2,1)S(1)} %get-tuple-element.43.refs_0_, bf16[1024,256]{1,0:T(8,128)(2,1)S(1)} %get-tuple-element.44.refs_1_, ...), custom_call_target="tpu_custom_call" | custom-call | flops 67108864 | bytes 2097152 | tf_op jit(solution)/shard_map/pallas_call | solution.py:258
  5.4 2.9 %collective-permute-start.4 = (bf16[32,1024]{1,0:T(8,128)(2,1)S(1)}, bf16[32,1024]{1,0:T(8,128)(2,1)S(1)}, u32[]{:S(2)}, u32[]{:S(2)}) collective-permute-start(bf16[32,1024]{1,0:T(8,128)(2,1)S(1)} %get-tuple-element.49.leave), channel_id=1, source_target_pairs={{0,16},{16,0},{8,24},{24,8},{1,17},{17,1},{9,25},{25,9},{2,18},{18... | collective-permute-start | bytes 196616 | tf_op jit(solution)/shard_map/ppermute | solution.py:439
  8.3 1.2 %shard_map.49 = (bf16[32,1024]{1,0:T(8,128)(2,1)S(1)}, f32[32,256]{1,0:T(8,128)S(1)}, bf16[32,1024]{1,0:T(8,128)(2,1)S(1)}, bf16[32,1024]{1,0:T(8,128)(2,1)S(1)}) custom-call(bf16[1024,256]{1,0:T(8,128)(2,1)S(1)} %get-tuple-element.48.expand_own.refs_1_, bf16[1024,256]{1,0:T(8,128)(2,1)S(1)} %collective-permute-done.3.expand_other.refs_3_, ...), custom_call_target="tpu_custom_call" | custom-call | tf_op jit(solution)/shard_map/pallas_call | solution.py:478
  9.5 0.0 collective-permute-done.2.refs_2_
  9.5 1.2 %collective-permute-done.4.refs_4_ = bf16[32,1024]{1,0:T(8,128)(2,1)S(1)} collective-permute-done((bf16[32,1024]{1,0:T(8,128)(2,1)S(1)}, bf16[32,1024]{1,0:T(8,128)(2,1)S(1)}, u32[]{:S(2)}, u32[]{:S(2)}) %collective-permute-start.4) | collective-permute-done | bytes 65568 | tf_op jit(solution)/shard_map/ppermute | solution.py:439
  10.7 1.8 %shard_map.50 = (bf16[2,32,1280]{2,1,0:T(8,128)(2,1)S(1)}, bf16[2,32,1024]{2,1,0:T(8,128)(2,1)S(1)}, bf16[2,32,256]{2,1,0:T(8,128)(2,1)S(1)}, bf16[32,1024]{1,0:T(8,128)(2,1)S(1)}) custom-call(bf16[1024,256]{1,0:T(8,128)(2,1)S(1)} %get-tuple-element.47.refs_0_, bf16[1024,256]{1,0:T(8,128)(2,1)S(1)} %get-tuple-element.48.expand_own.refs_1_, ...), custom_call_target="tpu_custom_call" | custom-call | flops 134217728 | bytes 2097152 | tf_op jit(solution)/shard_map/pallas_call | solution.py:258
  12.5 1.9 %collective-permute-start.8 = (bf16[32,1024]{1,0:T(8,128)(2,1)S(1)}, bf16[32,1024]{1,0:T(8,128)(2,1)S(1)}, u32[]{:S(2)}, u32[]{:S(2)}) collective-permute-start(bf16[32,1024]{1,0:T(8,128)(2,1)S(1)} %get-tuple-element.57), channel_id=1, source_target_pairs={{0,16},{16,0},{8,24},{24,8},{1,17},{17,1},{9,25},{25,9},{2,18},{18... | collective-permute-start | bytes 196616 | tf_op jit(solution)/shard_map/ppermute | solution.py:439
  14.5 0.1 collective-permute-start.5
  14.6 0.2 collective-permute-start.6
  14.8 2.1 %collective-permute-done.8.refs_4_ = bf16[32,1024]{1,0:T(8,128)(2,1)S(1)} collective-permute-done((bf16[32,1024]{1,0:T(8,128)(2,1)S(1)}, bf16[32,1024]{1,0:T(8,128)(2,1)S(1)}, u32[]{:S(2)}, u32[]{:S(2)}) %collective-permute-start.8) | collective-permute-done | bytes 65568 | tf_op jit(solution)/shard_map/ppermute | solution.py:439
  16.9 0.9 %shard_map.51 = (bf16[2,32,1024]{2,1,0:T(8,128)(2,1)S(1)}, bf16[2,32,256]{2,1,0:T(8,128)(2,1)S(1)}) custom-call(bf16[1024,256]{1,0:T(8,128)(2,1)S(1)} %get-tuple-element.43.refs_0_, bf16[1024,256]{1,0:T(8,128)(2,1)S(1)} %get-tuple-element.44.refs_1_, bf16[1024,256]{1,0:T(8,128)(2,1)S(1)} %collective-permute-done.refs_2_, ...), custom_call_target="tpu_custom_call" | custom-call | flops 67108864 | bytes 2097152 | tf_op jit(solution)/shard_map/pallas_call | solution.py:258
  17.8 0.1 collective-permute-start.9
  17.9 2.5 %collective-permute-start.10 = (bf16[2,32,256]{2,1,0:T(8,128)(2,1)S(1)}, bf16[2,32,256]{2,1,0:T(8,128)(2,1)S(1)}, u32[]{:S(2)}, u32[]{:S(2)}) collective-permute-start(bf16[2,32,256]{2,1,0:T(8,128)(2,1)S(1)} %broadcast_select_fusion.7), channel_id=1, source_target_pairs={{0,16},{8,24},{16,0},{24,8},{1,17},{9,25},{17,1},{25,9},{2,18},{10... | collective-permute-start | bytes 98312 | tf_op jit(solution)/shard_map/ppermute | solution.py:445
  20.5 0.2 collective-permute-start.15
  20.6 1.8 %collective-permute-done.10 = bf16[2,32,256]{2,1,0:T(8,128)(2,1)S(1)} collective-permute-done((bf16[2,32,256]{2,1,0:T(8,128)(2,1)S(1)}, bf16[2,32,256]{2,1,0:T(8,128)(2,1)S(1)}, u32[]{:S(2)}, u32[]{:S(2)}) %collective-permute-start.10) | collective-permute-done | bytes 32800 | tf_op jit(solution)/shard_map/ppermute | solution.py:445
  22.4 1.9 %collective-permute-start.16 = (bf16[32,1024]{1,0:T(8,128)(2,1)S(1)}, bf16[32,1024]{1,0:T(8,128)(2,1)S(1)}, u32[]{:S(2)}, u32[]{:S(2)}) collective-permute-start(bf16[32,1024]{1,0:T(8,128)(2,1)S(1)} %fusion.1), channel_id=1, source_target_pairs={{0,16},{8,24},{16,0},{24,8},{1,17},{9,25},{17,1},{25,9},{2,18},{10... | collective-permute-start | bytes 196616 | tf_op jit(solution)/shard_map/ppermute | solution.py:445
  24.4 0.0 collective-permute-start.11
  24.4 2.3 %collective-permute-done.16 = bf16[32,1024]{1,0:T(8,128)(2,1)S(1)} collective-permute-done((bf16[32,1024]{1,0:T(8,128)(2,1)S(1)}, bf16[32,1024]{1,0:T(8,128)(2,1)S(1)}, u32[]{:S(2)}, u32[]{:S(2)}) %collective-permute-start.16) | collective-permute-done | bytes 65568 | tf_op jit(solution)/shard_map/ppermute | solution.py:445
  26.7 0.0 collective-permute-start.7
  26.7 0.0 collective-permute-done.9.refs_7_
  26.7 0.6 %collective-permute-start.17 = (bf16[32,1024]{1,0:T(8,128)(2,1)S(1)}, bf16[32,1024]{1,0:T(8,128)(2,1)S(1)}, u32[]{:S(2)}, u32[]{:S(2)}) collective-permute-start(bf16[32,1024]{1,0:T(8,128)(2,1)S(1)} %get-tuple-element.79), channel_id=1, source_target_pairs={{0,8},{8,0},{16,24},{24,16},{1,9},{9,1},{17,25},{25,17},{2,10},{10... | collective-permute-start | bytes 196616 | tf_op jit(solution)/shard_map/ppermute | solution.py:442
  27.3 0.0 collective-permute-done.5.refs_2_
  27.3 0.7 %collective-permute-done.7.refs_4_ = bf16[32,1280]{1,0:T(8,128)(2,1)S(1)} collective-permute-done((bf16[32,1280]{1,0:T(8,128)(2,1)S(1)}, bf16[32,1280]{1,0:T(8,128)(2,1)S(1)}, u32[]{:S(2)}, u32[]{:S(2)}) %collective-permute-start.7) | collective-permute-done | bytes 81952 | tf_op jit(solution)/shard_map/ppermute | solution.py:442
  28.0 0.1 shard_map.52
  28.1 1.4 %collective-permute-start.12 = (bf16[128,768]{1,0:T(8,128)(2,1)S(1)}, bf16[128,768]{1,0:T(8,128)(2,1)S(1)}, u32[]{:S(2)}, u32[]{:S(2)}) collective-permute-start(bf16[128,768]{1,0:T(8,128)(2,1)S(1)} %get-tuple-element.64), channel_id=1, source_target_pairs={{0,1},{1,0},{2,3},{3,2},{4,5},{5,4},{6,7},{7,6},{8,10},{9,11},{10,... | collective-permute-start | bytes 589832 | tf_op jit(solution)/shard_map/ppermute | solution.py:564
  29.5 0.0 collective-permute-done.17.refs_9_
  29.5 0.1 shard_map.55
  29.6 0.8 %collective-permute-start.18 = (bf16[128,768]{1,0:T(8,128)(2,1)S(1)}, bf16[128,768]{1,0:T(8,128)(2,1)S(1)}, u32[]{:S(2)}, u32[]{:S(2)}) collective-permute-start(bf16[128,768]{1,0:T(8,128)(2,1)S(1)} %get-tuple-element.74), channel_id=1, source_target_pairs={{0,1},{1,0},{2,3},{3,2},{4,5},{5,4},{6,7},{7,6},{8,10},{9,11},{10,... | collective-permute-start | bytes 589832 | tf_op jit(solution)/shard_map/ppermute | solution.py:564
  30.4 3.5 %collective-permute-done.12.came = bf16[128,768]{1,0:T(8,128)(2,1)S(1)} collective-permute-done((bf16[128,768]{1,0:T(8,128)(2,1)S(1)}, bf16[128,768]{1,0:T(8,128)(2,1)S(1)}, u32[]{:S(2)}, u32[]{:S(2)}) %collective-permute-start.12) | collective-permute-done | bytes 196640 | tf_op jit(solution)/shard_map/ppermute | solution.py:564
  33.8 0.4 shard_map.53
  34.2 1.4 %collective-permute-start.13 = (bf16[2,128,256]{2,1,0:T(8,128)(2,1)S(1)}, bf16[2,128,256]{2,1,0:T(8,128)(2,1)S(1)}, u32[]{:S(2)}, u32[]{:S(2)}) collective-permute-start(bf16[2,128,256]{2,1,0:T(8,128)(2,1)S(1)} %get-tuple-element.66), channel_id=1, source_target_pairs={{0,2},{1,3},{2,0},{3,1},{4,6},{5,7},{6,4},{7,5},{8,9},{9,8},{10,11... | collective-permute-start | bytes 393224 | tf_op jit(solution)/shard_map/ppermute | solution.py:564
  35.7 0.3 collective-permute-done.18.came
  35.9 0.4 shard_map.56
  36.4 1.4 %collective-permute-start.19 = (bf16[2,128,256]{2,1,0:T(8,128)(2,1)S(1)}, bf16[2,128,256]{2,1,0:T(8,128)(2,1)S(1)}, u32[]{:S(2)}, u32[]{:S(2)}) collective-permute-start(bf16[2,128,256]{2,1,0:T(8,128)(2,1)S(1)} %get-tuple-element.76), channel_id=1, source_target_pairs={{0,2},{1,3},{2,0},{3,1},{4,6},{5,7},{6,4},{7,5},{8,9},{9,8},{10,11... | collective-permute-start | bytes 393224 | tf_op jit(solution)/shard_map/ppermute | solution.py:564
  37.8 1.5 %collective-permute-done.13.came = bf16[2,128,256]{2,1,0:T(8,128)(2,1)S(1)} collective-permute-done((bf16[2,128,256]{2,1,0:T(8,128)(2,1)S(1)}, bf16[2,128,256]{2,1,0:T(8,128)(2,1)S(1)}, u32[]{:S(2)}, u32[]{:S(2)}) %collective-permute-start.13) | collective-permute-done | bytes 131104 | tf_op jit(solution)/shard_map/ppermute | solution.py:564
  39.3 2.4 %collective-permute-start.14 = (bf16[1,128,256]{2,1,0:T(8,128)(2,1)S(1)}, bf16[1,128,256]{2,1,0:T(8,128)(2,1)S(1)}, u32[]{:S(2)}, u32[]{:S(2)}) collective-permute-start(bf16[1,128,256]{2,1,0:T(8,128)(2,1)S(1)} %get-tuple-element.68), channel_id=1, source_target_pairs={{0,4},{1,5},{2,6},{3,7},{4,0},{5,1},{6,2},{7,3},{8,12},{9,13},{10,... | collective-permute-start | bytes 196616 | tf_op jit(solution)/shard_map/ppermute | solution.py:564
  41.7 0.3 collective-permute-done.19.came
  42.1 2.4 %collective-permute-start.20 = (bf16[1,128,256]{2,1,0:T(8,128)(2,1)S(1)}, bf16[1,128,256]{2,1,0:T(8,128)(2,1)S(1)}, u32[]{:S(2)}, u32[]{:S(2)}) collective-permute-start(bf16[1,128,256]{2,1,0:T(8,128)(2,1)S(1)} %get-tuple-element.78), channel_id=1, source_target_pairs={{0,4},{1,5},{2,6},{3,7},{4,0},{5,1},{6,2},{7,3},{8,12},{9,13},{10,... | collective-permute-start | bytes 196616 | tf_op jit(solution)/shard_map/ppermute | solution.py:564
  44.5 1.5 %collective-permute-done.14.came_reduce = bf16[1,128,256]{2,1,0:T(8,128)(2,1)S(1)} collective-permute-done((bf16[1,128,256]{2,1,0:T(8,128)(2,1)S(1)}, bf16[1,128,256]{2,1,0:T(8,128)(2,1)S(1)}, u32[]{:S(2)}, u32[]{:S(2)}) %collective-permute-start.14) | collective-permute-done | bytes 65568 | tf_op jit(solution)/shard_map/ppermute | solution.py:564
  46.0 1.3 %collective-permute-done.20.came_expand = bf16[1,128,256]{2,1,0:T(8,128)(2,1)S(1)} collective-permute-done((bf16[1,128,256]{2,1,0:T(8,128)(2,1)S(1)}, bf16[1,128,256]{2,1,0:T(8,128)(2,1)S(1)}, u32[]{:S(2)}, u32[]{:S(2)}) %collective-permute-start.20) | collective-permute-done | bytes 65568 | tf_op jit(solution)/shard_map/ppermute | solution.py:564
  47.4 0.7 %shard_map.58 = f32[1,2,128,256]{3,2,1,0:T(8,128)} custom-call(f32[1,128,256]{2,1,0:T(8,128)S(1)} %get-tuple-element.67.keep_reduce, bf16[1,128,256]{2,1,0:T(8,128)(2,1)S(1)} %collective-permute-done.14.came_reduce, f32[1,128,256]{2,1,0:T(8,128)S(1)} %get-tuple-element.77.keep_expand, bf16[1,128,256]{2,1,0:T(8,128)(2,1)S(1)} %collective-permute-done.20.came_expand), custom_call_target="tpu_custom_call" | custom-call | tf_op jit(solution)/shard_map/pallas_call | solution.py:543
  (23 shorter events, 0.2 us)
Async XLA Ops:
  1.4 2.6 %collective-permute-start = (bf16[1024,256]{1,0:T(8,128)(2,1)S(1)}, bf16[1024,256]{1,0:T(8,128)(2,1)S(1)}, u32[]{:S(2)}, u32[]{:S(2)}) collective-permute-start(bf16[1024,256]{1,0:T(8,128)(2,1)S(1)} %get-tuple-element.43.refs_0_), channel_id=1, source_target_pairs={{0,8},{8,0},{16,24},{24,16},{1,9},{9,1},{17,25},{25,17},{2,10},{10... | collective-permute-start | bytes 1572872 | tf_op jit(solution)/shard_map/ppermute | solution.py:442
  2.0 2.3 %collective-permute-start.1 = (bf16[1024,256]{1,0:T(8,128)(2,1)S(1)}, bf16[1024,256]{1,0:T(8,128)(2,1)S(1)}, u32[]{:S(2)}, u32[]{:S(2)}) collective-permute-start(bf16[1024,256]{1,0:T(8,128)(2,1)S(1)} %get-tuple-element.44.refs_1_), channel_id=1, source_target_pairs={{0,8},{8,0},{16,24},{24,16},{1,9},{9,1},{17,25},{25,17},{2,10},{10... | collective-permute-start | bytes 1572872 | tf_op jit(solution)/shard_map/ppermute | solution.py:442
  3.4 4.9 %collective-permute-start.3 = (bf16[1024,256]{1,0:T(8,128)(2,1)S(1)}, bf16[1024,256]{1,0:T(8,128)(2,1)S(1)}, u32[]{:S(2)}, u32[]{:S(2)}) collective-permute-start(bf16[1024,256]{1,0:T(8,128)(2,1)S(1)} %get-tuple-element.48.expand_own.refs_1_), channel_id=1, source_target_pairs={{0,8},{8,0},{16,24},{24,16},{1,9},{9,1},{17,25},{25,17},{2,10},{10... | collective-permute-start | bytes 1572872 | tf_op jit(solution)/shard_map/ppermute | solution.py:442
  3.9 5.6 %collective-permute-start.2 = (bf16[1024,256]{1,0:T(8,128)(2,1)S(1)}, bf16[1024,256]{1,0:T(8,128)(2,1)S(1)}, u32[]{:S(2)}, u32[]{:S(2)}) collective-permute-start(bf16[1024,256]{1,0:T(8,128)(2,1)S(1)} %get-tuple-element.47.refs_0_), channel_id=1, source_target_pairs={{0,8},{8,0},{16,24},{24,16},{1,9},{9,1},{17,25},{25,17},{2,10},{10... | collective-permute-start | bytes 1572872 | tf_op jit(solution)/shard_map/ppermute | solution.py:442
  5.4 5.3 %collective-permute-start.4 = (bf16[32,1024]{1,0:T(8,128)(2,1)S(1)}, bf16[32,1024]{1,0:T(8,128)(2,1)S(1)}, u32[]{:S(2)}, u32[]{:S(2)}) collective-permute-start(bf16[32,1024]{1,0:T(8,128)(2,1)S(1)} %get-tuple-element.49.leave), channel_id=1, source_target_pairs={{0,16},{16,0},{8,24},{24,8},{1,17},{17,1},{9,25},{25,9},{2,18},{18... | collective-permute-start | bytes 196616 | tf_op jit(solution)/shard_map/ppermute | solution.py:439
  12.5 4.4 %collective-permute-start.8 = (bf16[32,1024]{1,0:T(8,128)(2,1)S(1)}, bf16[32,1024]{1,0:T(8,128)(2,1)S(1)}, u32[]{:S(2)}, u32[]{:S(2)}) collective-permute-start(bf16[32,1024]{1,0:T(8,128)(2,1)S(1)} %get-tuple-element.57), channel_id=1, source_target_pairs={{0,16},{16,0},{8,24},{24,8},{1,17},{17,1},{9,25},{25,9},{2,18},{18... | collective-permute-start | bytes 196616 | tf_op jit(solution)/shard_map/ppermute | solution.py:439
  14.5 12.9 %collective-permute-start.5 = (bf16[32,1280]{1,0:T(8,128)(2,1)S(1)}, bf16[32,1280]{1,0:T(8,128)(2,1)S(1)}, u32[]{:S(2)}, u32[]{:S(2)}) collective-permute-start(bf16[32,1280]{1,0:T(8,128)(2,1)S(1)} %fusion), channel_id=1, source_target_pairs={{0,8},{8,0},{16,24},{24,16},{1,9},{9,1},{17,25},{25,17},{2,10},{10... | collective-permute-start | bytes 245768 | tf_op jit(solution)/shard_map/ppermute | solution.py:442
  14.6 9.8 %collective-permute-start.6 = (bf16[32,1536]{1,0:T(8,128)(2,1)S(1)}, bf16[32,1536]{1,0:T(8,128)(2,1)S(1)}, u32[]{:S(2)}, u32[]{:S(2)}) collective-permute-start(bf16[32,1536]{1,0:T(8,128)(2,1)S(1)} %pad_maximum_fusion), channel_id=1, source_target_pairs={{0,16},{8,24},{16,0},{24,8},{1,17},{9,25},{17,1},{25,9},{2,18},{10... | collective-permute-start | bytes 294920 | tf_op jit(solution)/shard_map/ppermute | solution.py:445
  17.8 8.9 %collective-permute-start.9 = (bf16[32,256]{1,0:T(8,128)(2,1)S(1)}, bf16[32,256]{1,0:T(8,128)(2,1)S(1)}, u32[]{:S(2)}, u32[]{:S(2)}) collective-permute-start(bf16[32,256]{1,0:T(8,128)(2,1)S(1)} %fusion.4), channel_id=1, source_target_pairs={{0,8},{8,0},{16,24},{24,16},{1,9},{9,1},{17,25},{25,17},{2,10},{10... | collective-permute-start | bytes 49160 | tf_op jit(solution)/shard_map/ppermute | solution.py:442
  17.9 4.5 %collective-permute-start.10 = (bf16[2,32,256]{2,1,0:T(8,128)(2,1)S(1)}, bf16[2,32,256]{2,1,0:T(8,128)(2,1)S(1)}, u32[]{:S(2)}, u32[]{:S(2)}) collective-permute-start(bf16[2,32,256]{2,1,0:T(8,128)(2,1)S(1)} %broadcast_select_fusion.7), channel_id=1, source_target_pairs={{0,16},{8,24},{16,0},{24,8},{1,17},{9,25},{17,1},{25,9},{2,18},{10... | collective-permute-start | bytes 98312 | tf_op jit(solution)/shard_map/ppermute | solution.py:445
  20.5 9.0 %collective-permute-start.15 = (bf16[32,1024]{1,0:T(8,128)(2,1)S(1)}, bf16[32,1024]{1,0:T(8,128)(2,1)S(1)}, u32[]{:S(2)}, u32[]{:S(2)}) collective-permute-start(bf16[32,1024]{1,0:T(8,128)(2,1)S(1)} %fusion.2), channel_id=1, source_target_pairs={{0,8},{8,0},{16,24},{24,16},{1,9},{9,1},{17,25},{25,17},{2,10},{10... | collective-permute-start | bytes 196616 | tf_op jit(solution)/shard_map/ppermute | solution.py:442
  22.4 4.3 %collective-permute-start.16 = (bf16[32,1024]{1,0:T(8,128)(2,1)S(1)}, bf16[32,1024]{1,0:T(8,128)(2,1)S(1)}, u32[]{:S(2)}, u32[]{:S(2)}) collective-permute-start(bf16[32,1024]{1,0:T(8,128)(2,1)S(1)} %fusion.1), channel_id=1, source_target_pairs={{0,16},{8,24},{16,0},{24,8},{1,17},{9,25},{17,1},{25,9},{2,18},{10... | collective-permute-start | bytes 196616 | tf_op jit(solution)/shard_map/ppermute | solution.py:445
  24.4 2.9 %collective-permute-start.11 = (bf16[32,256]{1,0:T(8,128)(2,1)S(1)}, bf16[32,256]{1,0:T(8,128)(2,1)S(1)}, u32[]{:S(2)}, u32[]{:S(2)}) collective-permute-start(bf16[32,256]{1,0:T(8,128)(2,1)S(1)} %get-tuple-element.87), channel_id=1, source_target_pairs={{0,8},{8,0},{16,24},{24,16},{1,9},{9,1},{17,25},{25,17},{2,10},{10... | collective-permute-start | bytes 49160 | tf_op jit(solution)/shard_map/ppermute | solution.py:442
  26.7 1.3 %collective-permute-start.7 = (bf16[32,1280]{1,0:T(8,128)(2,1)S(1)}, bf16[32,1280]{1,0:T(8,128)(2,1)S(1)}, u32[]{:S(2)}, u32[]{:S(2)}) collective-permute-start(bf16[32,1280]{1,0:T(8,128)(2,1)S(1)} %pad_maximum_fusion.2), channel_id=1, source_target_pairs={{0,8},{8,0},{16,24},{24,16},{1,9},{9,1},{17,25},{25,17},{2,10},{10... | collective-permute-start | bytes 245768 | tf_op jit(solution)/shard_map/ppermute | solution.py:442
  26.7 2.7 %collective-permute-start.17 = (bf16[32,1024]{1,0:T(8,128)(2,1)S(1)}, bf16[32,1024]{1,0:T(8,128)(2,1)S(1)}, u32[]{:S(2)}, u32[]{:S(2)}) collective-permute-start(bf16[32,1024]{1,0:T(8,128)(2,1)S(1)} %get-tuple-element.79), channel_id=1, source_target_pairs={{0,8},{8,0},{16,24},{24,16},{1,9},{9,1},{17,25},{25,17},{2,10},{10... | collective-permute-start | bytes 196616 | tf_op jit(solution)/shard_map/ppermute | solution.py:442
  28.1 5.7 %collective-permute-start.12 = (bf16[128,768]{1,0:T(8,128)(2,1)S(1)}, bf16[128,768]{1,0:T(8,128)(2,1)S(1)}, u32[]{:S(2)}, u32[]{:S(2)}) collective-permute-start(bf16[128,768]{1,0:T(8,128)(2,1)S(1)} %get-tuple-element.64), channel_id=1, source_target_pairs={{0,1},{1,0},{2,3},{3,2},{4,5},{5,4},{6,7},{7,6},{8,10},{9,11},{10,... | collective-permute-start | bytes 589832 | tf_op jit(solution)/shard_map/ppermute | solution.py:564
  29.6 6.4 %collective-permute-start.18 = (bf16[128,768]{1,0:T(8,128)(2,1)S(1)}, bf16[128,768]{1,0:T(8,128)(2,1)S(1)}, u32[]{:S(2)}, u32[]{:S(2)}) collective-permute-start(bf16[128,768]{1,0:T(8,128)(2,1)S(1)} %get-tuple-element.74), channel_id=1, source_target_pairs={{0,1},{1,0},{2,3},{3,2},{4,5},{5,4},{6,7},{7,6},{8,10},{9,11},{10,... | collective-permute-start | bytes 589832 | tf_op jit(solution)/shard_map/ppermute | solution.py:564
  34.2 5.0 %collective-permute-start.13 = (bf16[2,128,256]{2,1,0:T(8,128)(2,1)S(1)}, bf16[2,128,256]{2,1,0:T(8,128)(2,1)S(1)}, u32[]{:S(2)}, u32[]{:S(2)}) collective-permute-start(bf16[2,128,256]{2,1,0:T(8,128)(2,1)S(1)} %get-tuple-element.66), channel_id=1, source_target_pairs={{0,2},{1,3},{2,0},{3,1},{4,6},{5,7},{6,4},{7,5},{8,9},{9,8},{10,11... | collective-permute-start | bytes 393224 | tf_op jit(solution)/shard_map/ppermute | solution.py:564
  36.4 5.7 %collective-permute-start.19 = (bf16[2,128,256]{2,1,0:T(8,128)(2,1)S(1)}, bf16[2,128,256]{2,1,0:T(8,128)(2,1)S(1)}, u32[]{:S(2)}, u32[]{:S(2)}) collective-permute-start(bf16[2,128,256]{2,1,0:T(8,128)(2,1)S(1)} %get-tuple-element.76), channel_id=1, source_target_pairs={{0,2},{1,3},{2,0},{3,1},{4,6},{5,7},{6,4},{7,5},{8,9},{9,8},{10,11... | collective-permute-start | bytes 393224 | tf_op jit(solution)/shard_map/ppermute | solution.py:564
  39.3 6.7 %collective-permute-start.14 = (bf16[1,128,256]{2,1,0:T(8,128)(2,1)S(1)}, bf16[1,128,256]{2,1,0:T(8,128)(2,1)S(1)}, u32[]{:S(2)}, u32[]{:S(2)}) collective-permute-start(bf16[1,128,256]{2,1,0:T(8,128)(2,1)S(1)} %get-tuple-element.68), channel_id=1, source_target_pairs={{0,4},{1,5},{2,6},{3,7},{4,0},{5,1},{6,2},{7,3},{8,12},{9,13},{10,... | collective-permute-start | bytes 196616 | tf_op jit(solution)/shard_map/ppermute | solution.py:564
  42.1 5.2 %collective-permute-start.20 = (bf16[1,128,256]{2,1,0:T(8,128)(2,1)S(1)}, bf16[1,128,256]{2,1,0:T(8,128)(2,1)S(1)}, u32[]{:S(2)}, u32[]{:S(2)}) collective-permute-start(bf16[1,128,256]{2,1,0:T(8,128)(2,1)S(1)} %get-tuple-element.78), channel_id=1, source_target_pairs={{0,4},{1,5},{2,6},{3,7},{4,0},{5,1},{6,2},{7,3},{8,12},{9,13},{10,... | collective-permute-start | bytes 196616 | tf_op jit(solution)/shard_map/ppermute | solution.py:564

commit v5 on v3

--- a/solution.py
+++ b/solution.py
@@ -346,47 +346,66 @@
             target[:, place * chunk : (place + 1) * chunk] = wide[:, source]
 
 
-def gather_rows(target, near, away):
+def near_body(stages, chunk, *refs):
+    parts = [refs[at * (stages + 1) : (at + 1) * (stages + 1)] for at in range(3)]
+    outs = refs[3 * (stages + 1) :]
+    keeps, send, wide = outs[:4], outs[4], outs[5]
+    rows, channels = wide.shape[0] // 2, wide.shape[1]
+    inner = keeps[1].shape[1]
     stage, _, _ = where_am_i(0)
-    rows = target.shape[0] // 4
-    for step, part in enumerate(near):
-
-        @pl.when(stage == step)
-        def _():
-            target[:rows] = part[...]
-
-    for at, part in enumerate(away):
-        target[(at + 1) * rows : (at + 2) * rows] = part[...]
-
-
-def flow_rows(arrays, stages, columns):
-    near = [flow.at[0, :, columns] for flow in arrays[:stages]]
-    return near, [part.at[:, columns] for part in arrays[stages : stages + 3]]
-
-
-def back_rows(arrays, stages):
-    return [back.at[0] for back in arrays[:stages]], arrays[stages : stages + 3]
-
-
-def late_body(stages, chunk, up, *refs):
-    left, right, send, wide = refs[2 * stages + 6 :]
+    flows, ups, backs = parts
+    everything = slice(None)
+    columns = 0
+    for at, (lefts, left_columns, rights, right_columns) in enumerate(
+        (
+            (ups, everything, flows, slice(channels, channels + inner)),
+            (flows, slice(0, channels), backs, everything),
+        )
+    ):
+        left, right = keeps[2 * at : 2 * at + 2]
+        for target, sources, span in ((wide, lefts, left_columns), (right, rights, right_columns)):
+            for step in range(stages):
+
+                @pl.when(stage == step)
+                def _():
+                    target[:rows] = sources[step][0, :, span]
+
+            target[rows:] = sources[stages][:, span]
+        split_columns(wide, left, send.at[:, columns : columns + channels // 2], chunk)
+        columns += channels // 2
+        send[:, columns : columns + inner] = right[...]
+        columns += inner
+
+
+def late_body(chunk, up, flow, cross_flow, back, cross_back, left, right, send, wide):
     channels = wide.shape[1]
-    backs = back_rows(refs[stages + 3 :], stages)
-    if up:
-        gather_rows(wide, *backs)
-        gather_rows(right, *flow_rows(refs, stages, slice(channels, None)))
-    else:
-        gather_rows(wide, *flow_rows(refs, stages, slice(0, channels)))
-        gather_rows(right, *backs)
+    rows = wide.shape[0] // 2
+    for at, (flow_rows, back_rows) in enumerate(((flow, back), (cross_flow, cross_back))):
+        place = slice(at * rows, (at + 1) * rows)
+        if up:
+            wide[place] = back_rows[...]
+            right[place] = flow_rows[:, channels:]
+        else:
+            wide[place] = flow_rows[:, :channels]
+            right[place] = back_rows[...]
     split_columns(wide, left, send, chunk)
     send[:, channels // 2 :] = right[...]
 
 
-def half_gradient_body(left, right, came, send, keep, full):
-    columns = left.shape[1]
-    full[...] = contract(left[...], right[...], 0, 0) + contract(
-        came[:, :columns], came[:, columns:], 0, 0
-    )
+def half_gradient_body(at, *refs):
+    lefts, rights, cames = refs[:2], refs[2:4], refs[4:6]
+    send, keep, full, left, right = refs[6:]
+    rows, columns = lefts[0].shape
+    inner = rights[0].shape[1]
+    starts = (at * (columns + inner), 0)
+    for group in range(2):
+        place = slice(group * rows, (group + 1) * rows)
+        left[place] = lefts[group][...]
+        right[place] = rights[group][...]
+        place = slice((group + 2) * rows, (group + 3) * rows)
+        left[place] = cames[group][:, starts[group] : starts[group] + columns]
+        right[place] = cames[group][:, starts[group] + columns : starts[group] + columns + inner]
+    full[...] = contract(left[...], right[...], 0, 0)
     _, _, side = first_sides()
     chunk = send.shape[1]
     for place in range(send.shape[0]):
@@ -559,28 +578,45 @@
 def halve_rows(stages, replicas, chunk, sizes, rows, fore, ups, backs):
     channels, inner = sizes
     shape = lambda *dims: jax.ShapeDtypeStruct(dims, jnp.bfloat16)
-    half = shape(4 * rows, channels // 2)
-    narrow = shape(4 * rows, inner)
+    half = shape(2 * rows, channels // 2)
+    narrow = shape(2 * rows, inner)
+    width = channels // 2 + inner
+    wide = pltpu.VMEM((2 * rows, channels), jnp.bfloat16)
+    near = [one for late in (fore, ups, backs) for one in late[: stages + 1]]
+    *keeps, send = pl.pallas_call(
+        functools.partial(near_body, stages, chunk),
+        out_shape=[half, narrow, half, narrow, shape(2 * rows, 2 * width)],
+        in_specs=[VMEM] * len(near),
+        out_specs=[VMEM] * 5,
+        scratch_shapes=[wide],
+        compiler_params=PARAMS,
+    )(*near)
+    came_near = exchange(send, stages, replicas, 1, 2)
     parts = []
-    for name, late in (("inner", backs), ("up", ups)):
+    for at, name, late in ((1, "inner", backs), (0, "up", ups)):
         left, right, send = pl.pallas_call(
-            functools.partial(late_body, stages, chunk, name == "up"),
-            out_shape=[half, narrow, shape(4 * rows, channels // 2 + inner)],
-            in_specs=[VMEM] * (len(fore) + len(late)),
+            functools.partial(late_body, chunk, name == "up"),
+            out_shape=[half, narrow, shape(2 * rows, width)],
+            in_specs=[VMEM] * 4,
             out_specs=[VMEM] * 3,
-            scratch_shapes=[pltpu.VMEM((4 * rows, channels), jnp.bfloat16)],
+            scratch_shapes=[wide],
             compiler_params=PARAMS,
-        )(*fore, *late)
+        )(*fore[stages + 1 :], *late[stages + 1 :])
         came = exchange(send, stages, replicas, 1, 2)
+        operands = (keeps[2 * at], left, keeps[2 * at + 1], right, came_near, came)
         count = replicas // 4
         send, keep = pl.pallas_call(
-            half_gradient_body,
+            functools.partial(half_gradient_body, at),
             out_shape=sums(count, chunk, inner),
-            in_specs=[VMEM] * 3,
+            in_specs=[VMEM] * 6,
             out_specs=[VMEM] * 2,
-            scratch_shapes=[pltpu.VMEM((channels // 2, inner), jnp.float32)],
+            scratch_shapes=[
+                pltpu.VMEM((channels // 2, inner), jnp.float32),
+                pltpu.VMEM((8 * rows, channels // 2), jnp.bfloat16),
+                pltpu.VMEM((8 * rows, inner), jnp.bfloat16),
+            ],
             compiler_params=PARAMS,
-        )(left, right, came)
+        )(*operands)
         came = exchange(send, stages, replicas, 2, 1)
         for bit in range(2, replicas.bit_length() - 1):
             count //= 2

time: 48.1 us -> 48.1 us (level)
  starting transfers between devices: 21.5 us -> 22.4 us
  waiting for transfers between devices: 16.8 us -> 16 us
    ppermute x6 -> x7, starting transfers between devices: 9.89 us -> 10.8 us  [exchange(): return lax.ppermute(shard, AXES, pairs)]
    ppermute x10, waiting for transfers between devices: 1.08 us -> 0.43 us  [swap_cores(): return lax.ppermute(shard, 'pipe', core_pairs)]
    pallas_call x4 -> x5, Pallas kernels: 1.03 us -> 0.89 us  [the longest x2 0.67 us: halve_rows(): pl.pallas_call(functools.partial(half_gradient_body, at), out_shape=sums(...]
    ppermute x6 -> x7, waiting for transfers between devices: 8.36 us -> 8.23 us  [exchange(): return lax.ppermute(shard, AXES, pairs)]
  transfers between devices with their start and end apart: 21 -> 22, of which waited for: 12 -> 9; matrix products, arithmetic and copies ran while one was open for 0% -> 0% of each run, Pallas kernels for 12% -> 11%
where the time goes in v5:
time: 48.1 us; the launch traced here: 47.9 us
  starting transfers between devices  22.4 us (47%)
  waiting for transfers between devices  16 us (33%)
  Pallas kernels  9.15 us (19%)
    ppermute x7, starting transfers between devices, exchange(): return lax.ppermute(shard, AXES, pairs)  10.8 us
    ppermute x7, waiting for transfers between devices, exchange(): return lax.ppermute(shard, AXES, pairs)  8.23 us
    ppermute x2, starting transfers between devices, hop(): return lax.ppermute(shard, 'pipe', pairs)  4.81 us
    ppermute x3, starting transfers between devices, mirror(): return lax.ppermute(shard, 'pipe', mirror_pairs)  4.7 us
    ppermute x3, waiting for transfers between devices, mirror(): return lax.ppermute(shard, 'pipe', mirror_pairs)  4.09 us
    pallas_call x3, Pallas kernels, run_stage(): pl.pallas_call(functools.partial(stage_body, step, forward, backward, las...  3.85 us
    ppermute x2, waiting for transfers between devices, hop(): return lax.ppermute(shard, 'pipe', pairs)  3.23 us
    pallas_call x2, Pallas kernels, load(): pl.pallas_call(functools.partial(load_body, step), out_shape=outs, in_spe...  2.44 us
  transfers between devices with their start and end apart: 22, of which 9 were waited for; matrix products, arithmetic and copies ran while one was open for 0% of the time, Pallas kernels for 11%

profile of v5, /device:TPU:0, one launch (start us, length us, event | category | flops | bytes accessed | tf_op | source)
XLA Modules:
  0.0 47.9 jit_solution(17167095167714804882)
XLA Ops:
  0.0 1.2 %shard_map.46 = (bf16[1024,256]{1,0:T(8,128)(2,1)S(1)}, bf16[1024,256]{1,0:T(8,128)(2,1)S(1)}, bf16[32,1024]{1,0:T(8,128)(2,1)S(1)}) custom-call(bf16[2,1024,256]{2,1,0:T(8,128)(2,1)} %bitcast.20, bf16[2,1024,256]{2,1,0:T(8,128)(2,1)} %bitcast.22, bf16[2,2,32,1024]{3,2,1,0:T(8,128)(2,1)} %inputs), custom_call_target="tpu_custom_call" | custom-call | tf_op jit(solution)/shard_map/pallas_call | solution.py:68
  1.2 0.6 %collective-permute-start = (bf16[1024,256]{1,0:T(8,128)(2,1)S(1)}, bf16[1024,256]{1,0:T(8,128)(2,1)S(1)}, u32[]{:S(2)}, u32[]{:S(2)}) collective-permute-start(bf16[1024,256]{1,0:T(8,128)(2,1)S(1)} %get-tuple-element.48.refs_0_), channel_id=1, source_target_pairs={{0,8},{8,0},{16,24},{24,16},{1,9},{9,1},{17,25},{25,17},{2,10},{10... | collective-permute-start | bytes 1572872 | tf_op jit(solution)/shard_map/ppermute | solution.py:453
  1.8 0.1 collective-permute-start.1
  1.9 1.2 %shard_map.48 = (bf16[1024,256]{1,0:T(8,128)(2,1)S(1)}, bf16[1024,256]{1,0:T(8,128)(2,1)S(1)}) custom-call(bf16[2,1024,256]{2,1,0:T(8,128)(2,1)} %bitcast.21, bf16[2,1024,256]{2,1,0:T(8,128)(2,1)} %bitcast.23), custom_call_target="tpu_custom_call" | custom-call | tf_op jit(solution)/shard_map/pallas_call | solution.py:68
  3.1 0.5 %collective-permute-start.3 = (bf16[1024,256]{1,0:T(8,128)(2,1)S(1)}, bf16[1024,256]{1,0:T(8,128)(2,1)S(1)}, u32[]{:S(2)}, u32[]{:S(2)}) collective-permute-start(bf16[1024,256]{1,0:T(8,128)(2,1)S(1)} %get-tuple-element.53.expand_own.refs_1_), channel_id=1, source_target_pairs={{0,8},{8,0},{16,24},{24,16},{1,9},{9,1},{17,25},{25,17},{2,10},{10... | collective-permute-start | bytes 1572872 | tf_op jit(solution)/shard_map/ppermute | solution.py:453
  3.6 0.1 collective-permute-start.2
  3.7 0.0 collective-permute-done.refs_2_
  3.7 0.4 collective-permute-done.1.refs_3_
  4.1 1.2 %shard_map.47 = (bf16[2,32,1280]{2,1,0:T(8,128)(2,1)S(1)}, bf16[32,1024]{1,0:T(8,128)(2,1)S(1)}, bf16[2,32,1024]{2,1,0:T(8,128)(2,1)S(1)}, f32[2,32,256]{2,1,0:T(8,128)S(1)}) custom-call(bf16[1024,256]{1,0:T(8,128)(2,1)S(1)} %get-tuple-element.48.refs_0_, bf16[1024,256]{1,0:T(8,128)(2,1)S(1)} %get-tuple-element.49.refs_1_, ...), custom_call_target="tpu_custom_call" | custom-call | flops 67108864 | bytes 2097152 | tf_op jit(solution)/shard_map/pallas_call | solution.py:250
  5.2 2.9 %collective-permute-start.4 = (bf16[32,1024]{1,0:T(8,128)(2,1)S(1)}, bf16[32,1024]{1,0:T(8,128)(2,1)S(1)}, u32[]{:S(2)}, u32[]{:S(2)}) collective-permute-start(bf16[32,1024]{1,0:T(8,128)(2,1)S(1)} %get-tuple-element.54.leave), channel_id=1, source_target_pairs={{0,16},{16,0},{8,24},{24,8},{1,17},{17,1},{9,25},{25,9},{2,18},{18... | collective-permute-start | bytes 196616 | tf_op jit(solution)/shard_map/ppermute | solution.py:450
  8.1 0.0 collective-permute-done.3.expand_other.refs_3_
  8.1 1.2 %shard_map.49 = (bf16[32,1024]{1,0:T(8,128)(2,1)S(1)}, f32[32,256]{1,0:T(8,128)S(1)}, bf16[32,1024]{1,0:T(8,128)(2,1)S(1)}, bf16[32,1024]{1,0:T(8,128)(2,1)S(1)}) custom-call(bf16[1024,256]{1,0:T(8,128)(2,1)S(1)} %get-tuple-element.53.expand_own.refs_1_, bf16[1024,256]{1,0:T(8,128)(2,1)S(1)} %collective-permute-done.3.expand_other.refs_3_, ...), custom_call_target="tpu_custom_call" | custom-call | tf_op jit(solution)/shard_map/pallas_call | solution.py:489
  9.3 0.0 collective-permute-done.2.refs_2_
  9.3 1.2 %collective-permute-done.4.refs_4_ = bf16[32,1024]{1,0:T(8,128)(2,1)S(1)} collective-permute-done((bf16[32,1024]{1,0:T(8,128)(2,1)S(1)}, bf16[32,1024]{1,0:T(8,128)(2,1)S(1)}, u32[]{:S(2)}, u32[]{:S(2)}) %collective-permute-start.4) | collective-permute-done | bytes 65568 | tf_op jit(solution)/shard_map/ppermute | solution.py:450
  10.5 1.8 %shard_map.50 = (bf16[2,32,1280]{2,1,0:T(8,128)(2,1)S(1)}, bf16[2,32,1024]{2,1,0:T(8,128)(2,1)S(1)}, bf16[2,32,256]{2,1,0:T(8,128)(2,1)S(1)}, bf16[32,1024]{1,0:T(8,128)(2,1)S(1)}) custom-call(bf16[1024,256]{1,0:T(8,128)(2,1)S(1)} %get-tuple-element.52.refs_0_, bf16[1024,256]{1,0:T(8,128)(2,1)S(1)} %get-tuple-element.53.expand_own.refs_1_, ...), custom_call_target="tpu_custom_call" | custom-call | flops 134217728 | bytes 2097152 | tf_op jit(solution)/shard_map/pallas_call | solution.py:250
  12.3 1.9 %collective-permute-start.6 = (bf16[32,1024]{1,0:T(8,128)(2,1)S(1)}, bf16[32,1024]{1,0:T(8,128)(2,1)S(1)}, u32[]{:S(2)}, u32[]{:S(2)}) collective-permute-start(bf16[32,1024]{1,0:T(8,128)(2,1)S(1)} %get-tuple-element.59), channel_id=1, source_target_pairs={{0,16},{16,0},{8,24},{24,8},{1,17},{17,1},{9,25},{25,9},{2,18},{18... | collective-permute-start | bytes 196616 | tf_op jit(solution)/shard_map/ppermute | solution.py:450
  14.3 0.1 collective-permute-start.5
  14.5 0.2 collective-permute-start.9
  14.7 2.1 %collective-permute-done.6.refs_4_ = bf16[32,1024]{1,0:T(8,128)(2,1)S(1)} collective-permute-done((bf16[32,1024]{1,0:T(8,128)(2,1)S(1)}, bf16[32,1024]{1,0:T(8,128)(2,1)S(1)}, u32[]{:S(2)}, u32[]{:S(2)}) %collective-permute-start.6) | collective-permute-done | bytes 65568 | tf_op jit(solution)/shard_map/ppermute | solution.py:450
  16.7 0.9 %shard_map.51 = (bf16[2,32,1024]{2,1,0:T(8,128)(2,1)S(1)}, bf16[2,32,256]{2,1,0:T(8,128)(2,1)S(1)}) custom-call(bf16[1024,256]{1,0:T(8,128)(2,1)S(1)} %get-tuple-element.48.refs_0_, bf16[1024,256]{1,0:T(8,128)(2,1)S(1)} %get-tuple-element.49.refs_1_, bf16[1024,256]{1,0:T(8,128)(2,1)S(1)} %collective-permute-done.refs_2_, ...), custom_call_target="tpu_custom_call" | custom-call | flops 67108864 | bytes 2097152 | tf_op jit(solution)/shard_map/pallas_call | solution.py:250
  17.7 0.1 collective-permute-start.8
  17.7 2.5 %collective-permute-start.11 = (bf16[2,32,256]{2,1,0:T(8,128)(2,1)S(1)}, bf16[2,32,256]{2,1,0:T(8,128)(2,1)S(1)}, u32[]{:S(2)}, u32[]{:S(2)}) collective-permute-start(bf16[2,32,256]{2,1,0:T(8,128)(2,1)S(1)} %broadcast_select_fusion.7), channel_id=1, source_target_pairs={{0,16},{8,24},{16,0},{24,8},{1,17},{9,25},{17,1},{25,9},{2,18},{10... | collective-permute-start | bytes 98312 | tf_op jit(solution)/shard_map/ppermute | solution.py:456
  20.3 0.2 collective-permute-start.7
  20.5 1.8 %collective-permute-done.11 = bf16[2,32,256]{2,1,0:T(8,128)(2,1)S(1)} collective-permute-done((bf16[2,32,256]{2,1,0:T(8,128)(2,1)S(1)}, bf16[2,32,256]{2,1,0:T(8,128)(2,1)S(1)}, u32[]{:S(2)}, u32[]{:S(2)}) %collective-permute-start.11) | collective-permute-done | bytes 32800 | tf_op jit(solution)/shard_map/ppermute | solution.py:456
  22.3 1.9 %collective-permute-start.17 = (bf16[32,1024]{1,0:T(8,128)(2,1)S(1)}, bf16[32,1024]{1,0:T(8,128)(2,1)S(1)}, u32[]{:S(2)}, u32[]{:S(2)}) collective-permute-start(bf16[32,1024]{1,0:T(8,128)(2,1)S(1)} %fusion.1), channel_id=1, source_target_pairs={{0,16},{8,24},{16,0},{24,8},{1,17},{9,25},{17,1},{25,9},{2,18},{10... | collective-permute-start | bytes 196616 | tf_op jit(solution)/shard_map/ppermute | solution.py:456
  24.3 2.3 %collective-permute-done.17 = bf16[32,1024]{1,0:T(8,128)(2,1)S(1)} collective-permute-done((bf16[32,1024]{1,0:T(8,128)(2,1)S(1)}, bf16[32,1024]{1,0:T(8,128)(2,1)S(1)}, u32[]{:S(2)}, u32[]{:S(2)}) %collective-permute-start.17) | collective-permute-done | bytes 65568 | tf_op jit(solution)/shard_map/ppermute | solution.py:456
  26.6 0.6 %collective-permute-start.18 = (bf16[32,1024]{1,0:T(8,128)(2,1)S(1)}, bf16[32,1024]{1,0:T(8,128)(2,1)S(1)}, u32[]{:S(2)}, u32[]{:S(2)}) collective-permute-start(bf16[32,1024]{1,0:T(8,128)(2,1)S(1)} %get-tuple-element.89), channel_id=1, source_target_pairs={{0,8},{8,0},{16,24},{24,16},{1,9},{9,1},{17,25},{25,17},{2,10},{10... | collective-permute-start | bytes 196616 | tf_op jit(solution)/shard_map/ppermute | solution.py:453
  27.2 0.0 collective-permute-done.5.refs_2_
  27.2 0.0 collective-permute-done.7.refs_5_
  27.2 0.1 shard_map.52
  27.3 1.4 %collective-permute-start.13 = (bf16[64,1536]{1,0:T(8,128)(2,1)S(1)}, bf16[64,1536]{1,0:T(8,128)(2,1)S(1)}, u32[]{:S(2)}, u32[]{:S(2)}) collective-permute-start(bf16[64,1536]{1,0:T(8,128)(2,1)S(1)} %get-tuple-element.73), channel_id=1, source_target_pairs={{0,1},{1,0},{2,3},{3,2},{4,5},{5,4},{6,7},{7,6},{8,10},{9,11},{10,... | collective-permute-start | bytes 589832 | tf_op jit(solution)/shard_map/ppermute | solution.py:575
  28.7 0.0 collective-permute-done.10.cross_flow
  28.7 0.1 shard_map.56
  28.7 0.8 %collective-permute-start.19 = (bf16[64,768]{1,0:T(8,128)(2,1)S(1)}, bf16[64,768]{1,0:T(8,128)(2,1)S(1)}, u32[]{:S(2)}, u32[]{:S(2)}) collective-permute-start(bf16[64,768]{1,0:T(8,128)(2,1)S(1)} %get-tuple-element.84), channel_id=1, source_target_pairs={{0,1},{1,0},{2,3},{3,2},{4,5},{5,4},{6,7},{7,6},{8,10},{9,11},{10,... | collective-permute-start | bytes 294920 | tf_op jit(solution)/shard_map/ppermute | solution.py:575
  29.5 0.0 collective-permute-done.12.cross_back
  29.6 1.4 %collective-permute-start.14 = (bf16[64,768]{1,0:T(8,128)(2,1)S(1)}, bf16[64,768]{1,0:T(8,128)(2,1)S(1)}, u32[]{:S(2)}, u32[]{:S(2)}) collective-permute-start(bf16[64,768]{1,0:T(8,128)(2,1)S(1)} %get-tuple-element.74), channel_id=1, source_target_pairs={{0,1},{1,0},{2,3},{3,2},{4,5},{5,4},{6,7},{7,6},{8,10},{9,11},{10,... | collective-permute-start | bytes 294920 | tf_op jit(solution)/shard_map/ppermute | solution.py:575
  30.9 3.1 %collective-permute-done.19.refs_5_ = bf16[64,768]{1,0:T(8,128)(2,1)S(1)} collective-permute-done((bf16[64,768]{1,0:T(8,128)(2,1)S(1)}, bf16[64,768]{1,0:T(8,128)(2,1)S(1)}, u32[]{:S(2)}, u32[]{:S(2)}) %collective-permute-start.19) | collective-permute-done | bytes 98336 | tf_op jit(solution)/shard_map/ppermute | solution.py:575
  34.1 0.3 shard_map.57
  34.4 1.4 %collective-permute-start.20 = (bf16[2,128,256]{2,1,0:T(8,128)(2,1)S(1)}, bf16[2,128,256]{2,1,0:T(8,128)(2,1)S(1)}, u32[]{:S(2)}, u32[]{:S(2)}) collective-permute-start(bf16[2,128,256]{2,1,0:T(8,128)(2,1)S(1)} %get-tuple-element.86), channel_id=1, source_target_pairs={{0,2},{1,3},{2,0},{3,1},{4,6},{5,7},{6,4},{7,5},{8,9},{9,8},{10,11... | collective-permute-start | bytes 393224 | tf_op jit(solution)/shard_map/ppermute | solution.py:575
  35.8 0.3 shard_map.54
  36.2 0.7 %collective-permute-start.15 = (bf16[2,128,256]{2,1,0:T(8,128)(2,1)S(1)}, bf16[2,128,256]{2,1,0:T(8,128)(2,1)S(1)}, u32[]{:S(2)}, u32[]{:S(2)}) collective-permute-start(bf16[2,128,256]{2,1,0:T(8,128)(2,1)S(1)} %get-tuple-element.76), channel_id=1, source_target_pairs={{0,2},{1,3},{2,0},{3,1},{4,6},{5,7},{6,4},{7,5},{8,9},{9,8},{10,11... | collective-permute-start | bytes 393224 | tf_op jit(solution)/shard_map/ppermute | solution.py:575
  36.9 2.5 %collective-permute-done.20.came = bf16[2,128,256]{2,1,0:T(8,128)(2,1)S(1)} collective-permute-done((bf16[2,128,256]{2,1,0:T(8,128)(2,1)S(1)}, bf16[2,128,256]{2,1,0:T(8,128)(2,1)S(1)}, u32[]{:S(2)}, u32[]{:S(2)}) %collective-permute-start.20) | collective-permute-done | bytes 131104 | tf_op jit(solution)/shard_map/ppermute | solution.py:575
  39.5 2.4 %collective-permute-start.21 = (bf16[1,128,256]{2,1,0:T(8,128)(2,1)S(1)}, bf16[1,128,256]{2,1,0:T(8,128)(2,1)S(1)}, u32[]{:S(2)}, u32[]{:S(2)}) collective-permute-start(bf16[1,128,256]{2,1,0:T(8,128)(2,1)S(1)} %get-tuple-element.88), channel_id=1, source_target_pairs={{0,4},{1,5},{2,6},{3,7},{4,0},{5,1},{6,2},{7,3},{8,12},{9,13},{10,... | collective-permute-start | bytes 196616 | tf_op jit(solution)/shard_map/ppermute | solution.py:575
  41.9 0.0 collective-permute-done.15.came
  41.9 2.7 %collective-permute-start.16 = (bf16[1,128,256]{2,1,0:T(8,128)(2,1)S(1)}, bf16[1,128,256]{2,1,0:T(8,128)(2,1)S(1)}, u32[]{:S(2)}, u32[]{:S(2)}) collective-permute-start(bf16[1,128,256]{2,1,0:T(8,128)(2,1)S(1)} %get-tuple-element.78), channel_id=1, source_target_pairs={{0,4},{1,5},{2,6},{3,7},{4,0},{5,1},{6,2},{7,3},{8,12},{9,13},{10,... | collective-permute-start | bytes 196616 | tf_op jit(solution)/shard_map/ppermute | solution.py:575
  44.6 1.5 %collective-permute-done.21.came_expand = bf16[1,128,256]{2,1,0:T(8,128)(2,1)S(1)} collective-permute-done((bf16[1,128,256]{2,1,0:T(8,128)(2,1)S(1)}, bf16[1,128,256]{2,1,0:T(8,128)(2,1)S(1)}, u32[]{:S(2)}, u32[]{:S(2)}) %collective-permute-start.21) | collective-permute-done | bytes 65568 | tf_op jit(solution)/shard_map/ppermute | solution.py:575
  46.1 1.1 %collective-permute-done.16.came_reduce = bf16[1,128,256]{2,1,0:T(8,128)(2,1)S(1)} collective-permute-done((bf16[1,128,256]{2,1,0:T(8,128)(2,1)S(1)}, bf16[1,128,256]{2,1,0:T(8,128)(2,1)S(1)}, u32[]{:S(2)}, u32[]{:S(2)}) %collective-permute-start.16) | collective-permute-done | bytes 65568 | tf_op jit(solution)/shard_map/ppermute | solution.py:575
  47.2 0.7 %shard_map.59 = f32[1,2,128,256]{3,2,1,0:T(8,128)} custom-call(f32[1,128,256]{2,1,0:T(8,128)S(1)} %get-tuple-element.77.keep_reduce, bf16[1,128,256]{2,1,0:T(8,128)(2,1)S(1)} %collective-permute-done.16.came_reduce, f32[1,128,256]{2,1,0:T(8,128)S(1)} %get-tuple-element.87.keep_expand, bf16[1,128,256]{2,1,0:T(8,128)(2,1)S(1)} %collective-permute-done.21.came_expand), custom_call_target="tpu_custom_call" | custom-call | tf_op jit(solution)/shard_map/pallas_call | solution.py:554
  (26 shorter events, 0.3 us)
Async XLA Ops:
  1.2 2.4 %collective-permute-start = (bf16[1024,256]{1,0:T(8,128)(2,1)S(1)}, bf16[1024,256]{1,0:T(8,128)(2,1)S(1)}, u32[]{:S(2)}, u32[]{:S(2)}) collective-permute-start(bf16[1024,256]{1,0:T(8,128)(2,1)S(1)} %get-tuple-element.48.refs_0_), channel_id=1, source_target_pairs={{0,8},{8,0},{16,24},{24,16},{1,9},{9,1},{17,25},{25,17},{2,10},{10... | collective-permute-start | bytes 1572872 | tf_op jit(solution)/shard_map/ppermute | solution.py:453
  1.8 2.3 %collective-permute-start.1 = (bf16[1024,256]{1,0:T(8,128)(2,1)S(1)}, bf16[1024,256]{1,0:T(8,128)(2,1)S(1)}, u32[]{:S(2)}, u32[]{:S(2)}) collective-permute-start(bf16[1024,256]{1,0:T(8,128)(2,1)S(1)} %get-tuple-element.49.refs_1_), channel_id=1, source_target_pairs={{0,8},{8,0},{16,24},{24,16},{1,9},{9,1},{17,25},{25,17},{2,10},{10... | collective-permute-start | bytes 1572872 | tf_op jit(solution)/shard_map/ppermute | solution.py:453
  3.1 5.0 %collective-permute-start.3 = (bf16[1024,256]{1,0:T(8,128)(2,1)S(1)}, bf16[1024,256]{1,0:T(8,128)(2,1)S(1)}, u32[]{:S(2)}, u32[]{:S(2)}) collective-permute-start(bf16[1024,256]{1,0:T(8,128)(2,1)S(1)} %get-tuple-element.53.expand_own.refs_1_), channel_id=1, source_target_pairs={{0,8},{8,0},{16,24},{24,16},{1,9},{9,1},{17,25},{25,17},{2,10},{10... | collective-permute-start | bytes 1572872 | tf_op jit(solution)/shard_map/ppermute | solution.py:453
  3.6 5.7 %collective-permute-start.2 = (bf16[1024,256]{1,0:T(8,128)(2,1)S(1)}, bf16[1024,256]{1,0:T(8,128)(2,1)S(1)}, u32[]{:S(2)}, u32[]{:S(2)}) collective-permute-start(bf16[1024,256]{1,0:T(8,128)(2,1)S(1)} %get-tuple-element.52.refs_0_), channel_id=1, source_target_pairs={{0,8},{8,0},{16,24},{24,16},{1,9},{9,1},{17,25},{25,17},{2,10},{10... | collective-permute-start | bytes 1572872 | tf_op jit(solution)/shard_map/ppermute | solution.py:453
  5.2 5.3 %collective-permute-start.4 = (bf16[32,1024]{1,0:T(8,128)(2,1)S(1)}, bf16[32,1024]{1,0:T(8,128)(2,1)S(1)}, u32[]{:S(2)}, u32[]{:S(2)}) collective-permute-start(bf16[32,1024]{1,0:T(8,128)(2,1)S(1)} %get-tuple-element.54.leave), channel_id=1, source_target_pairs={{0,16},{16,0},{8,24},{24,8},{1,17},{17,1},{9,25},{25,9},{2,18},{18... | collective-permute-start | bytes 196616 | tf_op jit(solution)/shard_map/ppermute | solution.py:450
  12.3 4.4 %collective-permute-start.6 = (bf16[32,1024]{1,0:T(8,128)(2,1)S(1)}, bf16[32,1024]{1,0:T(8,128)(2,1)S(1)}, u32[]{:S(2)}, u32[]{:S(2)}) collective-permute-start(bf16[32,1024]{1,0:T(8,128)(2,1)S(1)} %get-tuple-element.59), channel_id=1, source_target_pairs={{0,16},{16,0},{8,24},{24,8},{1,17},{17,1},{9,25},{25,9},{2,18},{18... | collective-permute-start | bytes 196616 | tf_op jit(solution)/shard_map/ppermute | solution.py:450
  14.3 12.9 %collective-permute-start.5 = (bf16[32,1280]{1,0:T(8,128)(2,1)S(1)}, bf16[32,1280]{1,0:T(8,128)(2,1)S(1)}, u32[]{:S(2)}, u32[]{:S(2)}) collective-permute-start(bf16[32,1280]{1,0:T(8,128)(2,1)S(1)} %fusion), channel_id=1, source_target_pairs={{0,8},{8,0},{16,24},{24,16},{1,9},{9,1},{17,25},{25,17},{2,10},{10... | collective-permute-start | bytes 245768 | tf_op jit(solution)/shard_map/ppermute | solution.py:453
  14.5 9.8 %collective-permute-start.9 = (bf16[32,1536]{1,0:T(8,128)(2,1)S(1)}, bf16[32,1536]{1,0:T(8,128)(2,1)S(1)}, u32[]{:S(2)}, u32[]{:S(2)}) collective-permute-start(bf16[32,1536]{1,0:T(8,128)(2,1)S(1)} %pad_maximum_fusion), channel_id=1, source_target_pairs={{0,16},{8,24},{16,0},{24,8},{1,17},{9,25},{17,1},{25,9},{2,18},{10... | collective-permute-start | bytes 294920 | tf_op jit(solution)/shard_map/ppermute | solution.py:456
  17.7 8.9 %collective-permute-start.8 = (bf16[32,256]{1,0:T(8,128)(2,1)S(1)}, bf16[32,256]{1,0:T(8,128)(2,1)S(1)}, u32[]{:S(2)}, u32[]{:S(2)}) collective-permute-start(bf16[32,256]{1,0:T(8,128)(2,1)S(1)} %fusion.4), channel_id=1, source_target_pairs={{0,8},{8,0},{16,24},{24,16},{1,9},{9,1},{17,25},{25,17},{2,10},{10... | collective-permute-start | bytes 49160 | tf_op jit(solution)/shard_map/ppermute | solution.py:453
  17.7 4.5 %collective-permute-start.11 = (bf16[2,32,256]{2,1,0:T(8,128)(2,1)S(1)}, bf16[2,32,256]{2,1,0:T(8,128)(2,1)S(1)}, u32[]{:S(2)}, u32[]{:S(2)}) collective-permute-start(bf16[2,32,256]{2,1,0:T(8,128)(2,1)S(1)} %broadcast_select_fusion.7), channel_id=1, source_target_pairs={{0,16},{8,24},{16,0},{24,8},{1,17},{9,25},{17,1},{25,9},{2,18},{10... | collective-permute-start | bytes 98312 | tf_op jit(solution)/shard_map/ppermute | solution.py:456
  20.3 6.9 %collective-permute-start.7 = (bf16[32,1024]{1,0:T(8,128)(2,1)S(1)}, bf16[32,1024]{1,0:T(8,128)(2,1)S(1)}, u32[]{:S(2)}, u32[]{:S(2)}) collective-permute-start(bf16[32,1024]{1,0:T(8,128)(2,1)S(1)} %fusion.3), channel_id=1, source_target_pairs={{0,8},{8,0},{16,24},{24,16},{1,9},{9,1},{17,25},{25,17},{2,10},{10... | collective-permute-start | bytes 196616 | tf_op jit(solution)/shard_map/ppermute | solution.py:453
  22.3 4.3 %collective-permute-start.17 = (bf16[32,1024]{1,0:T(8,128)(2,1)S(1)}, bf16[32,1024]{1,0:T(8,128)(2,1)S(1)}, u32[]{:S(2)}, u32[]{:S(2)}) collective-permute-start(bf16[32,1024]{1,0:T(8,128)(2,1)S(1)} %fusion.1), channel_id=1, source_target_pairs={{0,16},{8,24},{16,0},{24,8},{1,17},{9,25},{17,1},{25,9},{2,18},{10... | collective-permute-start | bytes 196616 | tf_op jit(solution)/shard_map/ppermute | solution.py:456
  24.2 5.3 %collective-permute-start.12 = (bf16[32,256]{1,0:T(8,128)(2,1)S(1)}, bf16[32,256]{1,0:T(8,128)(2,1)S(1)}, u32[]{:S(2)}, u32[]{:S(2)}) collective-permute-start(bf16[32,256]{1,0:T(8,128)(2,1)S(1)} %get-tuple-element.97), channel_id=1, source_target_pairs={{0,8},{8,0},{16,24},{24,16},{1,9},{9,1},{17,25},{25,17},{2,10},{10... | collective-permute-start | bytes 49160 | tf_op jit(solution)/shard_map/ppermute | solution.py:453
  26.5 2.1 %collective-permute-start.10 = (bf16[32,1280]{1,0:T(8,128)(2,1)S(1)}, bf16[32,1280]{1,0:T(8,128)(2,1)S(1)}, u32[]{:S(2)}, u32[]{:S(2)}) collective-permute-start(bf16[32,1280]{1,0:T(8,128)(2,1)S(1)} %pad_maximum_fusion.2), channel_id=1, source_target_pairs={{0,8},{8,0},{16,24},{24,16},{1,9},{9,1},{17,25},{25,17},{2,10},{10... | collective-permute-start | bytes 245768 | tf_op jit(solution)/shard_map/ppermute | solution.py:453
  26.6 2.1 %collective-permute-start.18 = (bf16[32,1024]{1,0:T(8,128)(2,1)S(1)}, bf16[32,1024]{1,0:T(8,128)(2,1)S(1)}, u32[]{:S(2)}, u32[]{:S(2)}) collective-permute-start(bf16[32,1024]{1,0:T(8,128)(2,1)S(1)} %get-tuple-element.89), channel_id=1, source_target_pairs={{0,8},{8,0},{16,24},{24,16},{1,9},{9,1},{17,25},{25,17},{2,10},{10... | collective-permute-start | bytes 196616 | tf_op jit(solution)/shard_map/ppermute | solution.py:453
  27.3 6.8 %collective-permute-start.13 = (bf16[64,1536]{1,0:T(8,128)(2,1)S(1)}, bf16[64,1536]{1,0:T(8,128)(2,1)S(1)}, u32[]{:S(2)}, u32[]{:S(2)}) collective-permute-start(bf16[64,1536]{1,0:T(8,128)(2,1)S(1)} %get-tuple-element.73), channel_id=1, source_target_pairs={{0,1},{1,0},{2,3},{3,2},{4,5},{5,4},{6,7},{7,6},{8,10},{9,11},{10,... | collective-permute-start | bytes 589832 | tf_op jit(solution)/shard_map/ppermute | solution.py:575
  28.7 5.3 %collective-permute-start.19 = (bf16[64,768]{1,0:T(8,128)(2,1)S(1)}, bf16[64,768]{1,0:T(8,128)(2,1)S(1)}, u32[]{:S(2)}, u32[]{:S(2)}) collective-permute-start(bf16[64,768]{1,0:T(8,128)(2,1)S(1)} %get-tuple-element.84), channel_id=1, source_target_pairs={{0,1},{1,0},{2,3},{3,2},{4,5},{5,4},{6,7},{7,6},{8,10},{9,11},{10,... | collective-permute-start | bytes 294920 | tf_op jit(solution)/shard_map/ppermute | solution.py:575
  29.6 6.3 %collective-permute-start.14 = (bf16[64,768]{1,0:T(8,128)(2,1)S(1)}, bf16[64,768]{1,0:T(8,128)(2,1)S(1)}, u32[]{:S(2)}, u32[]{:S(2)}) collective-permute-start(bf16[64,768]{1,0:T(8,128)(2,1)S(1)} %get-tuple-element.74), channel_id=1, source_target_pairs={{0,1},{1,0},{2,3},{3,2},{4,5},{5,4},{6,7},{7,6},{8,10},{9,11},{10,... | collective-permute-start | bytes 294920 | tf_op jit(solution)/shard_map/ppermute | solution.py:575
  34.4 5.0 %collective-permute-start.20 = (bf16[2,128,256]{2,1,0:T(8,128)(2,1)S(1)}, bf16[2,128,256]{2,1,0:T(8,128)(2,1)S(1)}, u32[]{:S(2)}, u32[]{:S(2)}) collective-permute-start(bf16[2,128,256]{2,1,0:T(8,128)(2,1)S(1)} %get-tuple-element.86), channel_id=1, source_target_pairs={{0,2},{1,3},{2,0},{3,1},{4,6},{5,7},{6,4},{7,5},{8,9},{9,8},{10,11... | collective-permute-start | bytes 393224 | tf_op jit(solution)/shard_map/ppermute | solution.py:575
  36.2 5.7 %collective-permute-start.15 = (bf16[2,128,256]{2,1,0:T(8,128)(2,1)S(1)}, bf16[2,128,256]{2,1,0:T(8,128)(2,1)S(1)}, u32[]{:S(2)}, u32[]{:S(2)}) collective-permute-start(bf16[2,128,256]{2,1,0:T(8,128)(2,1)S(1)} %get-tuple-element.76), channel_id=1, source_target_pairs={{0,2},{1,3},{2,0},{3,1},{4,6},{5,7},{6,4},{7,5},{8,9},{9,8},{10,11... | collective-permute-start | bytes 393224 | tf_op jit(solution)/shard_map/ppermute | solution.py:575
  39.5 6.6 %collective-permute-start.21 = (bf16[1,128,256]{2,1,0:T(8,128)(2,1)S(1)}, bf16[1,128,256]{2,1,0:T(8,128)(2,1)S(1)}, u32[]{:S(2)}, u32[]{:S(2)}) collective-permute-start(bf16[1,128,256]{2,1,0:T(8,128)(2,1)S(1)} %get-tuple-element.88), channel_id=1, source_target_pairs={{0,4},{1,5},{2,6},{3,7},{4,0},{5,1},{6,2},{7,3},{8,12},{9,13},{10,... | collective-permute-start | bytes 196616 | tf_op jit(solution)/shard_map/ppermute | solution.py:575
  41.9 5.2 %collective-permute-start.16 = (bf16[1,128,256]{2,1,0:T(8,128)(2,1)S(1)}, bf16[1,128,256]{2,1,0:T(8,128)(2,1)S(1)}, u32[]{:S(2)}, u32[]{:S(2)}) collective-permute-start(bf16[1,128,256]{2,1,0:T(8,128)(2,1)S(1)} %get-tuple-element.78), channel_id=1, source_target_pairs={{0,4},{1,5},{2,6},{3,7},{4,0},{5,1},{6,2},{7,3},{8,12},{9,13},{10,... | collective-permute-start | bytes 196616 | tf_op jit(solution)/shard_map/ppermute | solution.py:575

commit v6 on v3

--- a/solution.py
+++ b/solution.py
@@ -174,6 +174,8 @@
             for order in (1, 0):
                 slot = lax.rem(order + core, 2)
                 upstreams[slot] = upstream
+                if last and order == 0:
+                    break
                 if not forward:
                     wait(1, order)
                 if forward and order:
@@ -186,8 +188,6 @@
                 back_inners[slot] = back_inner
                 if not forward:
                     wait(0, order)
-                if last and order == 0:
-                    break
                 back_lifted = contract(back_inner, reduce_mats[order][...], 1, 1)
                 widened = trunks[order].astype(jnp.float32)
                 norm_scale = norm_of(widened)
@@ -221,6 +221,18 @@
             [held[1].at[order] for order in range(2)],
             lambda kind, order: copies[2 * order + kind][1].wait(),
         )
+
+
+def tail_body(own, other, upstreams, back_first, inners, back_inners):
+    _, core, way = where_am_i(0)
+
+    def run(expand_mat):
+        back_active = jnp.dot(upstreams[core], expand_mat[...], preferred_element_type=jnp.float32)
+        back_inners[core] = (back_active * smooth_slope(inners[0])).astype(jnp.bfloat16)
+        back_inners[1 - core] = back_first[1 - core]
+
+    pl.when(way == core)(lambda: run(own))
+    pl.when(way != core)(lambda: run(other))
 
 
 def run_stage(weights, step, forward, backward, near, rows, sizes, *arrays):
@@ -346,47 +358,49 @@
             target[:, place * chunk : (place + 1) * chunk] = wide[:, source]
 
 
-def gather_rows(target, near, away):
+def pack_body(stages, chunk, up, near, far, *refs):
+    refs = list(refs)
+    left, right, send, wide = refs[-4:]
+    channels = wide.shape[1]
+    spans = slice(0, channels), slice(channels, None), slice(None)
+    flow_span, back_span = (spans[1] if up else spans[0]), spans[2]
     stage, _, _ = where_am_i(0)
-    rows = target.shape[0] // 4
-    for step, part in enumerate(near):
-
-        @pl.when(stage == step)
-        def _():
-            target[:rows] = part[...]
-
-    for at, part in enumerate(away):
-        target[(at + 1) * rows : (at + 2) * rows] = part[...]
-
-
-def flow_rows(arrays, stages, columns):
-    near = [flow.at[0, :, columns] for flow in arrays[:stages]]
-    return near, [part.at[:, columns] for part in arrays[stages : stages + 3]]
-
-
-def back_rows(arrays, stages):
-    return [back.at[0] for back in arrays[:stages]], arrays[stages : stages + 3]
-
-
-def late_body(stages, chunk, up, *refs):
-    left, right, send, wide = refs[2 * stages + 6 :]
-    channels = wide.shape[1]
-    backs = back_rows(refs[stages + 3 :], stages)
-    if up:
-        gather_rows(wide, *backs)
-        gather_rows(right, *flow_rows(refs, stages, slice(channels, None)))
-    else:
-        gather_rows(wide, *flow_rows(refs, stages, slice(0, channels)))
-        gather_rows(right, *backs)
+    rows = wide.shape[0] // (2 * near + 2 * far)
+    start = 0
+    targets = (right, wide) if up else (wide, right)
+    for target, span in zip(targets, (flow_span, back_span)):
+        start = 0
+        if near:
+            parts = [refs.pop(0) for _ in range(stages + 1)]
+            for step in range(stages):
+
+                @pl.when(stage == step)
+                def _():
+                    target[:rows] = parts[step][0, :, span]
+
+            target[rows : 2 * rows] = parts[stages][:, span]
+            start = 2 * rows
+        if far:
+            for part in (refs.pop(0), refs.pop(0)):
+                target[start : start + rows] = part[:, span]
+                start += rows
     split_columns(wide, left, send, chunk)
     send[:, channels // 2 :] = right[...]
 
 
-def half_gradient_body(left, right, came, send, keep, full):
-    columns = left.shape[1]
-    full[...] = contract(left[...], right[...], 0, 0) + contract(
-        came[:, :columns], came[:, columns:], 0, 0
-    )
+def half_gradient_body(groups, *refs):
+    send, keep, full, left, right = refs[3 * groups :]
+    start = 0
+    for group in range(groups):
+        part_left, part_right, came = refs[3 * group : 3 * group + 3]
+        rows, columns = part_left.shape
+        left[start : start + rows] = part_left[...]
+        right[start : start + rows] = part_right[...]
+        start += rows
+        left[start : start + rows] = came[:, :columns]
+        right[start : start + rows] = came[:, columns:]
+        start += rows
+    full[...] = contract(left[...], right[...], 0, 0)
     _, _, side = first_sides()
     chunk = send.shape[1]
     for place in range(send.shape[0]):
@@ -509,9 +523,18 @@
             inners[step],
         )
         upstreams.insert(0, outs[0])
-        back_inners.insert(0, outs[1])
         if step:
             upstream = hop(outs[2], stages - 1 - step)
+            back_inners.insert(0, outs[1])
+            continue
+        tail = pl.pallas_call(
+            tail_body,
+            out_shape=jax.ShapeDtypeStruct(outs[1].shape, outs[1].dtype),
+            in_specs=[VMEM] * 5,
+            out_specs=VMEM,
+            compiler_params=PARAMS,
+        )(near[1], near[3], outs[0], outs[1], inners[0])
+        back_inners.insert(0, tail)
     going = pick(upstreams, True)
     far_up = mirror(near_core(going[0], going[1]) if mirrored else going)
     far_inner = mirror(pick(back_inners, True))
@@ -559,28 +582,47 @@
 def halve_rows(stages, replicas, chunk, sizes, rows, fore, ups, backs):
     channels, inner = sizes
     shape = lambda *dims: jax.ShapeDtypeStruct(dims, jnp.bfloat16)
-    half = shape(4 * rows, channels // 2)
-    narrow = shape(4 * rows, inner)
+
+    def pack(late, up, near, far):
+        count = 2 * (near + far)
+        arrays = []
+        for one in (fore, late):
+            arrays += one[: stages + 1] * near + one[stages + 1 :] * far
+        return pl.pallas_call(
+            functools.partial(pack_body, stages, chunk, up, near, far),
+            out_shape=[
+                shape(count * rows, channels // 2),
+                shape(count * rows, inner),
+                shape(count * rows, channels // 2 + inner),
+            ],
+            in_specs=[VMEM] * len(arrays),
+            out_specs=[VMEM] * 3,
+            scratch_shapes=[pltpu.VMEM((count * rows, channels), jnp.bfloat16)],
+            compiler_params=PARAMS,
+        )(*arrays)
+
+    near_left, near_right, send = pack(ups, True, True, False)
+    came_near = exchange(send, stages, replicas, 1, 2)
+    left, right, send = pack(ups, True, False, True)
+    came = exchange(send, stages, replicas, 1, 2)
+    up_operands = (near_left, near_right, came_near, left, right, came)
+    left, right, send = pack(backs, False, True, True)
+    came = exchange(send, stages, replicas, 1, 2)
     parts = []
-    for name, late in (("inner", backs), ("up", ups)):
-        left, right, send = pl.pallas_call(
-            functools.partial(late_body, stages, chunk, name == "up"),
-            out_shape=[half, narrow, shape(4 * rows, channels // 2 + inner)],
-            in_specs=[VMEM] * (len(fore) + len(late)),
-            out_specs=[VMEM] * 3,
-            scratch_shapes=[pltpu.VMEM((4 * rows, channels), jnp.bfloat16)],
-            compiler_params=PARAMS,
-        )(*fore, *late)
-        came = exchange(send, stages, replicas, 1, 2)
+    for operands in ((left, right, came), up_operands):
         count = replicas // 4
         send, keep = pl.pallas_call(
-            half_gradient_body,
+            functools.partial(half_gradient_body, len(operands) // 3),
             out_shape=sums(count, chunk, inner),
-            in_specs=[VMEM] * 3,
+            in_specs=[VMEM] * len(operands),
             out_specs=[VMEM] * 2,
-            scratch_shapes=[pltpu.VMEM((channels // 2, inner), jnp.float32)],
+            scratch_shapes=[
+                pltpu.VMEM((channels // 2, inner), jnp.float32),
+                pltpu.VMEM((8 * rows, channels // 2), jnp.bfloat16),
+                pltpu.VMEM((8 * rows, inner), jnp.bfloat16),
+            ],
             compiler_params=PARAMS,
-        )(left, right, came)
+        )(*operands)
         came = exchange(send, stages, replicas, 2, 1)
         for bit in range(2, replicas.bit_length() - 1):
             count //= 2

time: 48.1 us -> 46.1 us (0.958)
  waiting for transfers between devices: 16.8 us -> 15.7 us
  starting transfers between devices: 21.5 us -> 20.8 us
    ppermute x3, waiting for transfers between devices: 4.09 us -> 1.89 us  [mirror(): return lax.ppermute(shard, 'pipe', mirror_pairs)]
    ppermute x3, starting transfers between devices: 4.7 us -> 2.85 us  [mirror(): return lax.ppermute(shard, 'pipe', mirror_pairs)]
    ppermute x6 -> x7, starting transfers between devices: 9.89 us -> 10.9 us  [exchange(): return lax.ppermute(shard, AXES, pairs)]
    ppermute x6 -> x7, waiting for transfers between devices: 8.36 us -> 9.32 us  [exchange(): return lax.ppermute(shard, AXES, pairs)]
    pallas_call x4 -> x6, Pallas kernels: 1.03 us -> 1.1 us  [the longest x2 0.67 us: halve_rows(): pl.pallas_call(functools.partial(half_gradient_body, len(operands) // 3),...]
  transfers between devices with their start and end apart: 21 -> 22, of which waited for: 12 -> 11; matrix products, arithmetic and copies ran while one was open for 0% -> 0% of each run, Pallas kernels for 12% -> 12%
where the time goes in v6:
time: 46.1 us; the launch traced here: 45.9 us
  starting transfers between devices  20.8 us (45%)
  waiting for transfers between devices  15.7 us (34%)
  Pallas kernels  9.09 us (20%)
    ppermute x7, starting transfers between devices, exchange(): return lax.ppermute(shard, AXES, pairs)  10.9 us
    ppermute x7, waiting for transfers between devices, exchange(): return lax.ppermute(shard, AXES, pairs)  9.32 us
    ppermute x2, starting transfers between devices, hop(): return lax.ppermute(shard, 'pipe', pairs)  4.81 us
    pallas_call x3, Pallas kernels, run_stage(): pl.pallas_call(functools.partial(stage_body, step, forward, backward, las...  3.59 us
    ppermute x2, waiting for transfers between devices, hop(): return lax.ppermute(shard, 'pipe', pairs)  3.23 us
    ppermute x3, starting transfers between devices, mirror(): return lax.ppermute(shard, 'pipe', mirror_pairs)  2.85 us
    pallas_call x2, Pallas kernels, load(): pl.pallas_call(functools.partial(load_body, step), out_shape=outs, in_spe...  2.44 us
    ppermute x10, starting transfers between devices, swap_cores(): return lax.ppermute(shard, 'pipe', core_pairs)  2.2 us
  transfers between devices with their start and end apart: 22, of which 11 were waited for; matrix products, arithmetic and copies ran while one was open for 0% of the time, Pallas kernels for 12%

profile of v6, /device:TPU:0, one launch (start us, length us, event | category | flops | bytes accessed | tf_op | source)
XLA Modules:
  0.0 45.9 jit_solution(8718969315999476298)
XLA Ops:
  0.0 1.2 %shard_map.46 = (bf16[1024,256]{1,0:T(8,128)(2,1)S(1)}, bf16[1024,256]{1,0:T(8,128)(2,1)S(1)}, bf16[32,1024]{1,0:T(8,128)(2,1)S(1)}) custom-call(bf16[2,1024,256]{2,1,0:T(8,128)(2,1)} %bitcast.20, bf16[2,1024,256]{2,1,0:T(8,128)(2,1)} %bitcast.22, bf16[2,2,32,1024]{3,2,1,0:T(8,128)(2,1)} %inputs), custom_call_target="tpu_custom_call" | custom-call | tf_op jit(solution)/shard_map/pallas_call | solution.py:68
  1.2 0.6 %collective-permute-start = (bf16[1024,256]{1,0:T(8,128)(2,1)S(1)}, bf16[1024,256]{1,0:T(8,128)(2,1)S(1)}, u32[]{:S(2)}, u32[]{:S(2)}) collective-permute-start(bf16[1024,256]{1,0:T(8,128)(2,1)S(1)} %get-tuple-element.46.refs_0_), channel_id=1, source_target_pairs={{0,8},{8,0},{16,24},{24,16},{1,9},{9,1},{17,25},{25,17},{2,10},{10... | collective-permute-start | bytes 1572872 | tf_op jit(solution)/shard_map/ppermute | solution.py:448
  1.8 0.1 collective-permute-start.1
  1.9 1.2 %shard_map.48 = (bf16[1024,256]{1,0:T(8,128)(2,1)S(1)}, bf16[1024,256]{1,0:T(8,128)(2,1)S(1)}) custom-call(bf16[2,1024,256]{2,1,0:T(8,128)(2,1)} %bitcast.21, bf16[2,1024,256]{2,1,0:T(8,128)(2,1)} %bitcast.23), custom_call_target="tpu_custom_call" | custom-call | tf_op jit(solution)/shard_map/pallas_call | solution.py:68
  3.1 0.5 %collective-permute-start.3 = (bf16[1024,256]{1,0:T(8,128)(2,1)S(1)}, bf16[1024,256]{1,0:T(8,128)(2,1)S(1)}, u32[]{:S(2)}, u32[]{:S(2)}) collective-permute-start(bf16[1024,256]{1,0:T(8,128)(2,1)S(1)} %get-tuple-element.51.expand_own.refs_1_), channel_id=1, source_target_pairs={{0,8},{8,0},{16,24},{24,16},{1,9},{9,1},{17,25},{25,17},{2,10},{10... | collective-permute-start | bytes 1572872 | tf_op jit(solution)/shard_map/ppermute | solution.py:448
  3.6 0.1 collective-permute-start.2
  3.7 0.0 collective-permute-done.refs_2_
  3.7 0.4 collective-permute-done.1.refs_3_.other
  4.1 1.2 %shard_map.47 = (bf16[2,32,1280]{2,1,0:T(8,128)(2,1)S(1)}, bf16[32,1024]{1,0:T(8,128)(2,1)S(1)}, bf16[2,32,1024]{2,1,0:T(8,128)(2,1)S(1)}, f32[2,32,256]{2,1,0:T(8,128)S(1)}) custom-call(bf16[1024,256]{1,0:T(8,128)(2,1)S(1)} %get-tuple-element.46.refs_0_, bf16[1024,256]{1,0:T(8,128)(2,1)S(1)} %get-tuple-element.47.refs_1_.own, ...), custom_call_target="tpu_custom_call" | custom-call | flops 67108864 | bytes 2097152 | tf_op jit(solution)/shard_map/pallas_call | solution.py:262
  5.2 2.9 %collective-permute-start.4 = (bf16[32,1024]{1,0:T(8,128)(2,1)S(1)}, bf16[32,1024]{1,0:T(8,128)(2,1)S(1)}, u32[]{:S(2)}, u32[]{:S(2)}) collective-permute-start(bf16[32,1024]{1,0:T(8,128)(2,1)S(1)} %get-tuple-element.52.leave), channel_id=1, source_target_pairs={{0,16},{16,0},{8,24},{24,8},{1,17},{17,1},{9,25},{25,9},{2,18},{18... | collective-permute-start | bytes 196616 | tf_op jit(solution)/shard_map/ppermute | solution.py:445
  8.1 1.2 %shard_map.49 = (bf16[32,1024]{1,0:T(8,128)(2,1)S(1)}, f32[32,256]{1,0:T(8,128)S(1)}, bf16[32,1024]{1,0:T(8,128)(2,1)S(1)}, bf16[32,1024]{1,0:T(8,128)(2,1)S(1)}) custom-call(bf16[1024,256]{1,0:T(8,128)(2,1)S(1)} %get-tuple-element.51.expand_own.refs_1_, bf16[1024,256]{1,0:T(8,128)(2,1)S(1)} %collective-permute-done.3.expand_other.refs_3_, ...), custom_call_target="tpu_custom_call" | custom-call | tf_op jit(solution)/shard_map/pallas_call | solution.py:484
  9.3 1.2 %collective-permute-done.4.refs_4_ = bf16[32,1024]{1,0:T(8,128)(2,1)S(1)} collective-permute-done((bf16[32,1024]{1,0:T(8,128)(2,1)S(1)}, bf16[32,1024]{1,0:T(8,128)(2,1)S(1)}, u32[]{:S(2)}, u32[]{:S(2)}) %collective-permute-start.4) | collective-permute-done | bytes 65568 | tf_op jit(solution)/shard_map/ppermute | solution.py:445
  10.5 1.8 %shard_map.50 = (bf16[2,32,1280]{2,1,0:T(8,128)(2,1)S(1)}, bf16[2,32,1024]{2,1,0:T(8,128)(2,1)S(1)}, bf16[2,32,256]{2,1,0:T(8,128)(2,1)S(1)}, bf16[32,1024]{1,0:T(8,128)(2,1)S(1)}) custom-call(bf16[1024,256]{1,0:T(8,128)(2,1)S(1)} %get-tuple-element.50.refs_0_, bf16[1024,256]{1,0:T(8,128)(2,1)S(1)} %get-tuple-element.51.expand_own.refs_1_, ...), custom_call_target="tpu_custom_call" | custom-call | flops 134217728 | bytes 2097152 | tf_op jit(solution)/shard_map/pallas_call | solution.py:262
  12.3 1.9 %collective-permute-start.8 = (bf16[32,1024]{1,0:T(8,128)(2,1)S(1)}, bf16[32,1024]{1,0:T(8,128)(2,1)S(1)}, u32[]{:S(2)}, u32[]{:S(2)}) collective-permute-start(bf16[32,1024]{1,0:T(8,128)(2,1)S(1)} %get-tuple-element.60), channel_id=1, source_target_pairs={{0,16},{16,0},{8,24},{24,8},{1,17},{17,1},{9,25},{25,9},{2,18},{18... | collective-permute-start | bytes 196616 | tf_op jit(solution)/shard_map/ppermute | solution.py:445
  14.3 0.1 collective-permute-start.5
  14.5 0.2 collective-permute-start.6
  14.7 2.1 %collective-permute-done.8.refs_4_ = bf16[32,1024]{1,0:T(8,128)(2,1)S(1)} collective-permute-done((bf16[32,1024]{1,0:T(8,128)(2,1)S(1)}, bf16[32,1024]{1,0:T(8,128)(2,1)S(1)}, u32[]{:S(2)}, u32[]{:S(2)}) %collective-permute-start.8) | collective-permute-done | bytes 65568 | tf_op jit(solution)/shard_map/ppermute | solution.py:445
  16.7 0.6 %shard_map.51 = (bf16[2,32,1024]{2,1,0:T(8,128)(2,1)S(1)}, bf16[2,32,256]{2,1,0:T(8,128)(2,1)S(1)}) custom-call(bf16[1024,256]{1,0:T(8,128)(2,1)S(1)} %get-tuple-element.46.refs_0_, bf16[1024,256]{1,0:T(8,128)(2,1)S(1)} %get-tuple-element.47.refs_1_.own, bf16[1024,256]{1,0:T(8,128)(2,1)S(1)} %collective-permute-done.refs_2_, ...), custom_call_target="tpu_custom_call" | custom-call | flops 67108864 | bytes 2097152 | tf_op jit(solution)/shard_map/pallas_call | solution.py:262
  17.3 0.2 shard_map.52.refs_5_
  17.6 0.1 collective-permute-start.9
  17.7 2.5 %collective-permute-start.10 = (bf16[2,32,256]{2,1,0:T(8,128)(2,1)S(1)}, bf16[2,32,256]{2,1,0:T(8,128)(2,1)S(1)}, u32[]{:S(2)}, u32[]{:S(2)}) collective-permute-start(bf16[2,32,256]{2,1,0:T(8,128)(2,1)S(1)} %broadcast_select_fusion.7), channel_id=1, source_target_pairs={{0,16},{8,24},{16,0},{24,8},{1,17},{9,25},{17,1},{25,9},{2,18},{10... | collective-permute-start | bytes 98312 | tf_op jit(solution)/shard_map/ppermute | solution.py:451
  20.3 0.1 collective-permute-start.17
  20.4 1.9 %collective-permute-done.10 = bf16[2,32,256]{2,1,0:T(8,128)(2,1)S(1)} collective-permute-done((bf16[2,32,256]{2,1,0:T(8,128)(2,1)S(1)}, bf16[2,32,256]{2,1,0:T(8,128)(2,1)S(1)}, u32[]{:S(2)}, u32[]{:S(2)}) %collective-permute-start.10) | collective-permute-done | bytes 32800 | tf_op jit(solution)/shard_map/ppermute | solution.py:451
  22.3 0.0 collective-permute-done.6
  22.3 0.6 %collective-permute-start.7 = (bf16[32,1280]{1,0:T(8,128)(2,1)S(1)}, bf16[32,1280]{1,0:T(8,128)(2,1)S(1)}, u32[]{:S(2)}, u32[]{:S(2)}) collective-permute-start(bf16[32,1280]{1,0:T(8,128)(2,1)S(1)} %pad_maximum_fusion.2), channel_id=1, source_target_pairs={{0,8},{8,0},{16,24},{24,16},{1,9},{9,1},{17,25},{25,17},{2,10},{10... | collective-permute-start | bytes 245768 | tf_op jit(solution)/shard_map/ppermute | solution.py:448
  22.9 0.1 collective-permute-start.15
  23.0 0.5 collective-permute-done.11.refs_9_
  23.4 0.4 collective-permute-done.7.refs_4_.refs_1_
  23.8 0.1 shard_map.53
  23.9 1.4 %collective-permute-start.12 = (bf16[128,768]{1,0:T(8,128)(2,1)S(1)}, bf16[128,768]{1,0:T(8,128)(2,1)S(1)}, u32[]{:S(2)}, u32[]{:S(2)}) collective-permute-start(bf16[128,768]{1,0:T(8,128)(2,1)S(1)} %get-tuple-element.68), channel_id=1, source_target_pairs={{0,1},{1,0},{2,3},{3,2},{4,5},{5,4},{6,7},{7,6},{8,10},{9,11},{10,... | collective-permute-start | bytes 589832 | tf_op jit(solution)/shard_map/ppermute | solution.py:579
  25.3 0.2 collective-permute-start.18
  25.5 0.1 shard_map.56
  25.6 1.6 %collective-permute-start.16 = (bf16[64,768]{1,0:T(8,128)(2,1)S(1)}, bf16[64,768]{1,0:T(8,128)(2,1)S(1)}, u32[]{:S(2)}, u32[]{:S(2)}) collective-permute-start(bf16[64,768]{1,0:T(8,128)(2,1)S(1)} %get-tuple-element.76), channel_id=1, source_target_pairs={{0,1},{1,0},{2,3},{3,2},{4,5},{5,4},{6,7},{7,6},{8,10},{9,11},{10,... | collective-permute-start | bytes 294920 | tf_op jit(solution)/shard_map/ppermute | solution.py:579
  27.1 0.1 shard_map.57
  27.2 0.8 %collective-permute-start.19 = (bf16[64,768]{1,0:T(8,128)(2,1)S(1)}, bf16[64,768]{1,0:T(8,128)(2,1)S(1)}, u32[]{:S(2)}, u32[]{:S(2)}) collective-permute-start(bf16[64,768]{1,0:T(8,128)(2,1)S(1)} %get-tuple-element.80), channel_id=1, source_target_pairs={{0,1},{1,0},{2,3},{3,2},{4,5},{5,4},{6,7},{7,6},{8,10},{9,11},{10,... | collective-permute-start | bytes 294920 | tf_op jit(solution)/shard_map/ppermute | solution.py:579
  28.0 2.7 %collective-permute-done.16.refs_2_ = bf16[64,768]{1,0:T(8,128)(2,1)S(1)} collective-permute-done((bf16[64,768]{1,0:T(8,128)(2,1)S(1)}, bf16[64,768]{1,0:T(8,128)(2,1)S(1)}, u32[]{:S(2)}, u32[]{:S(2)}) %collective-permute-start.16) | collective-permute-done | bytes 98336 | tf_op jit(solution)/shard_map/ppermute | solution.py:579
  30.7 1.2 %collective-permute-done.19.refs_5_ = bf16[64,768]{1,0:T(8,128)(2,1)S(1)} collective-permute-done((bf16[64,768]{1,0:T(8,128)(2,1)S(1)}, bf16[64,768]{1,0:T(8,128)(2,1)S(1)}, u32[]{:S(2)}, u32[]{:S(2)}) %collective-permute-start.19) | collective-permute-done | bytes 98336 | tf_op jit(solution)/shard_map/ppermute | solution.py:579
  31.9 0.3 shard_map.58
  32.2 1.3 %collective-permute-start.20 = (bf16[2,128,256]{2,1,0:T(8,128)(2,1)S(1)}, bf16[2,128,256]{2,1,0:T(8,128)(2,1)S(1)}, u32[]{:S(2)}, u32[]{:S(2)}) collective-permute-start(bf16[2,128,256]{2,1,0:T(8,128)(2,1)S(1)} %get-tuple-element.82), channel_id=1, source_target_pairs={{0,2},{1,3},{2,0},{3,1},{4,6},{5,7},{6,4},{7,5},{8,9},{9,8},{10,11... | collective-permute-start | bytes 393224 | tf_op jit(solution)/shard_map/ppermute | solution.py:579
  33.5 0.3 shard_map.54
  33.9 0.9 %collective-permute-start.13 = (bf16[2,128,256]{2,1,0:T(8,128)(2,1)S(1)}, bf16[2,128,256]{2,1,0:T(8,128)(2,1)S(1)}, u32[]{:S(2)}, u32[]{:S(2)}) collective-permute-start(bf16[2,128,256]{2,1,0:T(8,128)(2,1)S(1)} %get-tuple-element.70), channel_id=1, source_target_pairs={{0,2},{1,3},{2,0},{3,1},{4,6},{5,7},{6,4},{7,5},{8,9},{9,8},{10,11... | collective-permute-start | bytes 393224 | tf_op jit(solution)/shard_map/ppermute | solution.py:579
  34.7 2.5 %collective-permute-done.20.came = bf16[2,128,256]{2,1,0:T(8,128)(2,1)S(1)} collective-permute-done((bf16[2,128,256]{2,1,0:T(8,128)(2,1)S(1)}, bf16[2,128,256]{2,1,0:T(8,128)(2,1)S(1)}, u32[]{:S(2)}, u32[]{:S(2)}) %collective-permute-start.20) | collective-permute-done | bytes 131104 | tf_op jit(solution)/shard_map/ppermute | solution.py:579
  37.3 2.7 %collective-permute-start.21 = (bf16[1,128,256]{2,1,0:T(8,128)(2,1)S(1)}, bf16[1,128,256]{2,1,0:T(8,128)(2,1)S(1)}, u32[]{:S(2)}, u32[]{:S(2)}) collective-permute-start(bf16[1,128,256]{2,1,0:T(8,128)(2,1)S(1)} %get-tuple-element.84), channel_id=1, source_target_pairs={{0,4},{1,5},{2,6},{3,7},{4,0},{5,1},{6,2},{7,3},{8,12},{9,13},{10,... | collective-permute-start | bytes 196616 | tf_op jit(solution)/shard_map/ppermute | solution.py:579
  39.9 0.0 collective-permute-done.13.came
  40.0 2.3 %collective-permute-start.14 = (bf16[1,128,256]{2,1,0:T(8,128)(2,1)S(1)}, bf16[1,128,256]{2,1,0:T(8,128)(2,1)S(1)}, u32[]{:S(2)}, u32[]{:S(2)}) collective-permute-start(bf16[1,128,256]{2,1,0:T(8,128)(2,1)S(1)} %get-tuple-element.72), channel_id=1, source_target_pairs={{0,4},{1,5},{2,6},{3,7},{4,0},{5,1},{6,2},{7,3},{8,12},{9,13},{10,... | collective-permute-start | bytes 196616 | tf_op jit(solution)/shard_map/ppermute | solution.py:579
  42.3 1.9 %collective-permute-done.21.came_expand = bf16[1,128,256]{2,1,0:T(8,128)(2,1)S(1)} collective-permute-done((bf16[1,128,256]{2,1,0:T(8,128)(2,1)S(1)}, bf16[1,128,256]{2,1,0:T(8,128)(2,1)S(1)}, u32[]{:S(2)}, u32[]{:S(2)}) %collective-permute-start.21) | collective-permute-done | bytes 65568 | tf_op jit(solution)/shard_map/ppermute | solution.py:579
  44.2 1.0 %collective-permute-done.14.came_reduce = bf16[1,128,256]{2,1,0:T(8,128)(2,1)S(1)} collective-permute-done((bf16[1,128,256]{2,1,0:T(8,128)(2,1)S(1)}, bf16[1,128,256]{2,1,0:T(8,128)(2,1)S(1)}, u32[]{:S(2)}, u32[]{:S(2)}) %collective-permute-start.14) | collective-permute-done | bytes 65568 | tf_op jit(solution)/shard_map/ppermute | solution.py:579
  45.2 0.7 %shard_map.60 = f32[1,2,128,256]{3,2,1,0:T(8,128)} custom-call(f32[1,128,256]{2,1,0:T(8,128)S(1)} %get-tuple-element.71.keep_reduce, bf16[1,128,256]{2,1,0:T(8,128)(2,1)S(1)} %collective-permute-done.14.came_reduce, f32[1,128,256]{2,1,0:T(8,128)S(1)} %get-tuple-element.83.keep_expand, bf16[1,128,256]{2,1,0:T(8,128)(2,1)S(1)} %collective-permute-done.21.came_expand), custom_call_target="tpu_custom_call" | custom-call | tf_op jit(solution)/shard_map/pallas_call | solution.py:558
  (27 shorter events, 0.2 us)
Async XLA Ops:
  1.2 2.4 %collective-permute-start = (bf16[1024,256]{1,0:T(8,128)(2,1)S(1)}, bf16[1024,256]{1,0:T(8,128)(2,1)S(1)}, u32[]{:S(2)}, u32[]{:S(2)}) collective-permute-start(bf16[1024,256]{1,0:T(8,128)(2,1)S(1)} %get-tuple-element.46.refs_0_), channel_id=1, source_target_pairs={{0,8},{8,0},{16,24},{24,16},{1,9},{9,1},{17,25},{25,17},{2,10},{10... | collective-permute-start | bytes 1572872 | tf_op jit(solution)/shard_map/ppermute | solution.py:448
  1.8 2.3 %collective-permute-start.1 = (bf16[1024,256]{1,0:T(8,128)(2,1)S(1)}, bf16[1024,256]{1,0:T(8,128)(2,1)S(1)}, u32[]{:S(2)}, u32[]{:S(2)}) collective-permute-start(bf16[1024,256]{1,0:T(8,128)(2,1)S(1)} %get-tuple-element.47.refs_1_.own), channel_id=1, source_target_pairs={{0,8},{8,0},{16,24},{24,16},{1,9},{9,1},{17,25},{25,17},{2,10},{10... | collective-permute-start | bytes 1572872 | tf_op jit(solution)/shard_map/ppermute | solution.py:448
  3.1 5.0 %collective-permute-start.3 = (bf16[1024,256]{1,0:T(8,128)(2,1)S(1)}, bf16[1024,256]{1,0:T(8,128)(2,1)S(1)}, u32[]{:S(2)}, u32[]{:S(2)}) collective-permute-start(bf16[1024,256]{1,0:T(8,128)(2,1)S(1)} %get-tuple-element.51.expand_own.refs_1_), channel_id=1, source_target_pairs={{0,8},{8,0},{16,24},{24,16},{1,9},{9,1},{17,25},{25,17},{2,10},{10... | collective-permute-start | bytes 1572872 | tf_op jit(solution)/shard_map/ppermute | solution.py:448
  3.6 5.7 %collective-permute-start.2 = (bf16[1024,256]{1,0:T(8,128)(2,1)S(1)}, bf16[1024,256]{1,0:T(8,128)(2,1)S(1)}, u32[]{:S(2)}, u32[]{:S(2)}) collective-permute-start(bf16[1024,256]{1,0:T(8,128)(2,1)S(1)} %get-tuple-element.50.refs_0_), channel_id=1, source_target_pairs={{0,8},{8,0},{16,24},{24,16},{1,9},{9,1},{17,25},{25,17},{2,10},{10... | collective-permute-start | bytes 1572872 | tf_op jit(solution)/shard_map/ppermute | solution.py:448
  5.2 5.3 %collective-permute-start.4 = (bf16[32,1024]{1,0:T(8,128)(2,1)S(1)}, bf16[32,1024]{1,0:T(8,128)(2,1)S(1)}, u32[]{:S(2)}, u32[]{:S(2)}) collective-permute-start(bf16[32,1024]{1,0:T(8,128)(2,1)S(1)} %get-tuple-element.52.leave), channel_id=1, source_target_pairs={{0,16},{16,0},{8,24},{24,8},{1,17},{17,1},{9,25},{25,9},{2,18},{18... | collective-permute-start | bytes 196616 | tf_op jit(solution)/shard_map/ppermute | solution.py:445
  12.3 4.4 %collective-permute-start.8 = (bf16[32,1024]{1,0:T(8,128)(2,1)S(1)}, bf16[32,1024]{1,0:T(8,128)(2,1)S(1)}, u32[]{:S(2)}, u32[]{:S(2)}) collective-permute-start(bf16[32,1024]{1,0:T(8,128)(2,1)S(1)} %get-tuple-element.60), channel_id=1, source_target_pairs={{0,16},{16,0},{8,24},{24,8},{1,17},{17,1},{9,25},{25,9},{2,18},{18... | collective-permute-start | bytes 196616 | tf_op jit(solution)/shard_map/ppermute | solution.py:445
  14.3 8.7 %collective-permute-start.5 = (bf16[32,1280]{1,0:T(8,128)(2,1)S(1)}, bf16[32,1280]{1,0:T(8,128)(2,1)S(1)}, u32[]{:S(2)}, u32[]{:S(2)}) collective-permute-start(bf16[32,1280]{1,0:T(8,128)(2,1)S(1)} %fusion), channel_id=1, source_target_pairs={{0,8},{8,0},{16,24},{24,16},{1,9},{9,1},{17,25},{25,17},{2,10},{10... | collective-permute-start | bytes 245768 | tf_op jit(solution)/shard_map/ppermute | solution.py:448
  14.5 7.8 %collective-permute-start.6 = (bf16[32,1536]{1,0:T(8,128)(2,1)S(1)}, bf16[32,1536]{1,0:T(8,128)(2,1)S(1)}, u32[]{:S(2)}, u32[]{:S(2)}) collective-permute-start(bf16[32,1536]{1,0:T(8,128)(2,1)S(1)} %pad_maximum_fusion), channel_id=1, source_target_pairs={{0,16},{8,24},{16,0},{24,8},{1,17},{9,25},{17,1},{25,9},{2,18},{10... | collective-permute-start | bytes 294920 | tf_op jit(solution)/shard_map/ppermute | solution.py:451
  17.6 5.2 %collective-permute-start.9 = (bf16[32,256]{1,0:T(8,128)(2,1)S(1)}, bf16[32,256]{1,0:T(8,128)(2,1)S(1)}, u32[]{:S(2)}, u32[]{:S(2)}) collective-permute-start(bf16[32,256]{1,0:T(8,128)(2,1)S(1)} %fusion.4), channel_id=1, source_target_pairs={{0,8},{8,0},{16,24},{24,16},{1,9},{9,1},{17,25},{25,17},{2,10},{10... | collective-permute-start | bytes 49160 | tf_op jit(solution)/shard_map/ppermute | solution.py:448
  17.7 4.5 %collective-permute-start.10 = (bf16[2,32,256]{2,1,0:T(8,128)(2,1)S(1)}, bf16[2,32,256]{2,1,0:T(8,128)(2,1)S(1)}, u32[]{:S(2)}, u32[]{:S(2)}) collective-permute-start(bf16[2,32,256]{2,1,0:T(8,128)(2,1)S(1)} %broadcast_select_fusion.7), channel_id=1, source_target_pairs={{0,16},{8,24},{16,0},{24,8},{1,17},{9,25},{17,1},{25,9},{2,18},{10... | collective-permute-start | bytes 98312 | tf_op jit(solution)/shard_map/ppermute | solution.py:451
  20.3 5.0 %collective-permute-start.17 = (bf16[32,1024]{1,0:T(8,128)(2,1)S(1)}, bf16[32,1024]{1,0:T(8,128)(2,1)S(1)}, u32[]{:S(2)}, u32[]{:S(2)}) collective-permute-start(bf16[32,1024]{1,0:T(8,128)(2,1)S(1)} %fusion.1), channel_id=1, source_target_pairs={{0,16},{8,24},{16,0},{24,8},{1,17},{9,25},{17,1},{25,9},{2,18},{10... | collective-permute-start | bytes 196616 | tf_op jit(solution)/shard_map/ppermute | solution.py:451
  22.2 1.2 %collective-permute-start.11 = (bf16[32,256]{1,0:T(8,128)(2,1)S(1)}, bf16[32,256]{1,0:T(8,128)(2,1)S(1)}, u32[]{:S(2)}, u32[]{:S(2)}) collective-permute-start(bf16[32,256]{1,0:T(8,128)(2,1)S(1)} %get-tuple-element.93), channel_id=1, source_target_pairs={{0,8},{8,0},{16,24},{24,16},{1,9},{9,1},{17,25},{25,17},{2,10},{10... | collective-permute-start | bytes 49160 | tf_op jit(solution)/shard_map/ppermute | solution.py:448
  22.3 1.5 %collective-permute-start.7 = (bf16[32,1280]{1,0:T(8,128)(2,1)S(1)}, bf16[32,1280]{1,0:T(8,128)(2,1)S(1)}, u32[]{:S(2)}, u32[]{:S(2)}) collective-permute-start(bf16[32,1280]{1,0:T(8,128)(2,1)S(1)} %pad_maximum_fusion.2), channel_id=1, source_target_pairs={{0,8},{8,0},{16,24},{24,16},{1,9},{9,1},{17,25},{25,17},{2,10},{10... | collective-permute-start | bytes 245768 | tf_op jit(solution)/shard_map/ppermute | solution.py:448
  22.9 2.6 %collective-permute-start.15 = (bf16[32,1024]{1,0:T(8,128)(2,1)S(1)}, bf16[32,1024]{1,0:T(8,128)(2,1)S(1)}, u32[]{:S(2)}, u32[]{:S(2)}) collective-permute-start(bf16[32,1024]{1,0:T(8,128)(2,1)S(1)} %fusion.2), channel_id=1, source_target_pairs={{0,8},{8,0},{16,24},{24,16},{1,9},{9,1},{17,25},{25,17},{2,10},{10... | collective-permute-start | bytes 196616 | tf_op jit(solution)/shard_map/ppermute | solution.py:448
  23.9 9.6 %collective-permute-start.12 = (bf16[128,768]{1,0:T(8,128)(2,1)S(1)}, bf16[128,768]{1,0:T(8,128)(2,1)S(1)}, u32[]{:S(2)}, u32[]{:S(2)}) collective-permute-start(bf16[128,768]{1,0:T(8,128)(2,1)S(1)} %get-tuple-element.68), channel_id=1, source_target_pairs={{0,1},{1,0},{2,3},{3,2},{4,5},{5,4},{6,7},{7,6},{8,10},{9,11},{10,... | collective-permute-start | bytes 589832 | tf_op jit(solution)/shard_map/ppermute | solution.py:579
  25.3 1.8 %collective-permute-start.18 = (bf16[32,1024]{1,0:T(8,128)(2,1)S(1)}, bf16[32,1024]{1,0:T(8,128)(2,1)S(1)}, u32[]{:S(2)}, u32[]{:S(2)}) collective-permute-start(bf16[32,1024]{1,0:T(8,128)(2,1)S(1)} %get-tuple-element.85), channel_id=1, source_target_pairs={{0,8},{8,0},{16,24},{24,16},{1,9},{9,1},{17,25},{25,17},{2,10},{10... | collective-permute-start | bytes 196616 | tf_op jit(solution)/shard_map/ppermute | solution.py:448
  25.6 5.1 %collective-permute-start.16 = (bf16[64,768]{1,0:T(8,128)(2,1)S(1)}, bf16[64,768]{1,0:T(8,128)(2,1)S(1)}, u32[]{:S(2)}, u32[]{:S(2)}) collective-permute-start(bf16[64,768]{1,0:T(8,128)(2,1)S(1)} %get-tuple-element.76), channel_id=1, source_target_pairs={{0,1},{1,0},{2,3},{3,2},{4,5},{5,4},{6,7},{7,6},{8,10},{9,11},{10,... | collective-permute-start | bytes 294920 | tf_op jit(solution)/shard_map/ppermute | solution.py:579
  27.2 4.7 %collective-permute-start.19 = (bf16[64,768]{1,0:T(8,128)(2,1)S(1)}, bf16[64,768]{1,0:T(8,128)(2,1)S(1)}, u32[]{:S(2)}, u32[]{:S(2)}) collective-permute-start(bf16[64,768]{1,0:T(8,128)(2,1)S(1)} %get-tuple-element.80), channel_id=1, source_target_pairs={{0,1},{1,0},{2,3},{3,2},{4,5},{5,4},{6,7},{7,6},{8,10},{9,11},{10,... | collective-permute-start | bytes 294920 | tf_op jit(solution)/shard_map/ppermute | solution.py:579
  32.2 5.0 %collective-permute-start.20 = (bf16[2,128,256]{2,1,0:T(8,128)(2,1)S(1)}, bf16[2,128,256]{2,1,0:T(8,128)(2,1)S(1)}, u32[]{:S(2)}, u32[]{:S(2)}) collective-permute-start(bf16[2,128,256]{2,1,0:T(8,128)(2,1)S(1)} %get-tuple-element.82), channel_id=1, source_target_pairs={{0,2},{1,3},{2,0},{3,1},{4,6},{5,7},{6,4},{7,5},{8,9},{9,8},{10,11... | collective-permute-start | bytes 393224 | tf_op jit(solution)/shard_map/ppermute | solution.py:579
  33.9 6.1 %collective-permute-start.13 = (bf16[2,128,256]{2,1,0:T(8,128)(2,1)S(1)}, bf16[2,128,256]{2,1,0:T(8,128)(2,1)S(1)}, u32[]{:S(2)}, u32[]{:S(2)}) collective-permute-start(bf16[2,128,256]{2,1,0:T(8,128)(2,1)S(1)} %get-tuple-element.70), channel_id=1, source_target_pairs={{0,2},{1,3},{2,0},{3,1},{4,6},{5,7},{6,4},{7,5},{8,9},{9,8},{10,11... | collective-permute-start | bytes 393224 | tf_op jit(solution)/shard_map/ppermute | solution.py:579
  37.3 6.9 %collective-permute-start.21 = (bf16[1,128,256]{2,1,0:T(8,128)(2,1)S(1)}, bf16[1,128,256]{2,1,0:T(8,128)(2,1)S(1)}, u32[]{:S(2)}, u32[]{:S(2)}) collective-permute-start(bf16[1,128,256]{2,1,0:T(8,128)(2,1)S(1)} %get-tuple-element.84), channel_id=1, source_target_pairs={{0,4},{1,5},{2,6},{3,7},{4,0},{5,1},{6,2},{7,3},{8,12},{9,13},{10,... | collective-permute-start | bytes 196616 | tf_op jit(solution)/shard_map/ppermute | solution.py:579
  40.0 5.2 %collective-permute-start.14 = (bf16[1,128,256]{2,1,0:T(8,128)(2,1)S(1)}, bf16[1,128,256]{2,1,0:T(8,128)(2,1)S(1)}, u32[]{:S(2)}, u32[]{:S(2)}) collective-permute-start(bf16[1,128,256]{2,1,0:T(8,128)(2,1)S(1)} %get-tuple-element.72), channel_id=1, source_target_pairs={{0,4},{1,5},{2,6},{3,7},{4,0},{5,1},{6,2},{7,3},{8,12},{9,13},{10,... | collective-permute-start | bytes 196616 | tf_op jit(solution)/shard_map/ppermute | solution.py:579

commit v7 on v6

--- a/solution.py
+++ b/solution.py
@@ -127,11 +127,27 @@
         pl.when(jnp.logical_not(is_own))(theirs.start)
 
 
+def head_body(own, other, rows_in, lifted_out, inner_out, active_out):
+    _, core, way = where_am_i(0)
+    widened = rows_in[...].astype(jnp.float32)
+    lifted = jax.nn.silu(widened * norm_of(widened)).astype(jnp.bfloat16)
+    lifted_out[...] = lifted
+
+    def run(reduce_mat):
+        inner_sum = jnp.dot(lifted, reduce_mat[...], preferred_element_type=jnp.float32)
+        inner_out[...] = inner_sum
+        active_out[...] = jax.nn.silu(inner_sum).astype(jnp.bfloat16)
+
+    pl.when(way == core)(lambda: run(own))
+    pl.when(way != core)(lambda: run(other))
+
+
 def stage_body(step, forward, backward, last, near, *refs):
     refs = list(refs)
     _, core, way = where_am_i(step)
     own, other = (refs.pop(0), refs.pop(0)), (refs.pop(0), refs.pop(0))
     enter = refs.pop(0) if forward else None
+    head = [refs.pop(0) for _ in range(3)] if forward and step == 0 else None
     upstream_in = refs.pop(0) if backward else None
     first_active = refs.pop(0) if forward and backward else None
     if not forward:
@@ -154,15 +170,18 @@
             for order in range(2):
                 slot = lax.rem(order + core, 2)
                 widened = rows.astype(jnp.float32)
-                normed = widened * norm_of(widened)
-                lifted = jax.nn.silu(normed).astype(jnp.bfloat16)
                 trunks[order] = rows
+                if head and order == 0:
+                    lifted, inner_sum, active = [part[...] for part in head]
+                else:
+                    normed = widened * norm_of(widened)
+                    lifted = jax.nn.silu(normed).astype(jnp.bfloat16)
+                    wait(0, order)
+                    inner_sum = jnp.dot(
+                        lifted, reduce_mats[order][...], preferred_element_type=jnp.float32
+                    )
+                    active = jax.nn.silu(inner_sum).astype(jnp.bfloat16)
                 flows[slot, :, :channels] = lifted
-                wait(0, order)
-                inner_sum = jnp.dot(
-                    lifted, reduce_mats[order][...], preferred_element_type=jnp.float32
-                )
-                active = jax.nn.silu(inner_sum).astype(jnp.bfloat16)
                 inners[order] = inner_sum
                 flows[slot, :, channels:] = active
                 wait(1, order)
@@ -388,7 +407,18 @@
     send[:, channels // 2 :] = right[...]
 
 
-def half_gradient_body(groups, *refs):
+def near_body(stages, chunk, *refs):
+    flows, ups, backs = [refs[at * (stages + 1) : (at + 1) * (stages + 1)] for at in range(3)]
+    left_up, right_up, left_inner, right_inner, send, wide = refs[3 * stages + 3 :]
+    width = send.shape[1] // 2
+    for at, (late, outs) in enumerate(
+        ((ups, (left_up, right_up)), (backs, (left_inner, right_inner)))
+    ):
+        part = send.at[:, at * width : (at + 1) * width]
+        pack_body(stages, chunk, at == 0, True, False, *flows, *late, *outs, part, wide)
+
+
+def half_gradient_body(at, groups, *refs):
     send, keep, full, left, right = refs[3 * groups :]
     start = 0
     for group in range(groups):
@@ -397,8 +427,10 @@
         left[start : start + rows] = part_left[...]
         right[start : start + rows] = part_right[...]
         start += rows
-        left[start : start + rows] = came[:, :columns]
-        right[start : start + rows] = came[:, columns:]
+        width = columns + right.shape[1]
+        offset = at * width if came.shape[1] > width else 0
+        left[start : start + rows] = came[:, offset : offset + columns]
+        right[start : start + rows] = came[:, offset + columns : offset + width]
         start += rows
     full[...] = contract(left[...], right[...], 0, 0)
     _, _, side = first_sides()
@@ -464,15 +496,28 @@
     in_hbm = lambda array: pltpu.with_memory_space_constraint(array, pltpu.HBM)
     own, entering, ending = [in_hbm(one) for one in own], in_hbm(entering), in_hbm(ending)
     *near, enter = load(0, own, entering)
-    near += [swap_cores(weight) for weight in near]
+    near.append(swap_cores(near[0]))
+    near.append(swap_cores(near[1]))
     turn = list(load(stages - 1, own))
     turn += [swap_cores(weight) for weight in turn]
     if stages > 2:
         weights = own + [swap_cores(weight) for weight in own]
     flows, trunks, inners = [], [], []
+    head = pl.pallas_call(
+        head_body,
+        out_shape=[
+            jax.ShapeDtypeStruct((rows, channels), jnp.bfloat16),
+            jax.ShapeDtypeStruct((rows, inner), jnp.float32),
+            jax.ShapeDtypeStruct((rows, inner), jnp.bfloat16),
+        ],
+        in_specs=[VMEM] * 3,
+        out_specs=[VMEM] * 3,
+        compiler_params=PARAMS,
+    )(near[0], near[2], enter)
     for step in range(stages - 1):
+        arrays = [enter] if step else [enter, *head]
         flow, leave, trunk, inner_sum = run_stage(
-            weights if step else near, step, True, False, step == 0, rows, sizes, enter
+            weights if step else near, step, True, False, step == 0, rows, sizes, *arrays
         )
         flows.append(flow)
         trunks.append(trunk)
@@ -601,18 +646,30 @@
             compiler_params=PARAMS,
         )(*arrays)
 
-    near_left, near_right, send = pack(ups, True, True, False)
+    near = fore[: stages + 1] + ups[: stages + 1] + backs[: stages + 1]
+    *kept, send = pl.pallas_call(
+        functools.partial(near_body, stages, chunk),
+        out_shape=[
+            shape(2 * rows, channels // 2),
+            shape(2 * rows, inner),
+            shape(2 * rows, channels // 2),
+            shape(2 * rows, inner),
+            shape(2 * rows, channels + 2 * inner),
+        ],
+        in_specs=[VMEM] * len(near),
+        out_specs=[VMEM] * 5,
+        scratch_shapes=[pltpu.VMEM((2 * rows, channels), jnp.bfloat16)],
+        compiler_params=PARAMS,
+    )(*near)
     came_near = exchange(send, stages, replicas, 1, 2)
-    left, right, send = pack(ups, True, False, True)
-    came = exchange(send, stages, replicas, 1, 2)
-    up_operands = (near_left, near_right, came_near, left, right, came)
-    left, right, send = pack(backs, False, True, True)
-    came = exchange(send, stages, replicas, 1, 2)
     parts = []
-    for operands in ((left, right, came), up_operands):
+    for at, name, late in ((1, "inner", backs), (0, "up", ups)):
+        left, right, send = pack(late, name == "up", False, True)
+        came = exchange(send, stages, replicas, 1, 2)
+        operands = (kept[2 * at], kept[2 * at + 1], came_near, left, right, came)
         count = replicas // 4
         send, keep = pl.pallas_call(
-            functools.partial(half_gradient_body, len(operands) // 3),
+            functools.partial(half_gradient_body, at, len(operands) // 3),
             out_shape=sums(count, chunk, inner),
             in_specs=[VMEM] * len(operands),
             out_specs=[VMEM] * 2,

time: 46.1 us -> 47.8 us (1.037)
  starting transfers between devices: 20.8 us -> 22.4 us
    ppermute x3, waiting for transfers between devices: 1.89 us -> 4.09 us  [mirror(): return lax.ppermute(shard, 'pipe', mirror_pairs)]
    ppermute x3, starting transfers between devices: 2.85 us -> 4.67 us  [mirror(): return lax.ppermute(shard, 'pipe', mirror_pairs)]
    ppermute x10, waiting for transfers between devices: 1.24 us -> 0.09 us  [swap_cores(): return lax.ppermute(shard, 'pipe', core_pairs)]
    ppermute x7, waiting for transfers between devices: 9.32 us -> 8.24 us  [exchange(): return lax.ppermute(shard, AXES, pairs)]
    pallas_call x2 -> x4, Pallas kernels: 0.67 us -> 1.11 us  [the longest x2 0.67 us: halve_rows(): pl.pallas_call(functools.partial(half_gradient_body, at, len(operands) //...]
  transfers between devices with their start and end apart: 22 -> 22, of which waited for: 11 -> 9; matrix products, arithmetic and copies ran while one was open for 0% -> 0% of each run, Pallas kernels for 12% -> 11%
where the time goes in v7:
time: 47.8 us; the launch traced here: 47.6 us
  starting transfers between devices  22.4 us (47%)
  waiting for transfers between devices  15.6 us (33%)
  Pallas kernels  9.11 us (19%)
    ppermute x7, starting transfers between devices, exchange(): return lax.ppermute(shard, AXES, pairs)  10.8 us
    ppermute x7, waiting for transfers between devices, exchange(): return lax.ppermute(shard, AXES, pairs)  8.24 us
    ppermute x2, starting transfers between devices, hop(): return lax.ppermute(shard, 'pipe', pairs)  4.86 us
    ppermute x3, starting transfers between devices, mirror(): return lax.ppermute(shard, 'pipe', mirror_pairs)  4.67 us
    ppermute x3, waiting for transfers between devices, mirror(): return lax.ppermute(shard, 'pipe', mirror_pairs)  4.09 us
    pallas_call x3, Pallas kernels, run_stage(): pl.pallas_call(functools.partial(stage_body, step, forward, backward, las...  3.26 us
    ppermute x2, waiting for transfers between devices, hop(): return lax.ppermute(shard, 'pipe', pairs)  3.23 us
    pallas_call x2, Pallas kernels, load(): pl.pallas_call(functools.partial(load_body, step), out_shape=outs, in_spe...  2.44 us
  transfers between devices with their start and end apart: 22, of which 9 were waited for; matrix products, arithmetic and copies ran while one was open for 0% of the time, Pallas kernels for 11%

profile of v7, /device:TPU:0, one launch (start us, length us, event | category | flops | bytes accessed | tf_op | source)
XLA Modules:
  0.0 47.6 jit_solution(10420049443551664251)
XLA Ops:
  0.0 1.2 %shard_map.46 = (bf16[1024,256]{1,0:T(8,128)(2,1)S(1)}, bf16[1024,256]{1,0:T(8,128)(2,1)S(1)}, bf16[32,1024]{1,0:T(8,128)(2,1)S(1)}) custom-call(bf16[2,1024,256]{2,1,0:T(8,128)(2,1)} %bitcast.20, bf16[2,1024,256]{2,1,0:T(8,128)(2,1)} %bitcast.22, bf16[2,2,32,1024]{3,2,1,0:T(8,128)(2,1)} %inputs), custom_call_target="tpu_custom_call" | custom-call | tf_op jit(solution)/shard_map/pallas_call | solution.py:68
  1.2 0.6 %collective-permute-start = (bf16[1024,256]{1,0:T(8,128)(2,1)S(1)}, bf16[1024,256]{1,0:T(8,128)(2,1)S(1)}, u32[]{:S(2)}, u32[]{:S(2)}) collective-permute-start(bf16[1024,256]{1,0:T(8,128)(2,1)S(1)} %get-tuple-element.51.own.refs_0_), channel_id=1, source_target_pairs={{0,8},{8,0},{16,24},{24,16},{1,9},{9,1},{17,25},{25,17},{2,10},{10... | collective-permute-start | bytes 1572872 | tf_op jit(solution)/shard_map/ppermute | solution.py:480
  1.8 0.1 collective-permute-start.1
  1.9 1.2 %shard_map.49 = (bf16[1024,256]{1,0:T(8,128)(2,1)S(1)}, bf16[1024,256]{1,0:T(8,128)(2,1)S(1)}) custom-call(bf16[2,1024,256]{2,1,0:T(8,128)(2,1)} %bitcast.21, bf16[2,1024,256]{2,1,0:T(8,128)(2,1)} %bitcast.23), custom_call_target="tpu_custom_call" | custom-call | tf_op jit(solution)/shard_map/pallas_call | solution.py:68
  3.1 0.5 %collective-permute-start.3 = (bf16[1024,256]{1,0:T(8,128)(2,1)S(1)}, bf16[1024,256]{1,0:T(8,128)(2,1)S(1)}, u32[]{:S(2)}, u32[]{:S(2)}) collective-permute-start(bf16[1024,256]{1,0:T(8,128)(2,1)S(1)} %get-tuple-element.59.expand_own.refs_1_), channel_id=1, source_target_pairs={{0,8},{8,0},{16,24},{24,16},{1,9},{9,1},{17,25},{25,17},{2,10},{10... | collective-permute-start | bytes 1572872 | tf_op jit(solution)/shard_map/ppermute | solution.py:480
  3.6 0.1 collective-permute-start.2
  3.7 0.3 shard_map.47
  4.0 0.1 collective-permute-done.1.refs_3_.other
  4.1 0.8 %shard_map.48 = (bf16[2,32,1280]{2,1,0:T(8,128)(2,1)S(1)}, bf16[32,1024]{1,0:T(8,128)(2,1)S(1)}, bf16[2,32,1024]{2,1,0:T(8,128)(2,1)S(1)}, f32[2,32,256]{2,1,0:T(8,128)S(1)}) custom-call(bf16[1024,256]{1,0:T(8,128)(2,1)S(1)} %get-tuple-element.51.own.refs_0_, bf16[1024,256]{1,0:T(8,128)(2,1)S(1)} %get-tuple-element.52.refs_1_.own, ...), custom_call_target="tpu_custom_call" | custom-call | flops 67108864 | bytes 2097152 | tf_op jit(solution)/shard_map/pallas_call | solution.py:281
  4.9 2.9 %collective-permute-start.4 = (bf16[32,1024]{1,0:T(8,128)(2,1)S(1)}, bf16[32,1024]{1,0:T(8,128)(2,1)S(1)}, u32[]{:S(2)}, u32[]{:S(2)}) collective-permute-start(bf16[32,1024]{1,0:T(8,128)(2,1)S(1)} %get-tuple-element.60.leave), channel_id=1, source_target_pairs={{0,16},{16,0},{8,24},{24,8},{1,17},{17,1},{9,25},{25,9},{2,18},{18... | collective-permute-start | bytes 196616 | tf_op jit(solution)/shard_map/ppermute | solution.py:477
  7.8 0.0 collective-permute-done.3.expand_other.refs_3_
  7.8 1.2 %shard_map.50 = (bf16[32,1024]{1,0:T(8,128)(2,1)S(1)}, f32[32,256]{1,0:T(8,128)S(1)}, bf16[32,1024]{1,0:T(8,128)(2,1)S(1)}, bf16[32,1024]{1,0:T(8,128)(2,1)S(1)}) custom-call(bf16[1024,256]{1,0:T(8,128)(2,1)S(1)} %get-tuple-element.59.expand_own.refs_1_, bf16[1024,256]{1,0:T(8,128)(2,1)S(1)} %collective-permute-done.3.expand_other.refs_3_, ...), custom_call_target="tpu_custom_call" | custom-call | tf_op jit(solution)/shard_map/pallas_call | solution.py:529
  9.0 0.0 collective-permute-done.2.refs_2_
  9.0 1.2 %collective-permute-done.4.refs_4_ = bf16[32,1024]{1,0:T(8,128)(2,1)S(1)} collective-permute-done((bf16[32,1024]{1,0:T(8,128)(2,1)S(1)}, bf16[32,1024]{1,0:T(8,128)(2,1)S(1)}, u32[]{:S(2)}, u32[]{:S(2)}) %collective-permute-start.4) | collective-permute-done | bytes 65568 | tf_op jit(solution)/shard_map/ppermute | solution.py:477
  10.2 1.8 %shard_map.51 = (bf16[2,32,1280]{2,1,0:T(8,128)(2,1)S(1)}, bf16[2,32,1024]{2,1,0:T(8,128)(2,1)S(1)}, bf16[2,32,256]{2,1,0:T(8,128)(2,1)S(1)}, bf16[32,1024]{1,0:T(8,128)(2,1)S(1)}) custom-call(bf16[1024,256]{1,0:T(8,128)(2,1)S(1)} %get-tuple-element.58.refs_0_, bf16[1024,256]{1,0:T(8,128)(2,1)S(1)} %get-tuple-element.59.expand_own.refs_1_, ...), custom_call_target="tpu_custom_call" | custom-call | flops 134217728 | bytes 2097152 | tf_op jit(solution)/shard_map/pallas_call | solution.py:281
  12.0 2.0 %collective-permute-start.6 = (bf16[32,1024]{1,0:T(8,128)(2,1)S(1)}, bf16[32,1024]{1,0:T(8,128)(2,1)S(1)}, u32[]{:S(2)}, u32[]{:S(2)}) collective-permute-start(bf16[32,1024]{1,0:T(8,128)(2,1)S(1)} %get-tuple-element.65), channel_id=1, source_target_pairs={{0,16},{16,0},{8,24},{24,8},{1,17},{17,1},{9,25},{25,9},{2,18},{18... | collective-permute-start | bytes 196616 | tf_op jit(solution)/shard_map/ppermute | solution.py:477
  14.0 0.1 collective-permute-start.5
  14.2 0.2 collective-permute-start.10
  14.3 2.1 %collective-permute-done.6.refs_4_ = bf16[32,1024]{1,0:T(8,128)(2,1)S(1)} collective-permute-done((bf16[32,1024]{1,0:T(8,128)(2,1)S(1)}, bf16[32,1024]{1,0:T(8,128)(2,1)S(1)}, u32[]{:S(2)}, u32[]{:S(2)}) %collective-permute-start.6) | collective-permute-done | bytes 65568 | tf_op jit(solution)/shard_map/ppermute | solution.py:477
  16.4 0.6 %shard_map.52 = (bf16[2,32,1024]{2,1,0:T(8,128)(2,1)S(1)}, bf16[2,32,256]{2,1,0:T(8,128)(2,1)S(1)}) custom-call(bf16[1024,256]{1,0:T(8,128)(2,1)S(1)} %get-tuple-element.51.own.refs_0_, bf16[1024,256]{1,0:T(8,128)(2,1)S(1)} %get-tuple-element.52.refs_1_.own, bf16[1024,256]{1,0:T(8,128)(2,1)S(1)} %collective-permute-done.other.refs_2_, ...), custom_call_target="tpu_custom_call" | custom-call | flops 67108864 | bytes 2097152 | tf_op jit(solution)/shard_map/pallas_call | solution.py:281
  17.0 0.2 shard_map.53.refs_6_
  17.3 0.1 collective-permute-start.8
  17.4 2.5 %collective-permute-start.12 = (bf16[2,32,256]{2,1,0:T(8,128)(2,1)S(1)}, bf16[2,32,256]{2,1,0:T(8,128)(2,1)S(1)}, u32[]{:S(2)}, u32[]{:S(2)}) collective-permute-start(bf16[2,32,256]{2,1,0:T(8,128)(2,1)S(1)} %broadcast_select_fusion.7), channel_id=1, source_target_pairs={{0,16},{8,24},{16,0},{24,8},{1,17},{9,25},{17,1},{25,9},{2,18},{10... | collective-permute-start | bytes 98312 | tf_op jit(solution)/shard_map/ppermute | solution.py:483
  20.0 0.2 collective-permute-start.7
  20.1 1.8 %collective-permute-done.12 = bf16[2,32,256]{2,1,0:T(8,128)(2,1)S(1)} collective-permute-done((bf16[2,32,256]{2,1,0:T(8,128)(2,1)S(1)}, bf16[2,32,256]{2,1,0:T(8,128)(2,1)S(1)}, u32[]{:S(2)}, u32[]{:S(2)}) %collective-permute-start.12) | collective-permute-done | bytes 32800 | tf_op jit(solution)/shard_map/ppermute | solution.py:483
  21.9 1.9 %collective-permute-start.17 = (bf16[32,1024]{1,0:T(8,128)(2,1)S(1)}, bf16[32,1024]{1,0:T(8,128)(2,1)S(1)}, u32[]{:S(2)}, u32[]{:S(2)}) collective-permute-start(bf16[32,1024]{1,0:T(8,128)(2,1)S(1)} %fusion.1), channel_id=1, source_target_pairs={{0,16},{8,24},{16,0},{24,8},{1,17},{9,25},{17,1},{25,9},{2,18},{10... | collective-permute-start | bytes 196616 | tf_op jit(solution)/shard_map/ppermute | solution.py:483
  23.9 0.0 collective-permute-done.10
  23.9 0.0 collective-permute-start.13
  23.9 2.3 %collective-permute-done.17 = bf16[32,1024]{1,0:T(8,128)(2,1)S(1)} collective-permute-done((bf16[32,1024]{1,0:T(8,128)(2,1)S(1)}, bf16[32,1024]{1,0:T(8,128)(2,1)S(1)}, u32[]{:S(2)}, u32[]{:S(2)}) %collective-permute-start.17) | collective-permute-done | bytes 65568 | tf_op jit(solution)/shard_map/ppermute | solution.py:483
  26.2 0.0 collective-permute-start.11
  26.2 0.6 %collective-permute-start.18 = (bf16[32,1024]{1,0:T(8,128)(2,1)S(1)}, bf16[32,1024]{1,0:T(8,128)(2,1)S(1)}, u32[]{:S(2)}, u32[]{:S(2)}) collective-permute-start(bf16[32,1024]{1,0:T(8,128)(2,1)S(1)} %get-tuple-element.95), channel_id=1, source_target_pairs={{0,8},{8,0},{16,24},{24,16},{1,9},{9,1},{17,25},{25,17},{2,10},{10... | collective-permute-start | bytes 196616 | tf_op jit(solution)/shard_map/ppermute | solution.py:480
  26.8 0.1 shard_map.54
  26.9 1.4 %collective-permute-start.9 = (bf16[64,1536]{1,0:T(8,128)(2,1)S(1)}, bf16[64,1536]{1,0:T(8,128)(2,1)S(1)}, u32[]{:S(2)}, u32[]{:S(2)}) collective-permute-start(bf16[64,1536]{1,0:T(8,128)(2,1)S(1)} %get-tuple-element.74), channel_id=1, source_target_pairs={{0,1},{1,0},{2,3},{3,2},{4,5},{5,4},{6,7},{7,6},{8,10},{9,11},{10,... | collective-permute-start | bytes 589832 | tf_op jit(solution)/shard_map/ppermute | solution.py:624
  28.3 0.1 shard_map.58
  28.4 0.8 %collective-permute-start.19 = (bf16[64,768]{1,0:T(8,128)(2,1)S(1)}, bf16[64,768]{1,0:T(8,128)(2,1)S(1)}, u32[]{:S(2)}, u32[]{:S(2)}) collective-permute-start(bf16[64,768]{1,0:T(8,128)(2,1)S(1)} %get-tuple-element.90), channel_id=1, source_target_pairs={{0,1},{1,0},{2,3},{3,2},{4,5},{5,4},{6,7},{7,6},{8,10},{9,11},{10,... | collective-permute-start | bytes 294920 | tf_op jit(solution)/shard_map/ppermute | solution.py:624
  29.2 1.4 %collective-permute-start.14 = (bf16[64,768]{1,0:T(8,128)(2,1)S(1)}, bf16[64,768]{1,0:T(8,128)(2,1)S(1)}, u32[]{:S(2)}, u32[]{:S(2)}) collective-permute-start(bf16[64,768]{1,0:T(8,128)(2,1)S(1)} %get-tuple-element.80), channel_id=1, source_target_pairs={{0,1},{1,0},{2,3},{3,2},{4,5},{5,4},{6,7},{7,6},{8,10},{9,11},{10,... | collective-permute-start | bytes 294920 | tf_op jit(solution)/shard_map/ppermute | solution.py:624
  30.6 3.1 %collective-permute-done.19.refs_5_ = bf16[64,768]{1,0:T(8,128)(2,1)S(1)} collective-permute-done((bf16[64,768]{1,0:T(8,128)(2,1)S(1)}, bf16[64,768]{1,0:T(8,128)(2,1)S(1)}, u32[]{:S(2)}, u32[]{:S(2)}) %collective-permute-start.19) | collective-permute-done | bytes 98336 | tf_op jit(solution)/shard_map/ppermute | solution.py:624
  33.7 0.3 shard_map.59
  34.1 1.4 %collective-permute-start.20 = (bf16[2,128,256]{2,1,0:T(8,128)(2,1)S(1)}, bf16[2,128,256]{2,1,0:T(8,128)(2,1)S(1)}, u32[]{:S(2)}, u32[]{:S(2)}) collective-permute-start(bf16[2,128,256]{2,1,0:T(8,128)(2,1)S(1)} %get-tuple-element.92), channel_id=1, source_target_pairs={{0,2},{1,3},{2,0},{3,1},{4,6},{5,7},{6,4},{7,5},{8,9},{9,8},{10,11... | collective-permute-start | bytes 393224 | tf_op jit(solution)/shard_map/ppermute | solution.py:624
  35.5 0.3 shard_map.56
  35.8 0.7 %collective-permute-start.15 = (bf16[2,128,256]{2,1,0:T(8,128)(2,1)S(1)}, bf16[2,128,256]{2,1,0:T(8,128)(2,1)S(1)}, u32[]{:S(2)}, u32[]{:S(2)}) collective-permute-start(bf16[2,128,256]{2,1,0:T(8,128)(2,1)S(1)} %get-tuple-element.82), channel_id=1, source_target_pairs={{0,2},{1,3},{2,0},{3,1},{4,6},{5,7},{6,4},{7,5},{8,9},{9,8},{10,11... | collective-permute-start | bytes 393224 | tf_op jit(solution)/shard_map/ppermute | solution.py:624
  36.6 2.5 %collective-permute-done.20.came = bf16[2,128,256]{2,1,0:T(8,128)(2,1)S(1)} collective-permute-done((bf16[2,128,256]{2,1,0:T(8,128)(2,1)S(1)}, bf16[2,128,256]{2,1,0:T(8,128)(2,1)S(1)}, u32[]{:S(2)}, u32[]{:S(2)}) %collective-permute-start.20) | collective-permute-done | bytes 131104 | tf_op jit(solution)/shard_map/ppermute | solution.py:624
  39.1 2.4 %collective-permute-start.21 = (bf16[1,128,256]{2,1,0:T(8,128)(2,1)S(1)}, bf16[1,128,256]{2,1,0:T(8,128)(2,1)S(1)}, u32[]{:S(2)}, u32[]{:S(2)}) collective-permute-start(bf16[1,128,256]{2,1,0:T(8,128)(2,1)S(1)} %get-tuple-element.94), channel_id=1, source_target_pairs={{0,4},{1,5},{2,6},{3,7},{4,0},{5,1},{6,2},{7,3},{8,12},{9,13},{10,... | collective-permute-start | bytes 196616 | tf_op jit(solution)/shard_map/ppermute | solution.py:624
  41.6 0.0 collective-permute-done.15.came
  41.6 2.6 %collective-permute-start.16 = (bf16[1,128,256]{2,1,0:T(8,128)(2,1)S(1)}, bf16[1,128,256]{2,1,0:T(8,128)(2,1)S(1)}, u32[]{:S(2)}, u32[]{:S(2)}) collective-permute-start(bf16[1,128,256]{2,1,0:T(8,128)(2,1)S(1)} %get-tuple-element.84), channel_id=1, source_target_pairs={{0,4},{1,5},{2,6},{3,7},{4,0},{5,1},{6,2},{7,3},{8,12},{9,13},{10,... | collective-permute-start | bytes 196616 | tf_op jit(solution)/shard_map/ppermute | solution.py:624
  44.3 1.5 %collective-permute-done.21.came_expand = bf16[1,128,256]{2,1,0:T(8,128)(2,1)S(1)} collective-permute-done((bf16[1,128,256]{2,1,0:T(8,128)(2,1)S(1)}, bf16[1,128,256]{2,1,0:T(8,128)(2,1)S(1)}, u32[]{:S(2)}, u32[]{:S(2)}) %collective-permute-start.21) | collective-permute-done | bytes 65568 | tf_op jit(solution)/shard_map/ppermute | solution.py:624
  45.8 1.1 %collective-permute-done.16.came_reduce = bf16[1,128,256]{2,1,0:T(8,128)(2,1)S(1)} collective-permute-done((bf16[1,128,256]{2,1,0:T(8,128)(2,1)S(1)}, bf16[1,128,256]{2,1,0:T(8,128)(2,1)S(1)}, u32[]{:S(2)}, u32[]{:S(2)}) %collective-permute-start.16) | collective-permute-done | bytes 65568 | tf_op jit(solution)/shard_map/ppermute | solution.py:624
  46.8 0.7 %shard_map.61 = f32[1,2,128,256]{3,2,1,0:T(8,128)} custom-call(f32[1,128,256]{2,1,0:T(8,128)S(1)} %get-tuple-element.83.keep_reduce, bf16[1,128,256]{2,1,0:T(8,128)(2,1)S(1)} %collective-permute-done.16.came_reduce, f32[1,128,256]{2,1,0:T(8,128)S(1)} %get-tuple-element.93.keep_expand, bf16[1,128,256]{2,1,0:T(8,128)(2,1)S(1)} %collective-permute-done.21.came_expand), custom_call_target="tpu_custom_call" | custom-call | tf_op jit(solution)/shard_map/pallas_call | solution.py:603
  (28 shorter events, 0.3 us)
Async XLA Ops:
  1.2 2.4 %collective-permute-start = (bf16[1024,256]{1,0:T(8,128)(2,1)S(1)}, bf16[1024,256]{1,0:T(8,128)(2,1)S(1)}, u32[]{:S(2)}, u32[]{:S(2)}) collective-permute-start(bf16[1024,256]{1,0:T(8,128)(2,1)S(1)} %get-tuple-element.51.own.refs_0_), channel_id=1, source_target_pairs={{0,8},{8,0},{16,24},{24,16},{1,9},{9,1},{17,25},{25,17},{2,10},{10... | collective-permute-start | bytes 1572872 | tf_op jit(solution)/shard_map/ppermute | solution.py:480
  1.8 2.3 %collective-permute-start.1 = (bf16[1024,256]{1,0:T(8,128)(2,1)S(1)}, bf16[1024,256]{1,0:T(8,128)(2,1)S(1)}, u32[]{:S(2)}, u32[]{:S(2)}) collective-permute-start(bf16[1024,256]{1,0:T(8,128)(2,1)S(1)} %get-tuple-element.52.refs_1_.own), channel_id=1, source_target_pairs={{0,8},{8,0},{16,24},{24,16},{1,9},{9,1},{17,25},{25,17},{2,10},{10... | collective-permute-start | bytes 1572872 | tf_op jit(solution)/shard_map/ppermute | solution.py:480
  3.1 4.7 %collective-permute-start.3 = (bf16[1024,256]{1,0:T(8,128)(2,1)S(1)}, bf16[1024,256]{1,0:T(8,128)(2,1)S(1)}, u32[]{:S(2)}, u32[]{:S(2)}) collective-permute-start(bf16[1024,256]{1,0:T(8,128)(2,1)S(1)} %get-tuple-element.59.expand_own.refs_1_), channel_id=1, source_target_pairs={{0,8},{8,0},{16,24},{24,16},{1,9},{9,1},{17,25},{25,17},{2,10},{10... | collective-permute-start | bytes 1572872 | tf_op jit(solution)/shard_map/ppermute | solution.py:480
  3.6 5.4 %collective-permute-start.2 = (bf16[1024,256]{1,0:T(8,128)(2,1)S(1)}, bf16[1024,256]{1,0:T(8,128)(2,1)S(1)}, u32[]{:S(2)}, u32[]{:S(2)}) collective-permute-start(bf16[1024,256]{1,0:T(8,128)(2,1)S(1)} %get-tuple-element.58.refs_0_), channel_id=1, source_target_pairs={{0,8},{8,0},{16,24},{24,16},{1,9},{9,1},{17,25},{25,17},{2,10},{10... | collective-permute-start | bytes 1572872 | tf_op jit(solution)/shard_map/ppermute | solution.py:480
  4.9 5.3 %collective-permute-start.4 = (bf16[32,1024]{1,0:T(8,128)(2,1)S(1)}, bf16[32,1024]{1,0:T(8,128)(2,1)S(1)}, u32[]{:S(2)}, u32[]{:S(2)}) collective-permute-start(bf16[32,1024]{1,0:T(8,128)(2,1)S(1)} %get-tuple-element.60.leave), channel_id=1, source_target_pairs={{0,16},{16,0},{8,24},{24,8},{1,17},{17,1},{9,25},{25,9},{2,18},{18... | collective-permute-start | bytes 196616 | tf_op jit(solution)/shard_map/ppermute | solution.py:477
  12.0 4.4 %collective-permute-start.6 = (bf16[32,1024]{1,0:T(8,128)(2,1)S(1)}, bf16[32,1024]{1,0:T(8,128)(2,1)S(1)}, u32[]{:S(2)}, u32[]{:S(2)}) collective-permute-start(bf16[32,1024]{1,0:T(8,128)(2,1)S(1)} %get-tuple-element.65), channel_id=1, source_target_pairs={{0,16},{16,0},{8,24},{24,8},{1,17},{17,1},{9,25},{25,9},{2,18},{18... | collective-permute-start | bytes 196616 | tf_op jit(solution)/shard_map/ppermute | solution.py:477
  14.0 12.8 %collective-permute-start.5 = (bf16[32,1280]{1,0:T(8,128)(2,1)S(1)}, bf16[32,1280]{1,0:T(8,128)(2,1)S(1)}, u32[]{:S(2)}, u32[]{:S(2)}) collective-permute-start(bf16[32,1280]{1,0:T(8,128)(2,1)S(1)} %fusion), channel_id=1, source_target_pairs={{0,8},{8,0},{16,24},{24,16},{1,9},{9,1},{17,25},{25,17},{2,10},{10... | collective-permute-start | bytes 245768 | tf_op jit(solution)/shard_map/ppermute | solution.py:480
  14.2 9.7 %collective-permute-start.10 = (bf16[32,1536]{1,0:T(8,128)(2,1)S(1)}, bf16[32,1536]{1,0:T(8,128)(2,1)S(1)}, u32[]{:S(2)}, u32[]{:S(2)}) collective-permute-start(bf16[32,1536]{1,0:T(8,128)(2,1)S(1)} %pad_maximum_fusion), channel_id=1, source_target_pairs={{0,16},{8,24},{16,0},{24,8},{1,17},{9,25},{17,1},{25,9},{2,18},{10... | collective-permute-start | bytes 294920 | tf_op jit(solution)/shard_map/ppermute | solution.py:483
  17.3 8.9 %collective-permute-start.8 = (bf16[32,256]{1,0:T(8,128)(2,1)S(1)}, bf16[32,256]{1,0:T(8,128)(2,1)S(1)}, u32[]{:S(2)}, u32[]{:S(2)}) collective-permute-start(bf16[32,256]{1,0:T(8,128)(2,1)S(1)} %fusion.4), channel_id=1, source_target_pairs={{0,8},{8,0},{16,24},{24,16},{1,9},{9,1},{17,25},{25,17},{2,10},{10... | collective-permute-start | bytes 49160 | tf_op jit(solution)/shard_map/ppermute | solution.py:480
  17.4 4.5 %collective-permute-start.12 = (bf16[2,32,256]{2,1,0:T(8,128)(2,1)S(1)}, bf16[2,32,256]{2,1,0:T(8,128)(2,1)S(1)}, u32[]{:S(2)}, u32[]{:S(2)}) collective-permute-start(bf16[2,32,256]{2,1,0:T(8,128)(2,1)S(1)} %broadcast_select_fusion.7), channel_id=1, source_target_pairs={{0,16},{8,24},{16,0},{24,8},{1,17},{9,25},{17,1},{25,9},{2,18},{10... | collective-permute-start | bytes 98312 | tf_op jit(solution)/shard_map/ppermute | solution.py:483
  20.0 6.9 %collective-permute-start.7 = (bf16[32,1024]{1,0:T(8,128)(2,1)S(1)}, bf16[32,1024]{1,0:T(8,128)(2,1)S(1)}, u32[]{:S(2)}, u32[]{:S(2)}) collective-permute-start(bf16[32,1024]{1,0:T(8,128)(2,1)S(1)} %fusion.3), channel_id=1, source_target_pairs={{0,8},{8,0},{16,24},{24,16},{1,9},{9,1},{17,25},{25,17},{2,10},{10... | collective-permute-start | bytes 196616 | tf_op jit(solution)/shard_map/ppermute | solution.py:480
  21.9 4.3 %collective-permute-start.17 = (bf16[32,1024]{1,0:T(8,128)(2,1)S(1)}, bf16[32,1024]{1,0:T(8,128)(2,1)S(1)}, u32[]{:S(2)}, u32[]{:S(2)}) collective-permute-start(bf16[32,1024]{1,0:T(8,128)(2,1)S(1)} %fusion.1), channel_id=1, source_target_pairs={{0,16},{8,24},{16,0},{24,8},{1,17},{9,25},{17,1},{25,9},{2,18},{10... | collective-permute-start | bytes 196616 | tf_op jit(solution)/shard_map/ppermute | solution.py:483
  23.9 5.3 %collective-permute-start.13 = (bf16[32,256]{1,0:T(8,128)(2,1)S(1)}, bf16[32,256]{1,0:T(8,128)(2,1)S(1)}, u32[]{:S(2)}, u32[]{:S(2)}) collective-permute-start(bf16[32,256]{1,0:T(8,128)(2,1)S(1)} %get-tuple-element.103), channel_id=1, source_target_pairs={{0,8},{8,0},{16,24},{24,16},{1,9},{9,1},{17,25},{25,17},{2,10},{10... | collective-permute-start | bytes 49160 | tf_op jit(solution)/shard_map/ppermute | solution.py:480
  26.2 2.1 %collective-permute-start.11 = (bf16[32,1280]{1,0:T(8,128)(2,1)S(1)}, bf16[32,1280]{1,0:T(8,128)(2,1)S(1)}, u32[]{:S(2)}, u32[]{:S(2)}) collective-permute-start(bf16[32,1280]{1,0:T(8,128)(2,1)S(1)} %pad_maximum_fusion.2), channel_id=1, source_target_pairs={{0,8},{8,0},{16,24},{24,16},{1,9},{9,1},{17,25},{25,17},{2,10},{10... | collective-permute-start | bytes 245768 | tf_op jit(solution)/shard_map/ppermute | solution.py:480
  26.2 2.1 %collective-permute-start.18 = (bf16[32,1024]{1,0:T(8,128)(2,1)S(1)}, bf16[32,1024]{1,0:T(8,128)(2,1)S(1)}, u32[]{:S(2)}, u32[]{:S(2)}) collective-permute-start(bf16[32,1024]{1,0:T(8,128)(2,1)S(1)} %get-tuple-element.95), channel_id=1, source_target_pairs={{0,8},{8,0},{16,24},{24,16},{1,9},{9,1},{17,25},{25,17},{2,10},{10... | collective-permute-start | bytes 196616 | tf_op jit(solution)/shard_map/ppermute | solution.py:480
  26.9 6.8 %collective-permute-start.9 = (bf16[64,1536]{1,0:T(8,128)(2,1)S(1)}, bf16[64,1536]{1,0:T(8,128)(2,1)S(1)}, u32[]{:S(2)}, u32[]{:S(2)}) collective-permute-start(bf16[64,1536]{1,0:T(8,128)(2,1)S(1)} %get-tuple-element.74), channel_id=1, source_target_pairs={{0,1},{1,0},{2,3},{3,2},{4,5},{5,4},{6,7},{7,6},{8,10},{9,11},{10,... | collective-permute-start | bytes 589832 | tf_op jit(solution)/shard_map/ppermute | solution.py:624
  28.4 5.3 %collective-permute-start.19 = (bf16[64,768]{1,0:T(8,128)(2,1)S(1)}, bf16[64,768]{1,0:T(8,128)(2,1)S(1)}, u32[]{:S(2)}, u32[]{:S(2)}) collective-permute-start(bf16[64,768]{1,0:T(8,128)(2,1)S(1)} %get-tuple-element.90), channel_id=1, source_target_pairs={{0,1},{1,0},{2,3},{3,2},{4,5},{5,4},{6,7},{7,6},{8,10},{9,11},{10,... | collective-permute-start | bytes 294920 | tf_op jit(solution)/shard_map/ppermute | solution.py:624
  29.2 6.3 %collective-permute-start.14 = (bf16[64,768]{1,0:T(8,128)(2,1)S(1)}, bf16[64,768]{1,0:T(8,128)(2,1)S(1)}, u32[]{:S(2)}, u32[]{:S(2)}) collective-permute-start(bf16[64,768]{1,0:T(8,128)(2,1)S(1)} %get-tuple-element.80), channel_id=1, source_target_pairs={{0,1},{1,0},{2,3},{3,2},{4,5},{5,4},{6,7},{7,6},{8,10},{9,11},{10,... | collective-permute-start | bytes 294920 | tf_op jit(solution)/shard_map/ppermute | solution.py:624
  34.1 5.0 %collective-permute-start.20 = (bf16[2,128,256]{2,1,0:T(8,128)(2,1)S(1)}, bf16[2,128,256]{2,1,0:T(8,128)(2,1)S(1)}, u32[]{:S(2)}, u32[]{:S(2)}) collective-permute-start(bf16[2,128,256]{2,1,0:T(8,128)(2,1)S(1)} %get-tuple-element.92), channel_id=1, source_target_pairs={{0,2},{1,3},{2,0},{3,1},{4,6},{5,7},{6,4},{7,5},{8,9},{9,8},{10,11... | collective-permute-start | bytes 393224 | tf_op jit(solution)/shard_map/ppermute | solution.py:624
  35.8 5.7 %collective-permute-start.15 = (bf16[2,128,256]{2,1,0:T(8,128)(2,1)S(1)}, bf16[2,128,256]{2,1,0:T(8,128)(2,1)S(1)}, u32[]{:S(2)}, u32[]{:S(2)}) collective-permute-start(bf16[2,128,256]{2,1,0:T(8,128)(2,1)S(1)} %get-tuple-element.82), channel_id=1, source_target_pairs={{0,2},{1,3},{2,0},{3,1},{4,6},{5,7},{6,4},{7,5},{8,9},{9,8},{10,11... | collective-permute-start | bytes 393224 | tf_op jit(solution)/shard_map/ppermute | solution.py:624
  39.1 6.6 %collective-permute-start.21 = (bf16[1,128,256]{2,1,0:T(8,128)(2,1)S(1)}, bf16[1,128,256]{2,1,0:T(8,128)(2,1)S(1)}, u32[]{:S(2)}, u32[]{:S(2)}) collective-permute-start(bf16[1,128,256]{2,1,0:T(8,128)(2,1)S(1)} %get-tuple-element.94), channel_id=1, source_target_pairs={{0,4},{1,5},{2,6},{3,7},{4,0},{5,1},{6,2},{7,3},{8,12},{9,13},{10,... | collective-permute-start | bytes 196616 | tf_op jit(solution)/shard_map/ppermute | solution.py:624
  41.6 5.2 %collective-permute-start.16 = (bf16[1,128,256]{2,1,0:T(8,128)(2,1)S(1)}, bf16[1,128,256]{2,1,0:T(8,128)(2,1)S(1)}, u32[]{:S(2)}, u32[]{:S(2)}) collective-permute-start(bf16[1,128,256]{2,1,0:T(8,128)(2,1)S(1)} %get-tuple-element.84), channel_id=1, source_target_pairs={{0,4},{1,5},{2,6},{3,7},{4,0},{5,1},{6,2},{7,3},{8,12},{9,13},{10,... | collective-permute-start | bytes 196616 | tf_op jit(solution)/shard_map/ppermute | solution.py:624

commit v8 on v7

--- a/solution.py
+++ b/solution.py
@@ -362,17 +362,33 @@
     return lax.rem(lax.div(value, 1 << bit), 2)
 
 
-def first_sides():
+BITS = ((0, 1, 2), (1, 2, 0))
+
+
+def split_bits(at):
+    return tuple(bits[at] if at < len(bits) else at for bits in BITS)
+
+
+def side_at(at):
     core, shard = lax.rem(lax.axis_index("pipe"), 2), lax.axis_index("dp")
-    low, high = bit_of(shard, 0), bit_of(shard, 1)
-    return core, jnp.where(core == 0, low, high), jnp.where(core == 0, high, low)
+    first, second = split_bits(at)
+    return core, jnp.where(core == 0, bit_of(shard, first), bit_of(shard, second))
+
+
+def chunk_of(core, side, place):
+    chunks = [0, 0]
+    for at in range(1, 2 + place.bit_length()):
+        for which, bit in enumerate(split_bits(at)):
+            chunks[which] |= (place >> (at - 1) & 1) << bit
+    first, second = split_bits(0)
+    return jnp.where(core == 0, chunks[0] + side * (1 << first), chunks[1] + side * (1 << second))
 
 
 def split_columns(wide, keep, send, chunk):
-    core, side, _ = first_sides()
+    core, side = side_at(0)
     for place in range(wide.shape[1] // (2 * chunk)):
         for target, at in ((keep, side), (send, 1 - side)):
-            block = jnp.where(core == 0, 2 * place + at, place // 2 * 4 + 2 * at + place % 2)
+            block = chunk_of(core, at, place)
             source = pl.ds(pl.multiple_of(block * chunk, chunk), chunk)
             target[:, place * chunk : (place + 1) * chunk] = wide[:, source]
 
@@ -433,7 +449,7 @@
         right[start : start + rows] = came[:, offset + columns : offset + width]
         start += rows
     full[...] = contract(left[...], right[...], 0, 0)
-    _, _, side = first_sides()
+    _, side = side_at(1)
     chunk = send.shape[1]
     for place in range(send.shape[0]):
         theirs = pl.ds(pl.multiple_of((2 * place + 1 - side) * chunk, chunk), chunk)
@@ -442,17 +458,32 @@
         keep[place] = full[mine]
 
 
-def next_body(bit, keep_in, came, send, keep):
-    side = bit_of(lax.axis_index("dp"), bit)
+def next_body(at, keep_in, came, send, keep):
+    _, side = side_at(at)
     for place in range(keep.shape[0]):
         theirs, mine = 2 * place + 1 - side, 2 * place + side
         send[place] = (keep_in[theirs] + came[theirs].astype(jnp.float32)).astype(jnp.bfloat16)
         keep[place] = keep_in[mine] + came[mine].astype(jnp.float32)
 
 
-def finish_body(keep_reduce, came_reduce, keep_expand, came_expand, out):
-    out[0, 0] = keep_reduce[0] + came_reduce[0].astype(jnp.float32)
-    out[0, 1] = keep_expand[0] + came_expand[0].astype(jnp.float32)
+def finish_body(which, keep, came, *refs):
+    out, held, sem = refs[-3:]
+    held[...] = keep[0] + came[0].astype(jnp.float32)
+    copy = pltpu.make_async_copy(held, out.at[0, which], sem)
+    copy.start()
+    copy.wait()
+
+
+def finish(which, keep, came, *out):
+    return pl.pallas_call(
+        functools.partial(finish_body, which),
+        out_shape=jax.ShapeDtypeStruct((1, 2) + keep.shape[1:], jnp.float32),
+        in_specs=[VMEM] * 2 + [HBM] * len(out),
+        out_specs=HBM,
+        scratch_shapes=[pltpu.VMEM(keep.shape[1:], jnp.float32), pltpu.SemaphoreType.DMA],
+        input_output_aliases={2: 0} if out else {},
+        compiler_params=PARAMS,
+    )(keep, came, *out)
 
 
 def shards(inputs, cotangent, reduce_weight, expand_weight):
@@ -598,15 +629,9 @@
     fore = flows + [side_flow, far_flow, cross_flow]
     ups = upstreams + [side_up, far_up, cross_up]
     backs = back_inners + [side_inner, far_inner, cross_inner]
-    halve = halve_rows if chunk % 128 == 0 and replicas >= 4 else halve_sums
-    parts = halve(stages, replicas, chunk, sizes, rows, fore, ups, backs)
-    return pl.pallas_call(
-        finish_body,
-        out_shape=jax.ShapeDtypeStruct((1, 2, chunk, inner), jnp.float32),
-        in_specs=[VMEM] * 4,
-        out_specs=VMEM,
-        compiler_params=PARAMS,
-    )(*parts)
+    halve = halve_rows if chunk % 128 == 0 and replicas >= 8 else halve_sums
+    keep, came, keep_up, came_up = halve(stages, replicas, chunk, sizes, rows, fore, ups, backs)
+    return finish(0, keep, came, finish(1, keep_up, came_up))
 
 
 def sums(count, chunk, inner):
@@ -616,8 +641,9 @@
     ]
 
 
-def exchange(shard, stages, replicas, first, second):
+def exchange(shard, stages, replicas, at):
     pairs = []
+    first, second = (1 << bit for bit in split_bits(at))
     for p in range(2 * stages):
         for q in range(replicas):
             pairs.append((p * replicas + q, p * replicas + (q ^ (second if p % 2 else first))))
@@ -661,11 +687,11 @@
         scratch_shapes=[pltpu.VMEM((2 * rows, channels), jnp.bfloat16)],
         compiler_params=PARAMS,
     )(*near)
-    came_near = exchange(send, stages, replicas, 1, 2)
+    came_near = exchange(send, stages, replicas, 0)
     parts = []
     for at, name, late in ((1, "inner", backs), (0, "up", ups)):
         left, right, send = pack(late, name == "up", False, True)
-        came = exchange(send, stages, replicas, 1, 2)
+        came = exchange(send, stages, replicas, 0)
         operands = (kept[2 * at], kept[2 * at + 1], came_near, left, right, came)
         count = replicas // 4
         send, keep = pl.pallas_call(
@@ -680,17 +706,17 @@
             ],
             compiler_params=PARAMS,
         )(*operands)
-        came = exchange(send, stages, replicas, 2, 1)
-        for bit in range(2, replicas.bit_length() - 1):
+        came = exchange(send, stages, replicas, 1)
+        for at in range(2, replicas.bit_length() - 1):
             count //= 2
             send, keep = pl.pallas_call(
-                functools.partial(next_body, bit),
+                functools.partial(next_body, at),
                 out_shape=sums(count, chunk, inner),
                 in_specs=[VMEM] * 2,
                 out_specs=[VMEM] * 2,
                 compiler_params=PARAMS,
             )(keep, came)
-            came = exchange(send, stages, replicas, 1 << bit, 1 << bit)
+            came = exchange(send, stages, replicas, at)
         parts += [keep, came]
     return parts
 

time: 47.8 us -> 48.6 us (1.017)
  Pallas kernels: 9.11 us -> 9.74 us
    pallas_call x3 -> x4, Pallas kernels: 0.77 us -> 1.4 us  [the longest x2 1.35 us: finish(): pl.pallas_call(functools.partial(finish_body, which), out_shape=jax.Shape...]
  transfers between devices with their start and end apart: 22 -> 22, of which waited for: 9 -> 9; matrix products, arithmetic and copies ran while one was open for 0% -> 0% of each run, Pallas kernels for 11% -> 12%
where the time goes in v8:
time: 48.6 us; the launch traced here: 48.4 us
  starting transfers between devices  22.3 us (46%)
  waiting for transfers between devices  15.9 us (33%)
  Pallas kernels  9.74 us (20%)
    ppermute x7, starting transfers between devices, exchange(): return lax.ppermute(shard, AXES, pairs)  10.7 us
    ppermute x7, waiting for transfers between devices, exchange(): return lax.ppermute(shard, AXES, pairs)  8.5 us
    ppermute x2, starting transfers between devices, hop(): return lax.ppermute(shard, 'pipe', pairs)  4.86 us
    ppermute x3, starting transfers between devices, mirror(): return lax.ppermute(shard, 'pipe', mirror_pairs)  4.67 us
    ppermute x3, waiting for transfers between devices, mirror(): return lax.ppermute(shard, 'pipe', mirror_pairs)  4.09 us
    pallas_call x3, Pallas kernels, run_stage(): pl.pallas_call(functools.partial(stage_body, step, forward, backward, las...  3.26 us
    ppermute x2, waiting for transfers between devices, hop(): return lax.ppermute(shard, 'pipe', pairs)  3.23 us
    pallas_call x2, Pallas kernels, load(): pl.pallas_call(functools.partial(load_body, step), out_shape=outs, in_spe...  2.44 us
  transfers between devices with their start and end apart: 22, of which 9 were waited for; matrix products, arithmetic and copies ran while one was open for 0% of the time, Pallas kernels for 12%

profile of v8, /device:TPU:0, one launch (start us, length us, event | category | flops | bytes accessed | tf_op | source)
XLA Modules:
  0.0 48.4 jit_solution(3012345284316892850)
XLA Ops:
  0.0 1.2 %shard_map.46 = (bf16[1024,256]{1,0:T(8,128)(2,1)S(1)}, bf16[1024,256]{1,0:T(8,128)(2,1)S(1)}, bf16[32,1024]{1,0:T(8,128)(2,1)S(1)}) custom-call(bf16[2,1024,256]{2,1,0:T(8,128)(2,1)} %bitcast.20, bf16[2,1024,256]{2,1,0:T(8,128)(2,1)} %bitcast.22, bf16[2,2,32,1024]{3,2,1,0:T(8,128)(2,1)} %inputs), custom_call_target="tpu_custom_call" | custom-call | tf_op jit(solution)/shard_map/pallas_call | solution.py:68
  1.2 0.6 %collective-permute-start = (bf16[1024,256]{1,0:T(8,128)(2,1)S(1)}, bf16[1024,256]{1,0:T(8,128)(2,1)S(1)}, u32[]{:S(2)}, u32[]{:S(2)}) collective-permute-start(bf16[1024,256]{1,0:T(8,128)(2,1)S(1)} %get-tuple-element.51.own.refs_0_), channel_id=1, source_target_pairs={{0,8},{8,0},{16,24},{24,16},{1,9},{9,1},{17,25},{25,17},{2,10},{10... | collective-permute-start | bytes 1572872 | tf_op jit(solution)/shard_map/ppermute | solution.py:511
  1.8 0.1 collective-permute-start.1
  1.9 1.2 %shard_map.49 = (bf16[1024,256]{1,0:T(8,128)(2,1)S(1)}, bf16[1024,256]{1,0:T(8,128)(2,1)S(1)}) custom-call(bf16[2,1024,256]{2,1,0:T(8,128)(2,1)} %bitcast.21, bf16[2,1024,256]{2,1,0:T(8,128)(2,1)} %bitcast.23), custom_call_target="tpu_custom_call" | custom-call | tf_op jit(solution)/shard_map/pallas_call | solution.py:68
  3.1 0.5 %collective-permute-start.3 = (bf16[1024,256]{1,0:T(8,128)(2,1)S(1)}, bf16[1024,256]{1,0:T(8,128)(2,1)S(1)}, u32[]{:S(2)}, u32[]{:S(2)}) collective-permute-start(bf16[1024,256]{1,0:T(8,128)(2,1)S(1)} %get-tuple-element.59.expand_own.refs_1_), channel_id=1, source_target_pairs={{0,8},{8,0},{16,24},{24,16},{1,9},{9,1},{17,25},{25,17},{2,10},{10... | collective-permute-start | bytes 1572872 | tf_op jit(solution)/shard_map/ppermute | solution.py:511
  3.6 0.1 collective-permute-start.2
  3.7 0.3 shard_map.47
  4.0 0.1 collective-permute-done.1.refs_3_.other
  4.1 0.8 %shard_map.48 = (bf16[2,32,1280]{2,1,0:T(8,128)(2,1)S(1)}, bf16[32,1024]{1,0:T(8,128)(2,1)S(1)}, bf16[2,32,1024]{2,1,0:T(8,128)(2,1)S(1)}, f32[2,32,256]{2,1,0:T(8,128)S(1)}) custom-call(bf16[1024,256]{1,0:T(8,128)(2,1)S(1)} %get-tuple-element.51.own.refs_0_, bf16[1024,256]{1,0:T(8,128)(2,1)S(1)} %get-tuple-element.52.refs_1_.own, ...), custom_call_target="tpu_custom_call" | custom-call | flops 67108864 | bytes 2097152 | tf_op jit(solution)/shard_map/pallas_call | solution.py:281
  4.9 2.9 %collective-permute-start.4 = (bf16[32,1024]{1,0:T(8,128)(2,1)S(1)}, bf16[32,1024]{1,0:T(8,128)(2,1)S(1)}, u32[]{:S(2)}, u32[]{:S(2)}) collective-permute-start(bf16[32,1024]{1,0:T(8,128)(2,1)S(1)} %get-tuple-element.60.leave), channel_id=1, source_target_pairs={{0,16},{16,0},{8,24},{24,8},{1,17},{17,1},{9,25},{25,9},{2,18},{18... | collective-permute-start | bytes 196616 | tf_op jit(solution)/shard_map/ppermute | solution.py:508
  7.8 0.0 collective-permute-done.3.expand_other.refs_3_
  7.8 1.2 %shard_map.50 = (bf16[32,1024]{1,0:T(8,128)(2,1)S(1)}, f32[32,256]{1,0:T(8,128)S(1)}, bf16[32,1024]{1,0:T(8,128)(2,1)S(1)}, bf16[32,1024]{1,0:T(8,128)(2,1)S(1)}) custom-call(bf16[1024,256]{1,0:T(8,128)(2,1)S(1)} %get-tuple-element.59.expand_own.refs_1_, bf16[1024,256]{1,0:T(8,128)(2,1)S(1)} %collective-permute-done.3.expand_other.refs_3_, ...), custom_call_target="tpu_custom_call" | custom-call | tf_op jit(solution)/shard_map/pallas_call | solution.py:560
  9.0 0.0 collective-permute-done.2.refs_2_
  9.0 1.2 %collective-permute-done.4.refs_4_ = bf16[32,1024]{1,0:T(8,128)(2,1)S(1)} collective-permute-done((bf16[32,1024]{1,0:T(8,128)(2,1)S(1)}, bf16[32,1024]{1,0:T(8,128)(2,1)S(1)}, u32[]{:S(2)}, u32[]{:S(2)}) %collective-permute-start.4) | collective-permute-done | bytes 65568 | tf_op jit(solution)/shard_map/ppermute | solution.py:508
  10.2 1.8 %shard_map.51 = (bf16[2,32,1280]{2,1,0:T(8,128)(2,1)S(1)}, bf16[2,32,1024]{2,1,0:T(8,128)(2,1)S(1)}, bf16[2,32,256]{2,1,0:T(8,128)(2,1)S(1)}, bf16[32,1024]{1,0:T(8,128)(2,1)S(1)}) custom-call(bf16[1024,256]{1,0:T(8,128)(2,1)S(1)} %get-tuple-element.58.refs_0_, bf16[1024,256]{1,0:T(8,128)(2,1)S(1)} %get-tuple-element.59.expand_own.refs_1_, ...), custom_call_target="tpu_custom_call" | custom-call | flops 134217728 | bytes 2097152 | tf_op jit(solution)/shard_map/pallas_call | solution.py:281
  12.0 2.0 %collective-permute-start.6 = (bf16[32,1024]{1,0:T(8,128)(2,1)S(1)}, bf16[32,1024]{1,0:T(8,128)(2,1)S(1)}, u32[]{:S(2)}, u32[]{:S(2)}) collective-permute-start(bf16[32,1024]{1,0:T(8,128)(2,1)S(1)} %get-tuple-element.65), channel_id=1, source_target_pairs={{0,16},{16,0},{8,24},{24,8},{1,17},{17,1},{9,25},{25,9},{2,18},{18... | collective-permute-start | bytes 196616 | tf_op jit(solution)/shard_map/ppermute | solution.py:508
  14.0 0.1 collective-permute-start.5
  14.2 0.2 collective-permute-start.10
  14.3 2.1 %collective-permute-done.6.refs_4_ = bf16[32,1024]{1,0:T(8,128)(2,1)S(1)} collective-permute-done((bf16[32,1024]{1,0:T(8,128)(2,1)S(1)}, bf16[32,1024]{1,0:T(8,128)(2,1)S(1)}, u32[]{:S(2)}, u32[]{:S(2)}) %collective-permute-start.6) | collective-permute-done | bytes 65568 | tf_op jit(solution)/shard_map/ppermute | solution.py:508
  16.4 0.6 %shard_map.52 = (bf16[2,32,1024]{2,1,0:T(8,128)(2,1)S(1)}, bf16[2,32,256]{2,1,0:T(8,128)(2,1)S(1)}) custom-call(bf16[1024,256]{1,0:T(8,128)(2,1)S(1)} %get-tuple-element.51.own.refs_0_, bf16[1024,256]{1,0:T(8,128)(2,1)S(1)} %get-tuple-element.52.refs_1_.own, bf16[1024,256]{1,0:T(8,128)(2,1)S(1)} %collective-permute-done.other.refs_2_, ...), custom_call_target="tpu_custom_call" | custom-call | flops 67108864 | bytes 2097152 | tf_op jit(solution)/shard_map/pallas_call | solution.py:281
  17.0 0.2 shard_map.53.refs_6_
  17.3 0.1 collective-permute-start.8
  17.4 2.5 %collective-permute-start.12 = (bf16[2,32,256]{2,1,0:T(8,128)(2,1)S(1)}, bf16[2,32,256]{2,1,0:T(8,128)(2,1)S(1)}, u32[]{:S(2)}, u32[]{:S(2)}) collective-permute-start(bf16[2,32,256]{2,1,0:T(8,128)(2,1)S(1)} %broadcast_select_fusion.7), channel_id=1, source_target_pairs={{0,16},{8,24},{16,0},{24,8},{1,17},{9,25},{17,1},{25,9},{2,18},{10... | collective-permute-start | bytes 98312 | tf_op jit(solution)/shard_map/ppermute | solution.py:514
  20.0 0.2 collective-permute-start.7
  20.1 1.8 %collective-permute-done.12 = bf16[2,32,256]{2,1,0:T(8,128)(2,1)S(1)} collective-permute-done((bf16[2,32,256]{2,1,0:T(8,128)(2,1)S(1)}, bf16[2,32,256]{2,1,0:T(8,128)(2,1)S(1)}, u32[]{:S(2)}, u32[]{:S(2)}) %collective-permute-start.12) | collective-permute-done | bytes 32800 | tf_op jit(solution)/shard_map/ppermute | solution.py:514
  21.9 1.9 %collective-permute-start.17 = (bf16[32,1024]{1,0:T(8,128)(2,1)S(1)}, bf16[32,1024]{1,0:T(8,128)(2,1)S(1)}, u32[]{:S(2)}, u32[]{:S(2)}) collective-permute-start(bf16[32,1024]{1,0:T(8,128)(2,1)S(1)} %fusion.1), channel_id=1, source_target_pairs={{0,16},{8,24},{16,0},{24,8},{1,17},{9,25},{17,1},{25,9},{2,18},{10... | collective-permute-start | bytes 196616 | tf_op jit(solution)/shard_map/ppermute | solution.py:514
  23.9 0.0 collective-permute-done.10
  23.9 0.0 collective-permute-start.13
  23.9 2.3 %collective-permute-done.17 = bf16[32,1024]{1,0:T(8,128)(2,1)S(1)} collective-permute-done((bf16[32,1024]{1,0:T(8,128)(2,1)S(1)}, bf16[32,1024]{1,0:T(8,128)(2,1)S(1)}, u32[]{:S(2)}, u32[]{:S(2)}) %collective-permute-start.17) | collective-permute-done | bytes 65568 | tf_op jit(solution)/shard_map/ppermute | solution.py:514
  26.2 0.0 collective-permute-start.11
  26.2 0.6 %collective-permute-start.18 = (bf16[32,1024]{1,0:T(8,128)(2,1)S(1)}, bf16[32,1024]{1,0:T(8,128)(2,1)S(1)}, u32[]{:S(2)}, u32[]{:S(2)}) collective-permute-start(bf16[32,1024]{1,0:T(8,128)(2,1)S(1)} %get-tuple-element.95), channel_id=1, source_target_pairs={{0,8},{8,0},{16,24},{24,16},{1,9},{9,1},{17,25},{25,17},{2,10},{10... | collective-permute-start | bytes 196616 | tf_op jit(solution)/shard_map/ppermute | solution.py:511
  26.8 0.1 shard_map.54
  26.9 1.4 %collective-permute-start.9 = (bf16[64,1536]{1,0:T(8,128)(2,1)S(1)}, bf16[64,1536]{1,0:T(8,128)(2,1)S(1)}, u32[]{:S(2)}, u32[]{:S(2)}) collective-permute-start(bf16[64,1536]{1,0:T(8,128)(2,1)S(1)} %get-tuple-element.74), channel_id=1, source_target_pairs={{0,1},{1,0},{2,3},{3,2},{4,5},{5,4},{6,7},{7,6},{8,10},{9,11},{10,... | collective-permute-start | bytes 589832 | tf_op jit(solution)/shard_map/ppermute | solution.py:650
  28.3 0.1 shard_map.58
  28.4 0.8 %collective-permute-start.19 = (bf16[64,768]{1,0:T(8,128)(2,1)S(1)}, bf16[64,768]{1,0:T(8,128)(2,1)S(1)}, u32[]{:S(2)}, u32[]{:S(2)}) collective-permute-start(bf16[64,768]{1,0:T(8,128)(2,1)S(1)} %get-tuple-element.90), channel_id=1, source_target_pairs={{0,1},{1,0},{2,3},{3,2},{4,5},{5,4},{6,7},{7,6},{8,10},{9,11},{10,... | collective-permute-start | bytes 294920 | tf_op jit(solution)/shard_map/ppermute | solution.py:650
  29.2 1.4 %collective-permute-start.14 = (bf16[64,768]{1,0:T(8,128)(2,1)S(1)}, bf16[64,768]{1,0:T(8,128)(2,1)S(1)}, u32[]{:S(2)}, u32[]{:S(2)}) collective-permute-start(bf16[64,768]{1,0:T(8,128)(2,1)S(1)} %get-tuple-element.80), channel_id=1, source_target_pairs={{0,1},{1,0},{2,3},{3,2},{4,5},{5,4},{6,7},{7,6},{8,10},{9,11},{10,... | collective-permute-start | bytes 294920 | tf_op jit(solution)/shard_map/ppermute | solution.py:650
  30.6 3.1 %collective-permute-done.19.refs_5_ = bf16[64,768]{1,0:T(8,128)(2,1)S(1)} collective-permute-done((bf16[64,768]{1,0:T(8,128)(2,1)S(1)}, bf16[64,768]{1,0:T(8,128)(2,1)S(1)}, u32[]{:S(2)}, u32[]{:S(2)}) %collective-permute-start.19) | collective-permute-done | bytes 98336 | tf_op jit(solution)/shard_map/ppermute | solution.py:650
  33.7 0.3 shard_map.59
  34.1 1.4 %collective-permute-start.20 = (bf16[2,128,256]{2,1,0:T(8,128)(2,1)S(1)}, bf16[2,128,256]{2,1,0:T(8,128)(2,1)S(1)}, u32[]{:S(2)}, u32[]{:S(2)}) collective-permute-start(bf16[2,128,256]{2,1,0:T(8,128)(2,1)S(1)} %get-tuple-element.92), channel_id=1, source_target_pairs={{0,2},{1,3},{2,0},{3,1},{4,6},{5,7},{6,4},{7,5},{8,12},{9,13},{10,... | collective-permute-start | bytes 393224 | tf_op jit(solution)/shard_map/ppermute | solution.py:650
  35.5 0.3 shard_map.56
  35.8 0.7 %collective-permute-start.15 = (bf16[2,128,256]{2,1,0:T(8,128)(2,1)S(1)}, bf16[2,128,256]{2,1,0:T(8,128)(2,1)S(1)}, u32[]{:S(2)}, u32[]{:S(2)}) collective-permute-start(bf16[2,128,256]{2,1,0:T(8,128)(2,1)S(1)} %get-tuple-element.82), channel_id=1, source_target_pairs={{0,2},{1,3},{2,0},{3,1},{4,6},{5,7},{6,4},{7,5},{8,12},{9,13},{10,... | collective-permute-start | bytes 393224 | tf_op jit(solution)/shard_map/ppermute | solution.py:650
  36.6 2.8 %collective-permute-done.20.came = bf16[2,128,256]{2,1,0:T(8,128)(2,1)S(1)} collective-permute-done((bf16[2,128,256]{2,1,0:T(8,128)(2,1)S(1)}, bf16[2,128,256]{2,1,0:T(8,128)(2,1)S(1)}, u32[]{:S(2)}, u32[]{:S(2)}) %collective-permute-start.20) | collective-permute-done | bytes 131104 | tf_op jit(solution)/shard_map/ppermute | solution.py:650
  39.4 2.7 %collective-permute-start.21 = (bf16[1,128,256]{2,1,0:T(8,128)(2,1)S(1)}, bf16[1,128,256]{2,1,0:T(8,128)(2,1)S(1)}, u32[]{:S(2)}, u32[]{:S(2)}) collective-permute-start(bf16[1,128,256]{2,1,0:T(8,128)(2,1)S(1)} %get-tuple-element.94), channel_id=1, source_target_pairs={{0,4},{1,5},{2,6},{3,7},{4,0},{5,1},{6,2},{7,3},{8,9},{9,8},{10,11... | collective-permute-start | bytes 196616 | tf_op jit(solution)/shard_map/ppermute | solution.py:650
  42.1 0.3 collective-permute-done.15.came
  42.5 2.3 %collective-permute-start.16 = (bf16[1,128,256]{2,1,0:T(8,128)(2,1)S(1)}, bf16[1,128,256]{2,1,0:T(8,128)(2,1)S(1)}, u32[]{:S(2)}, u32[]{:S(2)}) collective-permute-start(bf16[1,128,256]{2,1,0:T(8,128)(2,1)S(1)} %get-tuple-element.84), channel_id=1, source_target_pairs={{0,4},{1,5},{2,6},{3,7},{4,0},{5,1},{6,2},{7,3},{8,9},{9,8},{10,11... | collective-permute-start | bytes 196616 | tf_op jit(solution)/shard_map/ppermute | solution.py:650
  44.8 0.7 %shard_map.61.refs_0_ = f32[1,2,128,256]{3,2,1,0:T(8,128)} custom-call(f32[1,128,256]{2,1,0:T(8,128)S(1)} %get-tuple-element.93.keep, bf16[1,128,256]{2,1,0:T(8,128)(2,1)S(1)} %collective-permute-done.21.came), custom_call_target="tpu_custom_call" | custom-call | tf_op jit(solution)/shard_map/pallas_call | solution.py:478
  45.5 2.3 %collective-permute-done.16.came = bf16[1,128,256]{2,1,0:T(8,128)(2,1)S(1)} collective-permute-done((bf16[1,128,256]{2,1,0:T(8,128)(2,1)S(1)}, bf16[1,128,256]{2,1,0:T(8,128)(2,1)S(1)}, u32[]{:S(2)}, u32[]{:S(2)}) %collective-permute-start.16) | collective-permute-done | bytes 65568 | tf_op jit(solution)/shard_map/ppermute | solution.py:650
  47.7 0.7 %shard_map.62 = f32[1,2,128,256]{3,2,1,0:T(8,128)} custom-call(f32[1,128,256]{2,1,0:T(8,128)S(1)} %get-tuple-element.83.keep, bf16[1,128,256]{2,1,0:T(8,128)(2,1)S(1)} %collective-permute-done.16.came, f32[1,2,128,256]{3,2,1,0:T(8,128)} %shard_map.61.refs_0_), custom_call_target="tpu_custom_call", output_to_operand_aliasing={{}: (2, {})} | custom-call | tf_op jit(solution)/shard_map/pallas_call | solution.py:478
  (29 shorter events, 0.3 us)
Async XLA Ops:
  1.2 2.4 %collective-permute-start = (bf16[1024,256]{1,0:T(8,128)(2,1)S(1)}, bf16[1024,256]{1,0:T(8,128)(2,1)S(1)}, u32[]{:S(2)}, u32[]{:S(2)}) collective-permute-start(bf16[1024,256]{1,0:T(8,128)(2,1)S(1)} %get-tuple-element.51.own.refs_0_), channel_id=1, source_target_pairs={{0,8},{8,0},{16,24},{24,16},{1,9},{9,1},{17,25},{25,17},{2,10},{10... | collective-permute-start | bytes 1572872 | tf_op jit(solution)/shard_map/ppermute | solution.py:511
  1.8 2.3 %collective-permute-start.1 = (bf16[1024,256]{1,0:T(8,128)(2,1)S(1)}, bf16[1024,256]{1,0:T(8,128)(2,1)S(1)}, u32[]{:S(2)}, u32[]{:S(2)}) collective-permute-start(bf16[1024,256]{1,0:T(8,128)(2,1)S(1)} %get-tuple-element.52.refs_1_.own), channel_id=1, source_target_pairs={{0,8},{8,0},{16,24},{24,16},{1,9},{9,1},{17,25},{25,17},{2,10},{10... | collective-permute-start | bytes 1572872 | tf_op jit(solution)/shard_map/ppermute | solution.py:511
  3.1 4.7 %collective-permute-start.3 = (bf16[1024,256]{1,0:T(8,128)(2,1)S(1)}, bf16[1024,256]{1,0:T(8,128)(2,1)S(1)}, u32[]{:S(2)}, u32[]{:S(2)}) collective-permute-start(bf16[1024,256]{1,0:T(8,128)(2,1)S(1)} %get-tuple-element.59.expand_own.refs_1_), channel_id=1, source_target_pairs={{0,8},{8,0},{16,24},{24,16},{1,9},{9,1},{17,25},{25,17},{2,10},{10... | collective-permute-start | bytes 1572872 | tf_op jit(solution)/shard_map/ppermute | solution.py:511
  3.6 5.4 %collective-permute-start.2 = (bf16[1024,256]{1,0:T(8,128)(2,1)S(1)}, bf16[1024,256]{1,0:T(8,128)(2,1)S(1)}, u32[]{:S(2)}, u32[]{:S(2)}) collective-permute-start(bf16[1024,256]{1,0:T(8,128)(2,1)S(1)} %get-tuple-element.58.refs_0_), channel_id=1, source_target_pairs={{0,8},{8,0},{16,24},{24,16},{1,9},{9,1},{17,25},{25,17},{2,10},{10... | collective-permute-start | bytes 1572872 | tf_op jit(solution)/shard_map/ppermute | solution.py:511
  4.9 5.3 %collective-permute-start.4 = (bf16[32,1024]{1,0:T(8,128)(2,1)S(1)}, bf16[32,1024]{1,0:T(8,128)(2,1)S(1)}, u32[]{:S(2)}, u32[]{:S(2)}) collective-permute-start(bf16[32,1024]{1,0:T(8,128)(2,1)S(1)} %get-tuple-element.60.leave), channel_id=1, source_target_pairs={{0,16},{16,0},{8,24},{24,8},{1,17},{17,1},{9,25},{25,9},{2,18},{18... | collective-permute-start | bytes 196616 | tf_op jit(solution)/shard_map/ppermute | solution.py:508
  12.0 4.4 %collective-permute-start.6 = (bf16[32,1024]{1,0:T(8,128)(2,1)S(1)}, bf16[32,1024]{1,0:T(8,128)(2,1)S(1)}, u32[]{:S(2)}, u32[]{:S(2)}) collective-permute-start(bf16[32,1024]{1,0:T(8,128)(2,1)S(1)} %get-tuple-element.65), channel_id=1, source_target_pairs={{0,16},{16,0},{8,24},{24,8},{1,17},{17,1},{9,25},{25,9},{2,18},{18... | collective-permute-start | bytes 196616 | tf_op jit(solution)/shard_map/ppermute | solution.py:508
  14.0 12.8 %collective-permute-start.5 = (bf16[32,1280]{1,0:T(8,128)(2,1)S(1)}, bf16[32,1280]{1,0:T(8,128)(2,1)S(1)}, u32[]{:S(2)}, u32[]{:S(2)}) collective-permute-start(bf16[32,1280]{1,0:T(8,128)(2,1)S(1)} %fusion), channel_id=1, source_target_pairs={{0,8},{8,0},{16,24},{24,16},{1,9},{9,1},{17,25},{25,17},{2,10},{10... | collective-permute-start | bytes 245768 | tf_op jit(solution)/shard_map/ppermute | solution.py:511
  14.2 9.7 %collective-permute-start.10 = (bf16[32,1536]{1,0:T(8,128)(2,1)S(1)}, bf16[32,1536]{1,0:T(8,128)(2,1)S(1)}, u32[]{:S(2)}, u32[]{:S(2)}) collective-permute-start(bf16[32,1536]{1,0:T(8,128)(2,1)S(1)} %pad_maximum_fusion), channel_id=1, source_target_pairs={{0,16},{8,24},{16,0},{24,8},{1,17},{9,25},{17,1},{25,9},{2,18},{10... | collective-permute-start | bytes 294920 | tf_op jit(solution)/shard_map/ppermute | solution.py:514
  17.3 8.9 %collective-permute-start.8 = (bf16[32,256]{1,0:T(8,128)(2,1)S(1)}, bf16[32,256]{1,0:T(8,128)(2,1)S(1)}, u32[]{:S(2)}, u32[]{:S(2)}) collective-permute-start(bf16[32,256]{1,0:T(8,128)(2,1)S(1)} %fusion.4), channel_id=1, source_target_pairs={{0,8},{8,0},{16,24},{24,16},{1,9},{9,1},{17,25},{25,17},{2,10},{10... | collective-permute-start | bytes 49160 | tf_op jit(solution)/shard_map/ppermute | solution.py:511
  17.4 4.5 %collective-permute-start.12 = (bf16[2,32,256]{2,1,0:T(8,128)(2,1)S(1)}, bf16[2,32,256]{2,1,0:T(8,128)(2,1)S(1)}, u32[]{:S(2)}, u32[]{:S(2)}) collective-permute-start(bf16[2,32,256]{2,1,0:T(8,128)(2,1)S(1)} %broadcast_select_fusion.7), channel_id=1, source_target_pairs={{0,16},{8,24},{16,0},{24,8},{1,17},{9,25},{17,1},{25,9},{2,18},{10... | collective-permute-start | bytes 98312 | tf_op jit(solution)/shard_map/ppermute | solution.py:514
  20.0 6.9 %collective-permute-start.7 = (bf16[32,1024]{1,0:T(8,128)(2,1)S(1)}, bf16[32,1024]{1,0:T(8,128)(2,1)S(1)}, u32[]{:S(2)}, u32[]{:S(2)}) collective-permute-start(bf16[32,1024]{1,0:T(8,128)(2,1)S(1)} %fusion.3), channel_id=1, source_target_pairs={{0,8},{8,0},{16,24},{24,16},{1,9},{9,1},{17,25},{25,17},{2,10},{10... | collective-permute-start | bytes 196616 | tf_op jit(solution)/shard_map/ppermute | solution.py:511
  21.9 4.3 %collective-permute-start.17 = (bf16[32,1024]{1,0:T(8,128)(2,1)S(1)}, bf16[32,1024]{1,0:T(8,128)(2,1)S(1)}, u32[]{:S(2)}, u32[]{:S(2)}) collective-permute-start(bf16[32,1024]{1,0:T(8,128)(2,1)S(1)} %fusion.1), channel_id=1, source_target_pairs={{0,16},{8,24},{16,0},{24,8},{1,17},{9,25},{17,1},{25,9},{2,18},{10... | collective-permute-start | bytes 196616 | tf_op jit(solution)/shard_map/ppermute | solution.py:514
  23.9 5.3 %collective-permute-start.13 = (bf16[32,256]{1,0:T(8,128)(2,1)S(1)}, bf16[32,256]{1,0:T(8,128)(2,1)S(1)}, u32[]{:S(2)}, u32[]{:S(2)}) collective-permute-start(bf16[32,256]{1,0:T(8,128)(2,1)S(1)} %get-tuple-element.103), channel_id=1, source_target_pairs={{0,8},{8,0},{16,24},{24,16},{1,9},{9,1},{17,25},{25,17},{2,10},{10... | collective-permute-start | bytes 49160 | tf_op jit(solution)/shard_map/ppermute | solution.py:511
  26.2 2.1 %collective-permute-start.11 = (bf16[32,1280]{1,0:T(8,128)(2,1)S(1)}, bf16[32,1280]{1,0:T(8,128)(2,1)S(1)}, u32[]{:S(2)}, u32[]{:S(2)}) collective-permute-start(bf16[32,1280]{1,0:T(8,128)(2,1)S(1)} %pad_maximum_fusion.2), channel_id=1, source_target_pairs={{0,8},{8,0},{16,24},{24,16},{1,9},{9,1},{17,25},{25,17},{2,10},{10... | collective-permute-start | bytes 245768 | tf_op jit(solution)/shard_map/ppermute | solution.py:511
  26.2 2.1 %collective-permute-start.18 = (bf16[32,1024]{1,0:T(8,128)(2,1)S(1)}, bf16[32,1024]{1,0:T(8,128)(2,1)S(1)}, u32[]{:S(2)}, u32[]{:S(2)}) collective-permute-start(bf16[32,1024]{1,0:T(8,128)(2,1)S(1)} %get-tuple-element.95), channel_id=1, source_target_pairs={{0,8},{8,0},{16,24},{24,16},{1,9},{9,1},{17,25},{25,17},{2,10},{10... | collective-permute-start | bytes 196616 | tf_op jit(solution)/shard_map/ppermute | solution.py:511
  26.9 6.8 %collective-permute-start.9 = (bf16[64,1536]{1,0:T(8,128)(2,1)S(1)}, bf16[64,1536]{1,0:T(8,128)(2,1)S(1)}, u32[]{:S(2)}, u32[]{:S(2)}) collective-permute-start(bf16[64,1536]{1,0:T(8,128)(2,1)S(1)} %get-tuple-element.74), channel_id=1, source_target_pairs={{0,1},{1,0},{2,3},{3,2},{4,5},{5,4},{6,7},{7,6},{8,10},{9,11},{10,... | collective-permute-start | bytes 589832 | tf_op jit(solution)/shard_map/ppermute | solution.py:650
  28.4 5.3 %collective-permute-start.19 = (bf16[64,768]{1,0:T(8,128)(2,1)S(1)}, bf16[64,768]{1,0:T(8,128)(2,1)S(1)}, u32[]{:S(2)}, u32[]{:S(2)}) collective-permute-start(bf16[64,768]{1,0:T(8,128)(2,1)S(1)} %get-tuple-element.90), channel_id=1, source_target_pairs={{0,1},{1,0},{2,3},{3,2},{4,5},{5,4},{6,7},{7,6},{8,10},{9,11},{10,... | collective-permute-start | bytes 294920 | tf_op jit(solution)/shard_map/ppermute | solution.py:650
  29.2 6.3 %collective-permute-start.14 = (bf16[64,768]{1,0:T(8,128)(2,1)S(1)}, bf16[64,768]{1,0:T(8,128)(2,1)S(1)}, u32[]{:S(2)}, u32[]{:S(2)}) collective-permute-start(bf16[64,768]{1,0:T(8,128)(2,1)S(1)} %get-tuple-element.80), channel_id=1, source_target_pairs={{0,1},{1,0},{2,3},{3,2},{4,5},{5,4},{6,7},{7,6},{8,10},{9,11},{10,... | collective-permute-start | bytes 294920 | tf_op jit(solution)/shard_map/ppermute | solution.py:650
  34.1 5.3 %collective-permute-start.20 = (bf16[2,128,256]{2,1,0:T(8,128)(2,1)S(1)}, bf16[2,128,256]{2,1,0:T(8,128)(2,1)S(1)}, u32[]{:S(2)}, u32[]{:S(2)}) collective-permute-start(bf16[2,128,256]{2,1,0:T(8,128)(2,1)S(1)} %get-tuple-element.92), channel_id=1, source_target_pairs={{0,2},{1,3},{2,0},{3,1},{4,6},{5,7},{6,4},{7,5},{8,12},{9,13},{10,... | collective-permute-start | bytes 393224 | tf_op jit(solution)/shard_map/ppermute | solution.py:650
  35.8 6.6 %collective-permute-start.15 = (bf16[2,128,256]{2,1,0:T(8,128)(2,1)S(1)}, bf16[2,128,256]{2,1,0:T(8,128)(2,1)S(1)}, u32[]{:S(2)}, u32[]{:S(2)}) collective-permute-start(bf16[2,128,256]{2,1,0:T(8,128)(2,1)S(1)} %get-tuple-element.82), channel_id=1, source_target_pairs={{0,2},{1,3},{2,0},{3,1},{4,6},{5,7},{6,4},{7,5},{8,12},{9,13},{10,... | collective-permute-start | bytes 393224 | tf_op jit(solution)/shard_map/ppermute | solution.py:650
  39.4 5.4 %collective-permute-start.21 = (bf16[1,128,256]{2,1,0:T(8,128)(2,1)S(1)}, bf16[1,128,256]{2,1,0:T(8,128)(2,1)S(1)}, u32[]{:S(2)}, u32[]{:S(2)}) collective-permute-start(bf16[1,128,256]{2,1,0:T(8,128)(2,1)S(1)} %get-tuple-element.94), channel_id=1, source_target_pairs={{0,4},{1,5},{2,6},{3,7},{4,0},{5,1},{6,2},{7,3},{8,9},{9,8},{10,11... | collective-permute-start | bytes 196616 | tf_op jit(solution)/shard_map/ppermute | solution.py:650
  42.5 5.2 %collective-permute-start.16 = (bf16[1,128,256]{2,1,0:T(8,128)(2,1)S(1)}, bf16[1,128,256]{2,1,0:T(8,128)(2,1)S(1)}, u32[]{:S(2)}, u32[]{:S(2)}) collective-permute-start(bf16[1,128,256]{2,1,0:T(8,128)(2,1)S(1)} %get-tuple-element.84), channel_id=1, source_target_pairs={{0,4},{1,5},{2,6},{3,7},{4,0},{5,1},{6,2},{7,3},{8,9},{9,8},{10,11... | collective-permute-start | bytes 196616 | tf_op jit(solution)/shard_map/ppermute | solution.py:650

commit v9 on v7

--- a/solution.py
+++ b/solution.py
@@ -377,61 +377,65 @@
             target[:, place * chunk : (place + 1) * chunk] = wide[:, source]
 
 
-def pack_body(stages, chunk, up, near, far, *refs):
-    refs = list(refs)
-    left, right, send, wide = refs[-4:]
-    channels = wide.shape[1]
-    spans = slice(0, channels), slice(channels, None), slice(None)
-    flow_span, back_span = (spans[1] if up else spans[0]), spans[2]
+def take_rows(target, span, *arrays):
     stage, _, _ = where_am_i(0)
-    rows = wide.shape[0] // (2 * near + 2 * far)
-    start = 0
-    targets = (right, wide) if up else (wide, right)
-    for target, span in zip(targets, (flow_span, back_span)):
-        start = 0
-        if near:
-            parts = [refs.pop(0) for _ in range(stages + 1)]
-            for step in range(stages):
-
-                @pl.when(stage == step)
-                def _():
-                    target[:rows] = parts[step][0, :, span]
-
-            target[rows : 2 * rows] = parts[stages][:, span]
-            start = 2 * rows
-        if far:
-            for part in (refs.pop(0), refs.pop(0)):
-                target[start : start + rows] = part[:, span]
-                start += rows
-    split_columns(wide, left, send, chunk)
-    send[:, channels // 2 :] = right[...]
-
-
-def near_body(stages, chunk, *refs):
-    flows, ups, backs = [refs[at * (stages + 1) : (at + 1) * (stages + 1)] for at in range(3)]
-    left_up, right_up, left_inner, right_inner, send, wide = refs[3 * stages + 3 :]
-    width = send.shape[1] // 2
-    for at, (late, outs) in enumerate(
-        ((ups, (left_up, right_up)), (backs, (left_inner, right_inner)))
-    ):
-        part = send.at[:, at * width : (at + 1) * width]
-        pack_body(stages, chunk, at == 0, True, False, *flows, *late, *outs, part, wide)
-
-
-def half_gradient_body(at, groups, *refs):
-    send, keep, full, left, right = refs[3 * groups :]
-    start = 0
-    for group in range(groups):
-        part_left, part_right, came = refs[3 * group : 3 * group + 3]
-        rows, columns = part_left.shape
-        left[start : start + rows] = part_left[...]
-        right[start : start + rows] = part_right[...]
-        start += rows
-        width = columns + right.shape[1]
-        offset = at * width if came.shape[1] > width else 0
-        left[start : start + rows] = came[:, offset : offset + columns]
-        right[start : start + rows] = came[:, offset + columns : offset + width]
-        start += rows
+    *own, other = arrays
+    rows = target.shape[0] // 2
+    for step, part in enumerate(own):
+        part = part if len(part.shape) == 2 else part.at[0]
+
+        @pl.when((stage == step) | (len(own) == 1))
+        def _():
+            target[:rows] = part[:, span]
+
+    target[rows:] = other[:, span]
+
+
+def near_up_body(stages, chunk, *refs):
+    flows, ups = refs[: stages + 1], refs[stages + 1 : 2 * stages + 2]
+    up, active, lifted, send, wide = refs[2 * stages + 2 :]
+    half, channels = up.shape[1], wide.shape[1]
+    inner = active.shape[1]
+    take_rows(wide, slice(None), *ups)
+    split_columns(wide, up, send.at[:, :half], chunk)
+    take_rows(active, slice(channels, None), *flows)
+    send[:, half : half + inner] = active[...]
+    take_rows(wide, slice(0, channels), *flows)
+    split_columns(wide, lifted, send.at[:, half + inner :], chunk)
+
+
+def late_up_body(chunk, flow, cross_flow, far, cross, up, active, send, wide):
+    half, channels = up.shape[1], wide.shape[1]
+    take_rows(wide, slice(None), far, cross)
+    split_columns(wide, up, send.at[:, :half], chunk)
+    take_rows(active, slice(channels, None), flow, cross_flow)
+    send[:, half:] = active[...]
+
+
+def late_inner_body(chunk, flow, cross_flow, *refs):
+    *backs, far, cross, lifted, far_inner, near_inner, send, wide = refs
+    half, channels = lifted.shape[1], wide.shape[1]
+    inner = far_inner.shape[1]
+    take_rows(wide, slice(0, channels), flow, cross_flow)
+    split_columns(wide, lifted, send.at[:, :half], chunk)
+    take_rows(far_inner, slice(None), far, cross)
+    send[:, half : half + inner] = far_inner[...]
+    take_rows(near_inner, slice(None), *backs)
+    send[:, half + inner :] = near_inner[...]
+
+
+def half_gradient_body(starts, *refs):
+    lefts, rights, cames = refs[:2], refs[2:4], refs[4:6]
+    send, keep, full, left, right = refs[6:]
+    rows, columns = lefts[0].shape
+    inner = rights[0].shape[1]
+    for group, ((left_in, left_start), (right_in, right_start)) in enumerate(starts):
+        place = slice(2 * group * rows, (2 * group + 1) * rows)
+        left[place] = lefts[group][...]
+        right[place] = rights[group][...]
+        place = slice((2 * group + 1) * rows, (2 * group + 2) * rows)
+        left[place] = cames[left_in][:, left_start : left_start + columns]
+        right[place] = cames[right_in][:, right_start : right_start + inner]
     full[...] = contract(left[...], right[...], 0, 0)
     _, _, side = first_sides()
     chunk = send.shape[1]
@@ -626,50 +630,60 @@
 
 def halve_rows(stages, replicas, chunk, sizes, rows, fore, ups, backs):
     channels, inner = sizes
-    shape = lambda *dims: jax.ShapeDtypeStruct(dims, jnp.bfloat16)
-
-    def pack(late, up, near, far):
-        count = 2 * (near + far)
-        arrays = []
-        for one in (fore, late):
-            arrays += one[: stages + 1] * near + one[stages + 1 :] * far
+    half = channels // 2
+    count = stages + 1
+
+    def pack(body, arrays, *widths):
         return pl.pallas_call(
-            functools.partial(pack_body, stages, chunk, up, near, far),
-            out_shape=[
-                shape(count * rows, channels // 2),
-                shape(count * rows, inner),
-                shape(count * rows, channels // 2 + inner),
-            ],
+            body,
+            out_shape=[jax.ShapeDtypeStruct((2 * rows, width), jnp.bfloat16) for width in widths],
             in_specs=[VMEM] * len(arrays),
-            out_specs=[VMEM] * 3,
-            scratch_shapes=[pltpu.VMEM((count * rows, channels), jnp.bfloat16)],
+            out_specs=[VMEM] * len(widths),
+            scratch_shapes=[pltpu.VMEM((2 * rows, channels), jnp.bfloat16)],
             compiler_params=PARAMS,
         )(*arrays)
 
-    near = fore[: stages + 1] + ups[: stages + 1] + backs[: stages + 1]
-    *kept, send = pl.pallas_call(
-        functools.partial(near_body, stages, chunk),
-        out_shape=[
-            shape(2 * rows, channels // 2),
-            shape(2 * rows, inner),
-            shape(2 * rows, channels // 2),
-            shape(2 * rows, inner),
-            shape(2 * rows, channels + 2 * inner),
-        ],
-        in_specs=[VMEM] * len(near),
-        out_specs=[VMEM] * 5,
-        scratch_shapes=[pltpu.VMEM((2 * rows, channels), jnp.bfloat16)],
-        compiler_params=PARAMS,
-    )(*near)
+    near_up, near_active, near_lifted, send = pack(
+        functools.partial(near_up_body, stages, chunk),
+        fore[:count] + ups[:count],
+        half,
+        inner,
+        half,
+        2 * half + inner,
+    )
     came_near = exchange(send, stages, replicas, 1, 2)
+    far_up, far_active, send = pack(
+        functools.partial(late_up_body, chunk),
+        fore[count:] + ups[count:],
+        half,
+        inner,
+        half + inner,
+    )
+    came_up = exchange(send, stages, replicas, 1, 2)
+    far_lifted, far_inner, near_inner, send = pack(
+        functools.partial(late_inner_body, chunk),
+        fore[count:] + backs,
+        half,
+        inner,
+        inner,
+        half + 2 * inner,
+    )
+    came_inner = exchange(send, stages, replicas, 1, 2)
+    streams = (
+        (
+            (near_lifted, far_lifted, near_inner, far_inner, came_near, came_inner),
+            (((0, half + inner), (1, half + inner)), ((1, 0), (1, half))),
+        ),
+        (
+            (near_up, far_up, near_active, far_active, came_near, came_up),
+            (((0, 0), (0, half)), ((1, 0), (1, half))),
+        ),
+    )
     parts = []
-    for at, name, late in ((1, "inner", backs), (0, "up", ups)):
-        left, right, send = pack(late, name == "up", False, True)
-        came = exchange(send, stages, replicas, 1, 2)
-        operands = (kept[2 * at], kept[2 * at + 1], came_near, left, right, came)
+    for operands, starts in streams:
         count = replicas // 4
         send, keep = pl.pallas_call(
-            functools.partial(half_gradient_body, at, len(operands) // 3),
+            functools.partial(half_gradient_body, starts),
             out_shape=sums(count, chunk, inner),
             in_specs=[VMEM] * len(operands),
             out_specs=[VMEM] * 2,

time: 47.8 us -> 48.8 us (1.021)
  waiting for transfers between devices: 15.6 us -> 16.7 us
    ppermute x7, waiting for transfers between devices: 8.24 us -> 9.27 us  [exchange(): return lax.ppermute(shard, AXES, pairs)]
where the time goes in v9:
time: 48.8 us; the launch traced here: 48.6 us
  starting transfers between devices  22.4 us (46%)
  waiting for transfers between devices  16.7 us (34%)
  Pallas kernels  9.12 us (19%)
    ppermute x7, starting transfers between devices, exchange(): return lax.ppermute(shard, AXES, pairs)  10.8 us
    ppermute x7, waiting for transfers between devices, exchange(): return lax.ppermute(shard, AXES, pairs)  9.27 us
    ppermute x2, starting transfers between devices, hop(): return lax.ppermute(shard, 'pipe', pairs)  4.86 us
    ppermute x3, starting transfers between devices, mirror(): return lax.ppermute(shard, 'pipe', mirror_pairs)  4.67 us
    ppermute x3, waiting for transfers between devices, mirror(): return lax.ppermute(shard, 'pipe', mirror_pairs)  4.09 us
    pallas_call x3, Pallas kernels, run_stage(): pl.pallas_call(functools.partial(stage_body, step, forward, backward, las...  3.26 us
    ppermute x2, waiting for transfers between devices, hop(): return lax.ppermute(shard, 'pipe', pairs)  3.23 us
    pallas_call x2, Pallas kernels, load(): pl.pallas_call(functools.partial(load_body, step), out_shape=outs, in_spe...  2.44 us
  transfers between devices with their start and end apart: 22, of which 9 were waited for; matrix products, arithmetic and copies ran while one was open for 0% of the time, Pallas kernels for 11%

profile of v9, /device:TPU:0, one launch (start us, length us, event | category | flops | bytes accessed | tf_op | source)
XLA Modules:
  0.0 48.6 jit_solution(16263660998121055698)
XLA Ops:
  0.0 1.2 %shard_map.46 = (bf16[1024,256]{1,0:T(8,128)(2,1)S(1)}, bf16[1024,256]{1,0:T(8,128)(2,1)S(1)}, bf16[32,1024]{1,0:T(8,128)(2,1)S(1)}) custom-call(bf16[2,1024,256]{2,1,0:T(8,128)(2,1)} %bitcast.20, bf16[2,1024,256]{2,1,0:T(8,128)(2,1)} %bitcast.22, bf16[2,2,32,1024]{3,2,1,0:T(8,128)(2,1)} %inputs), custom_call_target="tpu_custom_call" | custom-call | tf_op jit(solution)/shard_map/pallas_call | solution.py:68
  1.2 0.6 %collective-permute-start = (bf16[1024,256]{1,0:T(8,128)(2,1)S(1)}, bf16[1024,256]{1,0:T(8,128)(2,1)S(1)}, u32[]{:S(2)}, u32[]{:S(2)}) collective-permute-start(bf16[1024,256]{1,0:T(8,128)(2,1)S(1)} %get-tuple-element.51.own.refs_0_), channel_id=1, source_target_pairs={{0,8},{8,0},{16,24},{24,16},{1,9},{9,1},{17,25},{25,17},{2,10},{10... | collective-permute-start | bytes 1572872 | tf_op jit(solution)/shard_map/ppermute | solution.py:484
  1.8 0.1 collective-permute-start.1
  1.9 1.2 %shard_map.49 = (bf16[1024,256]{1,0:T(8,128)(2,1)S(1)}, bf16[1024,256]{1,0:T(8,128)(2,1)S(1)}) custom-call(bf16[2,1024,256]{2,1,0:T(8,128)(2,1)} %bitcast.21, bf16[2,1024,256]{2,1,0:T(8,128)(2,1)} %bitcast.23), custom_call_target="tpu_custom_call" | custom-call | tf_op jit(solution)/shard_map/pallas_call | solution.py:68
  3.1 0.5 %collective-permute-start.3 = (bf16[1024,256]{1,0:T(8,128)(2,1)S(1)}, bf16[1024,256]{1,0:T(8,128)(2,1)S(1)}, u32[]{:S(2)}, u32[]{:S(2)}) collective-permute-start(bf16[1024,256]{1,0:T(8,128)(2,1)S(1)} %get-tuple-element.59.expand_own.refs_1_), channel_id=1, source_target_pairs={{0,8},{8,0},{16,24},{24,16},{1,9},{9,1},{17,25},{25,17},{2,10},{10... | collective-permute-start | bytes 1572872 | tf_op jit(solution)/shard_map/ppermute | solution.py:484
  3.6 0.1 collective-permute-start.2
  3.7 0.3 shard_map.47
  4.0 0.1 collective-permute-done.1.refs_3_.other
  4.1 0.8 %shard_map.48 = (bf16[2,32,1280]{2,1,0:T(8,128)(2,1)S(1)}, bf16[32,1024]{1,0:T(8,128)(2,1)S(1)}, bf16[2,32,1024]{2,1,0:T(8,128)(2,1)S(1)}, f32[2,32,256]{2,1,0:T(8,128)S(1)}) custom-call(bf16[1024,256]{1,0:T(8,128)(2,1)S(1)} %get-tuple-element.51.own.refs_0_, bf16[1024,256]{1,0:T(8,128)(2,1)S(1)} %get-tuple-element.52.refs_1_.own, ...), custom_call_target="tpu_custom_call" | custom-call | flops 67108864 | bytes 2097152 | tf_op jit(solution)/shard_map/pallas_call | solution.py:281
  4.9 2.9 %collective-permute-start.4 = (bf16[32,1024]{1,0:T(8,128)(2,1)S(1)}, bf16[32,1024]{1,0:T(8,128)(2,1)S(1)}, u32[]{:S(2)}, u32[]{:S(2)}) collective-permute-start(bf16[32,1024]{1,0:T(8,128)(2,1)S(1)} %get-tuple-element.60.leave), channel_id=1, source_target_pairs={{0,16},{16,0},{8,24},{24,8},{1,17},{17,1},{9,25},{25,9},{2,18},{18... | collective-permute-start | bytes 196616 | tf_op jit(solution)/shard_map/ppermute | solution.py:481
  7.8 0.0 collective-permute-done.3.expand_other.refs_3_
  7.8 1.2 %shard_map.50 = (bf16[32,1024]{1,0:T(8,128)(2,1)S(1)}, f32[32,256]{1,0:T(8,128)S(1)}, bf16[32,1024]{1,0:T(8,128)(2,1)S(1)}, bf16[32,1024]{1,0:T(8,128)(2,1)S(1)}) custom-call(bf16[1024,256]{1,0:T(8,128)(2,1)S(1)} %get-tuple-element.59.expand_own.refs_1_, bf16[1024,256]{1,0:T(8,128)(2,1)S(1)} %collective-permute-done.3.expand_other.refs_3_, ...), custom_call_target="tpu_custom_call" | custom-call | tf_op jit(solution)/shard_map/pallas_call | solution.py:533
  9.0 0.0 collective-permute-done.2.refs_2_
  9.0 1.2 %collective-permute-done.4.refs_4_ = bf16[32,1024]{1,0:T(8,128)(2,1)S(1)} collective-permute-done((bf16[32,1024]{1,0:T(8,128)(2,1)S(1)}, bf16[32,1024]{1,0:T(8,128)(2,1)S(1)}, u32[]{:S(2)}, u32[]{:S(2)}) %collective-permute-start.4) | collective-permute-done | bytes 65568 | tf_op jit(solution)/shard_map/ppermute | solution.py:481
  10.2 1.8 %shard_map.51 = (bf16[2,32,1280]{2,1,0:T(8,128)(2,1)S(1)}, bf16[2,32,1024]{2,1,0:T(8,128)(2,1)S(1)}, bf16[2,32,256]{2,1,0:T(8,128)(2,1)S(1)}, bf16[32,1024]{1,0:T(8,128)(2,1)S(1)}) custom-call(bf16[1024,256]{1,0:T(8,128)(2,1)S(1)} %get-tuple-element.58.refs_0_, bf16[1024,256]{1,0:T(8,128)(2,1)S(1)} %get-tuple-element.59.expand_own.refs_1_, ...), custom_call_target="tpu_custom_call" | custom-call | flops 134217728 | bytes 2097152 | tf_op jit(solution)/shard_map/pallas_call | solution.py:281
  12.0 2.0 %collective-permute-start.6 = (bf16[32,1024]{1,0:T(8,128)(2,1)S(1)}, bf16[32,1024]{1,0:T(8,128)(2,1)S(1)}, u32[]{:S(2)}, u32[]{:S(2)}) collective-permute-start(bf16[32,1024]{1,0:T(8,128)(2,1)S(1)} %get-tuple-element.65), channel_id=1, source_target_pairs={{0,16},{16,0},{8,24},{24,8},{1,17},{17,1},{9,25},{25,9},{2,18},{18... | collective-permute-start | bytes 196616 | tf_op jit(solution)/shard_map/ppermute | solution.py:481
  14.0 0.1 collective-permute-start.5
  14.2 0.2 collective-permute-start.8
  14.3 2.1 %collective-permute-done.6.refs_4_ = bf16[32,1024]{1,0:T(8,128)(2,1)S(1)} collective-permute-done((bf16[32,1024]{1,0:T(8,128)(2,1)S(1)}, bf16[32,1024]{1,0:T(8,128)(2,1)S(1)}, u32[]{:S(2)}, u32[]{:S(2)}) %collective-permute-start.6) | collective-permute-done | bytes 65568 | tf_op jit(solution)/shard_map/ppermute | solution.py:481
  16.4 0.6 %shard_map.52 = (bf16[2,32,1024]{2,1,0:T(8,128)(2,1)S(1)}, bf16[2,32,256]{2,1,0:T(8,128)(2,1)S(1)}) custom-call(bf16[1024,256]{1,0:T(8,128)(2,1)S(1)} %get-tuple-element.51.own.refs_0_, bf16[1024,256]{1,0:T(8,128)(2,1)S(1)} %get-tuple-element.52.refs_1_.own, bf16[1024,256]{1,0:T(8,128)(2,1)S(1)} %collective-permute-done.other.refs_2_, ...), custom_call_target="tpu_custom_call" | custom-call | flops 67108864 | bytes 2097152 | tf_op jit(solution)/shard_map/pallas_call | solution.py:281
  17.0 0.2 shard_map.54.refs_0_
  17.3 0.1 collective-permute-start.10
  17.4 2.5 %collective-permute-start.11 = (bf16[2,32,256]{2,1,0:T(8,128)(2,1)S(1)}, bf16[2,32,256]{2,1,0:T(8,128)(2,1)S(1)}, u32[]{:S(2)}, u32[]{:S(2)}) collective-permute-start(bf16[2,32,256]{2,1,0:T(8,128)(2,1)S(1)} %broadcast_select_fusion.7), channel_id=1, source_target_pairs={{0,16},{8,24},{16,0},{24,8},{1,17},{9,25},{17,1},{25,9},{2,18},{10... | collective-permute-start | bytes 98312 | tf_op jit(solution)/shard_map/ppermute | solution.py:487
  20.0 0.2 collective-permute-start.7
  20.1 1.8 %collective-permute-done.11 = bf16[2,32,256]{2,1,0:T(8,128)(2,1)S(1)} collective-permute-done((bf16[2,32,256]{2,1,0:T(8,128)(2,1)S(1)}, bf16[2,32,256]{2,1,0:T(8,128)(2,1)S(1)}, u32[]{:S(2)}, u32[]{:S(2)}) %collective-permute-start.11) | collective-permute-done | bytes 32800 | tf_op jit(solution)/shard_map/ppermute | solution.py:487
  21.9 1.9 %collective-permute-start.17 = (bf16[32,1024]{1,0:T(8,128)(2,1)S(1)}, bf16[32,1024]{1,0:T(8,128)(2,1)S(1)}, u32[]{:S(2)}, u32[]{:S(2)}) collective-permute-start(bf16[32,1024]{1,0:T(8,128)(2,1)S(1)} %fusion.1), channel_id=1, source_target_pairs={{0,16},{8,24},{16,0},{24,8},{1,17},{9,25},{17,1},{25,9},{2,18},{10... | collective-permute-start | bytes 196616 | tf_op jit(solution)/shard_map/ppermute | solution.py:487
  23.9 0.0 collective-permute-done.8
  23.9 0.0 collective-permute-start.12
  23.9 2.3 %collective-permute-done.17 = bf16[32,1024]{1,0:T(8,128)(2,1)S(1)} collective-permute-done((bf16[32,1024]{1,0:T(8,128)(2,1)S(1)}, bf16[32,1024]{1,0:T(8,128)(2,1)S(1)}, u32[]{:S(2)}, u32[]{:S(2)}) %collective-permute-start.17) | collective-permute-done | bytes 65568 | tf_op jit(solution)/shard_map/ppermute | solution.py:487
  26.2 0.0 collective-permute-start.9
  26.2 0.6 %collective-permute-start.18 = (bf16[32,1024]{1,0:T(8,128)(2,1)S(1)}, bf16[32,1024]{1,0:T(8,128)(2,1)S(1)}, u32[]{:S(2)}, u32[]{:S(2)}) collective-permute-start(bf16[32,1024]{1,0:T(8,128)(2,1)S(1)} %get-tuple-element.95), channel_id=1, source_target_pairs={{0,8},{8,0},{16,24},{24,16},{1,9},{9,1},{17,25},{25,17},{2,10},{10... | collective-permute-start | bytes 196616 | tf_op jit(solution)/shard_map/ppermute | solution.py:484
  26.8 0.1 shard_map.53
  26.9 1.4 %collective-permute-start.13 = (bf16[64,1280]{1,0:T(8,128)(2,1)S(1)}, bf16[64,1280]{1,0:T(8,128)(2,1)S(1)}, u32[]{:S(2)}, u32[]{:S(2)}) collective-permute-start(bf16[64,1280]{1,0:T(8,128)(2,1)S(1)} %get-tuple-element.79), channel_id=1, source_target_pairs={{0,1},{1,0},{2,3},{3,2},{4,5},{5,4},{6,7},{7,6},{8,10},{9,11},{10,... | collective-permute-start | bytes 491528 | tf_op jit(solution)/shard_map/ppermute | solution.py:628
  28.3 0.1 shard_map.55
  28.4 0.8 %collective-permute-start.14 = (bf16[64,1024]{1,0:T(8,128)(2,1)S(1)}, bf16[64,1024]{1,0:T(8,128)(2,1)S(1)}, u32[]{:S(2)}, u32[]{:S(2)}) collective-permute-start(bf16[64,1024]{1,0:T(8,128)(2,1)S(1)} %get-tuple-element.80), channel_id=1, source_target_pairs={{0,1},{1,0},{2,3},{3,2},{4,5},{5,4},{6,7},{7,6},{8,10},{9,11},{10,... | collective-permute-start | bytes 393224 | tf_op jit(solution)/shard_map/ppermute | solution.py:628
  29.3 1.4 %collective-permute-start.19 = (bf16[64,768]{1,0:T(8,128)(2,1)S(1)}, bf16[64,768]{1,0:T(8,128)(2,1)S(1)}, u32[]{:S(2)}, u32[]{:S(2)}) collective-permute-start(bf16[64,768]{1,0:T(8,128)(2,1)S(1)} %get-tuple-element.90), channel_id=1, source_target_pairs={{0,1},{1,0},{2,3},{3,2},{4,5},{5,4},{6,7},{7,6},{8,10},{9,11},{10,... | collective-permute-start | bytes 294920 | tf_op jit(solution)/shard_map/ppermute | solution.py:628
  30.6 4.1 %collective-permute-done.19.refs_5_ = bf16[64,768]{1,0:T(8,128)(2,1)S(1)} collective-permute-done((bf16[64,768]{1,0:T(8,128)(2,1)S(1)}, bf16[64,768]{1,0:T(8,128)(2,1)S(1)}, u32[]{:S(2)}, u32[]{:S(2)}) %collective-permute-start.19) | collective-permute-done | bytes 98336 | tf_op jit(solution)/shard_map/ppermute | solution.py:628
  34.8 0.3 shard_map.59
  35.1 1.4 %collective-permute-start.20 = (bf16[2,128,256]{2,1,0:T(8,128)(2,1)S(1)}, bf16[2,128,256]{2,1,0:T(8,128)(2,1)S(1)}, u32[]{:S(2)}, u32[]{:S(2)}) collective-permute-start(bf16[2,128,256]{2,1,0:T(8,128)(2,1)S(1)} %get-tuple-element.92), channel_id=1, source_target_pairs={{0,2},{1,3},{2,0},{3,1},{4,6},{5,7},{6,4},{7,5},{8,9},{9,8},{10,11... | collective-permute-start | bytes 393224 | tf_op jit(solution)/shard_map/ppermute | solution.py:628
  36.6 0.3 shard_map.56
  36.9 0.7 %collective-permute-start.15 = (bf16[2,128,256]{2,1,0:T(8,128)(2,1)S(1)}, bf16[2,128,256]{2,1,0:T(8,128)(2,1)S(1)}, u32[]{:S(2)}, u32[]{:S(2)}) collective-permute-start(bf16[2,128,256]{2,1,0:T(8,128)(2,1)S(1)} %get-tuple-element.82), channel_id=1, source_target_pairs={{0,2},{1,3},{2,0},{3,1},{4,6},{5,7},{6,4},{7,5},{8,9},{9,8},{10,11... | collective-permute-start | bytes 393224 | tf_op jit(solution)/shard_map/ppermute | solution.py:628
  37.6 2.5 %collective-permute-done.20.came = bf16[2,128,256]{2,1,0:T(8,128)(2,1)S(1)} collective-permute-done((bf16[2,128,256]{2,1,0:T(8,128)(2,1)S(1)}, bf16[2,128,256]{2,1,0:T(8,128)(2,1)S(1)}, u32[]{:S(2)}, u32[]{:S(2)}) %collective-permute-start.20) | collective-permute-done | bytes 131104 | tf_op jit(solution)/shard_map/ppermute | solution.py:628
  40.2 2.4 %collective-permute-start.21 = (bf16[1,128,256]{2,1,0:T(8,128)(2,1)S(1)}, bf16[1,128,256]{2,1,0:T(8,128)(2,1)S(1)}, u32[]{:S(2)}, u32[]{:S(2)}) collective-permute-start(bf16[1,128,256]{2,1,0:T(8,128)(2,1)S(1)} %get-tuple-element.94), channel_id=1, source_target_pairs={{0,4},{1,5},{2,6},{3,7},{4,0},{5,1},{6,2},{7,3},{8,12},{9,13},{10,... | collective-permute-start | bytes 196616 | tf_op jit(solution)/shard_map/ppermute | solution.py:628
  42.6 0.0 collective-permute-done.15.came
  42.7 2.7 %collective-permute-start.16 = (bf16[1,128,256]{2,1,0:T(8,128)(2,1)S(1)}, bf16[1,128,256]{2,1,0:T(8,128)(2,1)S(1)}, u32[]{:S(2)}, u32[]{:S(2)}) collective-permute-start(bf16[1,128,256]{2,1,0:T(8,128)(2,1)S(1)} %get-tuple-element.84), channel_id=1, source_target_pairs={{0,4},{1,5},{2,6},{3,7},{4,0},{5,1},{6,2},{7,3},{8,12},{9,13},{10,... | collective-permute-start | bytes 196616 | tf_op jit(solution)/shard_map/ppermute | solution.py:628
  45.3 1.5 %collective-permute-done.21.came_expand = bf16[1,128,256]{2,1,0:T(8,128)(2,1)S(1)} collective-permute-done((bf16[1,128,256]{2,1,0:T(8,128)(2,1)S(1)}, bf16[1,128,256]{2,1,0:T(8,128)(2,1)S(1)}, u32[]{:S(2)}, u32[]{:S(2)}) %collective-permute-start.21) | collective-permute-done | bytes 65568 | tf_op jit(solution)/shard_map/ppermute | solution.py:628
  46.8 1.1 %collective-permute-done.16.came_reduce = bf16[1,128,256]{2,1,0:T(8,128)(2,1)S(1)} collective-permute-done((bf16[1,128,256]{2,1,0:T(8,128)(2,1)S(1)}, bf16[1,128,256]{2,1,0:T(8,128)(2,1)S(1)}, u32[]{:S(2)}, u32[]{:S(2)}) %collective-permute-start.16) | collective-permute-done | bytes 65568 | tf_op jit(solution)/shard_map/ppermute | solution.py:628
  47.9 0.7 %shard_map.61 = f32[1,2,128,256]{3,2,1,0:T(8,128)} custom-call(f32[1,128,256]{2,1,0:T(8,128)S(1)} %get-tuple-element.83.keep_reduce, bf16[1,128,256]{2,1,0:T(8,128)(2,1)S(1)} %collective-permute-done.16.came_reduce, f32[1,128,256]{2,1,0:T(8,128)S(1)} %get-tuple-element.93.keep_expand, bf16[1,128,256]{2,1,0:T(8,128)(2,1)S(1)} %collective-permute-done.21.came_expand), custom_call_target="tpu_custom_call" | custom-call | tf_op jit(solution)/shard_map/pallas_call | solution.py:607
  (28 shorter events, 0.3 us)
Async XLA Ops:
  1.2 2.4 %collective-permute-start = (bf16[1024,256]{1,0:T(8,128)(2,1)S(1)}, bf16[1024,256]{1,0:T(8,128)(2,1)S(1)}, u32[]{:S(2)}, u32[]{:S(2)}) collective-permute-start(bf16[1024,256]{1,0:T(8,128)(2,1)S(1)} %get-tuple-element.51.own.refs_0_), channel_id=1, source_target_pairs={{0,8},{8,0},{16,24},{24,16},{1,9},{9,1},{17,25},{25,17},{2,10},{10... | collective-permute-start | bytes 1572872 | tf_op jit(solution)/shard_map/ppermute | solution.py:484
  1.8 2.3 %collective-permute-start.1 = (bf16[1024,256]{1,0:T(8,128)(2,1)S(1)}, bf16[1024,256]{1,0:T(8,128)(2,1)S(1)}, u32[]{:S(2)}, u32[]{:S(2)}) collective-permute-start(bf16[1024,256]{1,0:T(8,128)(2,1)S(1)} %get-tuple-element.52.refs_1_.own), channel_id=1, source_target_pairs={{0,8},{8,0},{16,24},{24,16},{1,9},{9,1},{17,25},{25,17},{2,10},{10... | collective-permute-start | bytes 1572872 | tf_op jit(solution)/shard_map/ppermute | solution.py:484
  3.1 4.7 %collective-permute-start.3 = (bf16[1024,256]{1,0:T(8,128)(2,1)S(1)}, bf16[1024,256]{1,0:T(8,128)(2,1)S(1)}, u32[]{:S(2)}, u32[]{:S(2)}) collective-permute-start(bf16[1024,256]{1,0:T(8,128)(2,1)S(1)} %get-tuple-element.59.expand_own.refs_1_), channel_id=1, source_target_pairs={{0,8},{8,0},{16,24},{24,16},{1,9},{9,1},{17,25},{25,17},{2,10},{10... | collective-permute-start | bytes 1572872 | tf_op jit(solution)/shard_map/ppermute | solution.py:484
  3.6 5.4 %collective-permute-start.2 = (bf16[1024,256]{1,0:T(8,128)(2,1)S(1)}, bf16[1024,256]{1,0:T(8,128)(2,1)S(1)}, u32[]{:S(2)}, u32[]{:S(2)}) collective-permute-start(bf16[1024,256]{1,0:T(8,128)(2,1)S(1)} %get-tuple-element.58.refs_0_), channel_id=1, source_target_pairs={{0,8},{8,0},{16,24},{24,16},{1,9},{9,1},{17,25},{25,17},{2,10},{10... | collective-permute-start | bytes 1572872 | tf_op jit(solution)/shard_map/ppermute | solution.py:484
  4.9 5.3 %collective-permute-start.4 = (bf16[32,1024]{1,0:T(8,128)(2,1)S(1)}, bf16[32,1024]{1,0:T(8,128)(2,1)S(1)}, u32[]{:S(2)}, u32[]{:S(2)}) collective-permute-start(bf16[32,1024]{1,0:T(8,128)(2,1)S(1)} %get-tuple-element.60.leave), channel_id=1, source_target_pairs={{0,16},{16,0},{8,24},{24,8},{1,17},{17,1},{9,25},{25,9},{2,18},{18... | collective-permute-start | bytes 196616 | tf_op jit(solution)/shard_map/ppermute | solution.py:481
  12.0 4.4 %collective-permute-start.6 = (bf16[32,1024]{1,0:T(8,128)(2,1)S(1)}, bf16[32,1024]{1,0:T(8,128)(2,1)S(1)}, u32[]{:S(2)}, u32[]{:S(2)}) collective-permute-start(bf16[32,1024]{1,0:T(8,128)(2,1)S(1)} %get-tuple-element.65), channel_id=1, source_target_pairs={{0,16},{16,0},{8,24},{24,8},{1,17},{17,1},{9,25},{25,9},{2,18},{18... | collective-permute-start | bytes 196616 | tf_op jit(solution)/shard_map/ppermute | solution.py:481
  14.0 12.2 %collective-permute-start.5 = (bf16[32,1280]{1,0:T(8,128)(2,1)S(1)}, bf16[32,1280]{1,0:T(8,128)(2,1)S(1)}, u32[]{:S(2)}, u32[]{:S(2)}) collective-permute-start(bf16[32,1280]{1,0:T(8,128)(2,1)S(1)} %fusion), channel_id=1, source_target_pairs={{0,8},{8,0},{16,24},{24,16},{1,9},{9,1},{17,25},{25,17},{2,10},{10... | collective-permute-start | bytes 245768 | tf_op jit(solution)/shard_map/ppermute | solution.py:484
  14.2 9.7 %collective-permute-start.8 = (bf16[32,1536]{1,0:T(8,128)(2,1)S(1)}, bf16[32,1536]{1,0:T(8,128)(2,1)S(1)}, u32[]{:S(2)}, u32[]{:S(2)}) collective-permute-start(bf16[32,1536]{1,0:T(8,128)(2,1)S(1)} %pad_maximum_fusion), channel_id=1, source_target_pairs={{0,16},{8,24},{16,0},{24,8},{1,17},{9,25},{17,1},{25,9},{2,18},{10... | collective-permute-start | bytes 294920 | tf_op jit(solution)/shard_map/ppermute | solution.py:487
  17.3 11.0 %collective-permute-start.10 = (bf16[32,256]{1,0:T(8,128)(2,1)S(1)}, bf16[32,256]{1,0:T(8,128)(2,1)S(1)}, u32[]{:S(2)}, u32[]{:S(2)}) collective-permute-start(bf16[32,256]{1,0:T(8,128)(2,1)S(1)} %fusion.4), channel_id=1, source_target_pairs={{0,8},{8,0},{16,24},{24,16},{1,9},{9,1},{17,25},{25,17},{2,10},{10... | collective-permute-start | bytes 49160 | tf_op jit(solution)/shard_map/ppermute | solution.py:484
  17.4 4.5 %collective-permute-start.11 = (bf16[2,32,256]{2,1,0:T(8,128)(2,1)S(1)}, bf16[2,32,256]{2,1,0:T(8,128)(2,1)S(1)}, u32[]{:S(2)}, u32[]{:S(2)}) collective-permute-start(bf16[2,32,256]{2,1,0:T(8,128)(2,1)S(1)} %broadcast_select_fusion.7), channel_id=1, source_target_pairs={{0,16},{8,24},{16,0},{24,8},{1,17},{9,25},{17,1},{25,9},{2,18},{10... | collective-permute-start | bytes 98312 | tf_op jit(solution)/shard_map/ppermute | solution.py:487
  20.0 6.9 %collective-permute-start.7 = (bf16[32,1024]{1,0:T(8,128)(2,1)S(1)}, bf16[32,1024]{1,0:T(8,128)(2,1)S(1)}, u32[]{:S(2)}, u32[]{:S(2)}) collective-permute-start(bf16[32,1024]{1,0:T(8,128)(2,1)S(1)} %fusion.3), channel_id=1, source_target_pairs={{0,8},{8,0},{16,24},{24,16},{1,9},{9,1},{17,25},{25,17},{2,10},{10... | collective-permute-start | bytes 196616 | tf_op jit(solution)/shard_map/ppermute | solution.py:484
  21.9 4.3 %collective-permute-start.17 = (bf16[32,1024]{1,0:T(8,128)(2,1)S(1)}, bf16[32,1024]{1,0:T(8,128)(2,1)S(1)}, u32[]{:S(2)}, u32[]{:S(2)}) collective-permute-start(bf16[32,1024]{1,0:T(8,128)(2,1)S(1)} %fusion.1), channel_id=1, source_target_pairs={{0,16},{8,24},{16,0},{24,8},{1,17},{9,25},{17,1},{25,9},{2,18},{10... | collective-permute-start | bytes 196616 | tf_op jit(solution)/shard_map/ppermute | solution.py:487
  23.9 4.4 %collective-permute-start.12 = (bf16[32,256]{1,0:T(8,128)(2,1)S(1)}, bf16[32,256]{1,0:T(8,128)(2,1)S(1)}, u32[]{:S(2)}, u32[]{:S(2)}) collective-permute-start(bf16[32,256]{1,0:T(8,128)(2,1)S(1)} %get-tuple-element.103), channel_id=1, source_target_pairs={{0,8},{8,0},{16,24},{24,16},{1,9},{9,1},{17,25},{25,17},{2,10},{10... | collective-permute-start | bytes 49160 | tf_op jit(solution)/shard_map/ppermute | solution.py:484
  26.2 2.1 %collective-permute-start.9 = (bf16[32,1280]{1,0:T(8,128)(2,1)S(1)}, bf16[32,1280]{1,0:T(8,128)(2,1)S(1)}, u32[]{:S(2)}, u32[]{:S(2)}) collective-permute-start(bf16[32,1280]{1,0:T(8,128)(2,1)S(1)} %pad_maximum_fusion.2), channel_id=1, source_target_pairs={{0,8},{8,0},{16,24},{24,16},{1,9},{9,1},{17,25},{25,17},{2,10},{10... | collective-permute-start | bytes 245768 | tf_op jit(solution)/shard_map/ppermute | solution.py:484
  26.2 3.0 %collective-permute-start.18 = (bf16[32,1024]{1,0:T(8,128)(2,1)S(1)}, bf16[32,1024]{1,0:T(8,128)(2,1)S(1)}, u32[]{:S(2)}, u32[]{:S(2)}) collective-permute-start(bf16[32,1024]{1,0:T(8,128)(2,1)S(1)} %get-tuple-element.95), channel_id=1, source_target_pairs={{0,8},{8,0},{16,24},{24,16},{1,9},{9,1},{17,25},{25,17},{2,10},{10... | collective-permute-start | bytes 196616 | tf_op jit(solution)/shard_map/ppermute | solution.py:484
  26.9 7.8 %collective-permute-start.13 = (bf16[64,1280]{1,0:T(8,128)(2,1)S(1)}, bf16[64,1280]{1,0:T(8,128)(2,1)S(1)}, u32[]{:S(2)}, u32[]{:S(2)}) collective-permute-start(bf16[64,1280]{1,0:T(8,128)(2,1)S(1)} %get-tuple-element.79), channel_id=1, source_target_pairs={{0,1},{1,0},{2,3},{3,2},{4,5},{5,4},{6,7},{7,6},{8,10},{9,11},{10,... | collective-permute-start | bytes 491528 | tf_op jit(solution)/shard_map/ppermute | solution.py:628
  28.4 8.1 %collective-permute-start.14 = (bf16[64,1024]{1,0:T(8,128)(2,1)S(1)}, bf16[64,1024]{1,0:T(8,128)(2,1)S(1)}, u32[]{:S(2)}, u32[]{:S(2)}) collective-permute-start(bf16[64,1024]{1,0:T(8,128)(2,1)S(1)} %get-tuple-element.80), channel_id=1, source_target_pairs={{0,1},{1,0},{2,3},{3,2},{4,5},{5,4},{6,7},{7,6},{8,10},{9,11},{10,... | collective-permute-start | bytes 393224 | tf_op jit(solution)/shard_map/ppermute | solution.py:628
  29.3 5.5 %collective-permute-start.19 = (bf16[64,768]{1,0:T(8,128)(2,1)S(1)}, bf16[64,768]{1,0:T(8,128)(2,1)S(1)}, u32[]{:S(2)}, u32[]{:S(2)}) collective-permute-start(bf16[64,768]{1,0:T(8,128)(2,1)S(1)} %get-tuple-element.90), channel_id=1, source_target_pairs={{0,1},{1,0},{2,3},{3,2},{4,5},{5,4},{6,7},{7,6},{8,10},{9,11},{10,... | collective-permute-start | bytes 294920 | tf_op jit(solution)/shard_map/ppermute | solution.py:628
  35.1 5.0 %collective-permute-start.20 = (bf16[2,128,256]{2,1,0:T(8,128)(2,1)S(1)}, bf16[2,128,256]{2,1,0:T(8,128)(2,1)S(1)}, u32[]{:S(2)}, u32[]{:S(2)}) collective-permute-start(bf16[2,128,256]{2,1,0:T(8,128)(2,1)S(1)} %get-tuple-element.92), channel_id=1, source_target_pairs={{0,2},{1,3},{2,0},{3,1},{4,6},{5,7},{6,4},{7,5},{8,9},{9,8},{10,11... | collective-permute-start | bytes 393224 | tf_op jit(solution)/shard_map/ppermute | solution.py:628
  36.9 5.7 %collective-permute-start.15 = (bf16[2,128,256]{2,1,0:T(8,128)(2,1)S(1)}, bf16[2,128,256]{2,1,0:T(8,128)(2,1)S(1)}, u32[]{:S(2)}, u32[]{:S(2)}) collective-permute-start(bf16[2,128,256]{2,1,0:T(8,128)(2,1)S(1)} %get-tuple-element.82), channel_id=1, source_target_pairs={{0,2},{1,3},{2,0},{3,1},{4,6},{5,7},{6,4},{7,5},{8,9},{9,8},{10,11... | collective-permute-start | bytes 393224 | tf_op jit(solution)/shard_map/ppermute | solution.py:628
  40.2 6.6 %collective-permute-start.21 = (bf16[1,128,256]{2,1,0:T(8,128)(2,1)S(1)}, bf16[1,128,256]{2,1,0:T(8,128)(2,1)S(1)}, u32[]{:S(2)}, u32[]{:S(2)}) collective-permute-start(bf16[1,128,256]{2,1,0:T(8,128)(2,1)S(1)} %get-tuple-element.94), channel_id=1, source_target_pairs={{0,4},{1,5},{2,6},{3,7},{4,0},{5,1},{6,2},{7,3},{8,12},{9,13},{10,... | collective-permute-start | bytes 196616 | tf_op jit(solution)/shard_map/ppermute | solution.py:628
  42.7 5.2 %collective-permute-start.16 = (bf16[1,128,256]{2,1,0:T(8,128)(2,1)S(1)}, bf16[1,128,256]{2,1,0:T(8,128)(2,1)S(1)}, u32[]{:S(2)}, u32[]{:S(2)}) collective-permute-start(bf16[1,128,256]{2,1,0:T(8,128)(2,1)S(1)} %get-tuple-element.84), channel_id=1, source_target_pairs={{0,4},{1,5},{2,6},{3,7},{4,0},{5,1},{6,2},{7,3},{8,12},{9,13},{10,... | collective-permute-start | bytes 196616 | tf_op jit(solution)/shard_map/ppermute | solution.py:628

commit v10 on v9

--- a/solution.py
+++ b/solution.py
@@ -391,37 +391,36 @@
     target[rows:] = other[:, span]
 
 
-def near_up_body(stages, chunk, *refs):
-    flows, ups = refs[: stages + 1], refs[stages + 1 : 2 * stages + 2]
-    up, active, lifted, send, wide = refs[2 * stages + 2 :]
+def early_body(stages, chunk, *refs):
+    count = stages + 1
+    flows, far, ups = refs[:count], refs[count : count + 2], refs[count + 2 : 2 * count + 2]
+    up, active, lifted, far_active, far_lifted, send, wide = refs[2 * count + 2 :]
     half, channels = up.shape[1], wide.shape[1]
     inner = active.shape[1]
     take_rows(wide, slice(None), *ups)
     split_columns(wide, up, send.at[:, :half], chunk)
-    take_rows(active, slice(channels, None), *flows)
-    send[:, half : half + inner] = active[...]
-    take_rows(wide, slice(0, channels), *flows)
-    split_columns(wide, lifted, send.at[:, half + inner :], chunk)
-
-
-def late_up_body(chunk, flow, cross_flow, far, cross, up, active, send, wide):
-    half, channels = up.shape[1], wide.shape[1]
+    start = half
+    for sources, narrow, broad in ((flows, active, lifted), (far, far_active, far_lifted)):
+        take_rows(narrow, slice(channels, None), *sources)
+        send[:, start : start + inner] = narrow[...]
+        start += inner
+        take_rows(wide, slice(0, channels), *sources)
+        split_columns(wide, broad, send.at[:, start : start + half], chunk)
+        start += half
+
+
+def late_up_body(chunk, far, cross, up, send, wide):
     take_rows(wide, slice(None), far, cross)
-    split_columns(wide, up, send.at[:, :half], chunk)
-    take_rows(active, slice(channels, None), flow, cross_flow)
-    send[:, half:] = active[...]
-
-
-def late_inner_body(chunk, flow, cross_flow, *refs):
-    *backs, far, cross, lifted, far_inner, near_inner, send, wide = refs
-    half, channels = lifted.shape[1], wide.shape[1]
+    split_columns(wide, up, send, chunk)
+
+
+def late_inner_body(*refs):
+    *backs, far, cross, far_inner, near_inner, send, _ = refs
     inner = far_inner.shape[1]
-    take_rows(wide, slice(0, channels), flow, cross_flow)
-    split_columns(wide, lifted, send.at[:, :half], chunk)
     take_rows(far_inner, slice(None), far, cross)
-    send[:, half : half + inner] = far_inner[...]
+    send[:, :inner] = far_inner[...]
     take_rows(near_inner, slice(None), *backs)
-    send[:, half + inner :] = near_inner[...]
+    send[:, inner:] = near_inner[...]
 
 
 def half_gradient_body(starts, *refs):
@@ -643,40 +642,30 @@
             compiler_params=PARAMS,
         )(*arrays)
 
-    near_up, near_active, near_lifted, send = pack(
-        functools.partial(near_up_body, stages, chunk),
-        fore[:count] + ups[:count],
+    near_up, near_active, near_lifted, far_active, far_lifted, send = pack(
+        functools.partial(early_body, stages, chunk),
+        fore + ups[:count],
         half,
         inner,
         half,
-        2 * half + inner,
+        inner,
+        half,
+        3 * half + 2 * inner,
     )
     came_near = exchange(send, stages, replicas, 1, 2)
-    far_up, far_active, send = pack(
-        functools.partial(late_up_body, chunk),
-        fore[count:] + ups[count:],
-        half,
-        inner,
-        half + inner,
-    )
+    far_up, send = pack(functools.partial(late_up_body, chunk), ups[count:], half, half)
     came_up = exchange(send, stages, replicas, 1, 2)
-    far_lifted, far_inner, near_inner, send = pack(
-        functools.partial(late_inner_body, chunk),
-        fore[count:] + backs,
-        half,
-        inner,
-        inner,
-        half + 2 * inner,
-    )
+    far_inner, near_inner, send = pack(late_inner_body, backs, inner, inner, 2 * inner)
     came_inner = exchange(send, stages, replicas, 1, 2)
+    step = half + inner
     streams = (
         (
             (near_lifted, far_lifted, near_inner, far_inner, came_near, came_inner),
-            (((0, half + inner), (1, half + inner)), ((1, 0), (1, half))),
+            (((0, step), (1, inner)), ((0, 2 * step), (1, 0))),
         ),
         (
             (near_up, far_up, near_active, far_active, came_near, came_up),
-            (((0, 0), (0, half)), ((1, 0), (1, half))),
+            (((0, 0), (0, half)), ((1, 0), (0, half + step))),
         ),
     )
     parts = []

time: 48.8 us -> 47.1 us (0.965)
  starting transfers between devices: 22.4 us -> 20.8 us
    ppermute x3, starting transfers between devices: 4.67 us -> 3.09 us  [mirror(): return lax.ppermute(shard, 'pipe', mirror_pairs)]
    ppermute x7, waiting for transfers between devices: 9.27 us -> 8.53 us  [exchange(): return lax.ppermute(shard, AXES, pairs)]
    ppermute x10, waiting for transfers between devices: 0.09 us -> 0.76 us  [swap_cores(): return lax.ppermute(shard, 'pipe', core_pairs)]
where the time goes in v10:
time: 47.1 us; the launch traced here: 46.9 us
  starting transfers between devices  20.8 us (44%)
  waiting for transfers between devices  16.5 us (35%)
  Pallas kernels  9.12 us (19%)
    ppermute x7, starting transfers between devices, exchange(): return lax.ppermute(shard, AXES, pairs)  10.8 us
    ppermute x7, waiting for transfers between devices, exchange(): return lax.ppermute(shard, AXES, pairs)  8.53 us
    ppermute x2, starting transfers between devices, hop(): return lax.ppermute(shard, 'pipe', pairs)  4.86 us
    ppermute x3, waiting for transfers between devices, mirror(): return lax.ppermute(shard, 'pipe', mirror_pairs)  4.03 us
    pallas_call x3, Pallas kernels, run_stage(): pl.pallas_call(functools.partial(stage_body, step, forward, backward, las...  3.26 us
    ppermute x2, waiting for transfers between devices, hop(): return lax.ppermute(shard, 'pipe', pairs)  3.23 us
    ppermute x3, starting transfers between devices, mirror(): return lax.ppermute(shard, 'pipe', mirror_pairs)  3.09 us
    pallas_call x2, Pallas kernels, load(): pl.pallas_call(functools.partial(load_body, step), out_shape=outs, in_spe...  2.44 us
  transfers between devices with their start and end apart: 22, of which 9 were waited for; matrix products, arithmetic and copies ran while one was open for 0% of the time, Pallas kernels for 11%

profile of v10, /device:TPU:0, one launch (start us, length us, event | category | flops | bytes accessed | tf_op | source)
XLA Modules:
  0.0 46.9 jit_solution(1988966286570978065)
XLA Ops:
  0.0 1.2 %shard_map.46 = (bf16[1024,256]{1,0:T(8,128)(2,1)S(1)}, bf16[1024,256]{1,0:T(8,128)(2,1)S(1)}, bf16[32,1024]{1,0:T(8,128)(2,1)S(1)}) custom-call(bf16[2,1024,256]{2,1,0:T(8,128)(2,1)} %bitcast.20, bf16[2,1024,256]{2,1,0:T(8,128)(2,1)} %bitcast.22, bf16[2,2,32,1024]{3,2,1,0:T(8,128)(2,1)} %inputs), custom_call_target="tpu_custom_call" | custom-call | tf_op jit(solution)/shard_map/pallas_call | solution.py:68
  1.2 0.6 %collective-permute-start = (bf16[1024,256]{1,0:T(8,128)(2,1)S(1)}, bf16[1024,256]{1,0:T(8,128)(2,1)S(1)}, u32[]{:S(2)}, u32[]{:S(2)}) collective-permute-start(bf16[1024,256]{1,0:T(8,128)(2,1)S(1)} %get-tuple-element.51.own.refs_0_), channel_id=1, source_target_pairs={{0,8},{8,0},{16,24},{24,16},{1,9},{9,1},{17,25},{25,17},{2,10},{10... | collective-permute-start | bytes 1572872 | tf_op jit(solution)/shard_map/ppermute | solution.py:483
  1.8 0.1 collective-permute-start.1
  1.9 1.2 %shard_map.49 = (bf16[1024,256]{1,0:T(8,128)(2,1)S(1)}, bf16[1024,256]{1,0:T(8,128)(2,1)S(1)}) custom-call(bf16[2,1024,256]{2,1,0:T(8,128)(2,1)} %bitcast.21, bf16[2,1024,256]{2,1,0:T(8,128)(2,1)} %bitcast.23), custom_call_target="tpu_custom_call" | custom-call | tf_op jit(solution)/shard_map/pallas_call | solution.py:68
  3.1 0.5 %collective-permute-start.3 = (bf16[1024,256]{1,0:T(8,128)(2,1)S(1)}, bf16[1024,256]{1,0:T(8,128)(2,1)S(1)}, u32[]{:S(2)}, u32[]{:S(2)}) collective-permute-start(bf16[1024,256]{1,0:T(8,128)(2,1)S(1)} %get-tuple-element.59.expand_own.refs_1_), channel_id=1, source_target_pairs={{0,8},{8,0},{16,24},{24,16},{1,9},{9,1},{17,25},{25,17},{2,10},{10... | collective-permute-start | bytes 1572872 | tf_op jit(solution)/shard_map/ppermute | solution.py:483
  3.6 0.1 collective-permute-start.2
  3.7 0.3 shard_map.47
  4.0 0.1 collective-permute-done.1.refs_3_.other
  4.1 0.8 %shard_map.48 = (bf16[2,32,1280]{2,1,0:T(8,128)(2,1)S(1)}, bf16[32,1024]{1,0:T(8,128)(2,1)S(1)}, bf16[2,32,1024]{2,1,0:T(8,128)(2,1)S(1)}, f32[2,32,256]{2,1,0:T(8,128)S(1)}) custom-call(bf16[1024,256]{1,0:T(8,128)(2,1)S(1)} %get-tuple-element.51.own.refs_0_, bf16[1024,256]{1,0:T(8,128)(2,1)S(1)} %get-tuple-element.52.refs_1_.own, ...), custom_call_target="tpu_custom_call" | custom-call | flops 67108864 | bytes 2097152 | tf_op jit(solution)/shard_map/pallas_call | solution.py:281
  4.9 2.9 %collective-permute-start.4 = (bf16[32,1024]{1,0:T(8,128)(2,1)S(1)}, bf16[32,1024]{1,0:T(8,128)(2,1)S(1)}, u32[]{:S(2)}, u32[]{:S(2)}) collective-permute-start(bf16[32,1024]{1,0:T(8,128)(2,1)S(1)} %get-tuple-element.60.leave), channel_id=1, source_target_pairs={{0,16},{16,0},{8,24},{24,8},{1,17},{17,1},{9,25},{25,9},{2,18},{18... | collective-permute-start | bytes 196616 | tf_op jit(solution)/shard_map/ppermute | solution.py:480
  7.8 0.0 collective-permute-done.3.expand_other.refs_3_
  7.8 1.2 %shard_map.50 = (bf16[32,1024]{1,0:T(8,128)(2,1)S(1)}, f32[32,256]{1,0:T(8,128)S(1)}, bf16[32,1024]{1,0:T(8,128)(2,1)S(1)}, bf16[32,1024]{1,0:T(8,128)(2,1)S(1)}) custom-call(bf16[1024,256]{1,0:T(8,128)(2,1)S(1)} %get-tuple-element.59.expand_own.refs_1_, bf16[1024,256]{1,0:T(8,128)(2,1)S(1)} %collective-permute-done.3.expand_other.refs_3_, ...), custom_call_target="tpu_custom_call" | custom-call | tf_op jit(solution)/shard_map/pallas_call | solution.py:532
  9.0 0.0 collective-permute-done.2.refs_2_
  9.0 1.2 %collective-permute-done.4.refs_4_ = bf16[32,1024]{1,0:T(8,128)(2,1)S(1)} collective-permute-done((bf16[32,1024]{1,0:T(8,128)(2,1)S(1)}, bf16[32,1024]{1,0:T(8,128)(2,1)S(1)}, u32[]{:S(2)}, u32[]{:S(2)}) %collective-permute-start.4) | collective-permute-done | bytes 65568 | tf_op jit(solution)/shard_map/ppermute | solution.py:480
  10.2 1.8 %shard_map.51 = (bf16[2,32,1280]{2,1,0:T(8,128)(2,1)S(1)}, bf16[2,32,1024]{2,1,0:T(8,128)(2,1)S(1)}, bf16[2,32,256]{2,1,0:T(8,128)(2,1)S(1)}, bf16[32,1024]{1,0:T(8,128)(2,1)S(1)}) custom-call(bf16[1024,256]{1,0:T(8,128)(2,1)S(1)} %get-tuple-element.58.refs_0_, bf16[1024,256]{1,0:T(8,128)(2,1)S(1)} %get-tuple-element.59.expand_own.refs_1_, ...), custom_call_target="tpu_custom_call" | custom-call | flops 134217728 | bytes 2097152 | tf_op jit(solution)/shard_map/pallas_call | solution.py:281
  12.0 2.0 %collective-permute-start.8 = (bf16[32,1024]{1,0:T(8,128)(2,1)S(1)}, bf16[32,1024]{1,0:T(8,128)(2,1)S(1)}, u32[]{:S(2)}, u32[]{:S(2)}) collective-permute-start(bf16[32,1024]{1,0:T(8,128)(2,1)S(1)} %get-tuple-element.68), channel_id=1, source_target_pairs={{0,16},{16,0},{8,24},{24,8},{1,17},{17,1},{9,25},{25,9},{2,18},{18... | collective-permute-start | bytes 196616 | tf_op jit(solution)/shard_map/ppermute | solution.py:480
  14.0 0.1 collective-permute-start.5
  14.2 0.2 collective-permute-start.6
  14.3 2.1 %collective-permute-done.8.refs_4_ = bf16[32,1024]{1,0:T(8,128)(2,1)S(1)} collective-permute-done((bf16[32,1024]{1,0:T(8,128)(2,1)S(1)}, bf16[32,1024]{1,0:T(8,128)(2,1)S(1)}, u32[]{:S(2)}, u32[]{:S(2)}) %collective-permute-start.8) | collective-permute-done | bytes 65568 | tf_op jit(solution)/shard_map/ppermute | solution.py:480
  16.4 0.6 %shard_map.52 = (bf16[2,32,1024]{2,1,0:T(8,128)(2,1)S(1)}, bf16[2,32,256]{2,1,0:T(8,128)(2,1)S(1)}) custom-call(bf16[1024,256]{1,0:T(8,128)(2,1)S(1)} %get-tuple-element.51.own.refs_0_, bf16[1024,256]{1,0:T(8,128)(2,1)S(1)} %get-tuple-element.52.refs_1_.own, bf16[1024,256]{1,0:T(8,128)(2,1)S(1)} %collective-permute-done.other.refs_2_, ...), custom_call_target="tpu_custom_call" | custom-call | flops 67108864 | bytes 2097152 | tf_op jit(solution)/shard_map/pallas_call | solution.py:281
  17.0 0.2 shard_map.54.refs_0_
  17.3 0.1 collective-permute-start.10
  17.4 2.5 %collective-permute-start.11 = (bf16[2,32,256]{2,1,0:T(8,128)(2,1)S(1)}, bf16[2,32,256]{2,1,0:T(8,128)(2,1)S(1)}, u32[]{:S(2)}, u32[]{:S(2)}) collective-permute-start(bf16[2,32,256]{2,1,0:T(8,128)(2,1)S(1)} %broadcast_select_fusion.7), channel_id=1, source_target_pairs={{0,16},{8,24},{16,0},{24,8},{1,17},{9,25},{17,1},{25,9},{2,18},{10... | collective-permute-start | bytes 98312 | tf_op jit(solution)/shard_map/ppermute | solution.py:486
  20.0 0.2 collective-permute-start.9
  20.1 0.3 collective-permute-start.17
  20.5 4.0 %collective-permute-done.17 = bf16[32,1024]{1,0:T(8,128)(2,1)S(1)} collective-permute-done((bf16[32,1024]{1,0:T(8,128)(2,1)S(1)}, bf16[32,1024]{1,0:T(8,128)(2,1)S(1)}, u32[]{:S(2)}, u32[]{:S(2)}) %collective-permute-start.17) | collective-permute-done | bytes 65568 | tf_op jit(solution)/shard_map/ppermute | solution.py:486
  24.6 0.0 collective-permute-start.7
  24.6 0.0 collective-permute-done.5.refs_2_
  24.6 0.6 %collective-permute-start.18 = (bf16[32,1024]{1,0:T(8,128)(2,1)S(1)}, bf16[32,1024]{1,0:T(8,128)(2,1)S(1)}, u32[]{:S(2)}, u32[]{:S(2)}) collective-permute-start(bf16[32,1024]{1,0:T(8,128)(2,1)S(1)} %get-tuple-element.95), channel_id=1, source_target_pairs={{0,8},{8,0},{16,24},{24,16},{1,9},{9,1},{17,25},{25,17},{2,10},{10... | collective-permute-start | bytes 196616 | tf_op jit(solution)/shard_map/ppermute | solution.py:483
  25.2 0.7 %collective-permute-done.7.refs_4_ = bf16[32,1280]{1,0:T(8,128)(2,1)S(1)} collective-permute-done((bf16[32,1280]{1,0:T(8,128)(2,1)S(1)}, bf16[32,1280]{1,0:T(8,128)(2,1)S(1)}, u32[]{:S(2)}, u32[]{:S(2)}) %collective-permute-start.7) | collective-permute-done | bytes 81952 | tf_op jit(solution)/shard_map/ppermute | solution.py:483
  25.8 0.1 shard_map.53
  26.0 1.3 %collective-permute-start.13 = (bf16[64,2048]{1,0:T(8,128)(2,1)S(1)}, bf16[64,2048]{1,0:T(8,128)(2,1)S(1)}, u32[]{:S(2)}, u32[]{:S(2)}) collective-permute-start(bf16[64,2048]{1,0:T(8,128)(2,1)S(1)} %get-tuple-element.79), channel_id=1, source_target_pairs={{0,1},{1,0},{2,3},{3,2},{4,5},{5,4},{6,7},{7,6},{8,10},{9,11},{10,... | collective-permute-start | bytes 786440 | tf_op jit(solution)/shard_map/ppermute | solution.py:627
  27.3 0.0 collective-permute-done.11
  27.3 0.0 collective-permute-start.12
  27.3 0.1 shard_map.58
  27.4 1.5 %collective-permute-start.19 = (bf16[64,512]{1,0:T(8,128)(2,1)S(1)}, bf16[64,512]{1,0:T(8,128)(2,1)S(1)}, u32[]{:S(2)}, u32[]{:S(2)}) collective-permute-start(bf16[64,512]{1,0:T(8,128)(2,1)S(1)} %get-tuple-element.90), channel_id=1, source_target_pairs={{0,1},{1,0},{2,3},{3,2},{4,5},{5,4},{6,7},{7,6},{8,10},{9,11},{10,... | collective-permute-start | bytes 196616 | tf_op jit(solution)/shard_map/ppermute | solution.py:627
  28.9 0.8 %collective-permute-start.14 = (bf16[64,512]{1,0:T(8,128)(2,1)S(1)}, bf16[64,512]{1,0:T(8,128)(2,1)S(1)}, u32[]{:S(2)}, u32[]{:S(2)}) collective-permute-start(bf16[64,512]{1,0:T(8,128)(2,1)S(1)} %get-tuple-element.80), channel_id=1, source_target_pairs={{0,1},{1,0},{2,3},{3,2},{4,5},{5,4},{6,7},{7,6},{8,10},{9,11},{10,... | collective-permute-start | bytes 196616 | tf_op jit(solution)/shard_map/ppermute | solution.py:627
  29.7 3.4 %collective-permute-done.19.refs_5_ = bf16[64,512]{1,0:T(8,128)(2,1)S(1)} collective-permute-done((bf16[64,512]{1,0:T(8,128)(2,1)S(1)}, bf16[64,512]{1,0:T(8,128)(2,1)S(1)}, u32[]{:S(2)}, u32[]{:S(2)}) %collective-permute-start.19) | collective-permute-done | bytes 65568 | tf_op jit(solution)/shard_map/ppermute | solution.py:627
  33.1 0.3 shard_map.59
  33.5 1.4 %collective-permute-start.20 = (bf16[2,128,256]{2,1,0:T(8,128)(2,1)S(1)}, bf16[2,128,256]{2,1,0:T(8,128)(2,1)S(1)}, u32[]{:S(2)}, u32[]{:S(2)}) collective-permute-start(bf16[2,128,256]{2,1,0:T(8,128)(2,1)S(1)} %get-tuple-element.92), channel_id=1, source_target_pairs={{0,2},{1,3},{2,0},{3,1},{4,6},{5,7},{6,4},{7,5},{8,9},{9,8},{10,11... | collective-permute-start | bytes 393224 | tf_op jit(solution)/shard_map/ppermute | solution.py:627
  34.9 0.3 shard_map.56
  35.2 0.8 %collective-permute-start.15 = (bf16[2,128,256]{2,1,0:T(8,128)(2,1)S(1)}, bf16[2,128,256]{2,1,0:T(8,128)(2,1)S(1)}, u32[]{:S(2)}, u32[]{:S(2)}) collective-permute-start(bf16[2,128,256]{2,1,0:T(8,128)(2,1)S(1)} %get-tuple-element.82), channel_id=1, source_target_pairs={{0,2},{1,3},{2,0},{3,1},{4,6},{5,7},{6,4},{7,5},{8,9},{9,8},{10,11... | collective-permute-start | bytes 393224 | tf_op jit(solution)/shard_map/ppermute | solution.py:627
  36.0 2.5 %collective-permute-done.20.came = bf16[2,128,256]{2,1,0:T(8,128)(2,1)S(1)} collective-permute-done((bf16[2,128,256]{2,1,0:T(8,128)(2,1)S(1)}, bf16[2,128,256]{2,1,0:T(8,128)(2,1)S(1)}, u32[]{:S(2)}, u32[]{:S(2)}) %collective-permute-start.20) | collective-permute-done | bytes 131104 | tf_op jit(solution)/shard_map/ppermute | solution.py:627
  38.5 2.4 %collective-permute-start.21 = (bf16[1,128,256]{2,1,0:T(8,128)(2,1)S(1)}, bf16[1,128,256]{2,1,0:T(8,128)(2,1)S(1)}, u32[]{:S(2)}, u32[]{:S(2)}) collective-permute-start(bf16[1,128,256]{2,1,0:T(8,128)(2,1)S(1)} %get-tuple-element.94), channel_id=1, source_target_pairs={{0,4},{1,5},{2,6},{3,7},{4,0},{5,1},{6,2},{7,3},{8,12},{9,13},{10,... | collective-permute-start | bytes 196616 | tf_op jit(solution)/shard_map/ppermute | solution.py:627
  41.0 2.7 %collective-permute-start.16 = (bf16[1,128,256]{2,1,0:T(8,128)(2,1)S(1)}, bf16[1,128,256]{2,1,0:T(8,128)(2,1)S(1)}, u32[]{:S(2)}, u32[]{:S(2)}) collective-permute-start(bf16[1,128,256]{2,1,0:T(8,128)(2,1)S(1)} %get-tuple-element.84), channel_id=1, source_target_pairs={{0,4},{1,5},{2,6},{3,7},{4,0},{5,1},{6,2},{7,3},{8,12},{9,13},{10,... | collective-permute-start | bytes 196616 | tf_op jit(solution)/shard_map/ppermute | solution.py:627
  43.6 1.6 %collective-permute-done.21.came_expand = bf16[1,128,256]{2,1,0:T(8,128)(2,1)S(1)} collective-permute-done((bf16[1,128,256]{2,1,0:T(8,128)(2,1)S(1)}, bf16[1,128,256]{2,1,0:T(8,128)(2,1)S(1)}, u32[]{:S(2)}, u32[]{:S(2)}) %collective-permute-start.21) | collective-permute-done | bytes 65568 | tf_op jit(solution)/shard_map/ppermute | solution.py:627
  45.2 1.0 %collective-permute-done.16.came_reduce = bf16[1,128,256]{2,1,0:T(8,128)(2,1)S(1)} collective-permute-done((bf16[1,128,256]{2,1,0:T(8,128)(2,1)S(1)}, bf16[1,128,256]{2,1,0:T(8,128)(2,1)S(1)}, u32[]{:S(2)}, u32[]{:S(2)}) %collective-permute-start.16) | collective-permute-done | bytes 65568 | tf_op jit(solution)/shard_map/ppermute | solution.py:627
  46.2 0.7 %shard_map.61 = f32[1,2,128,256]{3,2,1,0:T(8,128)} custom-call(f32[1,128,256]{2,1,0:T(8,128)S(1)} %get-tuple-element.83.keep_reduce, bf16[1,128,256]{2,1,0:T(8,128)(2,1)S(1)} %collective-permute-done.16.came_reduce, f32[1,128,256]{2,1,0:T(8,128)S(1)} %get-tuple-element.93.keep_expand, bf16[1,128,256]{2,1,0:T(8,128)(2,1)S(1)} %collective-permute-done.21.came_expand), custom_call_target="tpu_custom_call" | custom-call | tf_op jit(solution)/shard_map/pallas_call | solution.py:606
  (28 shorter events, 0.2 us)
Async XLA Ops:
  1.2 2.4 %collective-permute-start = (bf16[1024,256]{1,0:T(8,128)(2,1)S(1)}, bf16[1024,256]{1,0:T(8,128)(2,1)S(1)}, u32[]{:S(2)}, u32[]{:S(2)}) collective-permute-start(bf16[1024,256]{1,0:T(8,128)(2,1)S(1)} %get-tuple-element.51.own.refs_0_), channel_id=1, source_target_pairs={{0,8},{8,0},{16,24},{24,16},{1,9},{9,1},{17,25},{25,17},{2,10},{10... | collective-permute-start | bytes 1572872 | tf_op jit(solution)/shard_map/ppermute | solution.py:483
  1.8 2.3 %collective-permute-start.1 = (bf16[1024,256]{1,0:T(8,128)(2,1)S(1)}, bf16[1024,256]{1,0:T(8,128)(2,1)S(1)}, u32[]{:S(2)}, u32[]{:S(2)}) collective-permute-start(bf16[1024,256]{1,0:T(8,128)(2,1)S(1)} %get-tuple-element.52.refs_1_.own), channel_id=1, source_target_pairs={{0,8},{8,0},{16,24},{24,16},{1,9},{9,1},{17,25},{25,17},{2,10},{10... | collective-permute-start | bytes 1572872 | tf_op jit(solution)/shard_map/ppermute | solution.py:483
  3.1 4.7 %collective-permute-start.3 = (bf16[1024,256]{1,0:T(8,128)(2,1)S(1)}, bf16[1024,256]{1,0:T(8,128)(2,1)S(1)}, u32[]{:S(2)}, u32[]{:S(2)}) collective-permute-start(bf16[1024,256]{1,0:T(8,128)(2,1)S(1)} %get-tuple-element.59.expand_own.refs_1_), channel_id=1, source_target_pairs={{0,8},{8,0},{16,24},{24,16},{1,9},{9,1},{17,25},{25,17},{2,10},{10... | collective-permute-start | bytes 1572872 | tf_op jit(solution)/shard_map/ppermute | solution.py:483
  3.6 5.4 %collective-permute-start.2 = (bf16[1024,256]{1,0:T(8,128)(2,1)S(1)}, bf16[1024,256]{1,0:T(8,128)(2,1)S(1)}, u32[]{:S(2)}, u32[]{:S(2)}) collective-permute-start(bf16[1024,256]{1,0:T(8,128)(2,1)S(1)} %get-tuple-element.58.refs_0_), channel_id=1, source_target_pairs={{0,8},{8,0},{16,24},{24,16},{1,9},{9,1},{17,25},{25,17},{2,10},{10... | collective-permute-start | bytes 1572872 | tf_op jit(solution)/shard_map/ppermute | solution.py:483
  4.9 5.3 %collective-permute-start.4 = (bf16[32,1024]{1,0:T(8,128)(2,1)S(1)}, bf16[32,1024]{1,0:T(8,128)(2,1)S(1)}, u32[]{:S(2)}, u32[]{:S(2)}) collective-permute-start(bf16[32,1024]{1,0:T(8,128)(2,1)S(1)} %get-tuple-element.60.leave), channel_id=1, source_target_pairs={{0,16},{16,0},{8,24},{24,8},{1,17},{17,1},{9,25},{25,9},{2,18},{18... | collective-permute-start | bytes 196616 | tf_op jit(solution)/shard_map/ppermute | solution.py:480
  12.0 4.4 %collective-permute-start.8 = (bf16[32,1024]{1,0:T(8,128)(2,1)S(1)}, bf16[32,1024]{1,0:T(8,128)(2,1)S(1)}, u32[]{:S(2)}, u32[]{:S(2)}) collective-permute-start(bf16[32,1024]{1,0:T(8,128)(2,1)S(1)} %get-tuple-element.68), channel_id=1, source_target_pairs={{0,16},{16,0},{8,24},{24,8},{1,17},{17,1},{9,25},{25,9},{2,18},{18... | collective-permute-start | bytes 196616 | tf_op jit(solution)/shard_map/ppermute | solution.py:480
  14.0 10.6 %collective-permute-start.5 = (bf16[32,1280]{1,0:T(8,128)(2,1)S(1)}, bf16[32,1280]{1,0:T(8,128)(2,1)S(1)}, u32[]{:S(2)}, u32[]{:S(2)}) collective-permute-start(bf16[32,1280]{1,0:T(8,128)(2,1)S(1)} %fusion), channel_id=1, source_target_pairs={{0,8},{8,0},{16,24},{24,16},{1,9},{9,1},{17,25},{25,17},{2,10},{10... | collective-permute-start | bytes 245768 | tf_op jit(solution)/shard_map/ppermute | solution.py:483
  14.2 6.0 %collective-permute-start.6 = (bf16[32,1536]{1,0:T(8,128)(2,1)S(1)}, bf16[32,1536]{1,0:T(8,128)(2,1)S(1)}, u32[]{:S(2)}, u32[]{:S(2)}) collective-permute-start(bf16[32,1536]{1,0:T(8,128)(2,1)S(1)} %pad_maximum_fusion), channel_id=1, source_target_pairs={{0,16},{8,24},{16,0},{24,8},{1,17},{9,25},{17,1},{25,9},{2,18},{10... | collective-permute-start | bytes 294920 | tf_op jit(solution)/shard_map/ppermute | solution.py:486
  17.3 11.6 %collective-permute-start.10 = (bf16[32,256]{1,0:T(8,128)(2,1)S(1)}, bf16[32,256]{1,0:T(8,128)(2,1)S(1)}, u32[]{:S(2)}, u32[]{:S(2)}) collective-permute-start(bf16[32,256]{1,0:T(8,128)(2,1)S(1)} %fusion.4), channel_id=1, source_target_pairs={{0,8},{8,0},{16,24},{24,16},{1,9},{9,1},{17,25},{25,17},{2,10},{10... | collective-permute-start | bytes 49160 | tf_op jit(solution)/shard_map/ppermute | solution.py:483
  17.4 9.9 %collective-permute-start.11 = (bf16[2,32,256]{2,1,0:T(8,128)(2,1)S(1)}, bf16[2,32,256]{2,1,0:T(8,128)(2,1)S(1)}, u32[]{:S(2)}, u32[]{:S(2)}) collective-permute-start(bf16[2,32,256]{2,1,0:T(8,128)(2,1)S(1)} %broadcast_select_fusion.7), channel_id=1, source_target_pairs={{0,16},{8,24},{16,0},{24,8},{1,17},{9,25},{17,1},{25,9},{2,18},{10... | collective-permute-start | bytes 98312 | tf_op jit(solution)/shard_map/ppermute | solution.py:486
  20.0 5.2 %collective-permute-start.9 = (bf16[32,1024]{1,0:T(8,128)(2,1)S(1)}, bf16[32,1024]{1,0:T(8,128)(2,1)S(1)}, u32[]{:S(2)}, u32[]{:S(2)}) collective-permute-start(bf16[32,1024]{1,0:T(8,128)(2,1)S(1)} %fusion.2), channel_id=1, source_target_pairs={{0,8},{8,0},{16,24},{24,16},{1,9},{9,1},{17,25},{25,17},{2,10},{10... | collective-permute-start | bytes 196616 | tf_op jit(solution)/shard_map/ppermute | solution.py:483
  20.1 4.4 %collective-permute-start.17 = (bf16[32,1024]{1,0:T(8,128)(2,1)S(1)}, bf16[32,1024]{1,0:T(8,128)(2,1)S(1)}, u32[]{:S(2)}, u32[]{:S(2)}) collective-permute-start(bf16[32,1024]{1,0:T(8,128)(2,1)S(1)} %fusion.1), channel_id=1, source_target_pairs={{0,16},{8,24},{16,0},{24,8},{1,17},{9,25},{17,1},{25,9},{2,18},{10... | collective-permute-start | bytes 196616 | tf_op jit(solution)/shard_map/ppermute | solution.py:486
  24.6 1.3 %collective-permute-start.7 = (bf16[32,1280]{1,0:T(8,128)(2,1)S(1)}, bf16[32,1280]{1,0:T(8,128)(2,1)S(1)}, u32[]{:S(2)}, u32[]{:S(2)}) collective-permute-start(bf16[32,1280]{1,0:T(8,128)(2,1)S(1)} %pad_maximum_fusion.2), channel_id=1, source_target_pairs={{0,8},{8,0},{16,24},{24,16},{1,9},{9,1},{17,25},{25,17},{2,10},{10... | collective-permute-start | bytes 245768 | tf_op jit(solution)/shard_map/ppermute | solution.py:483
  24.6 2.7 %collective-permute-start.18 = (bf16[32,1024]{1,0:T(8,128)(2,1)S(1)}, bf16[32,1024]{1,0:T(8,128)(2,1)S(1)}, u32[]{:S(2)}, u32[]{:S(2)}) collective-permute-start(bf16[32,1024]{1,0:T(8,128)(2,1)S(1)} %get-tuple-element.95), channel_id=1, source_target_pairs={{0,8},{8,0},{16,24},{24,16},{1,9},{9,1},{17,25},{25,17},{2,10},{10... | collective-permute-start | bytes 196616 | tf_op jit(solution)/shard_map/ppermute | solution.py:483
  26.0 7.1 %collective-permute-start.13 = (bf16[64,2048]{1,0:T(8,128)(2,1)S(1)}, bf16[64,2048]{1,0:T(8,128)(2,1)S(1)}, u32[]{:S(2)}, u32[]{:S(2)}) collective-permute-start(bf16[64,2048]{1,0:T(8,128)(2,1)S(1)} %get-tuple-element.79), channel_id=1, source_target_pairs={{0,1},{1,0},{2,3},{3,2},{4,5},{5,4},{6,7},{7,6},{8,10},{9,11},{10,... | collective-permute-start | bytes 786440 | tf_op jit(solution)/shard_map/ppermute | solution.py:627
  27.3 1.6 %collective-permute-start.12 = (bf16[32,256]{1,0:T(8,128)(2,1)S(1)}, bf16[32,256]{1,0:T(8,128)(2,1)S(1)}, u32[]{:S(2)}, u32[]{:S(2)}) collective-permute-start(bf16[32,256]{1,0:T(8,128)(2,1)S(1)} %get-tuple-element.103), channel_id=1, source_target_pairs={{0,8},{8,0},{16,24},{24,16},{1,9},{9,1},{17,25},{25,17},{2,10},{10... | collective-permute-start | bytes 49160 | tf_op jit(solution)/shard_map/ppermute | solution.py:483
  27.4 5.7 %collective-permute-start.19 = (bf16[64,512]{1,0:T(8,128)(2,1)S(1)}, bf16[64,512]{1,0:T(8,128)(2,1)S(1)}, u32[]{:S(2)}, u32[]{:S(2)}) collective-permute-start(bf16[64,512]{1,0:T(8,128)(2,1)S(1)} %get-tuple-element.90), channel_id=1, source_target_pairs={{0,1},{1,0},{2,3},{3,2},{4,5},{5,4},{6,7},{7,6},{8,10},{9,11},{10,... | collective-permute-start | bytes 196616 | tf_op jit(solution)/shard_map/ppermute | solution.py:627
  28.9 5.9 %collective-permute-start.14 = (bf16[64,512]{1,0:T(8,128)(2,1)S(1)}, bf16[64,512]{1,0:T(8,128)(2,1)S(1)}, u32[]{:S(2)}, u32[]{:S(2)}) collective-permute-start(bf16[64,512]{1,0:T(8,128)(2,1)S(1)} %get-tuple-element.80), channel_id=1, source_target_pairs={{0,1},{1,0},{2,3},{3,2},{4,5},{5,4},{6,7},{7,6},{8,10},{9,11},{10,... | collective-permute-start | bytes 196616 | tf_op jit(solution)/shard_map/ppermute | solution.py:627
  33.5 5.0 %collective-permute-start.20 = (bf16[2,128,256]{2,1,0:T(8,128)(2,1)S(1)}, bf16[2,128,256]{2,1,0:T(8,128)(2,1)S(1)}, u32[]{:S(2)}, u32[]{:S(2)}) collective-permute-start(bf16[2,128,256]{2,1,0:T(8,128)(2,1)S(1)} %get-tuple-element.92), channel_id=1, source_target_pairs={{0,2},{1,3},{2,0},{3,1},{4,6},{5,7},{6,4},{7,5},{8,9},{9,8},{10,11... | collective-permute-start | bytes 393224 | tf_op jit(solution)/shard_map/ppermute | solution.py:627
  35.2 5.7 %collective-permute-start.15 = (bf16[2,128,256]{2,1,0:T(8,128)(2,1)S(1)}, bf16[2,128,256]{2,1,0:T(8,128)(2,1)S(1)}, u32[]{:S(2)}, u32[]{:S(2)}) collective-permute-start(bf16[2,128,256]{2,1,0:T(8,128)(2,1)S(1)} %get-tuple-element.82), channel_id=1, source_target_pairs={{0,2},{1,3},{2,0},{3,1},{4,6},{5,7},{6,4},{7,5},{8,9},{9,8},{10,11... | collective-permute-start | bytes 393224 | tf_op jit(solution)/shard_map/ppermute | solution.py:627
  38.5 6.7 %collective-permute-start.21 = (bf16[1,128,256]{2,1,0:T(8,128)(2,1)S(1)}, bf16[1,128,256]{2,1,0:T(8,128)(2,1)S(1)}, u32[]{:S(2)}, u32[]{:S(2)}) collective-permute-start(bf16[1,128,256]{2,1,0:T(8,128)(2,1)S(1)} %get-tuple-element.94), channel_id=1, source_target_pairs={{0,4},{1,5},{2,6},{3,7},{4,0},{5,1},{6,2},{7,3},{8,12},{9,13},{10,... | collective-permute-start | bytes 196616 | tf_op jit(solution)/shard_map/ppermute | solution.py:627
  41.0 5.2 %collective-permute-start.16 = (bf16[1,128,256]{2,1,0:T(8,128)(2,1)S(1)}, bf16[1,128,256]{2,1,0:T(8,128)(2,1)S(1)}, u32[]{:S(2)}, u32[]{:S(2)}) collective-permute-start(bf16[1,128,256]{2,1,0:T(8,128)(2,1)S(1)} %get-tuple-element.84), channel_id=1, source_target_pairs={{0,4},{1,5},{2,6},{3,7},{4,0},{5,1},{6,2},{7,3},{8,12},{9,13},{10,... | collective-permute-start | bytes 196616 | tf_op jit(solution)/shard_map/ppermute | solution.py:627

commit v11 on v9

--- a/solution.py
+++ b/solution.py
@@ -235,11 +235,6 @@
         held = (refs.pop(0), refs.pop(0))
         copies = weight_copies(own, other, held, refs.pop(0), core, way)
         start_all(copies if forward else copies[2:] + copies[:2])
-        run(
-            [held[0].at[order] for order in range(2)],
-            [held[1].at[order] for order in range(2)],
-            lambda kind, order: copies[2 * order + kind][1].wait(),
-        )
 
 
 def tail_body(own, other, upstreams, back_first, inners, back_inners):

time: 48.8 us -> 48.8 us (level)
  no operation moved by 1% of the time
where the time goes in v11:
time: 48.8 us; the launch traced here: 48.6 us
  starting transfers between devices  22.4 us (46%)
  waiting for transfers between devices  16.7 us (34%)
  Pallas kernels  9.12 us (19%)
    ppermute x7, starting transfers between devices, exchange(): return lax.ppermute(shard, AXES, pairs)  10.8 us
    ppermute x7, waiting for transfers between devices, exchange(): return lax.ppermute(shard, AXES, pairs)  9.27 us
    ppermute x2, starting transfers between devices, hop(): return lax.ppermute(shard, 'pipe', pairs)  4.86 us
    ppermute x3, starting transfers between devices, mirror(): return lax.ppermute(shard, 'pipe', mirror_pairs)  4.67 us
    ppermute x3, waiting for transfers between devices, mirror(): return lax.ppermute(shard, 'pipe', mirror_pairs)  4.09 us
    pallas_call x3, Pallas kernels, run_stage(): pl.pallas_call(functools.partial(stage_body, step, forward, backward, las...  3.26 us
    ppermute x2, waiting for transfers between devices, hop(): return lax.ppermute(shard, 'pipe', pairs)  3.23 us
    pallas_call x2, Pallas kernels, load(): pl.pallas_call(functools.partial(load_body, step), out_shape=outs, in_spe...  2.44 us
  transfers between devices with their start and end apart: 22, of which 9 were waited for; matrix products, arithmetic and copies ran while one was open for 0% of the time, Pallas kernels for 11%

profile of v11, /device:TPU:0, one launch (start us, length us, event | category | flops | bytes accessed | tf_op | source)
XLA Modules:
  0.0 48.6 jit_solution(16263660998121055698)
XLA Ops:
  0.0 1.2 %shard_map.46 = (bf16[1024,256]{1,0:T(8,128)(2,1)S(1)}, bf16[1024,256]{1,0:T(8,128)(2,1)S(1)}, bf16[32,1024]{1,0:T(8,128)(2,1)S(1)}) custom-call(bf16[2,1024,256]{2,1,0:T(8,128)(2,1)} %bitcast.20, bf16[2,1024,256]{2,1,0:T(8,128)(2,1)} %bitcast.22, bf16[2,2,32,1024]{3,2,1,0:T(8,128)(2,1)} %inputs), custom_call_target="tpu_custom_call" | custom-call | tf_op jit(solution)/shard_map/pallas_call | solution.py:68
  1.2 0.6 %collective-permute-start = (bf16[1024,256]{1,0:T(8,128)(2,1)S(1)}, bf16[1024,256]{1,0:T(8,128)(2,1)S(1)}, u32[]{:S(2)}, u32[]{:S(2)}) collective-permute-start(bf16[1024,256]{1,0:T(8,128)(2,1)S(1)} %get-tuple-element.51.own.refs_0_), channel_id=1, source_target_pairs={{0,8},{8,0},{16,24},{24,16},{1,9},{9,1},{17,25},{25,17},{2,10},{10... | collective-permute-start | bytes 1572872 | tf_op jit(solution)/shard_map/ppermute | solution.py:479
  1.8 0.1 collective-permute-start.1
  1.9 1.2 %shard_map.49 = (bf16[1024,256]{1,0:T(8,128)(2,1)S(1)}, bf16[1024,256]{1,0:T(8,128)(2,1)S(1)}) custom-call(bf16[2,1024,256]{2,1,0:T(8,128)(2,1)} %bitcast.21, bf16[2,1024,256]{2,1,0:T(8,128)(2,1)} %bitcast.23), custom_call_target="tpu_custom_call" | custom-call | tf_op jit(solution)/shard_map/pallas_call | solution.py:68
  3.1 0.5 %collective-permute-start.3 = (bf16[1024,256]{1,0:T(8,128)(2,1)S(1)}, bf16[1024,256]{1,0:T(8,128)(2,1)S(1)}, u32[]{:S(2)}, u32[]{:S(2)}) collective-permute-start(bf16[1024,256]{1,0:T(8,128)(2,1)S(1)} %get-tuple-element.59.expand_own.refs_1_), channel_id=1, source_target_pairs={{0,8},{8,0},{16,24},{24,16},{1,9},{9,1},{17,25},{25,17},{2,10},{10... | collective-permute-start | bytes 1572872 | tf_op jit(solution)/shard_map/ppermute | solution.py:479
  3.6 0.1 collective-permute-start.2
  3.7 0.3 shard_map.47
  4.0 0.1 collective-permute-done.1.refs_3_.other
  4.1 0.8 %shard_map.48 = (bf16[2,32,1280]{2,1,0:T(8,128)(2,1)S(1)}, bf16[32,1024]{1,0:T(8,128)(2,1)S(1)}, bf16[2,32,1024]{2,1,0:T(8,128)(2,1)S(1)}, f32[2,32,256]{2,1,0:T(8,128)S(1)}) custom-call(bf16[1024,256]{1,0:T(8,128)(2,1)S(1)} %get-tuple-element.51.own.refs_0_, bf16[1024,256]{1,0:T(8,128)(2,1)S(1)} %get-tuple-element.52.refs_1_.own, ...), custom_call_target="tpu_custom_call" | custom-call | flops 67108864 | bytes 2097152 | tf_op jit(solution)/shard_map/pallas_call | solution.py:276
  4.9 2.9 %collective-permute-start.4 = (bf16[32,1024]{1,0:T(8,128)(2,1)S(1)}, bf16[32,1024]{1,0:T(8,128)(2,1)S(1)}, u32[]{:S(2)}, u32[]{:S(2)}) collective-permute-start(bf16[32,1024]{1,0:T(8,128)(2,1)S(1)} %get-tuple-element.60.leave), channel_id=1, source_target_pairs={{0,16},{16,0},{8,24},{24,8},{1,17},{17,1},{9,25},{25,9},{2,18},{18... | collective-permute-start | bytes 196616 | tf_op jit(solution)/shard_map/ppermute | solution.py:476
  7.8 0.0 collective-permute-done.3.expand_other.refs_3_
  7.8 1.2 %shard_map.50 = (bf16[32,1024]{1,0:T(8,128)(2,1)S(1)}, f32[32,256]{1,0:T(8,128)S(1)}, bf16[32,1024]{1,0:T(8,128)(2,1)S(1)}, bf16[32,1024]{1,0:T(8,128)(2,1)S(1)}) custom-call(bf16[1024,256]{1,0:T(8,128)(2,1)S(1)} %get-tuple-element.59.expand_own.refs_1_, bf16[1024,256]{1,0:T(8,128)(2,1)S(1)} %collective-permute-done.3.expand_other.refs_3_, ...), custom_call_target="tpu_custom_call" | custom-call | tf_op jit(solution)/shard_map/pallas_call | solution.py:528
  9.0 0.0 collective-permute-done.2.refs_2_
  9.0 1.2 %collective-permute-done.4.refs_4_ = bf16[32,1024]{1,0:T(8,128)(2,1)S(1)} collective-permute-done((bf16[32,1024]{1,0:T(8,128)(2,1)S(1)}, bf16[32,1024]{1,0:T(8,128)(2,1)S(1)}, u32[]{:S(2)}, u32[]{:S(2)}) %collective-permute-start.4) | collective-permute-done | bytes 65568 | tf_op jit(solution)/shard_map/ppermute | solution.py:476
  10.2 1.8 %shard_map.51 = (bf16[2,32,1280]{2,1,0:T(8,128)(2,1)S(1)}, bf16[2,32,1024]{2,1,0:T(8,128)(2,1)S(1)}, bf16[2,32,256]{2,1,0:T(8,128)(2,1)S(1)}, bf16[32,1024]{1,0:T(8,128)(2,1)S(1)}) custom-call(bf16[1024,256]{1,0:T(8,128)(2,1)S(1)} %get-tuple-element.58.refs_0_, bf16[1024,256]{1,0:T(8,128)(2,1)S(1)} %get-tuple-element.59.expand_own.refs_1_, ...), custom_call_target="tpu_custom_call" | custom-call | flops 134217728 | bytes 2097152 | tf_op jit(solution)/shard_map/pallas_call | solution.py:276
  12.0 2.0 %collective-permute-start.6 = (bf16[32,1024]{1,0:T(8,128)(2,1)S(1)}, bf16[32,1024]{1,0:T(8,128)(2,1)S(1)}, u32[]{:S(2)}, u32[]{:S(2)}) collective-permute-start(bf16[32,1024]{1,0:T(8,128)(2,1)S(1)} %get-tuple-element.65), channel_id=1, source_target_pairs={{0,16},{16,0},{8,24},{24,8},{1,17},{17,1},{9,25},{25,9},{2,18},{18... | collective-permute-start | bytes 196616 | tf_op jit(solution)/shard_map/ppermute | solution.py:476
  14.0 0.1 collective-permute-start.5
  14.2 0.2 collective-permute-start.8
  14.3 2.1 %collective-permute-done.6.refs_4_ = bf16[32,1024]{1,0:T(8,128)(2,1)S(1)} collective-permute-done((bf16[32,1024]{1,0:T(8,128)(2,1)S(1)}, bf16[32,1024]{1,0:T(8,128)(2,1)S(1)}, u32[]{:S(2)}, u32[]{:S(2)}) %collective-permute-start.6) | collective-permute-done | bytes 65568 | tf_op jit(solution)/shard_map/ppermute | solution.py:476
  16.4 0.6 %shard_map.52 = (bf16[2,32,1024]{2,1,0:T(8,128)(2,1)S(1)}, bf16[2,32,256]{2,1,0:T(8,128)(2,1)S(1)}) custom-call(bf16[1024,256]{1,0:T(8,128)(2,1)S(1)} %get-tuple-element.51.own.refs_0_, bf16[1024,256]{1,0:T(8,128)(2,1)S(1)} %get-tuple-element.52.refs_1_.own, bf16[1024,256]{1,0:T(8,128)(2,1)S(1)} %collective-permute-done.other.refs_2_, ...), custom_call_target="tpu_custom_call" | custom-call | flops 67108864 | bytes 2097152 | tf_op jit(solution)/shard_map/pallas_call | solution.py:276
  17.0 0.2 shard_map.54.refs_0_
  17.3 0.1 collective-permute-start.10
  17.4 2.5 %collective-permute-start.11 = (bf16[2,32,256]{2,1,0:T(8,128)(2,1)S(1)}, bf16[2,32,256]{2,1,0:T(8,128)(2,1)S(1)}, u32[]{:S(2)}, u32[]{:S(2)}) collective-permute-start(bf16[2,32,256]{2,1,0:T(8,128)(2,1)S(1)} %broadcast_select_fusion.7), channel_id=1, source_target_pairs={{0,16},{8,24},{16,0},{24,8},{1,17},{9,25},{17,1},{25,9},{2,18},{10... | collective-permute-start | bytes 98312 | tf_op jit(solution)/shard_map/ppermute | solution.py:482
  20.0 0.2 collective-permute-start.7
  20.1 1.8 %collective-permute-done.11 = bf16[2,32,256]{2,1,0:T(8,128)(2,1)S(1)} collective-permute-done((bf16[2,32,256]{2,1,0:T(8,128)(2,1)S(1)}, bf16[2,32,256]{2,1,0:T(8,128)(2,1)S(1)}, u32[]{:S(2)}, u32[]{:S(2)}) %collective-permute-start.11) | collective-permute-done | bytes 32800 | tf_op jit(solution)/shard_map/ppermute | solution.py:482
  21.9 1.9 %collective-permute-start.17 = (bf16[32,1024]{1,0:T(8,128)(2,1)S(1)}, bf16[32,1024]{1,0:T(8,128)(2,1)S(1)}, u32[]{:S(2)}, u32[]{:S(2)}) collective-permute-start(bf16[32,1024]{1,0:T(8,128)(2,1)S(1)} %fusion.1), channel_id=1, source_target_pairs={{0,16},{8,24},{16,0},{24,8},{1,17},{9,25},{17,1},{25,9},{2,18},{10... | collective-permute-start | bytes 196616 | tf_op jit(solution)/shard_map/ppermute | solution.py:482
  23.9 0.0 collective-permute-done.8
  23.9 0.0 collective-permute-start.12
  23.9 2.3 %collective-permute-done.17 = bf16[32,1024]{1,0:T(8,128)(2,1)S(1)} collective-permute-done((bf16[32,1024]{1,0:T(8,128)(2,1)S(1)}, bf16[32,1024]{1,0:T(8,128)(2,1)S(1)}, u32[]{:S(2)}, u32[]{:S(2)}) %collective-permute-start.17) | collective-permute-done | bytes 65568 | tf_op jit(solution)/shard_map/ppermute | solution.py:482
  26.2 0.0 collective-permute-start.9
  26.2 0.6 %collective-permute-start.18 = (bf16[32,1024]{1,0:T(8,128)(2,1)S(1)}, bf16[32,1024]{1,0:T(8,128)(2,1)S(1)}, u32[]{:S(2)}, u32[]{:S(2)}) collective-permute-start(bf16[32,1024]{1,0:T(8,128)(2,1)S(1)} %get-tuple-element.95), channel_id=1, source_target_pairs={{0,8},{8,0},{16,24},{24,16},{1,9},{9,1},{17,25},{25,17},{2,10},{10... | collective-permute-start | bytes 196616 | tf_op jit(solution)/shard_map/ppermute | solution.py:479
  26.8 0.1 shard_map.53
  26.9 1.4 %collective-permute-start.13 = (bf16[64,1280]{1,0:T(8,128)(2,1)S(1)}, bf16[64,1280]{1,0:T(8,128)(2,1)S(1)}, u32[]{:S(2)}, u32[]{:S(2)}) collective-permute-start(bf16[64,1280]{1,0:T(8,128)(2,1)S(1)} %get-tuple-element.79), channel_id=1, source_target_pairs={{0,1},{1,0},{2,3},{3,2},{4,5},{5,4},{6,7},{7,6},{8,10},{9,11},{10,... | collective-permute-start | bytes 491528 | tf_op jit(solution)/shard_map/ppermute | solution.py:623
  28.3 0.1 shard_map.55
  28.4 0.8 %collective-permute-start.14 = (bf16[64,1024]{1,0:T(8,128)(2,1)S(1)}, bf16[64,1024]{1,0:T(8,128)(2,1)S(1)}, u32[]{:S(2)}, u32[]{:S(2)}) collective-permute-start(bf16[64,1024]{1,0:T(8,128)(2,1)S(1)} %get-tuple-element.80), channel_id=1, source_target_pairs={{0,1},{1,0},{2,3},{3,2},{4,5},{5,4},{6,7},{7,6},{8,10},{9,11},{10,... | collective-permute-start | bytes 393224 | tf_op jit(solution)/shard_map/ppermute | solution.py:623
  29.3 1.4 %collective-permute-start.19 = (bf16[64,768]{1,0:T(8,128)(2,1)S(1)}, bf16[64,768]{1,0:T(8,128)(2,1)S(1)}, u32[]{:S(2)}, u32[]{:S(2)}) collective-permute-start(bf16[64,768]{1,0:T(8,128)(2,1)S(1)} %get-tuple-element.90), channel_id=1, source_target_pairs={{0,1},{1,0},{2,3},{3,2},{4,5},{5,4},{6,7},{7,6},{8,10},{9,11},{10,... | collective-permute-start | bytes 294920 | tf_op jit(solution)/shard_map/ppermute | solution.py:623
  30.6 4.1 %collective-permute-done.19.refs_5_ = bf16[64,768]{1,0:T(8,128)(2,1)S(1)} collective-permute-done((bf16[64,768]{1,0:T(8,128)(2,1)S(1)}, bf16[64,768]{1,0:T(8,128)(2,1)S(1)}, u32[]{:S(2)}, u32[]{:S(2)}) %collective-permute-start.19) | collective-permute-done | bytes 98336 | tf_op jit(solution)/shard_map/ppermute | solution.py:623
  34.8 0.3 shard_map.59
  35.1 1.4 %collective-permute-start.20 = (bf16[2,128,256]{2,1,0:T(8,128)(2,1)S(1)}, bf16[2,128,256]{2,1,0:T(8,128)(2,1)S(1)}, u32[]{:S(2)}, u32[]{:S(2)}) collective-permute-start(bf16[2,128,256]{2,1,0:T(8,128)(2,1)S(1)} %get-tuple-element.92), channel_id=1, source_target_pairs={{0,2},{1,3},{2,0},{3,1},{4,6},{5,7},{6,4},{7,5},{8,9},{9,8},{10,11... | collective-permute-start | bytes 393224 | tf_op jit(solution)/shard_map/ppermute | solution.py:623
  36.6 0.3 shard_map.56
  36.9 0.7 %collective-permute-start.15 = (bf16[2,128,256]{2,1,0:T(8,128)(2,1)S(1)}, bf16[2,128,256]{2,1,0:T(8,128)(2,1)S(1)}, u32[]{:S(2)}, u32[]{:S(2)}) collective-permute-start(bf16[2,128,256]{2,1,0:T(8,128)(2,1)S(1)} %get-tuple-element.82), channel_id=1, source_target_pairs={{0,2},{1,3},{2,0},{3,1},{4,6},{5,7},{6,4},{7,5},{8,9},{9,8},{10,11... | collective-permute-start | bytes 393224 | tf_op jit(solution)/shard_map/ppermute | solution.py:623
  37.6 2.5 %collective-permute-done.20.came = bf16[2,128,256]{2,1,0:T(8,128)(2,1)S(1)} collective-permute-done((bf16[2,128,256]{2,1,0:T(8,128)(2,1)S(1)}, bf16[2,128,256]{2,1,0:T(8,128)(2,1)S(1)}, u32[]{:S(2)}, u32[]{:S(2)}) %collective-permute-start.20) | collective-permute-done | bytes 131104 | tf_op jit(solution)/shard_map/ppermute | solution.py:623
  40.2 2.4 %collective-permute-start.21 = (bf16[1,128,256]{2,1,0:T(8,128)(2,1)S(1)}, bf16[1,128,256]{2,1,0:T(8,128)(2,1)S(1)}, u32[]{:S(2)}, u32[]{:S(2)}) collective-permute-start(bf16[1,128,256]{2,1,0:T(8,128)(2,1)S(1)} %get-tuple-element.94), channel_id=1, source_target_pairs={{0,4},{1,5},{2,6},{3,7},{4,0},{5,1},{6,2},{7,3},{8,12},{9,13},{10,... | collective-permute-start | bytes 196616 | tf_op jit(solution)/shard_map/ppermute | solution.py:623
  42.6 0.0 collective-permute-done.15.came
  42.7 2.7 %collective-permute-start.16 = (bf16[1,128,256]{2,1,0:T(8,128)(2,1)S(1)}, bf16[1,128,256]{2,1,0:T(8,128)(2,1)S(1)}, u32[]{:S(2)}, u32[]{:S(2)}) collective-permute-start(bf16[1,128,256]{2,1,0:T(8,128)(2,1)S(1)} %get-tuple-element.84), channel_id=1, source_target_pairs={{0,4},{1,5},{2,6},{3,7},{4,0},{5,1},{6,2},{7,3},{8,12},{9,13},{10,... | collective-permute-start | bytes 196616 | tf_op jit(solution)/shard_map/ppermute | solution.py:623
  45.3 1.5 %collective-permute-done.21.came_expand = bf16[1,128,256]{2,1,0:T(8,128)(2,1)S(1)} collective-permute-done((bf16[1,128,256]{2,1,0:T(8,128)(2,1)S(1)}, bf16[1,128,256]{2,1,0:T(8,128)(2,1)S(1)}, u32[]{:S(2)}, u32[]{:S(2)}) %collective-permute-start.21) | collective-permute-done | bytes 65568 | tf_op jit(solution)/shard_map/ppermute | solution.py:623
  46.8 1.1 %collective-permute-done.16.came_reduce = bf16[1,128,256]{2,1,0:T(8,128)(2,1)S(1)} collective-permute-done((bf16[1,128,256]{2,1,0:T(8,128)(2,1)S(1)}, bf16[1,128,256]{2,1,0:T(8,128)(2,1)S(1)}, u32[]{:S(2)}, u32[]{:S(2)}) %collective-permute-start.16) | collective-permute-done | bytes 65568 | tf_op jit(solution)/shard_map/ppermute | solution.py:623
  47.9 0.7 %shard_map.61 = f32[1,2,128,256]{3,2,1,0:T(8,128)} custom-call(f32[1,128,256]{2,1,0:T(8,128)S(1)} %get-tuple-element.83.keep_reduce, bf16[1,128,256]{2,1,0:T(8,128)(2,1)S(1)} %collective-permute-done.16.came_reduce, f32[1,128,256]{2,1,0:T(8,128)S(1)} %get-tuple-element.93.keep_expand, bf16[1,128,256]{2,1,0:T(8,128)(2,1)S(1)} %collective-permute-done.21.came_expand), custom_call_target="tpu_custom_call" | custom-call | tf_op jit(solution)/shard_map/pallas_call | solution.py:602
  (28 shorter events, 0.3 us)
Async XLA Ops:
  1.2 2.4 %collective-permute-start = (bf16[1024,256]{1,0:T(8,128)(2,1)S(1)}, bf16[1024,256]{1,0:T(8,128)(2,1)S(1)}, u32[]{:S(2)}, u32[]{:S(2)}) collective-permute-start(bf16[1024,256]{1,0:T(8,128)(2,1)S(1)} %get-tuple-element.51.own.refs_0_), channel_id=1, source_target_pairs={{0,8},{8,0},{16,24},{24,16},{1,9},{9,1},{17,25},{25,17},{2,10},{10... | collective-permute-start | bytes 1572872 | tf_op jit(solution)/shard_map/ppermute | solution.py:479
  1.8 2.3 %collective-permute-start.1 = (bf16[1024,256]{1,0:T(8,128)(2,1)S(1)}, bf16[1024,256]{1,0:T(8,128)(2,1)S(1)}, u32[]{:S(2)}, u32[]{:S(2)}) collective-permute-start(bf16[1024,256]{1,0:T(8,128)(2,1)S(1)} %get-tuple-element.52.refs_1_.own), channel_id=1, source_target_pairs={{0,8},{8,0},{16,24},{24,16},{1,9},{9,1},{17,25},{25,17},{2,10},{10... | collective-permute-start | bytes 1572872 | tf_op jit(solution)/shard_map/ppermute | solution.py:479
  3.1 4.7 %collective-permute-start.3 = (bf16[1024,256]{1,0:T(8,128)(2,1)S(1)}, bf16[1024,256]{1,0:T(8,128)(2,1)S(1)}, u32[]{:S(2)}, u32[]{:S(2)}) collective-permute-start(bf16[1024,256]{1,0:T(8,128)(2,1)S(1)} %get-tuple-element.59.expand_own.refs_1_), channel_id=1, source_target_pairs={{0,8},{8,0},{16,24},{24,16},{1,9},{9,1},{17,25},{25,17},{2,10},{10... | collective-permute-start | bytes 1572872 | tf_op jit(solution)/shard_map/ppermute | solution.py:479
  3.6 5.4 %collective-permute-start.2 = (bf16[1024,256]{1,0:T(8,128)(2,1)S(1)}, bf16[1024,256]{1,0:T(8,128)(2,1)S(1)}, u32[]{:S(2)}, u32[]{:S(2)}) collective-permute-start(bf16[1024,256]{1,0:T(8,128)(2,1)S(1)} %get-tuple-element.58.refs_0_), channel_id=1, source_target_pairs={{0,8},{8,0},{16,24},{24,16},{1,9},{9,1},{17,25},{25,17},{2,10},{10... | collective-permute-start | bytes 1572872 | tf_op jit(solution)/shard_map/ppermute | solution.py:479
  4.9 5.3 %collective-permute-start.4 = (bf16[32,1024]{1,0:T(8,128)(2,1)S(1)}, bf16[32,1024]{1,0:T(8,128)(2,1)S(1)}, u32[]{:S(2)}, u32[]{:S(2)}) collective-permute-start(bf16[32,1024]{1,0:T(8,128)(2,1)S(1)} %get-tuple-element.60.leave), channel_id=1, source_target_pairs={{0,16},{16,0},{8,24},{24,8},{1,17},{17,1},{9,25},{25,9},{2,18},{18... | collective-permute-start | bytes 196616 | tf_op jit(solution)/shard_map/ppermute | solution.py:476
  12.0 4.4 %collective-permute-start.6 = (bf16[32,1024]{1,0:T(8,128)(2,1)S(1)}, bf16[32,1024]{1,0:T(8,128)(2,1)S(1)}, u32[]{:S(2)}, u32[]{:S(2)}) collective-permute-start(bf16[32,1024]{1,0:T(8,128)(2,1)S(1)} %get-tuple-element.65), channel_id=1, source_target_pairs={{0,16},{16,0},{8,24},{24,8},{1,17},{17,1},{9,25},{25,9},{2,18},{18... | collective-permute-start | bytes 196616 | tf_op jit(solution)/shard_map/ppermute | solution.py:476
  14.0 12.2 %collective-permute-start.5 = (bf16[32,1280]{1,0:T(8,128)(2,1)S(1)}, bf16[32,1280]{1,0:T(8,128)(2,1)S(1)}, u32[]{:S(2)}, u32[]{:S(2)}) collective-permute-start(bf16[32,1280]{1,0:T(8,128)(2,1)S(1)} %fusion), channel_id=1, source_target_pairs={{0,8},{8,0},{16,24},{24,16},{1,9},{9,1},{17,25},{25,17},{2,10},{10... | collective-permute-start | bytes 245768 | tf_op jit(solution)/shard_map/ppermute | solution.py:479
  14.2 9.7 %collective-permute-start.8 = (bf16[32,1536]{1,0:T(8,128)(2,1)S(1)}, bf16[32,1536]{1,0:T(8,128)(2,1)S(1)}, u32[]{:S(2)}, u32[]{:S(2)}) collective-permute-start(bf16[32,1536]{1,0:T(8,128)(2,1)S(1)} %pad_maximum_fusion), channel_id=1, source_target_pairs={{0,16},{8,24},{16,0},{24,8},{1,17},{9,25},{17,1},{25,9},{2,18},{10... | collective-permute-start | bytes 294920 | tf_op jit(solution)/shard_map/ppermute | solution.py:482
  17.3 11.0 %collective-permute-start.10 = (bf16[32,256]{1,0:T(8,128)(2,1)S(1)}, bf16[32,256]{1,0:T(8,128)(2,1)S(1)}, u32[]{:S(2)}, u32[]{:S(2)}) collective-permute-start(bf16[32,256]{1,0:T(8,128)(2,1)S(1)} %fusion.4), channel_id=1, source_target_pairs={{0,8},{8,0},{16,24},{24,16},{1,9},{9,1},{17,25},{25,17},{2,10},{10... | collective-permute-start | bytes 49160 | tf_op jit(solution)/shard_map/ppermute | solution.py:479
  17.4 4.5 %collective-permute-start.11 = (bf16[2,32,256]{2,1,0:T(8,128)(2,1)S(1)}, bf16[2,32,256]{2,1,0:T(8,128)(2,1)S(1)}, u32[]{:S(2)}, u32[]{:S(2)}) collective-permute-start(bf16[2,32,256]{2,1,0:T(8,128)(2,1)S(1)} %broadcast_select_fusion.7), channel_id=1, source_target_pairs={{0,16},{8,24},{16,0},{24,8},{1,17},{9,25},{17,1},{25,9},{2,18},{10... | collective-permute-start | bytes 98312 | tf_op jit(solution)/shard_map/ppermute | solution.py:482
  20.0 6.9 %collective-permute-start.7 = (bf16[32,1024]{1,0:T(8,128)(2,1)S(1)}, bf16[32,1024]{1,0:T(8,128)(2,1)S(1)}, u32[]{:S(2)}, u32[]{:S(2)}) collective-permute-start(bf16[32,1024]{1,0:T(8,128)(2,1)S(1)} %fusion.3), channel_id=1, source_target_pairs={{0,8},{8,0},{16,24},{24,16},{1,9},{9,1},{17,25},{25,17},{2,10},{10... | collective-permute-start | bytes 196616 | tf_op jit(solution)/shard_map/ppermute | solution.py:479
  21.9 4.3 %collective-permute-start.17 = (bf16[32,1024]{1,0:T(8,128)(2,1)S(1)}, bf16[32,1024]{1,0:T(8,128)(2,1)S(1)}, u32[]{:S(2)}, u32[]{:S(2)}) collective-permute-start(bf16[32,1024]{1,0:T(8,128)(2,1)S(1)} %fusion.1), channel_id=1, source_target_pairs={{0,16},{8,24},{16,0},{24,8},{1,17},{9,25},{17,1},{25,9},{2,18},{10... | collective-permute-start | bytes 196616 | tf_op jit(solution)/shard_map/ppermute | solution.py:482
  23.9 4.4 %collective-permute-start.12 = (bf16[32,256]{1,0:T(8,128)(2,1)S(1)}, bf16[32,256]{1,0:T(8,128)(2,1)S(1)}, u32[]{:S(2)}, u32[]{:S(2)}) collective-permute-start(bf16[32,256]{1,0:T(8,128)(2,1)S(1)} %get-tuple-element.103), channel_id=1, source_target_pairs={{0,8},{8,0},{16,24},{24,16},{1,9},{9,1},{17,25},{25,17},{2,10},{10... | collective-permute-start | bytes 49160 | tf_op jit(solution)/shard_map/ppermute | solution.py:479
  26.2 2.1 %collective-permute-start.9 = (bf16[32,1280]{1,0:T(8,128)(2,1)S(1)}, bf16[32,1280]{1,0:T(8,128)(2,1)S(1)}, u32[]{:S(2)}, u32[]{:S(2)}) collective-permute-start(bf16[32,1280]{1,0:T(8,128)(2,1)S(1)} %pad_maximum_fusion.2), channel_id=1, source_target_pairs={{0,8},{8,0},{16,24},{24,16},{1,9},{9,1},{17,25},{25,17},{2,10},{10... | collective-permute-start | bytes 245768 | tf_op jit(solution)/shard_map/ppermute | solution.py:479
  26.2 3.0 %collective-permute-start.18 = (bf16[32,1024]{1,0:T(8,128)(2,1)S(1)}, bf16[32,1024]{1,0:T(8,128)(2,1)S(1)}, u32[]{:S(2)}, u32[]{:S(2)}) collective-permute-start(bf16[32,1024]{1,0:T(8,128)(2,1)S(1)} %get-tuple-element.95), channel_id=1, source_target_pairs={{0,8},{8,0},{16,24},{24,16},{1,9},{9,1},{17,25},{25,17},{2,10},{10... | collective-permute-start | bytes 196616 | tf_op jit(solution)/shard_map/ppermute | solution.py:479
  26.9 7.8 %collective-permute-start.13 = (bf16[64,1280]{1,0:T(8,128)(2,1)S(1)}, bf16[64,1280]{1,0:T(8,128)(2,1)S(1)}, u32[]{:S(2)}, u32[]{:S(2)}) collective-permute-start(bf16[64,1280]{1,0:T(8,128)(2,1)S(1)} %get-tuple-element.79), channel_id=1, source_target_pairs={{0,1},{1,0},{2,3},{3,2},{4,5},{5,4},{6,7},{7,6},{8,10},{9,11},{10,... | collective-permute-start | bytes 491528 | tf_op jit(solution)/shard_map/ppermute | solution.py:623
  28.4 8.1 %collective-permute-start.14 = (bf16[64,1024]{1,0:T(8,128)(2,1)S(1)}, bf16[64,1024]{1,0:T(8,128)(2,1)S(1)}, u32[]{:S(2)}, u32[]{:S(2)}) collective-permute-start(bf16[64,1024]{1,0:T(8,128)(2,1)S(1)} %get-tuple-element.80), channel_id=1, source_target_pairs={{0,1},{1,0},{2,3},{3,2},{4,5},{5,4},{6,7},{7,6},{8,10},{9,11},{10,... | collective-permute-start | bytes 393224 | tf_op jit(solution)/shard_map/ppermute | solution.py:623
  29.3 5.5 %collective-permute-start.19 = (bf16[64,768]{1,0:T(8,128)(2,1)S(1)}, bf16[64,768]{1,0:T(8,128)(2,1)S(1)}, u32[]{:S(2)}, u32[]{:S(2)}) collective-permute-start(bf16[64,768]{1,0:T(8,128)(2,1)S(1)} %get-tuple-element.90), channel_id=1, source_target_pairs={{0,1},{1,0},{2,3},{3,2},{4,5},{5,4},{6,7},{7,6},{8,10},{9,11},{10,... | collective-permute-start | bytes 294920 | tf_op jit(solution)/shard_map/ppermute | solution.py:623
  35.1 5.0 %collective-permute-start.20 = (bf16[2,128,256]{2,1,0:T(8,128)(2,1)S(1)}, bf16[2,128,256]{2,1,0:T(8,128)(2,1)S(1)}, u32[]{:S(2)}, u32[]{:S(2)}) collective-permute-start(bf16[2,128,256]{2,1,0:T(8,128)(2,1)S(1)} %get-tuple-element.92), channel_id=1, source_target_pairs={{0,2},{1,3},{2,0},{3,1},{4,6},{5,7},{6,4},{7,5},{8,9},{9,8},{10,11... | collective-permute-start | bytes 393224 | tf_op jit(solution)/shard_map/ppermute | solution.py:623
  36.9 5.7 %collective-permute-start.15 = (bf16[2,128,256]{2,1,0:T(8,128)(2,1)S(1)}, bf16[2,128,256]{2,1,0:T(8,128)(2,1)S(1)}, u32[]{:S(2)}, u32[]{:S(2)}) collective-permute-start(bf16[2,128,256]{2,1,0:T(8,128)(2,1)S(1)} %get-tuple-element.82), channel_id=1, source_target_pairs={{0,2},{1,3},{2,0},{3,1},{4,6},{5,7},{6,4},{7,5},{8,9},{9,8},{10,11... | collective-permute-start | bytes 393224 | tf_op jit(solution)/shard_map/ppermute | solution.py:623
  40.2 6.6 %collective-permute-start.21 = (bf16[1,128,256]{2,1,0:T(8,128)(2,1)S(1)}, bf16[1,128,256]{2,1,0:T(8,128)(2,1)S(1)}, u32[]{:S(2)}, u32[]{:S(2)}) collective-permute-start(bf16[1,128,256]{2,1,0:T(8,128)(2,1)S(1)} %get-tuple-element.94), channel_id=1, source_target_pairs={{0,4},{1,5},{2,6},{3,7},{4,0},{5,1},{6,2},{7,3},{8,12},{9,13},{10,... | collective-permute-start | bytes 196616 | tf_op jit(solution)/shard_map/ppermute | solution.py:623
  42.7 5.2 %collective-permute-start.16 = (bf16[1,128,256]{2,1,0:T(8,128)(2,1)S(1)}, bf16[1,128,256]{2,1,0:T(8,128)(2,1)S(1)}, u32[]{:S(2)}, u32[]{:S(2)}) collective-permute-start(bf16[1,128,256]{2,1,0:T(8,128)(2,1)S(1)} %get-tuple-element.84), channel_id=1, source_target_pairs={{0,4},{1,5},{2,6},{3,7},{4,0},{5,1},{6,2},{7,3},{8,12},{9,13},{10,... | collective-permute-start | bytes 196616 | tf_op jit(solution)/shard_map/ppermute | solution.py:623

commit v12 on v7

--- a/solution.py
+++ b/solution.py
@@ -235,11 +235,6 @@
         held = (refs.pop(0), refs.pop(0))
         copies = weight_copies(own, other, held, refs.pop(0), core, way)
         start_all(copies if forward else copies[2:] + copies[:2])
-        run(
-            [held[0].at[order] for order in range(2)],
-            [held[1].at[order] for order in range(2)],
-            lambda kind, order: copies[2 * order + kind][1].wait(),
-        )
 
 
 def tail_body(own, other, upstreams, back_first, inners, back_inners):
@@ -407,31 +402,56 @@
     send[:, channels // 2 :] = right[...]
 
 
+def pick_stage(target, parts, span):
+    stage, _, _ = where_am_i(0)
+    for step, part in enumerate(parts):
+
+        @pl.when(stage == step)
+        def _():
+            target[...] = part[0, :, span]
+
+
+def own_body(stages, chunk, *refs):
+    send, wide, spare = refs[stages:]
+    channels = wide.shape[1]
+    pick_stage(wide, refs[:stages], slice(0, channels))
+    split_columns(wide, spare, send.at[:, : channels // 2], chunk)
+    pick_stage(send.at[:, channels // 2 :], refs[:stages], slice(channels, None))
+
+
 def near_body(stages, chunk, *refs):
     flows, ups, backs = [refs[at * (stages + 1) : (at + 1) * (stages + 1)] for at in range(3)]
-    left_up, right_up, left_inner, right_inner, send, wide = refs[3 * stages + 3 :]
-    width = send.shape[1] // 2
-    for at, (late, outs) in enumerate(
-        ((ups, (left_up, right_up)), (backs, (left_inner, right_inner)))
-    ):
-        part = send.at[:, at * width : (at + 1) * width]
-        pack_body(stages, chunk, at == 0, True, False, *flows, *late, *outs, part, wide)
-
-
-def half_gradient_body(at, groups, *refs):
-    send, keep, full, left, right = refs[3 * groups :]
-    start = 0
-    for group in range(groups):
-        part_left, part_right, came = refs[3 * group : 3 * group + 3]
-        rows, columns = part_left.shape
-        left[start : start + rows] = part_left[...]
-        right[start : start + rows] = part_right[...]
-        start += rows
-        width = columns + right.shape[1]
-        offset = at * width if came.shape[1] > width else 0
-        left[start : start + rows] = came[:, offset : offset + columns]
-        right[start : start + rows] = came[:, offset + columns : offset + width]
-        start += rows
+    up, active, lifted, inner, send, wide, spare = refs[3 * stages + 3 :]
+    half, channels = up.shape[1], wide.shape[1]
+    rows = wide.shape[0] // 2
+    everything, broad, narrow = slice(None), slice(0, channels), slice(channels, None)
+    for target, sources, span in ((wide, ups, everything), (active, flows, narrow)):
+        pick_stage(target.at[:rows], sources[:-1], span)
+        target[rows:] = sources[-1][:, span]
+    split_columns(wide, up, send.at[: 2 * rows, :half], chunk)
+    send[2 * rows :, half:] = active[rows:]
+    for target, sources, span in ((wide, flows, broad), (inner, backs, everything)):
+        pick_stage(target.at[:rows], sources[:-1], span)
+        target[rows:] = sources[-1][:, span]
+    split_columns(wide.at[:rows], lifted.at[:rows], spare, chunk)
+    split_columns(wide.at[rows:], lifted.at[rows:], send.at[2 * rows :, :half], chunk)
+    send[: 2 * rows, half:] = inner[...]
+
+
+def half_gradient_body(up, *refs):
+    near, far, (own_came, near_came, far_came) = refs[:2], refs[2:4], refs[4:7]
+    send, keep, full, left, right = refs[7:]
+    rows, columns = own_came.shape[0], near[0].shape[1]
+    spans = slice(0, columns), slice(columns, None)
+    for at, target in enumerate((left, right)):
+        target[: 2 * rows] = near[at][...]
+        if up == (at == 0):
+            target[2 * rows : 4 * rows] = near_came[: 2 * rows, spans[at]]
+        else:
+            target[2 * rows : 3 * rows] = own_came[:, spans[at]]
+            target[3 * rows : 4 * rows] = near_came[2 * rows :, spans[at]]
+        target[4 * rows : 6 * rows] = far[at][...]
+        target[6 * rows :] = far_came[:, spans[at]]
     full[...] = contract(left[...], right[...], 0, 0)
     _, _, side = first_sides()
     chunk = send.shape[1]
@@ -646,6 +666,18 @@
             compiler_params=PARAMS,
         )(*arrays)
 
+    send = pl.pallas_call(
+        functools.partial(own_body, stages, chunk),
+        out_shape=shape(rows, channels // 2 + inner),
+        in_specs=[VMEM] * stages,
+        out_specs=VMEM,
+        scratch_shapes=[
+            pltpu.VMEM((rows, channels), jnp.bfloat16),
+            pltpu.VMEM((rows, channels // 2), jnp.bfloat16),
+        ],
+        compiler_params=PARAMS,
+    )(*fore[:stages])
+    came_own = exchange(send, stages, replicas, 1, 2)
     near = fore[: stages + 1] + ups[: stages + 1] + backs[: stages + 1]
     *kept, send = pl.pallas_call(
         functools.partial(near_body, stages, chunk),
@@ -654,11 +686,14 @@
             shape(2 * rows, inner),
             shape(2 * rows, channels // 2),
             shape(2 * rows, inner),
-            shape(2 * rows, channels + 2 * inner),
+            shape(3 * rows, channels // 2 + inner),
         ],
         in_specs=[VMEM] * len(near),
         out_specs=[VMEM] * 5,
-        scratch_shapes=[pltpu.VMEM((2 * rows, channels), jnp.bfloat16)],
+        scratch_shapes=[
+            pltpu.VMEM((2 * rows, channels), jnp.bfloat16),
+            pltpu.VMEM((rows, channels // 2), jnp.bfloat16),
+        ],
         compiler_params=PARAMS,
     )(*near)
     came_near = exchange(send, stages, replicas, 1, 2)
@@ -666,10 +701,10 @@
     for at, name, late in ((1, "inner", backs), (0, "up", ups)):
         left, right, send = pack(late, name == "up", False, True)
         came = exchange(send, stages, replicas, 1, 2)
-        operands = (kept[2 * at], kept[2 * at + 1], came_near, left, right, came)
+        operands = (kept[2 * at], kept[2 * at + 1], left, right, came_own, came_near, came)
         count = replicas // 4
         send, keep = pl.pallas_call(
-            functools.partial(half_gradient_body, at, len(operands) // 3),
+            functools.partial(half_gradient_body, at == 0),
             out_shape=sums(count, chunk, inner),
             in_specs=[VMEM] * len(operands),
             out_specs=[VMEM] * 2,

time: 47.8 us -> 49 us (1.025)
  starting transfers between devices: 22.4 us -> 23.2 us
  waiting for transfers between devices: 15.6 us -> 16.1 us
    ppermute x7 -> x8, starting transfers between devices: 10.8 us -> 11.6 us  [exchange(): return lax.ppermute(shard, AXES, pairs)]
    ppermute x7 -> x8, waiting for transfers between devices: 8.24 us -> 8.68 us  [exchange(): return lax.ppermute(shard, AXES, pairs)]
  transfers between devices with their start and end apart: 22 -> 23, of which waited for: 9 -> 9; matrix products, arithmetic and copies ran while one was open for 0% -> 0% of each run, Pallas kernels for 11% -> 11%
where the time goes in v12:
time: 49 us; the launch traced here: 48.8 us
  starting transfers between devices  23.2 us (47%)
  waiting for transfers between devices  16.1 us (33%)
  Pallas kernels  9.13 us (19%)
    ppermute x8, starting transfers between devices, exchange(): return lax.ppermute(shard, AXES, pairs)  11.6 us
    ppermute x8, waiting for transfers between devices, exchange(): return lax.ppermute(shard, AXES, pairs)  8.68 us
    ppermute x2, starting transfers between devices, hop(): return lax.ppermute(shard, 'pipe', pairs)  4.86 us
    ppermute x3, starting transfers between devices, mirror(): return lax.ppermute(shard, 'pipe', mirror_pairs)  4.67 us
    ppermute x3, waiting for transfers between devices, mirror(): return lax.ppermute(shard, 'pipe', mirror_pairs)  4.09 us
    pallas_call x3, Pallas kernels, run_stage(): pl.pallas_call(functools.partial(stage_body, step, forward, backward, las...  3.26 us
    ppermute x2, waiting for transfers between devices, hop(): return lax.ppermute(shard, 'pipe', pairs)  3.23 us
    pallas_call x2, Pallas kernels, load(): pl.pallas_call(functools.partial(load_body, step), out_shape=outs, in_spe...  2.44 us
  transfers between devices with their start and end apart: 23, of which 9 were waited for; matrix products, arithmetic and copies ran while one was open for 0% of the time, Pallas kernels for 11%

profile of v12, /device:TPU:0, one launch (start us, length us, event | category | flops | bytes accessed | tf_op | source)
XLA Modules:
  0.0 48.8 jit_solution(10720784423128071678)
XLA Ops:
  0.0 1.2 %shard_map.46 = (bf16[1024,256]{1,0:T(8,128)(2,1)S(1)}, bf16[1024,256]{1,0:T(8,128)(2,1)S(1)}, bf16[32,1024]{1,0:T(8,128)(2,1)S(1)}) custom-call(bf16[2,1024,256]{2,1,0:T(8,128)(2,1)} %bitcast.20, bf16[2,1024,256]{2,1,0:T(8,128)(2,1)} %bitcast.22, bf16[2,2,32,1024]{3,2,1,0:T(8,128)(2,1)} %inputs), custom_call_target="tpu_custom_call" | custom-call | tf_op jit(solution)/shard_map/pallas_call | solution.py:68
  1.2 0.6 %collective-permute-start = (bf16[1024,256]{1,0:T(8,128)(2,1)S(1)}, bf16[1024,256]{1,0:T(8,128)(2,1)S(1)}, u32[]{:S(2)}, u32[]{:S(2)}) collective-permute-start(bf16[1024,256]{1,0:T(8,128)(2,1)S(1)} %get-tuple-element.51.own.refs_0_), channel_id=1, source_target_pairs={{0,8},{8,0},{16,24},{24,16},{1,9},{9,1},{17,25},{25,17},{2,10},{10... | collective-permute-start | bytes 1572872 | tf_op jit(solution)/shard_map/ppermute | solution.py:500
  1.8 0.1 collective-permute-start.1
  1.9 1.2 %shard_map.49 = (bf16[1024,256]{1,0:T(8,128)(2,1)S(1)}, bf16[1024,256]{1,0:T(8,128)(2,1)S(1)}) custom-call(bf16[2,1024,256]{2,1,0:T(8,128)(2,1)} %bitcast.21, bf16[2,1024,256]{2,1,0:T(8,128)(2,1)} %bitcast.23), custom_call_target="tpu_custom_call" | custom-call | tf_op jit(solution)/shard_map/pallas_call | solution.py:68
  3.1 0.5 %collective-permute-start.3 = (bf16[1024,256]{1,0:T(8,128)(2,1)S(1)}, bf16[1024,256]{1,0:T(8,128)(2,1)S(1)}, u32[]{:S(2)}, u32[]{:S(2)}) collective-permute-start(bf16[1024,256]{1,0:T(8,128)(2,1)S(1)} %get-tuple-element.59.expand_own.refs_1_), channel_id=1, source_target_pairs={{0,8},{8,0},{16,24},{24,16},{1,9},{9,1},{17,25},{25,17},{2,10},{10... | collective-permute-start | bytes 1572872 | tf_op jit(solution)/shard_map/ppermute | solution.py:500
  3.6 0.1 collective-permute-start.2
  3.7 0.3 shard_map.47
  4.0 0.1 collective-permute-done.1.refs_3_.other
  4.1 0.8 %shard_map.48 = (bf16[2,32,1280]{2,1,0:T(8,128)(2,1)S(1)}, bf16[32,1024]{1,0:T(8,128)(2,1)S(1)}, bf16[2,32,1024]{2,1,0:T(8,128)(2,1)S(1)}, f32[2,32,256]{2,1,0:T(8,128)S(1)}) custom-call(bf16[1024,256]{1,0:T(8,128)(2,1)S(1)} %get-tuple-element.51.own.refs_0_, bf16[1024,256]{1,0:T(8,128)(2,1)S(1)} %get-tuple-element.52.refs_1_.own, ...), custom_call_target="tpu_custom_call" | custom-call | flops 67108864 | bytes 2097152 | tf_op jit(solution)/shard_map/pallas_call | solution.py:276
  4.9 2.9 %collective-permute-start.4 = (bf16[32,1024]{1,0:T(8,128)(2,1)S(1)}, bf16[32,1024]{1,0:T(8,128)(2,1)S(1)}, u32[]{:S(2)}, u32[]{:S(2)}) collective-permute-start(bf16[32,1024]{1,0:T(8,128)(2,1)S(1)} %get-tuple-element.60.leave), channel_id=1, source_target_pairs={{0,16},{16,0},{8,24},{24,8},{1,17},{17,1},{9,25},{25,9},{2,18},{18... | collective-permute-start | bytes 196616 | tf_op jit(solution)/shard_map/ppermute | solution.py:497
  7.8 0.0 collective-permute-done.3.expand_other.refs_3_
  7.8 1.2 %shard_map.50 = (bf16[32,1024]{1,0:T(8,128)(2,1)S(1)}, f32[32,256]{1,0:T(8,128)S(1)}, bf16[32,1024]{1,0:T(8,128)(2,1)S(1)}, bf16[32,1024]{1,0:T(8,128)(2,1)S(1)}) custom-call(bf16[1024,256]{1,0:T(8,128)(2,1)S(1)} %get-tuple-element.59.expand_own.refs_1_, bf16[1024,256]{1,0:T(8,128)(2,1)S(1)} %collective-permute-done.3.expand_other.refs_3_, ...), custom_call_target="tpu_custom_call" | custom-call | tf_op jit(solution)/shard_map/pallas_call | solution.py:549
  9.0 0.0 collective-permute-done.2.refs_2_
  9.0 1.2 %collective-permute-done.4.refs_4_ = bf16[32,1024]{1,0:T(8,128)(2,1)S(1)} collective-permute-done((bf16[32,1024]{1,0:T(8,128)(2,1)S(1)}, bf16[32,1024]{1,0:T(8,128)(2,1)S(1)}, u32[]{:S(2)}, u32[]{:S(2)}) %collective-permute-start.4) | collective-permute-done | bytes 65568 | tf_op jit(solution)/shard_map/ppermute | solution.py:497
  10.2 1.8 %shard_map.51 = (bf16[2,32,1280]{2,1,0:T(8,128)(2,1)S(1)}, bf16[2,32,1024]{2,1,0:T(8,128)(2,1)S(1)}, bf16[2,32,256]{2,1,0:T(8,128)(2,1)S(1)}, bf16[32,1024]{1,0:T(8,128)(2,1)S(1)}) custom-call(bf16[1024,256]{1,0:T(8,128)(2,1)S(1)} %get-tuple-element.58.refs_0_, bf16[1024,256]{1,0:T(8,128)(2,1)S(1)} %get-tuple-element.59.expand_own.refs_1_, ...), custom_call_target="tpu_custom_call" | custom-call | flops 134217728 | bytes 2097152 | tf_op jit(solution)/shard_map/pallas_call | solution.py:276
  12.0 2.0 %collective-permute-start.6 = (bf16[32,1024]{1,0:T(8,128)(2,1)S(1)}, bf16[32,1024]{1,0:T(8,128)(2,1)S(1)}, u32[]{:S(2)}, u32[]{:S(2)}) collective-permute-start(bf16[32,1024]{1,0:T(8,128)(2,1)S(1)} %get-tuple-element.65), channel_id=1, source_target_pairs={{0,16},{16,0},{8,24},{24,8},{1,17},{17,1},{9,25},{25,9},{2,18},{18... | collective-permute-start | bytes 196616 | tf_op jit(solution)/shard_map/ppermute | solution.py:497
  14.0 0.1 collective-permute-start.5
  14.2 0.2 collective-permute-start.9
  14.3 2.1 %collective-permute-done.6.refs_4_ = bf16[32,1024]{1,0:T(8,128)(2,1)S(1)} collective-permute-done((bf16[32,1024]{1,0:T(8,128)(2,1)S(1)}, bf16[32,1024]{1,0:T(8,128)(2,1)S(1)}, u32[]{:S(2)}, u32[]{:S(2)}) %collective-permute-start.6) | collective-permute-done | bytes 65568 | tf_op jit(solution)/shard_map/ppermute | solution.py:497
  16.4 0.6 %shard_map.52 = (bf16[2,32,1024]{2,1,0:T(8,128)(2,1)S(1)}, bf16[2,32,256]{2,1,0:T(8,128)(2,1)S(1)}) custom-call(bf16[1024,256]{1,0:T(8,128)(2,1)S(1)} %get-tuple-element.51.own.refs_0_, bf16[1024,256]{1,0:T(8,128)(2,1)S(1)} %get-tuple-element.52.refs_1_.own, bf16[1024,256]{1,0:T(8,128)(2,1)S(1)} %collective-permute-done.other.refs_2_, ...), custom_call_target="tpu_custom_call" | custom-call | flops 67108864 | bytes 2097152 | tf_op jit(solution)/shard_map/pallas_call | solution.py:276
  17.0 0.2 shard_map.53.refs_6_
  17.3 0.1 collective-permute-start.8
  17.4 2.5 %collective-permute-start.11 = (bf16[2,32,256]{2,1,0:T(8,128)(2,1)S(1)}, bf16[2,32,256]{2,1,0:T(8,128)(2,1)S(1)}, u32[]{:S(2)}, u32[]{:S(2)}) collective-permute-start(bf16[2,32,256]{2,1,0:T(8,128)(2,1)S(1)} %broadcast_select_fusion.7), channel_id=1, source_target_pairs={{0,16},{8,24},{16,0},{24,8},{1,17},{9,25},{17,1},{25,9},{2,18},{10... | collective-permute-start | bytes 98312 | tf_op jit(solution)/shard_map/ppermute | solution.py:503
  20.0 0.2 collective-permute-start.7
  20.1 1.8 %collective-permute-done.11 = bf16[2,32,256]{2,1,0:T(8,128)(2,1)S(1)} collective-permute-done((bf16[2,32,256]{2,1,0:T(8,128)(2,1)S(1)}, bf16[2,32,256]{2,1,0:T(8,128)(2,1)S(1)}, u32[]{:S(2)}, u32[]{:S(2)}) %collective-permute-start.11) | collective-permute-done | bytes 32800 | tf_op jit(solution)/shard_map/ppermute | solution.py:503
  21.9 1.9 %collective-permute-start.18 = (bf16[32,1024]{1,0:T(8,128)(2,1)S(1)}, bf16[32,1024]{1,0:T(8,128)(2,1)S(1)}, u32[]{:S(2)}, u32[]{:S(2)}) collective-permute-start(bf16[32,1024]{1,0:T(8,128)(2,1)S(1)} %fusion.1), channel_id=1, source_target_pairs={{0,16},{8,24},{16,0},{24,8},{1,17},{9,25},{17,1},{25,9},{2,18},{10... | collective-permute-start | bytes 196616 | tf_op jit(solution)/shard_map/ppermute | solution.py:503
  23.9 0.0 collective-permute-done.9
  23.9 2.3 %collective-permute-done.18 = bf16[32,1024]{1,0:T(8,128)(2,1)S(1)} collective-permute-done((bf16[32,1024]{1,0:T(8,128)(2,1)S(1)}, bf16[32,1024]{1,0:T(8,128)(2,1)S(1)}, u32[]{:S(2)}, u32[]{:S(2)}) %collective-permute-start.18) | collective-permute-done | bytes 65568 | tf_op jit(solution)/shard_map/ppermute | solution.py:503
  26.2 0.6 %collective-permute-start.19 = (bf16[32,1024]{1,0:T(8,128)(2,1)S(1)}, bf16[32,1024]{1,0:T(8,128)(2,1)S(1)}, u32[]{:S(2)}, u32[]{:S(2)}) collective-permute-start(bf16[32,1024]{1,0:T(8,128)(2,1)S(1)} %get-tuple-element.95), channel_id=1, source_target_pairs={{0,8},{8,0},{16,24},{24,16},{1,9},{9,1},{17,25},{25,17},{2,10},{10... | collective-permute-start | bytes 196616 | tf_op jit(solution)/shard_map/ppermute | solution.py:500
  26.8 0.1 shard_map.54
  26.9 1.4 %collective-permute-start.14 = (bf16[96,768]{1,0:T(8,128)(2,1)S(1)}, bf16[96,768]{1,0:T(8,128)(2,1)S(1)}, u32[]{:S(2)}, u32[]{:S(2)}) collective-permute-start(bf16[96,768]{1,0:T(8,128)(2,1)S(1)} %get-tuple-element.79), channel_id=1, source_target_pairs={{0,1},{1,0},{2,3},{3,2},{4,5},{5,4},{6,7},{7,6},{8,10},{9,11},{10,... | collective-permute-start | bytes 442376 | tf_op jit(solution)/shard_map/ppermute | solution.py:644
  28.3 0.1 shard_map.55
  28.4 0.8 %collective-permute-start.15 = (bf16[64,768]{1,0:T(8,128)(2,1)S(1)}, bf16[64,768]{1,0:T(8,128)(2,1)S(1)}, u32[]{:S(2)}, u32[]{:S(2)}) collective-permute-start(bf16[64,768]{1,0:T(8,128)(2,1)S(1)} %get-tuple-element.80), channel_id=1, source_target_pairs={{0,1},{1,0},{2,3},{3,2},{4,5},{5,4},{6,7},{7,6},{8,10},{9,11},{10,... | collective-permute-start | bytes 294920 | tf_op jit(solution)/shard_map/ppermute | solution.py:644
  29.2 0.1 shard_map.59
  29.2 1.4 %collective-permute-start.20 = (bf16[64,768]{1,0:T(8,128)(2,1)S(1)}, bf16[64,768]{1,0:T(8,128)(2,1)S(1)}, u32[]{:S(2)}, u32[]{:S(2)}) collective-permute-start(bf16[64,768]{1,0:T(8,128)(2,1)S(1)} %get-tuple-element.90), channel_id=1, source_target_pairs={{0,1},{1,0},{2,3},{3,2},{4,5},{5,4},{6,7},{7,6},{8,10},{9,11},{10,... | collective-permute-start | bytes 294920 | tf_op jit(solution)/shard_map/ppermute | solution.py:644
  30.6 0.8 %collective-permute-start.13 = (bf16[32,768]{1,0:T(8,128)(2,1)S(1)}, bf16[32,768]{1,0:T(8,128)(2,1)S(1)}, u32[]{:S(2)}, u32[]{:S(2)}) collective-permute-start(bf16[32,768]{1,0:T(8,128)(2,1)S(1)} %shard_map.56), channel_id=1, source_target_pairs={{0,1},{1,0},{2,3},{3,2},{4,5},{5,4},{6,7},{7,6},{8,10},{9,11},{10,... | collective-permute-start | bytes 147464 | tf_op jit(solution)/shard_map/ppermute | solution.py:644
  31.4 3.4 %collective-permute-done.13.refs_4_ = bf16[32,768]{1,0:T(8,128)(2,1)S(1)} collective-permute-done((bf16[32,768]{1,0:T(8,128)(2,1)S(1)}, bf16[32,768]{1,0:T(8,128)(2,1)S(1)}, u32[]{:S(2)}, u32[]{:S(2)}) %collective-permute-start.13) | collective-permute-done | bytes 49184 | tf_op jit(solution)/shard_map/ppermute | solution.py:644
  34.8 0.3 shard_map.57
  35.1 1.6 %collective-permute-start.16 = (bf16[2,128,256]{2,1,0:T(8,128)(2,1)S(1)}, bf16[2,128,256]{2,1,0:T(8,128)(2,1)S(1)}, u32[]{:S(2)}, u32[]{:S(2)}) collective-permute-start(bf16[2,128,256]{2,1,0:T(8,128)(2,1)S(1)} %get-tuple-element.82), channel_id=1, source_target_pairs={{0,2},{1,3},{2,0},{3,1},{4,6},{5,7},{6,4},{7,5},{8,9},{9,8},{10,11... | collective-permute-start | bytes 393224 | tf_op jit(solution)/shard_map/ppermute | solution.py:644
  36.8 0.3 shard_map.60
  37.1 0.5 %collective-permute-start.21 = (bf16[2,128,256]{2,1,0:T(8,128)(2,1)S(1)}, bf16[2,128,256]{2,1,0:T(8,128)(2,1)S(1)}, u32[]{:S(2)}, u32[]{:S(2)}) collective-permute-start(bf16[2,128,256]{2,1,0:T(8,128)(2,1)S(1)} %get-tuple-element.92), channel_id=1, source_target_pairs={{0,2},{1,3},{2,0},{3,1},{4,6},{5,7},{6,4},{7,5},{8,9},{9,8},{10,11... | collective-permute-start | bytes 393224 | tf_op jit(solution)/shard_map/ppermute | solution.py:644
  37.6 2.5 %collective-permute-done.16.came = bf16[2,128,256]{2,1,0:T(8,128)(2,1)S(1)} collective-permute-done((bf16[2,128,256]{2,1,0:T(8,128)(2,1)S(1)}, bf16[2,128,256]{2,1,0:T(8,128)(2,1)S(1)}, u32[]{:S(2)}, u32[]{:S(2)}) %collective-permute-start.16) | collective-permute-done | bytes 131104 | tf_op jit(solution)/shard_map/ppermute | solution.py:644
  40.2 2.7 %collective-permute-start.17 = (bf16[1,128,256]{2,1,0:T(8,128)(2,1)S(1)}, bf16[1,128,256]{2,1,0:T(8,128)(2,1)S(1)}, u32[]{:S(2)}, u32[]{:S(2)}) collective-permute-start(bf16[1,128,256]{2,1,0:T(8,128)(2,1)S(1)} %get-tuple-element.84), channel_id=1, source_target_pairs={{0,4},{1,5},{2,6},{3,7},{4,0},{5,1},{6,2},{7,3},{8,12},{9,13},{10,... | collective-permute-start | bytes 196616 | tf_op jit(solution)/shard_map/ppermute | solution.py:644
  42.9 0.0 collective-permute-done.21.came
  42.9 2.5 %collective-permute-start.22 = (bf16[1,128,256]{2,1,0:T(8,128)(2,1)S(1)}, bf16[1,128,256]{2,1,0:T(8,128)(2,1)S(1)}, u32[]{:S(2)}, u32[]{:S(2)}) collective-permute-start(bf16[1,128,256]{2,1,0:T(8,128)(2,1)S(1)} %get-tuple-element.94), channel_id=1, source_target_pairs={{0,4},{1,5},{2,6},{3,7},{4,0},{5,1},{6,2},{7,3},{8,12},{9,13},{10,... | collective-permute-start | bytes 196616 | tf_op jit(solution)/shard_map/ppermute | solution.py:644
  45.3 1.5 %collective-permute-done.17.came_reduce = bf16[1,128,256]{2,1,0:T(8,128)(2,1)S(1)} collective-permute-done((bf16[1,128,256]{2,1,0:T(8,128)(2,1)S(1)}, bf16[1,128,256]{2,1,0:T(8,128)(2,1)S(1)}, u32[]{:S(2)}, u32[]{:S(2)}) %collective-permute-start.17) | collective-permute-done | bytes 65568 | tf_op jit(solution)/shard_map/ppermute | solution.py:644
  46.8 1.3 %collective-permute-done.22.came_expand = bf16[1,128,256]{2,1,0:T(8,128)(2,1)S(1)} collective-permute-done((bf16[1,128,256]{2,1,0:T(8,128)(2,1)S(1)}, bf16[1,128,256]{2,1,0:T(8,128)(2,1)S(1)}, u32[]{:S(2)}, u32[]{:S(2)}) %collective-permute-start.22) | collective-permute-done | bytes 65568 | tf_op jit(solution)/shard_map/ppermute | solution.py:644
  48.1 0.7 %shard_map.62 = f32[1,2,128,256]{3,2,1,0:T(8,128)} custom-call(f32[1,128,256]{2,1,0:T(8,128)S(1)} %get-tuple-element.83.keep_reduce, bf16[1,128,256]{2,1,0:T(8,128)(2,1)S(1)} %collective-permute-done.17.came_reduce, f32[1,128,256]{2,1,0:T(8,128)S(1)} %get-tuple-element.93.keep_expand, bf16[1,128,256]{2,1,0:T(8,128)(2,1)S(1)} %collective-permute-done.22.came_expand), custom_call_target="tpu_custom_call" | custom-call | tf_op jit(solution)/shard_map/pallas_call | solution.py:623
  (31 shorter events, 0.3 us)
Async XLA Ops:
  1.2 2.4 %collective-permute-start = (bf16[1024,256]{1,0:T(8,128)(2,1)S(1)}, bf16[1024,256]{1,0:T(8,128)(2,1)S(1)}, u32[]{:S(2)}, u32[]{:S(2)}) collective-permute-start(bf16[1024,256]{1,0:T(8,128)(2,1)S(1)} %get-tuple-element.51.own.refs_0_), channel_id=1, source_target_pairs={{0,8},{8,0},{16,24},{24,16},{1,9},{9,1},{17,25},{25,17},{2,10},{10... | collective-permute-start | bytes 1572872 | tf_op jit(solution)/shard_map/ppermute | solution.py:500
  1.8 2.3 %collective-permute-start.1 = (bf16[1024,256]{1,0:T(8,128)(2,1)S(1)}, bf16[1024,256]{1,0:T(8,128)(2,1)S(1)}, u32[]{:S(2)}, u32[]{:S(2)}) collective-permute-start(bf16[1024,256]{1,0:T(8,128)(2,1)S(1)} %get-tuple-element.52.refs_1_.own), channel_id=1, source_target_pairs={{0,8},{8,0},{16,24},{24,16},{1,9},{9,1},{17,25},{25,17},{2,10},{10... | collective-permute-start | bytes 1572872 | tf_op jit(solution)/shard_map/ppermute | solution.py:500
  3.1 4.7 %collective-permute-start.3 = (bf16[1024,256]{1,0:T(8,128)(2,1)S(1)}, bf16[1024,256]{1,0:T(8,128)(2,1)S(1)}, u32[]{:S(2)}, u32[]{:S(2)}) collective-permute-start(bf16[1024,256]{1,0:T(8,128)(2,1)S(1)} %get-tuple-element.59.expand_own.refs_1_), channel_id=1, source_target_pairs={{0,8},{8,0},{16,24},{24,16},{1,9},{9,1},{17,25},{25,17},{2,10},{10... | collective-permute-start | bytes 1572872 | tf_op jit(solution)/shard_map/ppermute | solution.py:500
  3.6 5.4 %collective-permute-start.2 = (bf16[1024,256]{1,0:T(8,128)(2,1)S(1)}, bf16[1024,256]{1,0:T(8,128)(2,1)S(1)}, u32[]{:S(2)}, u32[]{:S(2)}) collective-permute-start(bf16[1024,256]{1,0:T(8,128)(2,1)S(1)} %get-tuple-element.58.refs_0_), channel_id=1, source_target_pairs={{0,8},{8,0},{16,24},{24,16},{1,9},{9,1},{17,25},{25,17},{2,10},{10... | collective-permute-start | bytes 1572872 | tf_op jit(solution)/shard_map/ppermute | solution.py:500
  4.9 5.3 %collective-permute-start.4 = (bf16[32,1024]{1,0:T(8,128)(2,1)S(1)}, bf16[32,1024]{1,0:T(8,128)(2,1)S(1)}, u32[]{:S(2)}, u32[]{:S(2)}) collective-permute-start(bf16[32,1024]{1,0:T(8,128)(2,1)S(1)} %get-tuple-element.60.leave), channel_id=1, source_target_pairs={{0,16},{16,0},{8,24},{24,8},{1,17},{17,1},{9,25},{25,9},{2,18},{18... | collective-permute-start | bytes 196616 | tf_op jit(solution)/shard_map/ppermute | solution.py:497
  12.0 4.4 %collective-permute-start.6 = (bf16[32,1024]{1,0:T(8,128)(2,1)S(1)}, bf16[32,1024]{1,0:T(8,128)(2,1)S(1)}, u32[]{:S(2)}, u32[]{:S(2)}) collective-permute-start(bf16[32,1024]{1,0:T(8,128)(2,1)S(1)} %get-tuple-element.65), channel_id=1, source_target_pairs={{0,16},{16,0},{8,24},{24,8},{1,17},{17,1},{9,25},{25,9},{2,18},{18... | collective-permute-start | bytes 196616 | tf_op jit(solution)/shard_map/ppermute | solution.py:497
  14.0 12.8 %collective-permute-start.5 = (bf16[32,1280]{1,0:T(8,128)(2,1)S(1)}, bf16[32,1280]{1,0:T(8,128)(2,1)S(1)}, u32[]{:S(2)}, u32[]{:S(2)}) collective-permute-start(bf16[32,1280]{1,0:T(8,128)(2,1)S(1)} %fusion), channel_id=1, source_target_pairs={{0,8},{8,0},{16,24},{24,16},{1,9},{9,1},{17,25},{25,17},{2,10},{10... | collective-permute-start | bytes 245768 | tf_op jit(solution)/shard_map/ppermute | solution.py:500
  14.2 9.7 %collective-permute-start.9 = (bf16[32,1536]{1,0:T(8,128)(2,1)S(1)}, bf16[32,1536]{1,0:T(8,128)(2,1)S(1)}, u32[]{:S(2)}, u32[]{:S(2)}) collective-permute-start(bf16[32,1536]{1,0:T(8,128)(2,1)S(1)} %pad_maximum_fusion), channel_id=1, source_target_pairs={{0,16},{8,24},{16,0},{24,8},{1,17},{9,25},{17,1},{25,9},{2,18},{10... | collective-permute-start | bytes 294920 | tf_op jit(solution)/shard_map/ppermute | solution.py:503
  17.3 8.9 %collective-permute-start.8 = (bf16[32,256]{1,0:T(8,128)(2,1)S(1)}, bf16[32,256]{1,0:T(8,128)(2,1)S(1)}, u32[]{:S(2)}, u32[]{:S(2)}) collective-permute-start(bf16[32,256]{1,0:T(8,128)(2,1)S(1)} %fusion.4), channel_id=1, source_target_pairs={{0,8},{8,0},{16,24},{24,16},{1,9},{9,1},{17,25},{25,17},{2,10},{10... | collective-permute-start | bytes 49160 | tf_op jit(solution)/shard_map/ppermute | solution.py:500
  17.4 4.5 %collective-permute-start.11 = (bf16[2,32,256]{2,1,0:T(8,128)(2,1)S(1)}, bf16[2,32,256]{2,1,0:T(8,128)(2,1)S(1)}, u32[]{:S(2)}, u32[]{:S(2)}) collective-permute-start(bf16[2,32,256]{2,1,0:T(8,128)(2,1)S(1)} %broadcast_select_fusion.7), channel_id=1, source_target_pairs={{0,16},{8,24},{16,0},{24,8},{1,17},{9,25},{17,1},{25,9},{2,18},{10... | collective-permute-start | bytes 98312 | tf_op jit(solution)/shard_map/ppermute | solution.py:503
  20.0 6.9 %collective-permute-start.7 = (bf16[32,1024]{1,0:T(8,128)(2,1)S(1)}, bf16[32,1024]{1,0:T(8,128)(2,1)S(1)}, u32[]{:S(2)}, u32[]{:S(2)}) collective-permute-start(bf16[32,1024]{1,0:T(8,128)(2,1)S(1)} %fusion.3), channel_id=1, source_target_pairs={{0,8},{8,0},{16,24},{24,16},{1,9},{9,1},{17,25},{25,17},{2,10},{10... | collective-permute-start | bytes 196616 | tf_op jit(solution)/shard_map/ppermute | solution.py:500
  21.9 4.3 %collective-permute-start.18 = (bf16[32,1024]{1,0:T(8,128)(2,1)S(1)}, bf16[32,1024]{1,0:T(8,128)(2,1)S(1)}, u32[]{:S(2)}, u32[]{:S(2)}) collective-permute-start(bf16[32,1024]{1,0:T(8,128)(2,1)S(1)} %fusion.1), channel_id=1, source_target_pairs={{0,16},{8,24},{16,0},{24,8},{1,17},{9,25},{17,1},{25,9},{2,18},{10... | collective-permute-start | bytes 196616 | tf_op jit(solution)/shard_map/ppermute | solution.py:503
  23.9 4.4 %collective-permute-start.12 = (bf16[32,256]{1,0:T(8,128)(2,1)S(1)}, bf16[32,256]{1,0:T(8,128)(2,1)S(1)}, u32[]{:S(2)}, u32[]{:S(2)}) collective-permute-start(bf16[32,256]{1,0:T(8,128)(2,1)S(1)} %get-tuple-element.103), channel_id=1, source_target_pairs={{0,8},{8,0},{16,24},{24,16},{1,9},{9,1},{17,25},{25,17},{2,10},{10... | collective-permute-start | bytes 49160 | tf_op jit(solution)/shard_map/ppermute | solution.py:500
  26.2 2.1 %collective-permute-start.10 = (bf16[32,1280]{1,0:T(8,128)(2,1)S(1)}, bf16[32,1280]{1,0:T(8,128)(2,1)S(1)}, u32[]{:S(2)}, u32[]{:S(2)}) collective-permute-start(bf16[32,1280]{1,0:T(8,128)(2,1)S(1)} %pad_maximum_fusion.2), channel_id=1, source_target_pairs={{0,8},{8,0},{16,24},{24,16},{1,9},{9,1},{17,25},{25,17},{2,10},{10... | collective-permute-start | bytes 245768 | tf_op jit(solution)/shard_map/ppermute | solution.py:500
  26.2 2.9 %collective-permute-start.19 = (bf16[32,1024]{1,0:T(8,128)(2,1)S(1)}, bf16[32,1024]{1,0:T(8,128)(2,1)S(1)}, u32[]{:S(2)}, u32[]{:S(2)}) collective-permute-start(bf16[32,1024]{1,0:T(8,128)(2,1)S(1)} %get-tuple-element.95), channel_id=1, source_target_pairs={{0,8},{8,0},{16,24},{24,16},{1,9},{9,1},{17,25},{25,17},{2,10},{10... | collective-permute-start | bytes 196616 | tf_op jit(solution)/shard_map/ppermute | solution.py:500
  26.9 7.9 %collective-permute-start.14 = (bf16[96,768]{1,0:T(8,128)(2,1)S(1)}, bf16[96,768]{1,0:T(8,128)(2,1)S(1)}, u32[]{:S(2)}, u32[]{:S(2)}) collective-permute-start(bf16[96,768]{1,0:T(8,128)(2,1)S(1)} %get-tuple-element.79), channel_id=1, source_target_pairs={{0,1},{1,0},{2,3},{3,2},{4,5},{5,4},{6,7},{7,6},{8,10},{9,11},{10,... | collective-permute-start | bytes 442376 | tf_op jit(solution)/shard_map/ppermute | solution.py:644
  28.4 6.4 %collective-permute-start.15 = (bf16[64,768]{1,0:T(8,128)(2,1)S(1)}, bf16[64,768]{1,0:T(8,128)(2,1)S(1)}, u32[]{:S(2)}, u32[]{:S(2)}) collective-permute-start(bf16[64,768]{1,0:T(8,128)(2,1)S(1)} %get-tuple-element.80), channel_id=1, source_target_pairs={{0,1},{1,0},{2,3},{3,2},{4,5},{5,4},{6,7},{7,6},{8,10},{9,11},{10,... | collective-permute-start | bytes 294920 | tf_op jit(solution)/shard_map/ppermute | solution.py:644
  29.2 7.5 %collective-permute-start.20 = (bf16[64,768]{1,0:T(8,128)(2,1)S(1)}, bf16[64,768]{1,0:T(8,128)(2,1)S(1)}, u32[]{:S(2)}, u32[]{:S(2)}) collective-permute-start(bf16[64,768]{1,0:T(8,128)(2,1)S(1)} %get-tuple-element.90), channel_id=1, source_target_pairs={{0,1},{1,0},{2,3},{3,2},{4,5},{5,4},{6,7},{7,6},{8,10},{9,11},{10,... | collective-permute-start | bytes 294920 | tf_op jit(solution)/shard_map/ppermute | solution.py:644
  30.6 4.2 %collective-permute-start.13 = (bf16[32,768]{1,0:T(8,128)(2,1)S(1)}, bf16[32,768]{1,0:T(8,128)(2,1)S(1)}, u32[]{:S(2)}, u32[]{:S(2)}) collective-permute-start(bf16[32,768]{1,0:T(8,128)(2,1)S(1)} %shard_map.56), channel_id=1, source_target_pairs={{0,1},{1,0},{2,3},{3,2},{4,5},{5,4},{6,7},{7,6},{8,10},{9,11},{10,... | collective-permute-start | bytes 147464 | tf_op jit(solution)/shard_map/ppermute | solution.py:644
  35.1 5.0 %collective-permute-start.16 = (bf16[2,128,256]{2,1,0:T(8,128)(2,1)S(1)}, bf16[2,128,256]{2,1,0:T(8,128)(2,1)S(1)}, u32[]{:S(2)}, u32[]{:S(2)}) collective-permute-start(bf16[2,128,256]{2,1,0:T(8,128)(2,1)S(1)} %get-tuple-element.82), channel_id=1, source_target_pairs={{0,2},{1,3},{2,0},{3,1},{4,6},{5,7},{6,4},{7,5},{8,9},{9,8},{10,11... | collective-permute-start | bytes 393224 | tf_op jit(solution)/shard_map/ppermute | solution.py:644
  37.1 5.7 %collective-permute-start.21 = (bf16[2,128,256]{2,1,0:T(8,128)(2,1)S(1)}, bf16[2,128,256]{2,1,0:T(8,128)(2,1)S(1)}, u32[]{:S(2)}, u32[]{:S(2)}) collective-permute-start(bf16[2,128,256]{2,1,0:T(8,128)(2,1)S(1)} %get-tuple-element.92), channel_id=1, source_target_pairs={{0,2},{1,3},{2,0},{3,1},{4,6},{5,7},{6,4},{7,5},{8,9},{9,8},{10,11... | collective-permute-start | bytes 393224 | tf_op jit(solution)/shard_map/ppermute | solution.py:644
  40.2 6.6 %collective-permute-start.17 = (bf16[1,128,256]{2,1,0:T(8,128)(2,1)S(1)}, bf16[1,128,256]{2,1,0:T(8,128)(2,1)S(1)}, u32[]{:S(2)}, u32[]{:S(2)}) collective-permute-start(bf16[1,128,256]{2,1,0:T(8,128)(2,1)S(1)} %get-tuple-element.84), channel_id=1, source_target_pairs={{0,4},{1,5},{2,6},{3,7},{4,0},{5,1},{6,2},{7,3},{8,12},{9,13},{10,... | collective-permute-start | bytes 196616 | tf_op jit(solution)/shard_map/ppermute | solution.py:644
  42.9 5.2 %collective-permute-start.22 = (bf16[1,128,256]{2,1,0:T(8,128)(2,1)S(1)}, bf16[1,128,256]{2,1,0:T(8,128)(2,1)S(1)}, u32[]{:S(2)}, u32[]{:S(2)}) collective-permute-start(bf16[1,128,256]{2,1,0:T(8,128)(2,1)S(1)} %get-tuple-element.94), channel_id=1, source_target_pairs={{0,4},{1,5},{2,6},{3,7},{4,0},{5,1},{6,2},{7,3},{8,12},{9,13},{10,... | collective-permute-start | bytes 196616 | tf_op jit(solution)/shard_map/ppermute | solution.py:644

commit v13 on v7

--- a/solution.py
+++ b/solution.py
@@ -14,6 +14,7 @@
 ANY = pl.BlockSpec(memory_space=pl.ANY)
 VMEM = pl.BlockSpec(memory_space=pltpu.VMEM)
 PARAMS = pltpu.CompilerParams(vmem_limit_bytes=16 << 20)
+PACKED = pltpu.CompilerParams(vmem_limit_bytes=16 << 20)
 
 
 def contract(first_op, second_op, first_dim, second_dim):
@@ -284,7 +285,7 @@
         in_specs=[VMEM if near else ANY] * 4 + [VMEM] * len(arrays),
         out_specs=[VMEM] * len(outs),
         scratch_shapes=scratch,
-        compiler_params=PARAMS,
+        compiler_params=PARAMS if forward else PACKED,
         cost_estimate=pl.CostEstimate(
             flops=2 * passes * rows * channels * inner,
             bytes_accessed=8 * channels * inner,
@@ -512,7 +513,7 @@
         ],
         in_specs=[VMEM] * 3,
         out_specs=[VMEM] * 3,
-        compiler_params=PARAMS,
+        compiler_params=PACKED,
     )(near[0], near[2], enter)
     for step in range(stages - 1):
         arrays = [enter] if step else [enter, *head]
@@ -577,7 +578,7 @@
             out_shape=jax.ShapeDtypeStruct(outs[1].shape, outs[1].dtype),
             in_specs=[VMEM] * 5,
             out_specs=VMEM,
-            compiler_params=PARAMS,
+            compiler_params=PACKED,
         )(near[1], near[3], outs[0], outs[1], inners[0])
         back_inners.insert(0, tail)
     going = pick(upstreams, True)
@@ -678,7 +679,7 @@
                 pltpu.VMEM((8 * rows, channels // 2), jnp.bfloat16),
                 pltpu.VMEM((8 * rows, inner), jnp.bfloat16),
             ],
-            compiler_params=PARAMS,
+            compiler_params=PACKED,
         )(*operands)
         came = exchange(send, stages, replicas, 2, 1)
         for bit in range(2, replicas.bit_length() - 1):

time: 47.8 us -> 47.8 us (level)
  no operation moved by 1% of the time
where the time goes in v13:
time: 47.8 us; the launch traced here: 47.6 us
  starting transfers between devices  22.4 us (47%)
  waiting for transfers between devices  15.6 us (33%)
  Pallas kernels  9.11 us (19%)
    ppermute x7, starting transfers between devices, exchange(): return lax.ppermute(shard, AXES, pairs)  10.8 us
    ppermute x7, waiting for transfers between devices, exchange(): return lax.ppermute(shard, AXES, pairs)  8.24 us
    ppermute x2, starting transfers between devices, hop(): return lax.ppermute(shard, 'pipe', pairs)  4.86 us
    ppermute x3, starting transfers between devices, mirror(): return lax.ppermute(shard, 'pipe', mirror_pairs)  4.67 us
    ppermute x3, waiting for transfers between devices, mirror(): return lax.ppermute(shard, 'pipe', mirror_pairs)  4.09 us
    pallas_call x3, Pallas kernels, run_stage(): pl.pallas_call(functools.partial(stage_body, step, forward, backward, las...  3.26 us
    ppermute x2, waiting for transfers between devices, hop(): return lax.ppermute(shard, 'pipe', pairs)  3.23 us
    pallas_call x2, Pallas kernels, load(): pl.pallas_call(functools.partial(load_body, step), out_shape=outs, in_spe...  2.44 us
  transfers between devices with their start and end apart: 22, of which 9 were waited for; matrix products, arithmetic and copies ran while one was open for 0% of the time, Pallas kernels for 11%

profile of v13, /device:TPU:0, one launch (start us, length us, event | category | flops | bytes accessed | tf_op | source)
XLA Modules:
  0.0 47.6 jit_solution(10420049443551664251)
XLA Ops:
  0.0 1.2 %shard_map.46 = (bf16[1024,256]{1,0:T(8,128)(2,1)S(1)}, bf16[1024,256]{1,0:T(8,128)(2,1)S(1)}, bf16[32,1024]{1,0:T(8,128)(2,1)S(1)}) custom-call(bf16[2,1024,256]{2,1,0:T(8,128)(2,1)} %bitcast.20, bf16[2,1024,256]{2,1,0:T(8,128)(2,1)} %bitcast.22, bf16[2,2,32,1024]{3,2,1,0:T(8,128)(2,1)} %inputs), custom_call_target="tpu_custom_call" | custom-call | tf_op jit(solution)/shard_map/pallas_call | solution.py:69
  1.2 0.6 %collective-permute-start = (bf16[1024,256]{1,0:T(8,128)(2,1)S(1)}, bf16[1024,256]{1,0:T(8,128)(2,1)S(1)}, u32[]{:S(2)}, u32[]{:S(2)}) collective-permute-start(bf16[1024,256]{1,0:T(8,128)(2,1)S(1)} %get-tuple-element.51.own.refs_0_), channel_id=1, source_target_pairs={{0,8},{8,0},{16,24},{24,16},{1,9},{9,1},{17,25},{25,17},{2,10},{10... | collective-permute-start | bytes 1572872 | tf_op jit(solution)/shard_map/ppermute | solution.py:481
  1.8 0.1 collective-permute-start.1
  1.9 1.2 %shard_map.49 = (bf16[1024,256]{1,0:T(8,128)(2,1)S(1)}, bf16[1024,256]{1,0:T(8,128)(2,1)S(1)}) custom-call(bf16[2,1024,256]{2,1,0:T(8,128)(2,1)} %bitcast.21, bf16[2,1024,256]{2,1,0:T(8,128)(2,1)} %bitcast.23), custom_call_target="tpu_custom_call" | custom-call | tf_op jit(solution)/shard_map/pallas_call | solution.py:69
  3.1 0.5 %collective-permute-start.3 = (bf16[1024,256]{1,0:T(8,128)(2,1)S(1)}, bf16[1024,256]{1,0:T(8,128)(2,1)S(1)}, u32[]{:S(2)}, u32[]{:S(2)}) collective-permute-start(bf16[1024,256]{1,0:T(8,128)(2,1)S(1)} %get-tuple-element.59.expand_own.refs_1_), channel_id=1, source_target_pairs={{0,8},{8,0},{16,24},{24,16},{1,9},{9,1},{17,25},{25,17},{2,10},{10... | collective-permute-start | bytes 1572872 | tf_op jit(solution)/shard_map/ppermute | solution.py:481
  3.6 0.1 collective-permute-start.2
  3.7 0.3 shard_map.47
  4.0 0.1 collective-permute-done.1.refs_3_.other
  4.1 0.8 %shard_map.48 = (bf16[2,32,1280]{2,1,0:T(8,128)(2,1)S(1)}, bf16[32,1024]{1,0:T(8,128)(2,1)S(1)}, bf16[2,32,1024]{2,1,0:T(8,128)(2,1)S(1)}, f32[2,32,256]{2,1,0:T(8,128)S(1)}) custom-call(bf16[1024,256]{1,0:T(8,128)(2,1)S(1)} %get-tuple-element.51.own.refs_0_, bf16[1024,256]{1,0:T(8,128)(2,1)S(1)} %get-tuple-element.52.refs_1_.own, ...), custom_call_target="tpu_custom_call" | custom-call | flops 67108864 | bytes 2097152 | tf_op jit(solution)/shard_map/pallas_call | solution.py:282
  4.9 2.9 %collective-permute-start.4 = (bf16[32,1024]{1,0:T(8,128)(2,1)S(1)}, bf16[32,1024]{1,0:T(8,128)(2,1)S(1)}, u32[]{:S(2)}, u32[]{:S(2)}) collective-permute-start(bf16[32,1024]{1,0:T(8,128)(2,1)S(1)} %get-tuple-element.60.leave), channel_id=1, source_target_pairs={{0,16},{16,0},{8,24},{24,8},{1,17},{17,1},{9,25},{25,9},{2,18},{18... | collective-permute-start | bytes 196616 | tf_op jit(solution)/shard_map/ppermute | solution.py:478
  7.8 0.0 collective-permute-done.3.expand_other.refs_3_
  7.8 1.2 %shard_map.50 = (bf16[32,1024]{1,0:T(8,128)(2,1)S(1)}, f32[32,256]{1,0:T(8,128)S(1)}, bf16[32,1024]{1,0:T(8,128)(2,1)S(1)}, bf16[32,1024]{1,0:T(8,128)(2,1)S(1)}) custom-call(bf16[1024,256]{1,0:T(8,128)(2,1)S(1)} %get-tuple-element.59.expand_own.refs_1_, bf16[1024,256]{1,0:T(8,128)(2,1)S(1)} %collective-permute-done.3.expand_other.refs_3_, ...), custom_call_target="tpu_custom_call" | custom-call | tf_op jit(solution)/shard_map/pallas_call | solution.py:530
  9.0 0.0 collective-permute-done.2.refs_2_
  9.0 1.2 %collective-permute-done.4.refs_4_ = bf16[32,1024]{1,0:T(8,128)(2,1)S(1)} collective-permute-done((bf16[32,1024]{1,0:T(8,128)(2,1)S(1)}, bf16[32,1024]{1,0:T(8,128)(2,1)S(1)}, u32[]{:S(2)}, u32[]{:S(2)}) %collective-permute-start.4) | collective-permute-done | bytes 65568 | tf_op jit(solution)/shard_map/ppermute | solution.py:478
  10.2 1.8 %shard_map.51 = (bf16[2,32,1280]{2,1,0:T(8,128)(2,1)S(1)}, bf16[2,32,1024]{2,1,0:T(8,128)(2,1)S(1)}, bf16[2,32,256]{2,1,0:T(8,128)(2,1)S(1)}, bf16[32,1024]{1,0:T(8,128)(2,1)S(1)}) custom-call(bf16[1024,256]{1,0:T(8,128)(2,1)S(1)} %get-tuple-element.58.refs_0_, bf16[1024,256]{1,0:T(8,128)(2,1)S(1)} %get-tuple-element.59.expand_own.refs_1_, ...), custom_call_target="tpu_custom_call" | custom-call | flops 134217728 | bytes 2097152 | tf_op jit(solution)/shard_map/pallas_call | solution.py:282
  12.0 2.0 %collective-permute-start.6 = (bf16[32,1024]{1,0:T(8,128)(2,1)S(1)}, bf16[32,1024]{1,0:T(8,128)(2,1)S(1)}, u32[]{:S(2)}, u32[]{:S(2)}) collective-permute-start(bf16[32,1024]{1,0:T(8,128)(2,1)S(1)} %get-tuple-element.65), channel_id=1, source_target_pairs={{0,16},{16,0},{8,24},{24,8},{1,17},{17,1},{9,25},{25,9},{2,18},{18... | collective-permute-start | bytes 196616 | tf_op jit(solution)/shard_map/ppermute | solution.py:478
  14.0 0.1 collective-permute-start.5
  14.2 0.2 collective-permute-start.10
  14.3 2.1 %collective-permute-done.6.refs_4_ = bf16[32,1024]{1,0:T(8,128)(2,1)S(1)} collective-permute-done((bf16[32,1024]{1,0:T(8,128)(2,1)S(1)}, bf16[32,1024]{1,0:T(8,128)(2,1)S(1)}, u32[]{:S(2)}, u32[]{:S(2)}) %collective-permute-start.6) | collective-permute-done | bytes 65568 | tf_op jit(solution)/shard_map/ppermute | solution.py:478
  16.4 0.6 %shard_map.52 = (bf16[2,32,1024]{2,1,0:T(8,128)(2,1)S(1)}, bf16[2,32,256]{2,1,0:T(8,128)(2,1)S(1)}) custom-call(bf16[1024,256]{1,0:T(8,128)(2,1)S(1)} %get-tuple-element.51.own.refs_0_, bf16[1024,256]{1,0:T(8,128)(2,1)S(1)} %get-tuple-element.52.refs_1_.own, bf16[1024,256]{1,0:T(8,128)(2,1)S(1)} %collective-permute-done.other.refs_2_, ...), custom_call_target="tpu_custom_call" | custom-call | flops 67108864 | bytes 2097152 | tf_op jit(solution)/shard_map/pallas_call | solution.py:282
  17.0 0.2 shard_map.53.refs_6_
  17.3 0.1 collective-permute-start.8
  17.4 2.5 %collective-permute-start.12 = (bf16[2,32,256]{2,1,0:T(8,128)(2,1)S(1)}, bf16[2,32,256]{2,1,0:T(8,128)(2,1)S(1)}, u32[]{:S(2)}, u32[]{:S(2)}) collective-permute-start(bf16[2,32,256]{2,1,0:T(8,128)(2,1)S(1)} %broadcast_select_fusion.7), channel_id=1, source_target_pairs={{0,16},{8,24},{16,0},{24,8},{1,17},{9,25},{17,1},{25,9},{2,18},{10... | collective-permute-start | bytes 98312 | tf_op jit(solution)/shard_map/ppermute | solution.py:484
  20.0 0.2 collective-permute-start.7
  20.1 1.8 %collective-permute-done.12 = bf16[2,32,256]{2,1,0:T(8,128)(2,1)S(1)} collective-permute-done((bf16[2,32,256]{2,1,0:T(8,128)(2,1)S(1)}, bf16[2,32,256]{2,1,0:T(8,128)(2,1)S(1)}, u32[]{:S(2)}, u32[]{:S(2)}) %collective-permute-start.12) | collective-permute-done | bytes 32800 | tf_op jit(solution)/shard_map/ppermute | solution.py:484
  21.9 1.9 %collective-permute-start.17 = (bf16[32,1024]{1,0:T(8,128)(2,1)S(1)}, bf16[32,1024]{1,0:T(8,128)(2,1)S(1)}, u32[]{:S(2)}, u32[]{:S(2)}) collective-permute-start(bf16[32,1024]{1,0:T(8,128)(2,1)S(1)} %fusion.1), channel_id=1, source_target_pairs={{0,16},{8,24},{16,0},{24,8},{1,17},{9,25},{17,1},{25,9},{2,18},{10... | collective-permute-start | bytes 196616 | tf_op jit(solution)/shard_map/ppermute | solution.py:484
  23.9 0.0 collective-permute-done.10
  23.9 0.0 collective-permute-start.13
  23.9 2.3 %collective-permute-done.17 = bf16[32,1024]{1,0:T(8,128)(2,1)S(1)} collective-permute-done((bf16[32,1024]{1,0:T(8,128)(2,1)S(1)}, bf16[32,1024]{1,0:T(8,128)(2,1)S(1)}, u32[]{:S(2)}, u32[]{:S(2)}) %collective-permute-start.17) | collective-permute-done | bytes 65568 | tf_op jit(solution)/shard_map/ppermute | solution.py:484
  26.2 0.0 collective-permute-start.11
  26.2 0.6 %collective-permute-start.18 = (bf16[32,1024]{1,0:T(8,128)(2,1)S(1)}, bf16[32,1024]{1,0:T(8,128)(2,1)S(1)}, u32[]{:S(2)}, u32[]{:S(2)}) collective-permute-start(bf16[32,1024]{1,0:T(8,128)(2,1)S(1)} %get-tuple-element.95), channel_id=1, source_target_pairs={{0,8},{8,0},{16,24},{24,16},{1,9},{9,1},{17,25},{25,17},{2,10},{10... | collective-permute-start | bytes 196616 | tf_op jit(solution)/shard_map/ppermute | solution.py:481
  26.8 0.1 shard_map.54
  26.9 1.4 %collective-permute-start.9 = (bf16[64,1536]{1,0:T(8,128)(2,1)S(1)}, bf16[64,1536]{1,0:T(8,128)(2,1)S(1)}, u32[]{:S(2)}, u32[]{:S(2)}) collective-permute-start(bf16[64,1536]{1,0:T(8,128)(2,1)S(1)} %get-tuple-element.74), channel_id=1, source_target_pairs={{0,1},{1,0},{2,3},{3,2},{4,5},{5,4},{6,7},{7,6},{8,10},{9,11},{10,... | collective-permute-start | bytes 589832 | tf_op jit(solution)/shard_map/ppermute | solution.py:625
  28.3 0.1 shard_map.58
  28.4 0.8 %collective-permute-start.19 = (bf16[64,768]{1,0:T(8,128)(2,1)S(1)}, bf16[64,768]{1,0:T(8,128)(2,1)S(1)}, u32[]{:S(2)}, u32[]{:S(2)}) collective-permute-start(bf16[64,768]{1,0:T(8,128)(2,1)S(1)} %get-tuple-element.90), channel_id=1, source_target_pairs={{0,1},{1,0},{2,3},{3,2},{4,5},{5,4},{6,7},{7,6},{8,10},{9,11},{10,... | collective-permute-start | bytes 294920 | tf_op jit(solution)/shard_map/ppermute | solution.py:625
  29.2 1.4 %collective-permute-start.14 = (bf16[64,768]{1,0:T(8,128)(2,1)S(1)}, bf16[64,768]{1,0:T(8,128)(2,1)S(1)}, u32[]{:S(2)}, u32[]{:S(2)}) collective-permute-start(bf16[64,768]{1,0:T(8,128)(2,1)S(1)} %get-tuple-element.80), channel_id=1, source_target_pairs={{0,1},{1,0},{2,3},{3,2},{4,5},{5,4},{6,7},{7,6},{8,10},{9,11},{10,... | collective-permute-start | bytes 294920 | tf_op jit(solution)/shard_map/ppermute | solution.py:625
  30.6 3.1 %collective-permute-done.19.refs_5_ = bf16[64,768]{1,0:T(8,128)(2,1)S(1)} collective-permute-done((bf16[64,768]{1,0:T(8,128)(2,1)S(1)}, bf16[64,768]{1,0:T(8,128)(2,1)S(1)}, u32[]{:S(2)}, u32[]{:S(2)}) %collective-permute-start.19) | collective-permute-done | bytes 98336 | tf_op jit(solution)/shard_map/ppermute | solution.py:625
  33.7 0.3 shard_map.59
  34.1 1.4 %collective-permute-start.20 = (bf16[2,128,256]{2,1,0:T(8,128)(2,1)S(1)}, bf16[2,128,256]{2,1,0:T(8,128)(2,1)S(1)}, u32[]{:S(2)}, u32[]{:S(2)}) collective-permute-start(bf16[2,128,256]{2,1,0:T(8,128)(2,1)S(1)} %get-tuple-element.92), channel_id=1, source_target_pairs={{0,2},{1,3},{2,0},{3,1},{4,6},{5,7},{6,4},{7,5},{8,9},{9,8},{10,11... | collective-permute-start | bytes 393224 | tf_op jit(solution)/shard_map/ppermute | solution.py:625
  35.5 0.3 shard_map.56
  35.8 0.7 %collective-permute-start.15 = (bf16[2,128,256]{2,1,0:T(8,128)(2,1)S(1)}, bf16[2,128,256]{2,1,0:T(8,128)(2,1)S(1)}, u32[]{:S(2)}, u32[]{:S(2)}) collective-permute-start(bf16[2,128,256]{2,1,0:T(8,128)(2,1)S(1)} %get-tuple-element.82), channel_id=1, source_target_pairs={{0,2},{1,3},{2,0},{3,1},{4,6},{5,7},{6,4},{7,5},{8,9},{9,8},{10,11... | collective-permute-start | bytes 393224 | tf_op jit(solution)/shard_map/ppermute | solution.py:625
  36.6 2.5 %collective-permute-done.20.came = bf16[2,128,256]{2,1,0:T(8,128)(2,1)S(1)} collective-permute-done((bf16[2,128,256]{2,1,0:T(8,128)(2,1)S(1)}, bf16[2,128,256]{2,1,0:T(8,128)(2,1)S(1)}, u32[]{:S(2)}, u32[]{:S(2)}) %collective-permute-start.20) | collective-permute-done | bytes 131104 | tf_op jit(solution)/shard_map/ppermute | solution.py:625
  39.1 2.4 %collective-permute-start.21 = (bf16[1,128,256]{2,1,0:T(8,128)(2,1)S(1)}, bf16[1,128,256]{2,1,0:T(8,128)(2,1)S(1)}, u32[]{:S(2)}, u32[]{:S(2)}) collective-permute-start(bf16[1,128,256]{2,1,0:T(8,128)(2,1)S(1)} %get-tuple-element.94), channel_id=1, source_target_pairs={{0,4},{1,5},{2,6},{3,7},{4,0},{5,1},{6,2},{7,3},{8,12},{9,13},{10,... | collective-permute-start | bytes 196616 | tf_op jit(solution)/shard_map/ppermute | solution.py:625
  41.6 0.0 collective-permute-done.15.came
  41.6 2.6 %collective-permute-start.16 = (bf16[1,128,256]{2,1,0:T(8,128)(2,1)S(1)}, bf16[1,128,256]{2,1,0:T(8,128)(2,1)S(1)}, u32[]{:S(2)}, u32[]{:S(2)}) collective-permute-start(bf16[1,128,256]{2,1,0:T(8,128)(2,1)S(1)} %get-tuple-element.84), channel_id=1, source_target_pairs={{0,4},{1,5},{2,6},{3,7},{4,0},{5,1},{6,2},{7,3},{8,12},{9,13},{10,... | collective-permute-start | bytes 196616 | tf_op jit(solution)/shard_map/ppermute | solution.py:625
  44.3 1.5 %collective-permute-done.21.came_expand = bf16[1,128,256]{2,1,0:T(8,128)(2,1)S(1)} collective-permute-done((bf16[1,128,256]{2,1,0:T(8,128)(2,1)S(1)}, bf16[1,128,256]{2,1,0:T(8,128)(2,1)S(1)}, u32[]{:S(2)}, u32[]{:S(2)}) %collective-permute-start.21) | collective-permute-done | bytes 65568 | tf_op jit(solution)/shard_map/ppermute | solution.py:625
  45.8 1.1 %collective-permute-done.16.came_reduce = bf16[1,128,256]{2,1,0:T(8,128)(2,1)S(1)} collective-permute-done((bf16[1,128,256]{2,1,0:T(8,128)(2,1)S(1)}, bf16[1,128,256]{2,1,0:T(8,128)(2,1)S(1)}, u32[]{:S(2)}, u32[]{:S(2)}) %collective-permute-start.16) | collective-permute-done | bytes 65568 | tf_op jit(solution)/shard_map/ppermute | solution.py:625
  46.8 0.7 %shard_map.61 = f32[1,2,128,256]{3,2,1,0:T(8,128)} custom-call(f32[1,128,256]{2,1,0:T(8,128)S(1)} %get-tuple-element.83.keep_reduce, bf16[1,128,256]{2,1,0:T(8,128)(2,1)S(1)} %collective-permute-done.16.came_reduce, f32[1,128,256]{2,1,0:T(8,128)S(1)} %get-tuple-element.93.keep_expand, bf16[1,128,256]{2,1,0:T(8,128)(2,1)S(1)} %collective-permute-done.21.came_expand), custom_call_target="tpu_custom_call" | custom-call | tf_op jit(solution)/shard_map/pallas_call | solution.py:604
  (28 shorter events, 0.3 us)
Async XLA Ops:
  1.2 2.4 %collective-permute-start = (bf16[1024,256]{1,0:T(8,128)(2,1)S(1)}, bf16[1024,256]{1,0:T(8,128)(2,1)S(1)}, u32[]{:S(2)}, u32[]{:S(2)}) collective-permute-start(bf16[1024,256]{1,0:T(8,128)(2,1)S(1)} %get-tuple-element.51.own.refs_0_), channel_id=1, source_target_pairs={{0,8},{8,0},{16,24},{24,16},{1,9},{9,1},{17,25},{25,17},{2,10},{10... | collective-permute-start | bytes 1572872 | tf_op jit(solution)/shard_map/ppermute | solution.py:481
  1.8 2.3 %collective-permute-start.1 = (bf16[1024,256]{1,0:T(8,128)(2,1)S(1)}, bf16[1024,256]{1,0:T(8,128)(2,1)S(1)}, u32[]{:S(2)}, u32[]{:S(2)}) collective-permute-start(bf16[1024,256]{1,0:T(8,128)(2,1)S(1)} %get-tuple-element.52.refs_1_.own), channel_id=1, source_target_pairs={{0,8},{8,0},{16,24},{24,16},{1,9},{9,1},{17,25},{25,17},{2,10},{10... | collective-permute-start | bytes 1572872 | tf_op jit(solution)/shard_map/ppermute | solution.py:481
  3.1 4.7 %collective-permute-start.3 = (bf16[1024,256]{1,0:T(8,128)(2,1)S(1)}, bf16[1024,256]{1,0:T(8,128)(2,1)S(1)}, u32[]{:S(2)}, u32[]{:S(2)}) collective-permute-start(bf16[1024,256]{1,0:T(8,128)(2,1)S(1)} %get-tuple-element.59.expand_own.refs_1_), channel_id=1, source_target_pairs={{0,8},{8,0},{16,24},{24,16},{1,9},{9,1},{17,25},{25,17},{2,10},{10... | collective-permute-start | bytes 1572872 | tf_op jit(solution)/shard_map/ppermute | solution.py:481
  3.6 5.4 %collective-permute-start.2 = (bf16[1024,256]{1,0:T(8,128)(2,1)S(1)}, bf16[1024,256]{1,0:T(8,128)(2,1)S(1)}, u32[]{:S(2)}, u32[]{:S(2)}) collective-permute-start(bf16[1024,256]{1,0:T(8,128)(2,1)S(1)} %get-tuple-element.58.refs_0_), channel_id=1, source_target_pairs={{0,8},{8,0},{16,24},{24,16},{1,9},{9,1},{17,25},{25,17},{2,10},{10... | collective-permute-start | bytes 1572872 | tf_op jit(solution)/shard_map/ppermute | solution.py:481
  4.9 5.3 %collective-permute-start.4 = (bf16[32,1024]{1,0:T(8,128)(2,1)S(1)}, bf16[32,1024]{1,0:T(8,128)(2,1)S(1)}, u32[]{:S(2)}, u32[]{:S(2)}) collective-permute-start(bf16[32,1024]{1,0:T(8,128)(2,1)S(1)} %get-tuple-element.60.leave), channel_id=1, source_target_pairs={{0,16},{16,0},{8,24},{24,8},{1,17},{17,1},{9,25},{25,9},{2,18},{18... | collective-permute-start | bytes 196616 | tf_op jit(solution)/shard_map/ppermute | solution.py:478
  12.0 4.4 %collective-permute-start.6 = (bf16[32,1024]{1,0:T(8,128)(2,1)S(1)}, bf16[32,1024]{1,0:T(8,128)(2,1)S(1)}, u32[]{:S(2)}, u32[]{:S(2)}) collective-permute-start(bf16[32,1024]{1,0:T(8,128)(2,1)S(1)} %get-tuple-element.65), channel_id=1, source_target_pairs={{0,16},{16,0},{8,24},{24,8},{1,17},{17,1},{9,25},{25,9},{2,18},{18... | collective-permute-start | bytes 196616 | tf_op jit(solution)/shard_map/ppermute | solution.py:478
  14.0 12.8 %collective-permute-start.5 = (bf16[32,1280]{1,0:T(8,128)(2,1)S(1)}, bf16[32,1280]{1,0:T(8,128)(2,1)S(1)}, u32[]{:S(2)}, u32[]{:S(2)}) collective-permute-start(bf16[32,1280]{1,0:T(8,128)(2,1)S(1)} %fusion), channel_id=1, source_target_pairs={{0,8},{8,0},{16,24},{24,16},{1,9},{9,1},{17,25},{25,17},{2,10},{10... | collective-permute-start | bytes 245768 | tf_op jit(solution)/shard_map/ppermute | solution.py:481
  14.2 9.7 %collective-permute-start.10 = (bf16[32,1536]{1,0:T(8,128)(2,1)S(1)}, bf16[32,1536]{1,0:T(8,128)(2,1)S(1)}, u32[]{:S(2)}, u32[]{:S(2)}) collective-permute-start(bf16[32,1536]{1,0:T(8,128)(2,1)S(1)} %pad_maximum_fusion), channel_id=1, source_target_pairs={{0,16},{8,24},{16,0},{24,8},{1,17},{9,25},{17,1},{25,9},{2,18},{10... | collective-permute-start | bytes 294920 | tf_op jit(solution)/shard_map/ppermute | solution.py:484
  17.3 8.9 %collective-permute-start.8 = (bf16[32,256]{1,0:T(8,128)(2,1)S(1)}, bf16[32,256]{1,0:T(8,128)(2,1)S(1)}, u32[]{:S(2)}, u32[]{:S(2)}) collective-permute-start(bf16[32,256]{1,0:T(8,128)(2,1)S(1)} %fusion.4), channel_id=1, source_target_pairs={{0,8},{8,0},{16,24},{24,16},{1,9},{9,1},{17,25},{25,17},{2,10},{10... | collective-permute-start | bytes 49160 | tf_op jit(solution)/shard_map/ppermute | solution.py:481
  17.4 4.5 %collective-permute-start.12 = (bf16[2,32,256]{2,1,0:T(8,128)(2,1)S(1)}, bf16[2,32,256]{2,1,0:T(8,128)(2,1)S(1)}, u32[]{:S(2)}, u32[]{:S(2)}) collective-permute-start(bf16[2,32,256]{2,1,0:T(8,128)(2,1)S(1)} %broadcast_select_fusion.7), channel_id=1, source_target_pairs={{0,16},{8,24},{16,0},{24,8},{1,17},{9,25},{17,1},{25,9},{2,18},{10... | collective-permute-start | bytes 98312 | tf_op jit(solution)/shard_map/ppermute | solution.py:484
  20.0 6.9 %collective-permute-start.7 = (bf16[32,1024]{1,0:T(8,128)(2,1)S(1)}, bf16[32,1024]{1,0:T(8,128)(2,1)S(1)}, u32[]{:S(2)}, u32[]{:S(2)}) collective-permute-start(bf16[32,1024]{1,0:T(8,128)(2,1)S(1)} %fusion.3), channel_id=1, source_target_pairs={{0,8},{8,0},{16,24},{24,16},{1,9},{9,1},{17,25},{25,17},{2,10},{10... | collective-permute-start | bytes 196616 | tf_op jit(solution)/shard_map/ppermute | solution.py:481
  21.9 4.3 %collective-permute-start.17 = (bf16[32,1024]{1,0:T(8,128)(2,1)S(1)}, bf16[32,1024]{1,0:T(8,128)(2,1)S(1)}, u32[]{:S(2)}, u32[]{:S(2)}) collective-permute-start(bf16[32,1024]{1,0:T(8,128)(2,1)S(1)} %fusion.1), channel_id=1, source_target_pairs={{0,16},{8,24},{16,0},{24,8},{1,17},{9,25},{17,1},{25,9},{2,18},{10... | collective-permute-start | bytes 196616 | tf_op jit(solution)/shard_map/ppermute | solution.py:484
  23.9 5.3 %collective-permute-start.13 = (bf16[32,256]{1,0:T(8,128)(2,1)S(1)}, bf16[32,256]{1,0:T(8,128)(2,1)S(1)}, u32[]{:S(2)}, u32[]{:S(2)}) collective-permute-start(bf16[32,256]{1,0:T(8,128)(2,1)S(1)} %get-tuple-element.103), channel_id=1, source_target_pairs={{0,8},{8,0},{16,24},{24,16},{1,9},{9,1},{17,25},{25,17},{2,10},{10... | collective-permute-start | bytes 49160 | tf_op jit(solution)/shard_map/ppermute | solution.py:481
  26.2 2.1 %collective-permute-start.11 = (bf16[32,1280]{1,0:T(8,128)(2,1)S(1)}, bf16[32,1280]{1,0:T(8,128)(2,1)S(1)}, u32[]{:S(2)}, u32[]{:S(2)}) collective-permute-start(bf16[32,1280]{1,0:T(8,128)(2,1)S(1)} %pad_maximum_fusion.2), channel_id=1, source_target_pairs={{0,8},{8,0},{16,24},{24,16},{1,9},{9,1},{17,25},{25,17},{2,10},{10... | collective-permute-start | bytes 245768 | tf_op jit(solution)/shard_map/ppermute | solution.py:481
  26.2 2.1 %collective-permute-start.18 = (bf16[32,1024]{1,0:T(8,128)(2,1)S(1)}, bf16[32,1024]{1,0:T(8,128)(2,1)S(1)}, u32[]{:S(2)}, u32[]{:S(2)}) collective-permute-start(bf16[32,1024]{1,0:T(8,128)(2,1)S(1)} %get-tuple-element.95), channel_id=1, source_target_pairs={{0,8},{8,0},{16,24},{24,16},{1,9},{9,1},{17,25},{25,17},{2,10},{10... | collective-permute-start | bytes 196616 | tf_op jit(solution)/shard_map/ppermute | solution.py:481
  26.9 6.8 %collective-permute-start.9 = (bf16[64,1536]{1,0:T(8,128)(2,1)S(1)}, bf16[64,1536]{1,0:T(8,128)(2,1)S(1)}, u32[]{:S(2)}, u32[]{:S(2)}) collective-permute-start(bf16[64,1536]{1,0:T(8,128)(2,1)S(1)} %get-tuple-element.74), channel_id=1, source_target_pairs={{0,1},{1,0},{2,3},{3,2},{4,5},{5,4},{6,7},{7,6},{8,10},{9,11},{10,... | collective-permute-start | bytes 589832 | tf_op jit(solution)/shard_map/ppermute | solution.py:625
  28.4 5.3 %collective-permute-start.19 = (bf16[64,768]{1,0:T(8,128)(2,1)S(1)}, bf16[64,768]{1,0:T(8,128)(2,1)S(1)}, u32[]{:S(2)}, u32[]{:S(2)}) collective-permute-start(bf16[64,768]{1,0:T(8,128)(2,1)S(1)} %get-tuple-element.90), channel_id=1, source_target_pairs={{0,1},{1,0},{2,3},{3,2},{4,5},{5,4},{6,7},{7,6},{8,10},{9,11},{10,... | collective-permute-start | bytes 294920 | tf_op jit(solution)/shard_map/ppermute | solution.py:625
  29.2 6.3 %collective-permute-start.14 = (bf16[64,768]{1,0:T(8,128)(2,1)S(1)}, bf16[64,768]{1,0:T(8,128)(2,1)S(1)}, u32[]{:S(2)}, u32[]{:S(2)}) collective-permute-start(bf16[64,768]{1,0:T(8,128)(2,1)S(1)} %get-tuple-element.80), channel_id=1, source_target_pairs={{0,1},{1,0},{2,3},{3,2},{4,5},{5,4},{6,7},{7,6},{8,10},{9,11},{10,... | collective-permute-start | bytes 294920 | tf_op jit(solution)/shard_map/ppermute | solution.py:625
  34.1 5.0 %collective-permute-start.20 = (bf16[2,128,256]{2,1,0:T(8,128)(2,1)S(1)}, bf16[2,128,256]{2,1,0:T(8,128)(2,1)S(1)}, u32[]{:S(2)}, u32[]{:S(2)}) collective-permute-start(bf16[2,128,256]{2,1,0:T(8,128)(2,1)S(1)} %get-tuple-element.92), channel_id=1, source_target_pairs={{0,2},{1,3},{2,0},{3,1},{4,6},{5,7},{6,4},{7,5},{8,9},{9,8},{10,11... | collective-permute-start | bytes 393224 | tf_op jit(solution)/shard_map/ppermute | solution.py:625
  35.8 5.7 %collective-permute-start.15 = (bf16[2,128,256]{2,1,0:T(8,128)(2,1)S(1)}, bf16[2,128,256]{2,1,0:T(8,128)(2,1)S(1)}, u32[]{:S(2)}, u32[]{:S(2)}) collective-permute-start(bf16[2,128,256]{2,1,0:T(8,128)(2,1)S(1)} %get-tuple-element.82), channel_id=1, source_target_pairs={{0,2},{1,3},{2,0},{3,1},{4,6},{5,7},{6,4},{7,5},{8,9},{9,8},{10,11... | collective-permute-start | bytes 393224 | tf_op jit(solution)/shard_map/ppermute | solution.py:625
  39.1 6.6 %collective-permute-start.21 = (bf16[1,128,256]{2,1,0:T(8,128)(2,1)S(1)}, bf16[1,128,256]{2,1,0:T(8,128)(2,1)S(1)}, u32[]{:S(2)}, u32[]{:S(2)}) collective-permute-start(bf16[1,128,256]{2,1,0:T(8,128)(2,1)S(1)} %get-tuple-element.94), channel_id=1, source_target_pairs={{0,4},{1,5},{2,6},{3,7},{4,0},{5,1},{6,2},{7,3},{8,12},{9,13},{10,... | collective-permute-start | bytes 196616 | tf_op jit(solution)/shard_map/ppermute | solution.py:625
  41.6 5.2 %collective-permute-start.16 = (bf16[1,128,256]{2,1,0:T(8,128)(2,1)S(1)}, bf16[1,128,256]{2,1,0:T(8,128)(2,1)S(1)}, u32[]{:S(2)}, u32[]{:S(2)}) collective-permute-start(bf16[1,128,256]{2,1,0:T(8,128)(2,1)S(1)} %get-tuple-element.84), channel_id=1, source_target_pairs={{0,4},{1,5},{2,6},{3,7},{4,0},{5,1},{6,2},{7,3},{8,12},{9,13},{10,... | collective-permute-start | bytes 196616 | tf_op jit(solution)/shard_map/ppermute | solution.py:625

commit v14 on v13

--- a/solution.py
+++ b/solution.py
@@ -451,9 +451,14 @@
         keep[place] = keep_in[mine] + came[mine].astype(jnp.float32)
 
 
-def finish_body(keep_reduce, came_reduce, keep_expand, came_expand, out):
-    out[0, 0] = keep_reduce[0] + came_reduce[0].astype(jnp.float32)
-    out[0, 1] = keep_expand[0] + came_expand[0].astype(jnp.float32)
+def finish_body(keep_reduce, came_reduce, keep_expand, came_expand, out, held, sems):
+    copies = []
+    for at, keep, came in ((1, keep_expand, came_expand), (0, keep_reduce, came_reduce)):
+        held[at] = keep[0] + came[0].astype(jnp.float32)
+        copies.append(pltpu.make_async_copy(held.at[at], out.at[0, at], sems.at[at]))
+        copies[-1].start()
+    for copy in copies:
+        copy.wait()
 
 
 def shards(inputs, cotangent, reduce_weight, expand_weight):
@@ -584,8 +589,9 @@
     going = pick(upstreams, True)
     far_up = mirror(near_core(going[0], going[1]) if mirrored else going)
     far_inner = mirror(pick(back_inners, True))
-    side_up = swap_cores(pick(upstreams)[1])
-    side_inner = swap_cores(pick(back_inners)[1])
+    side = [pick(upstreams)[1], pick(back_inners)[1]]
+    side = swap_cores(jnp.concatenate(side, axis=1))
+    side_up, side_inner = side[:, :channels], side[:, channels:]
     if mirrored:
         top = jnp.where(at_stage[0], leave, known[0])
         far_up, cross_up = near_core(far_up, top), near_core(top, far_up)
@@ -605,7 +611,11 @@
         finish_body,
         out_shape=jax.ShapeDtypeStruct((1, 2, chunk, inner), jnp.float32),
         in_specs=[VMEM] * 4,
-        out_specs=VMEM,
+        out_specs=HBM,
+        scratch_shapes=[
+            pltpu.VMEM((2, chunk, inner), jnp.float32),
+            pltpu.SemaphoreType.DMA((2,)),
+        ],
         compiler_params=PARAMS,
     )(*parts)
 

time: 47.8 us -> 45.9 us (0.960)
  starting transfers between devices: 22.4 us -> 20.3 us
    ppermute x3, starting transfers between devices: 4.67 us -> 2.9 us  [mirror(): return lax.ppermute(shard, 'pipe', mirror_pairs)]
    ppermute x10 -> x9, starting transfers between devices: 2.08 us -> 1.91 us  [swap_cores(): return lax.ppermute(shard, 'pipe', core_pairs)]
  transfers between devices with their start and end apart: 22 -> 21, of which waited for: 9 -> 9; matrix products, arithmetic and copies ran while one was open for 0% -> 0% of each run, Pallas kernels for 11% -> 12%
where the time goes in v14:
time: 45.9 us; the launch traced here: 45.7 us
  starting transfers between devices  20.3 us (44%)
  waiting for transfers between devices  15.7 us (34%)
  Pallas kernels  9.14 us (20%)
    ppermute x7, starting transfers between devices, exchange(): return lax.ppermute(shard, AXES, pairs)  10.7 us
    ppermute x7, waiting for transfers between devices, exchange(): return lax.ppermute(shard, AXES, pairs)  8.65 us
    ppermute x2, starting transfers between devices, hop(): return lax.ppermute(shard, 'pipe', pairs)  4.86 us
    ppermute x3, waiting for transfers between devices, mirror(): return lax.ppermute(shard, 'pipe', mirror_pairs)  3.78 us
    pallas_call x3, Pallas kernels, run_stage(): pl.pallas_call(functools.partial(stage_body, step, forward, backward, las...  3.26 us
    ppermute x2, waiting for transfers between devices, hop(): return lax.ppermute(shard, 'pipe', pairs)  3.23 us
    ppermute x3, starting transfers between devices, mirror(): return lax.ppermute(shard, 'pipe', mirror_pairs)  2.9 us
    pallas_call x2, Pallas kernels, load(): pl.pallas_call(functools.partial(load_body, step), out_shape=outs, in_spe...  2.44 us
  transfers between devices with their start and end apart: 21, of which 9 were waited for; matrix products, arithmetic and copies ran while one was open for 0% of the time, Pallas kernels for 12%

profile of v14, /device:TPU:0, one launch (start us, length us, event | category | flops | bytes accessed | tf_op | source)
XLA Modules:
  0.0 45.7 jit_solution(12655062793541336495)
XLA Ops:
  0.0 1.2 %shard_map.46 = (bf16[1024,256]{1,0:T(8,128)(2,1)S(1)}, bf16[1024,256]{1,0:T(8,128)(2,1)S(1)}, bf16[32,1024]{1,0:T(8,128)(2,1)S(1)}) custom-call(bf16[2,1024,256]{2,1,0:T(8,128)(2,1)} %bitcast.20, bf16[2,1024,256]{2,1,0:T(8,128)(2,1)} %bitcast.22, bf16[2,2,32,1024]{3,2,1,0:T(8,128)(2,1)} %inputs), custom_call_target="tpu_custom_call" | custom-call | tf_op jit(solution)/shard_map/pallas_call | solution.py:69
  1.2 0.6 %collective-permute-start = (bf16[1024,256]{1,0:T(8,128)(2,1)S(1)}, bf16[1024,256]{1,0:T(8,128)(2,1)S(1)}, u32[]{:S(2)}, u32[]{:S(2)}) collective-permute-start(bf16[1024,256]{1,0:T(8,128)(2,1)S(1)} %get-tuple-element.51.own.refs_0_), channel_id=1, source_target_pairs={{0,8},{8,0},{16,24},{24,16},{1,9},{9,1},{17,25},{25,17},{2,10},{10... | collective-permute-start | bytes 1572872 | tf_op jit(solution)/shard_map/ppermute | solution.py:486
  1.8 0.1 collective-permute-start.1
  1.9 1.2 %shard_map.49 = (bf16[1024,256]{1,0:T(8,128)(2,1)S(1)}, bf16[1024,256]{1,0:T(8,128)(2,1)S(1)}) custom-call(bf16[2,1024,256]{2,1,0:T(8,128)(2,1)} %bitcast.21, bf16[2,1024,256]{2,1,0:T(8,128)(2,1)} %bitcast.23), custom_call_target="tpu_custom_call" | custom-call | tf_op jit(solution)/shard_map/pallas_call | solution.py:69
  3.1 0.5 %collective-permute-start.3 = (bf16[1024,256]{1,0:T(8,128)(2,1)S(1)}, bf16[1024,256]{1,0:T(8,128)(2,1)S(1)}, u32[]{:S(2)}, u32[]{:S(2)}) collective-permute-start(bf16[1024,256]{1,0:T(8,128)(2,1)S(1)} %get-tuple-element.59.expand_own.refs_1_), channel_id=1, source_target_pairs={{0,8},{8,0},{16,24},{24,16},{1,9},{9,1},{17,25},{25,17},{2,10},{10... | collective-permute-start | bytes 1572872 | tf_op jit(solution)/shard_map/ppermute | solution.py:486
  3.6 0.1 collective-permute-start.2
  3.7 0.3 shard_map.47
  4.0 0.1 collective-permute-done.1.refs_3_.other
  4.1 0.8 %shard_map.48 = (bf16[2,32,1280]{2,1,0:T(8,128)(2,1)S(1)}, bf16[32,1024]{1,0:T(8,128)(2,1)S(1)}, bf16[2,32,1024]{2,1,0:T(8,128)(2,1)S(1)}, f32[2,32,256]{2,1,0:T(8,128)S(1)}) custom-call(bf16[1024,256]{1,0:T(8,128)(2,1)S(1)} %get-tuple-element.51.own.refs_0_, bf16[1024,256]{1,0:T(8,128)(2,1)S(1)} %get-tuple-element.52.refs_1_.own, ...), custom_call_target="tpu_custom_call" | custom-call | flops 67108864 | bytes 2097152 | tf_op jit(solution)/shard_map/pallas_call | solution.py:282
  4.9 2.9 %collective-permute-start.4 = (bf16[32,1024]{1,0:T(8,128)(2,1)S(1)}, bf16[32,1024]{1,0:T(8,128)(2,1)S(1)}, u32[]{:S(2)}, u32[]{:S(2)}) collective-permute-start(bf16[32,1024]{1,0:T(8,128)(2,1)S(1)} %get-tuple-element.60.leave), channel_id=1, source_target_pairs={{0,16},{16,0},{8,24},{24,8},{1,17},{17,1},{9,25},{25,9},{2,18},{18... | collective-permute-start | bytes 196616 | tf_op jit(solution)/shard_map/ppermute | solution.py:483
  7.8 0.0 collective-permute-done.3.expand_other.refs_3_
  7.8 1.2 %shard_map.50 = (bf16[32,1024]{1,0:T(8,128)(2,1)S(1)}, f32[32,256]{1,0:T(8,128)S(1)}, bf16[32,1024]{1,0:T(8,128)(2,1)S(1)}, bf16[32,1024]{1,0:T(8,128)(2,1)S(1)}) custom-call(bf16[1024,256]{1,0:T(8,128)(2,1)S(1)} %get-tuple-element.59.expand_own.refs_1_, bf16[1024,256]{1,0:T(8,128)(2,1)S(1)} %collective-permute-done.3.expand_other.refs_3_, ...), custom_call_target="tpu_custom_call" | custom-call | tf_op jit(solution)/shard_map/pallas_call | solution.py:535
  9.0 0.0 collective-permute-done.2.refs_2_
  9.0 1.2 %collective-permute-done.4.refs_4_ = bf16[32,1024]{1,0:T(8,128)(2,1)S(1)} collective-permute-done((bf16[32,1024]{1,0:T(8,128)(2,1)S(1)}, bf16[32,1024]{1,0:T(8,128)(2,1)S(1)}, u32[]{:S(2)}, u32[]{:S(2)}) %collective-permute-start.4) | collective-permute-done | bytes 65568 | tf_op jit(solution)/shard_map/ppermute | solution.py:483
  10.2 1.8 %shard_map.51 = (bf16[2,32,1280]{2,1,0:T(8,128)(2,1)S(1)}, bf16[2,32,1024]{2,1,0:T(8,128)(2,1)S(1)}, bf16[2,32,256]{2,1,0:T(8,128)(2,1)S(1)}, bf16[32,1024]{1,0:T(8,128)(2,1)S(1)}) custom-call(bf16[1024,256]{1,0:T(8,128)(2,1)S(1)} %get-tuple-element.58.refs_0_, bf16[1024,256]{1,0:T(8,128)(2,1)S(1)} %get-tuple-element.59.expand_own.refs_1_, ...), custom_call_target="tpu_custom_call" | custom-call | flops 134217728 | bytes 2097152 | tf_op jit(solution)/shard_map/pallas_call | solution.py:282
  12.0 2.0 %collective-permute-start.6 = (bf16[32,1024]{1,0:T(8,128)(2,1)S(1)}, bf16[32,1024]{1,0:T(8,128)(2,1)S(1)}, u32[]{:S(2)}, u32[]{:S(2)}) collective-permute-start(bf16[32,1024]{1,0:T(8,128)(2,1)S(1)} %get-tuple-element.65), channel_id=1, source_target_pairs={{0,16},{16,0},{8,24},{24,8},{1,17},{17,1},{9,25},{25,9},{2,18},{18... | collective-permute-start | bytes 196616 | tf_op jit(solution)/shard_map/ppermute | solution.py:483
  14.0 0.1 collective-permute-start.5
  14.2 0.2 collective-permute-start.9
  14.3 2.1 %collective-permute-done.6.refs_4_ = bf16[32,1024]{1,0:T(8,128)(2,1)S(1)} collective-permute-done((bf16[32,1024]{1,0:T(8,128)(2,1)S(1)}, bf16[32,1024]{1,0:T(8,128)(2,1)S(1)}, u32[]{:S(2)}, u32[]{:S(2)}) %collective-permute-start.6) | collective-permute-done | bytes 65568 | tf_op jit(solution)/shard_map/ppermute | solution.py:483
  16.4 0.6 %shard_map.52 = (bf16[2,32,1024]{2,1,0:T(8,128)(2,1)S(1)}, bf16[2,32,256]{2,1,0:T(8,128)(2,1)S(1)}) custom-call(bf16[1024,256]{1,0:T(8,128)(2,1)S(1)} %get-tuple-element.51.own.refs_0_, bf16[1024,256]{1,0:T(8,128)(2,1)S(1)} %get-tuple-element.52.refs_1_.own, bf16[1024,256]{1,0:T(8,128)(2,1)S(1)} %collective-permute-done.other.refs_2_, ...), custom_call_target="tpu_custom_call" | custom-call | flops 67108864 | bytes 2097152 | tf_op jit(solution)/shard_map/pallas_call | solution.py:282
  17.0 0.2 shard_map.53.refs_6_
  17.3 2.5 %collective-permute-start.11 = (bf16[2,32,256]{2,1,0:T(8,128)(2,1)S(1)}, bf16[2,32,256]{2,1,0:T(8,128)(2,1)S(1)}, u32[]{:S(2)}, u32[]{:S(2)}) collective-permute-start(bf16[2,32,256]{2,1,0:T(8,128)(2,1)S(1)} %broadcast_select_fusion.7), channel_id=1, source_target_pairs={{0,16},{8,24},{16,0},{24,8},{1,17},{9,25},{17,1},{25,9},{2,18},{10... | collective-permute-start | bytes 98312 | tf_op jit(solution)/shard_map/ppermute | solution.py:489
  19.9 0.2 collective-permute-start.16
  20.1 1.7 %collective-permute-done.11 = bf16[2,32,256]{2,1,0:T(8,128)(2,1)S(1)} collective-permute-done((bf16[2,32,256]{2,1,0:T(8,128)(2,1)S(1)}, bf16[2,32,256]{2,1,0:T(8,128)(2,1)S(1)}, u32[]{:S(2)}, u32[]{:S(2)}) %collective-permute-start.11) | collective-permute-done | bytes 32800 | tf_op jit(solution)/shard_map/ppermute | solution.py:489
  21.8 0.0 collective-permute-start.12
  21.8 0.0 collective-permute-done.9
  21.8 0.6 %collective-permute-start.10 = (bf16[32,1280]{1,0:T(8,128)(2,1)S(1)}, bf16[32,1280]{1,0:T(8,128)(2,1)S(1)}, u32[]{:S(2)}, u32[]{:S(2)}) collective-permute-start(bf16[32,1280]{1,0:T(8,128)(2,1)S(1)} %pad_maximum_fusion.3), channel_id=1, source_target_pairs={{0,8},{8,0},{16,24},{24,16},{1,9},{9,1},{17,25},{25,17},{2,10},{10... | collective-permute-start | bytes 245768 | tf_op jit(solution)/shard_map/ppermute | solution.py:486
  22.4 2.1 %collective-permute-done.16 = bf16[32,1024]{1,0:T(8,128)(2,1)S(1)} collective-permute-done((bf16[32,1024]{1,0:T(8,128)(2,1)S(1)}, bf16[32,1024]{1,0:T(8,128)(2,1)S(1)}, u32[]{:S(2)}, u32[]{:S(2)}) %collective-permute-start.16) | collective-permute-done | bytes 65568 | tf_op jit(solution)/shard_map/ppermute | solution.py:489
  24.5 0.1 collective-permute-start.17
  24.6 0.0 collective-permute-done.5.refs_2_
  24.6 0.1 shard_map.54
  24.8 1.3 %collective-permute-start.8 = (bf16[64,1536]{1,0:T(8,128)(2,1)S(1)}, bf16[64,1536]{1,0:T(8,128)(2,1)S(1)}, u32[]{:S(2)}, u32[]{:S(2)}) collective-permute-start(bf16[64,1536]{1,0:T(8,128)(2,1)S(1)} %get-tuple-element.74), channel_id=1, source_target_pairs={{0,1},{1,0},{2,3},{3,2},{4,5},{5,4},{6,7},{7,6},{8,10},{9,11},{10,... | collective-permute-start | bytes 589832 | tf_op jit(solution)/shard_map/ppermute | solution.py:635
  26.1 0.0 collective-permute-done.17.refs_3_
  26.1 0.1 shard_map.58
  26.2 1.0 %collective-permute-start.18 = (bf16[64,768]{1,0:T(8,128)(2,1)S(1)}, bf16[64,768]{1,0:T(8,128)(2,1)S(1)}, u32[]{:S(2)}, u32[]{:S(2)}) collective-permute-start(bf16[64,768]{1,0:T(8,128)(2,1)S(1)} %get-tuple-element.90), channel_id=1, source_target_pairs={{0,1},{1,0},{2,3},{3,2},{4,5},{5,4},{6,7},{7,6},{8,10},{9,11},{10,... | collective-permute-start | bytes 294920 | tf_op jit(solution)/shard_map/ppermute | solution.py:635
  27.2 0.0 collective-permute-done.12.refs_3_
  27.3 1.1 %collective-permute-start.13 = (bf16[64,768]{1,0:T(8,128)(2,1)S(1)}, bf16[64,768]{1,0:T(8,128)(2,1)S(1)}, u32[]{:S(2)}, u32[]{:S(2)}) collective-permute-start(bf16[64,768]{1,0:T(8,128)(2,1)S(1)} %get-tuple-element.80), channel_id=1, source_target_pairs={{0,1},{1,0},{2,3},{3,2},{4,5},{5,4},{6,7},{7,6},{8,10},{9,11},{10,... | collective-permute-start | bytes 294920 | tf_op jit(solution)/shard_map/ppermute | solution.py:635
  28.4 3.1 %collective-permute-done.18.refs_5_ = bf16[64,768]{1,0:T(8,128)(2,1)S(1)} collective-permute-done((bf16[64,768]{1,0:T(8,128)(2,1)S(1)}, bf16[64,768]{1,0:T(8,128)(2,1)S(1)}, u32[]{:S(2)}, u32[]{:S(2)}) %collective-permute-start.18) | collective-permute-done | bytes 98336 | tf_op jit(solution)/shard_map/ppermute | solution.py:635
  31.5 0.3 shard_map.59
  31.9 1.4 %collective-permute-start.19 = (bf16[2,128,256]{2,1,0:T(8,128)(2,1)S(1)}, bf16[2,128,256]{2,1,0:T(8,128)(2,1)S(1)}, u32[]{:S(2)}, u32[]{:S(2)}) collective-permute-start(bf16[2,128,256]{2,1,0:T(8,128)(2,1)S(1)} %get-tuple-element.92), channel_id=1, source_target_pairs={{0,2},{1,3},{2,0},{3,1},{4,6},{5,7},{6,4},{7,5},{8,9},{9,8},{10,11... | collective-permute-start | bytes 393224 | tf_op jit(solution)/shard_map/ppermute | solution.py:635
  33.3 0.3 shard_map.56
  33.6 0.8 %collective-permute-start.14 = (bf16[2,128,256]{2,1,0:T(8,128)(2,1)S(1)}, bf16[2,128,256]{2,1,0:T(8,128)(2,1)S(1)}, u32[]{:S(2)}, u32[]{:S(2)}) collective-permute-start(bf16[2,128,256]{2,1,0:T(8,128)(2,1)S(1)} %get-tuple-element.82), channel_id=1, source_target_pairs={{0,2},{1,3},{2,0},{3,1},{4,6},{5,7},{6,4},{7,5},{8,9},{9,8},{10,11... | collective-permute-start | bytes 393224 | tf_op jit(solution)/shard_map/ppermute | solution.py:635
  34.4 2.5 %collective-permute-done.19.came = bf16[2,128,256]{2,1,0:T(8,128)(2,1)S(1)} collective-permute-done((bf16[2,128,256]{2,1,0:T(8,128)(2,1)S(1)}, bf16[2,128,256]{2,1,0:T(8,128)(2,1)S(1)}, u32[]{:S(2)}, u32[]{:S(2)}) %collective-permute-start.19) | collective-permute-done | bytes 131104 | tf_op jit(solution)/shard_map/ppermute | solution.py:635
  37.0 2.4 %collective-permute-start.20 = (bf16[1,128,256]{2,1,0:T(8,128)(2,1)S(1)}, bf16[1,128,256]{2,1,0:T(8,128)(2,1)S(1)}, u32[]{:S(2)}, u32[]{:S(2)}) collective-permute-start(bf16[1,128,256]{2,1,0:T(8,128)(2,1)S(1)} %get-tuple-element.94), channel_id=1, source_target_pairs={{0,4},{1,5},{2,6},{3,7},{4,0},{5,1},{6,2},{7,3},{8,12},{9,13},{10,... | collective-permute-start | bytes 196616 | tf_op jit(solution)/shard_map/ppermute | solution.py:635
  39.4 2.6 %collective-permute-start.15 = (bf16[1,128,256]{2,1,0:T(8,128)(2,1)S(1)}, bf16[1,128,256]{2,1,0:T(8,128)(2,1)S(1)}, u32[]{:S(2)}, u32[]{:S(2)}) collective-permute-start(bf16[1,128,256]{2,1,0:T(8,128)(2,1)S(1)} %get-tuple-element.84), channel_id=1, source_target_pairs={{0,4},{1,5},{2,6},{3,7},{4,0},{5,1},{6,2},{7,3},{8,12},{9,13},{10,... | collective-permute-start | bytes 196616 | tf_op jit(solution)/shard_map/ppermute | solution.py:635
  42.0 2.2 %collective-permute-done.20.came_expand = bf16[1,128,256]{2,1,0:T(8,128)(2,1)S(1)} collective-permute-done((bf16[1,128,256]{2,1,0:T(8,128)(2,1)S(1)}, bf16[1,128,256]{2,1,0:T(8,128)(2,1)S(1)}, u32[]{:S(2)}, u32[]{:S(2)}) %collective-permute-start.20) | collective-permute-done | bytes 65568 | tf_op jit(solution)/shard_map/ppermute | solution.py:635
  44.2 0.7 %collective-permute-done.15.came_reduce = bf16[1,128,256]{2,1,0:T(8,128)(2,1)S(1)} collective-permute-done((bf16[1,128,256]{2,1,0:T(8,128)(2,1)S(1)}, bf16[1,128,256]{2,1,0:T(8,128)(2,1)S(1)}, u32[]{:S(2)}, u32[]{:S(2)}) %collective-permute-start.15) | collective-permute-done | bytes 65568 | tf_op jit(solution)/shard_map/ppermute | solution.py:635
  45.0 0.7 %shard_map.61 = f32[1,2,128,256]{3,2,1,0:T(8,128)} custom-call(f32[1,128,256]{2,1,0:T(8,128)S(1)} %get-tuple-element.83.keep_reduce, bf16[1,128,256]{2,1,0:T(8,128)(2,1)S(1)} %collective-permute-done.15.came_reduce, f32[1,128,256]{2,1,0:T(8,128)S(1)} %get-tuple-element.93.keep_expand, bf16[1,128,256]{2,1,0:T(8,128)(2,1)S(1)} %collective-permute-done.20.came_expand), custom_call_target="tpu_custom_call" | custom-call | tf_op jit(solution)/shard_map/pallas_call | solution.py:610
  (29 shorter events, 0.3 us)
Async XLA Ops:
  1.2 2.4 %collective-permute-start = (bf16[1024,256]{1,0:T(8,128)(2,1)S(1)}, bf16[1024,256]{1,0:T(8,128)(2,1)S(1)}, u32[]{:S(2)}, u32[]{:S(2)}) collective-permute-start(bf16[1024,256]{1,0:T(8,128)(2,1)S(1)} %get-tuple-element.51.own.refs_0_), channel_id=1, source_target_pairs={{0,8},{8,0},{16,24},{24,16},{1,9},{9,1},{17,25},{25,17},{2,10},{10... | collective-permute-start | bytes 1572872 | tf_op jit(solution)/shard_map/ppermute | solution.py:486
  1.8 2.3 %collective-permute-start.1 = (bf16[1024,256]{1,0:T(8,128)(2,1)S(1)}, bf16[1024,256]{1,0:T(8,128)(2,1)S(1)}, u32[]{:S(2)}, u32[]{:S(2)}) collective-permute-start(bf16[1024,256]{1,0:T(8,128)(2,1)S(1)} %get-tuple-element.52.refs_1_.own), channel_id=1, source_target_pairs={{0,8},{8,0},{16,24},{24,16},{1,9},{9,1},{17,25},{25,17},{2,10},{10... | collective-permute-start | bytes 1572872 | tf_op jit(solution)/shard_map/ppermute | solution.py:486
  3.1 4.7 %collective-permute-start.3 = (bf16[1024,256]{1,0:T(8,128)(2,1)S(1)}, bf16[1024,256]{1,0:T(8,128)(2,1)S(1)}, u32[]{:S(2)}, u32[]{:S(2)}) collective-permute-start(bf16[1024,256]{1,0:T(8,128)(2,1)S(1)} %get-tuple-element.59.expand_own.refs_1_), channel_id=1, source_target_pairs={{0,8},{8,0},{16,24},{24,16},{1,9},{9,1},{17,25},{25,17},{2,10},{10... | collective-permute-start | bytes 1572872 | tf_op jit(solution)/shard_map/ppermute | solution.py:486
  3.6 5.4 %collective-permute-start.2 = (bf16[1024,256]{1,0:T(8,128)(2,1)S(1)}, bf16[1024,256]{1,0:T(8,128)(2,1)S(1)}, u32[]{:S(2)}, u32[]{:S(2)}) collective-permute-start(bf16[1024,256]{1,0:T(8,128)(2,1)S(1)} %get-tuple-element.58.refs_0_), channel_id=1, source_target_pairs={{0,8},{8,0},{16,24},{24,16},{1,9},{9,1},{17,25},{25,17},{2,10},{10... | collective-permute-start | bytes 1572872 | tf_op jit(solution)/shard_map/ppermute | solution.py:486
  4.9 5.3 %collective-permute-start.4 = (bf16[32,1024]{1,0:T(8,128)(2,1)S(1)}, bf16[32,1024]{1,0:T(8,128)(2,1)S(1)}, u32[]{:S(2)}, u32[]{:S(2)}) collective-permute-start(bf16[32,1024]{1,0:T(8,128)(2,1)S(1)} %get-tuple-element.60.leave), channel_id=1, source_target_pairs={{0,16},{16,0},{8,24},{24,8},{1,17},{17,1},{9,25},{25,9},{2,18},{18... | collective-permute-start | bytes 196616 | tf_op jit(solution)/shard_map/ppermute | solution.py:483
  12.0 4.4 %collective-permute-start.6 = (bf16[32,1024]{1,0:T(8,128)(2,1)S(1)}, bf16[32,1024]{1,0:T(8,128)(2,1)S(1)}, u32[]{:S(2)}, u32[]{:S(2)}) collective-permute-start(bf16[32,1024]{1,0:T(8,128)(2,1)S(1)} %get-tuple-element.65), channel_id=1, source_target_pairs={{0,16},{16,0},{8,24},{24,8},{1,17},{17,1},{9,25},{25,9},{2,18},{18... | collective-permute-start | bytes 196616 | tf_op jit(solution)/shard_map/ppermute | solution.py:483
  14.0 10.6 %collective-permute-start.5 = (bf16[32,1280]{1,0:T(8,128)(2,1)S(1)}, bf16[32,1280]{1,0:T(8,128)(2,1)S(1)}, u32[]{:S(2)}, u32[]{:S(2)}) collective-permute-start(bf16[32,1280]{1,0:T(8,128)(2,1)S(1)} %fusion), channel_id=1, source_target_pairs={{0,8},{8,0},{16,24},{24,16},{1,9},{9,1},{17,25},{25,17},{2,10},{10... | collective-permute-start | bytes 245768 | tf_op jit(solution)/shard_map/ppermute | solution.py:486
  14.2 7.6 %collective-permute-start.9 = (bf16[32,1536]{1,0:T(8,128)(2,1)S(1)}, bf16[32,1536]{1,0:T(8,128)(2,1)S(1)}, u32[]{:S(2)}, u32[]{:S(2)}) collective-permute-start(bf16[32,1536]{1,0:T(8,128)(2,1)S(1)} %pad_maximum_fusion), channel_id=1, source_target_pairs={{0,16},{8,24},{16,0},{24,8},{1,17},{9,25},{17,1},{25,9},{2,18},{10... | collective-permute-start | bytes 294920 | tf_op jit(solution)/shard_map/ppermute | solution.py:489
  17.3 4.4 %collective-permute-start.11 = (bf16[2,32,256]{2,1,0:T(8,128)(2,1)S(1)}, bf16[2,32,256]{2,1,0:T(8,128)(2,1)S(1)}, u32[]{:S(2)}, u32[]{:S(2)}) collective-permute-start(bf16[2,32,256]{2,1,0:T(8,128)(2,1)S(1)} %broadcast_select_fusion.7), channel_id=1, source_target_pairs={{0,16},{8,24},{16,0},{24,8},{1,17},{9,25},{17,1},{25,9},{2,18},{10... | collective-permute-start | bytes 98312 | tf_op jit(solution)/shard_map/ppermute | solution.py:489
  19.9 4.7 %collective-permute-start.7 = (bf16[32,1280]{1,0:T(8,128)(2,1)S(1)}, bf16[32,1280]{1,0:T(8,128)(2,1)S(1)}, u32[]{:S(2)}, u32[]{:S(2)}) collective-permute-start(bf16[32,1280]{1,0:T(8,128)(2,1)S(1)} %pad_maximum_fusion.1), channel_id=1, source_target_pairs={{0,8},{8,0},{16,24},{24,16},{1,9},{9,1},{17,25},{25,17},{2,10},{10... | collective-permute-start | bytes 245768 | tf_op jit(solution)/shard_map/ppermute | solution.py:486
  19.9 4.6 %collective-permute-start.16 = (bf16[32,1024]{1,0:T(8,128)(2,1)S(1)}, bf16[32,1024]{1,0:T(8,128)(2,1)S(1)}, u32[]{:S(2)}, u32[]{:S(2)}) collective-permute-start(bf16[32,1024]{1,0:T(8,128)(2,1)S(1)} %fusion.1), channel_id=1, source_target_pairs={{0,16},{8,24},{16,0},{24,8},{1,17},{9,25},{17,1},{25,9},{2,18},{10... | collective-permute-start | bytes 196616 | tf_op jit(solution)/shard_map/ppermute | solution.py:489
  21.8 5.4 %collective-permute-start.12 = (bf16[32,256]{1,0:T(8,128)(2,1)S(1)}, bf16[32,256]{1,0:T(8,128)(2,1)S(1)}, u32[]{:S(2)}, u32[]{:S(2)}) collective-permute-start(bf16[32,256]{1,0:T(8,128)(2,1)S(1)} %get-tuple-element.103), channel_id=1, source_target_pairs={{0,8},{8,0},{16,24},{24,16},{1,9},{9,1},{17,25},{25,17},{2,10},{10... | collective-permute-start | bytes 49160 | tf_op jit(solution)/shard_map/ppermute | solution.py:486
  21.8 4.3 %collective-permute-start.10 = (bf16[32,1280]{1,0:T(8,128)(2,1)S(1)}, bf16[32,1280]{1,0:T(8,128)(2,1)S(1)}, u32[]{:S(2)}, u32[]{:S(2)}) collective-permute-start(bf16[32,1280]{1,0:T(8,128)(2,1)S(1)} %pad_maximum_fusion.3), channel_id=1, source_target_pairs={{0,8},{8,0},{16,24},{24,16},{1,9},{9,1},{17,25},{25,17},{2,10},{10... | collective-permute-start | bytes 245768 | tf_op jit(solution)/shard_map/ppermute | solution.py:486
  24.5 1.6 %collective-permute-start.17 = (bf16[32,1024]{1,0:T(8,128)(2,1)S(1)}, bf16[32,1024]{1,0:T(8,128)(2,1)S(1)}, u32[]{:S(2)}, u32[]{:S(2)}) collective-permute-start(bf16[32,1024]{1,0:T(8,128)(2,1)S(1)} %get-tuple-element.95), channel_id=1, source_target_pairs={{0,8},{8,0},{16,24},{24,16},{1,9},{9,1},{17,25},{25,17},{2,10},{10... | collective-permute-start | bytes 196616 | tf_op jit(solution)/shard_map/ppermute | solution.py:486
  24.8 6.8 %collective-permute-start.8 = (bf16[64,1536]{1,0:T(8,128)(2,1)S(1)}, bf16[64,1536]{1,0:T(8,128)(2,1)S(1)}, u32[]{:S(2)}, u32[]{:S(2)}) collective-permute-start(bf16[64,1536]{1,0:T(8,128)(2,1)S(1)} %get-tuple-element.74), channel_id=1, source_target_pairs={{0,1},{1,0},{2,3},{3,2},{4,5},{5,4},{6,7},{7,6},{8,10},{9,11},{10,... | collective-permute-start | bytes 589832 | tf_op jit(solution)/shard_map/ppermute | solution.py:635
  26.2 5.4 %collective-permute-start.18 = (bf16[64,768]{1,0:T(8,128)(2,1)S(1)}, bf16[64,768]{1,0:T(8,128)(2,1)S(1)}, u32[]{:S(2)}, u32[]{:S(2)}) collective-permute-start(bf16[64,768]{1,0:T(8,128)(2,1)S(1)} %get-tuple-element.90), channel_id=1, source_target_pairs={{0,1},{1,0},{2,3},{3,2},{4,5},{5,4},{6,7},{7,6},{8,10},{9,11},{10,... | collective-permute-start | bytes 294920 | tf_op jit(solution)/shard_map/ppermute | solution.py:635
  27.3 6.0 %collective-permute-start.13 = (bf16[64,768]{1,0:T(8,128)(2,1)S(1)}, bf16[64,768]{1,0:T(8,128)(2,1)S(1)}, u32[]{:S(2)}, u32[]{:S(2)}) collective-permute-start(bf16[64,768]{1,0:T(8,128)(2,1)S(1)} %get-tuple-element.80), channel_id=1, source_target_pairs={{0,1},{1,0},{2,3},{3,2},{4,5},{5,4},{6,7},{7,6},{8,10},{9,11},{10,... | collective-permute-start | bytes 294920 | tf_op jit(solution)/shard_map/ppermute | solution.py:635
  31.9 5.0 %collective-permute-start.19 = (bf16[2,128,256]{2,1,0:T(8,128)(2,1)S(1)}, bf16[2,128,256]{2,1,0:T(8,128)(2,1)S(1)}, u32[]{:S(2)}, u32[]{:S(2)}) collective-permute-start(bf16[2,128,256]{2,1,0:T(8,128)(2,1)S(1)} %get-tuple-element.92), channel_id=1, source_target_pairs={{0,2},{1,3},{2,0},{3,1},{4,6},{5,7},{6,4},{7,5},{8,9},{9,8},{10,11... | collective-permute-start | bytes 393224 | tf_op jit(solution)/shard_map/ppermute | solution.py:635
  33.6 5.7 %collective-permute-start.14 = (bf16[2,128,256]{2,1,0:T(8,128)(2,1)S(1)}, bf16[2,128,256]{2,1,0:T(8,128)(2,1)S(1)}, u32[]{:S(2)}, u32[]{:S(2)}) collective-permute-start(bf16[2,128,256]{2,1,0:T(8,128)(2,1)S(1)} %get-tuple-element.82), channel_id=1, source_target_pairs={{0,2},{1,3},{2,0},{3,1},{4,6},{5,7},{6,4},{7,5},{8,9},{9,8},{10,11... | collective-permute-start | bytes 393224 | tf_op jit(solution)/shard_map/ppermute | solution.py:635
  37.0 7.3 %collective-permute-start.20 = (bf16[1,128,256]{2,1,0:T(8,128)(2,1)S(1)}, bf16[1,128,256]{2,1,0:T(8,128)(2,1)S(1)}, u32[]{:S(2)}, u32[]{:S(2)}) collective-permute-start(bf16[1,128,256]{2,1,0:T(8,128)(2,1)S(1)} %get-tuple-element.94), channel_id=1, source_target_pairs={{0,4},{1,5},{2,6},{3,7},{4,0},{5,1},{6,2},{7,3},{8,12},{9,13},{10,... | collective-permute-start | bytes 196616 | tf_op jit(solution)/shard_map/ppermute | solution.py:635
  39.4 5.6 %collective-permute-start.15 = (bf16[1,128,256]{2,1,0:T(8,128)(2,1)S(1)}, bf16[1,128,256]{2,1,0:T(8,128)(2,1)S(1)}, u32[]{:S(2)}, u32[]{:S(2)}) collective-permute-start(bf16[1,128,256]{2,1,0:T(8,128)(2,1)S(1)} %get-tuple-element.84), channel_id=1, source_target_pairs={{0,4},{1,5},{2,6},{3,7},{4,0},{5,1},{6,2},{7,3},{8,12},{9,13},{10,... | collective-permute-start | bytes 196616 | tf_op jit(solution)/shard_map/ppermute | solution.py:635

commit v15 on v14

--- a/solution.py
+++ b/solution.py
@@ -589,17 +589,16 @@
     going = pick(upstreams, True)
     far_up = mirror(near_core(going[0], going[1]) if mirrored else going)
     far_inner = mirror(pick(back_inners, True))
-    side = [pick(upstreams)[1], pick(back_inners)[1]]
-    side = swap_cores(jnp.concatenate(side, axis=1))
-    side_up, side_inner = side[:, :channels], side[:, channels:]
+    side_up = swap_cores(pick(upstreams)[1])
+    side_inner = swap_cores(pick(back_inners)[1])
     if mirrored:
         top = jnp.where(at_stage[0], leave, known[0])
         far_up, cross_up = near_core(far_up, top), near_core(top, far_up)
     else:
         far_up, cross_up = far_up[0], far_up[1]
-    cross_up = swap_cores(cross_up)
     far_inner, cross_inner = far_inner[0], far_inner[1]
-    cross_inner = swap_cores(cross_inner)
+    crossed = swap_cores(jnp.concatenate([cross_up, cross_inner], axis=1))
+    cross_up, cross_inner = crossed[:, :channels], crossed[:, channels:]
 
     chunk = channels // replicas
     fore = flows + [side_flow, far_flow, cross_flow]

time: 45.9 us -> 46 us (level)
  no operation moved by 1% of the time
where the time goes in v15:
time: 46 us; the launch traced here: 45.8 us
  starting transfers between devices  20.2 us (44%)
  waiting for transfers between devices  16 us (35%)
  Pallas kernels  9.14 us (20%)
    ppermute x7, starting transfers between devices, exchange(): return lax.ppermute(shard, AXES, pairs)  10.7 us
    ppermute x7, waiting for transfers between devices, exchange(): return lax.ppermute(shard, AXES, pairs)  8.64 us
    ppermute x2, starting transfers between devices, hop(): return lax.ppermute(shard, 'pipe', pairs)  4.86 us
    ppermute x3, waiting for transfers between devices, mirror(): return lax.ppermute(shard, 'pipe', mirror_pairs)  4.03 us
    pallas_call x3, Pallas kernels, run_stage(): pl.pallas_call(functools.partial(stage_body, step, forward, backward, las...  3.26 us
    ppermute x2, waiting for transfers between devices, hop(): return lax.ppermute(shard, 'pipe', pairs)  3.23 us
    ppermute x3, starting transfers between devices, mirror(): return lax.ppermute(shard, 'pipe', mirror_pairs)  3.09 us
    pallas_call x2, Pallas kernels, load(): pl.pallas_call(functools.partial(load_body, step), out_shape=outs, in_spe...  2.44 us
  transfers between devices with their start and end apart: 21, of which 9 were waited for; matrix products, arithmetic and copies ran while one was open for 0% of the time, Pallas kernels for 12%

profile of v15, /device:TPU:0, one launch (start us, length us, event | category | flops | bytes accessed | tf_op | source)
XLA Modules:
  0.0 45.8 jit_solution(5745307363618724178)
XLA Ops:
  0.0 1.2 %shard_map.46 = (bf16[1024,256]{1,0:T(8,128)(2,1)S(1)}, bf16[1024,256]{1,0:T(8,128)(2,1)S(1)}, bf16[32,1024]{1,0:T(8,128)(2,1)S(1)}) custom-call(bf16[2,1024,256]{2,1,0:T(8,128)(2,1)} %bitcast.20, bf16[2,1024,256]{2,1,0:T(8,128)(2,1)} %bitcast.22, bf16[2,2,32,1024]{3,2,1,0:T(8,128)(2,1)} %inputs), custom_call_target="tpu_custom_call" | custom-call | tf_op jit(solution)/shard_map/pallas_call | solution.py:69
  1.2 0.6 %collective-permute-start = (bf16[1024,256]{1,0:T(8,128)(2,1)S(1)}, bf16[1024,256]{1,0:T(8,128)(2,1)S(1)}, u32[]{:S(2)}, u32[]{:S(2)}) collective-permute-start(bf16[1024,256]{1,0:T(8,128)(2,1)S(1)} %get-tuple-element.51.own.refs_0_), channel_id=1, source_target_pairs={{0,8},{8,0},{16,24},{24,16},{1,9},{9,1},{17,25},{25,17},{2,10},{10... | collective-permute-start | bytes 1572872 | tf_op jit(solution)/shard_map/ppermute | solution.py:486
  1.8 0.1 collective-permute-start.1
  1.9 1.2 %shard_map.49 = (bf16[1024,256]{1,0:T(8,128)(2,1)S(1)}, bf16[1024,256]{1,0:T(8,128)(2,1)S(1)}) custom-call(bf16[2,1024,256]{2,1,0:T(8,128)(2,1)} %bitcast.21, bf16[2,1024,256]{2,1,0:T(8,128)(2,1)} %bitcast.23), custom_call_target="tpu_custom_call" | custom-call | tf_op jit(solution)/shard_map/pallas_call | solution.py:69
  3.1 0.5 %collective-permute-start.3 = (bf16[1024,256]{1,0:T(8,128)(2,1)S(1)}, bf16[1024,256]{1,0:T(8,128)(2,1)S(1)}, u32[]{:S(2)}, u32[]{:S(2)}) collective-permute-start(bf16[1024,256]{1,0:T(8,128)(2,1)S(1)} %get-tuple-element.59.expand_own.refs_1_), channel_id=1, source_target_pairs={{0,8},{8,0},{16,24},{24,16},{1,9},{9,1},{17,25},{25,17},{2,10},{10... | collective-permute-start | bytes 1572872 | tf_op jit(solution)/shard_map/ppermute | solution.py:486
  3.6 0.1 collective-permute-start.2
  3.7 0.3 shard_map.47
  4.0 0.1 collective-permute-done.1.refs_3_.other
  4.1 0.8 %shard_map.48 = (bf16[2,32,1280]{2,1,0:T(8,128)(2,1)S(1)}, bf16[32,1024]{1,0:T(8,128)(2,1)S(1)}, bf16[2,32,1024]{2,1,0:T(8,128)(2,1)S(1)}, f32[2,32,256]{2,1,0:T(8,128)S(1)}) custom-call(bf16[1024,256]{1,0:T(8,128)(2,1)S(1)} %get-tuple-element.51.own.refs_0_, bf16[1024,256]{1,0:T(8,128)(2,1)S(1)} %get-tuple-element.52.refs_1_.own, ...), custom_call_target="tpu_custom_call" | custom-call | flops 67108864 | bytes 2097152 | tf_op jit(solution)/shard_map/pallas_call | solution.py:282
  4.9 2.9 %collective-permute-start.4 = (bf16[32,1024]{1,0:T(8,128)(2,1)S(1)}, bf16[32,1024]{1,0:T(8,128)(2,1)S(1)}, u32[]{:S(2)}, u32[]{:S(2)}) collective-permute-start(bf16[32,1024]{1,0:T(8,128)(2,1)S(1)} %get-tuple-element.60.leave), channel_id=1, source_target_pairs={{0,16},{16,0},{8,24},{24,8},{1,17},{17,1},{9,25},{25,9},{2,18},{18... | collective-permute-start | bytes 196616 | tf_op jit(solution)/shard_map/ppermute | solution.py:483
  7.8 0.0 collective-permute-done.3.expand_other.refs_3_
  7.8 1.2 %shard_map.50 = (bf16[32,1024]{1,0:T(8,128)(2,1)S(1)}, f32[32,256]{1,0:T(8,128)S(1)}, bf16[32,1024]{1,0:T(8,128)(2,1)S(1)}, bf16[32,1024]{1,0:T(8,128)(2,1)S(1)}) custom-call(bf16[1024,256]{1,0:T(8,128)(2,1)S(1)} %get-tuple-element.59.expand_own.refs_1_, bf16[1024,256]{1,0:T(8,128)(2,1)S(1)} %collective-permute-done.3.expand_other.refs_3_, ...), custom_call_target="tpu_custom_call" | custom-call | tf_op jit(solution)/shard_map/pallas_call | solution.py:535
  9.0 0.0 collective-permute-done.2.refs_2_
  9.0 1.2 %collective-permute-done.4.refs_4_ = bf16[32,1024]{1,0:T(8,128)(2,1)S(1)} collective-permute-done((bf16[32,1024]{1,0:T(8,128)(2,1)S(1)}, bf16[32,1024]{1,0:T(8,128)(2,1)S(1)}, u32[]{:S(2)}, u32[]{:S(2)}) %collective-permute-start.4) | collective-permute-done | bytes 65568 | tf_op jit(solution)/shard_map/ppermute | solution.py:483
  10.2 1.8 %shard_map.51 = (bf16[2,32,1280]{2,1,0:T(8,128)(2,1)S(1)}, bf16[2,32,1024]{2,1,0:T(8,128)(2,1)S(1)}, bf16[2,32,256]{2,1,0:T(8,128)(2,1)S(1)}, bf16[32,1024]{1,0:T(8,128)(2,1)S(1)}) custom-call(bf16[1024,256]{1,0:T(8,128)(2,1)S(1)} %get-tuple-element.58.refs_0_, bf16[1024,256]{1,0:T(8,128)(2,1)S(1)} %get-tuple-element.59.expand_own.refs_1_, ...), custom_call_target="tpu_custom_call" | custom-call | flops 134217728 | bytes 2097152 | tf_op jit(solution)/shard_map/pallas_call | solution.py:282
  12.0 2.0 %collective-permute-start.6 = (bf16[32,1024]{1,0:T(8,128)(2,1)S(1)}, bf16[32,1024]{1,0:T(8,128)(2,1)S(1)}, u32[]{:S(2)}, u32[]{:S(2)}) collective-permute-start(bf16[32,1024]{1,0:T(8,128)(2,1)S(1)} %get-tuple-element.65), channel_id=1, source_target_pairs={{0,16},{16,0},{8,24},{24,8},{1,17},{17,1},{9,25},{25,9},{2,18},{18... | collective-permute-start | bytes 196616 | tf_op jit(solution)/shard_map/ppermute | solution.py:483
  14.0 0.1 collective-permute-start.5
  14.2 0.2 collective-permute-start.10
  14.3 2.1 %collective-permute-done.6.refs_4_ = bf16[32,1024]{1,0:T(8,128)(2,1)S(1)} collective-permute-done((bf16[32,1024]{1,0:T(8,128)(2,1)S(1)}, bf16[32,1024]{1,0:T(8,128)(2,1)S(1)}, u32[]{:S(2)}, u32[]{:S(2)}) %collective-permute-start.6) | collective-permute-done | bytes 65568 | tf_op jit(solution)/shard_map/ppermute | solution.py:483
  16.4 0.6 %shard_map.52 = (bf16[2,32,1024]{2,1,0:T(8,128)(2,1)S(1)}, bf16[2,32,256]{2,1,0:T(8,128)(2,1)S(1)}) custom-call(bf16[1024,256]{1,0:T(8,128)(2,1)S(1)} %get-tuple-element.51.own.refs_0_, bf16[1024,256]{1,0:T(8,128)(2,1)S(1)} %get-tuple-element.52.refs_1_.own, bf16[1024,256]{1,0:T(8,128)(2,1)S(1)} %collective-permute-done.other.refs_2_, ...), custom_call_target="tpu_custom_call" | custom-call | flops 67108864 | bytes 2097152 | tf_op jit(solution)/shard_map/pallas_call | solution.py:282
  17.0 0.2 shard_map.53.refs_6_
  17.3 0.1 collective-permute-start.8
  17.4 2.5 %collective-permute-start.12 = (bf16[2,32,256]{2,1,0:T(8,128)(2,1)S(1)}, bf16[2,32,256]{2,1,0:T(8,128)(2,1)S(1)}, u32[]{:S(2)}, u32[]{:S(2)}) collective-permute-start(bf16[2,32,256]{2,1,0:T(8,128)(2,1)S(1)} %broadcast_select_fusion.7), channel_id=1, source_target_pairs={{0,16},{8,24},{16,0},{24,8},{1,17},{9,25},{17,1},{25,9},{2,18},{10... | collective-permute-start | bytes 98312 | tf_op jit(solution)/shard_map/ppermute | solution.py:489
  20.0 0.2 collective-permute-start.7
  20.1 0.3 collective-permute-start.13
  20.5 1.4 %collective-permute-done.12 = bf16[2,32,256]{2,1,0:T(8,128)(2,1)S(1)} collective-permute-done((bf16[2,32,256]{2,1,0:T(8,128)(2,1)S(1)}, bf16[2,32,256]{2,1,0:T(8,128)(2,1)S(1)}, u32[]{:S(2)}, u32[]{:S(2)}) %collective-permute-start.12) | collective-permute-done | bytes 32800 | tf_op jit(solution)/shard_map/ppermute | solution.py:489
  21.9 0.0 collective-permute-start.11
  22.0 2.6 %collective-permute-done.13 = bf16[32,1024]{1,0:T(8,128)(2,1)S(1)} collective-permute-done((bf16[32,1024]{1,0:T(8,128)(2,1)S(1)}, bf16[32,1024]{1,0:T(8,128)(2,1)S(1)}, u32[]{:S(2)}, u32[]{:S(2)}) %collective-permute-start.13) | collective-permute-done | bytes 65568 | tf_op jit(solution)/shard_map/ppermute | solution.py:489
  24.6 0.1 collective-permute-start.14
  24.7 0.0 collective-permute-done.5.refs_2_
  24.7 0.0 collective-permute-done.7.refs_5_
  24.7 0.1 shard_map.54
  24.8 1.3 %collective-permute-start.9 = (bf16[64,1536]{1,0:T(8,128)(2,1)S(1)}, bf16[64,1536]{1,0:T(8,128)(2,1)S(1)}, u32[]{:S(2)}, u32[]{:S(2)}) collective-permute-start(bf16[64,1536]{1,0:T(8,128)(2,1)S(1)} %get-tuple-element.74), channel_id=1, source_target_pairs={{0,1},{1,0},{2,3},{3,2},{4,5},{5,4},{6,7},{7,6},{8,10},{9,11},{10,... | collective-permute-start | bytes 589832 | tf_op jit(solution)/shard_map/ppermute | solution.py:634
  26.2 0.1 shard_map.58
  26.3 1.1 %collective-permute-start.18 = (bf16[64,768]{1,0:T(8,128)(2,1)S(1)}, bf16[64,768]{1,0:T(8,128)(2,1)S(1)}, u32[]{:S(2)}, u32[]{:S(2)}) collective-permute-start(bf16[64,768]{1,0:T(8,128)(2,1)S(1)} %get-tuple-element.90), channel_id=1, source_target_pairs={{0,1},{1,0},{2,3},{3,2},{4,5},{5,4},{6,7},{7,6},{8,10},{9,11},{10,... | collective-permute-start | bytes 294920 | tf_op jit(solution)/shard_map/ppermute | solution.py:634
  27.4 1.1 %collective-permute-start.15 = (bf16[64,768]{1,0:T(8,128)(2,1)S(1)}, bf16[64,768]{1,0:T(8,128)(2,1)S(1)}, u32[]{:S(2)}, u32[]{:S(2)}) collective-permute-start(bf16[64,768]{1,0:T(8,128)(2,1)S(1)} %get-tuple-element.81), channel_id=1, source_target_pairs={{0,1},{1,0},{2,3},{3,2},{4,5},{5,4},{6,7},{7,6},{8,10},{9,11},{10,... | collective-permute-start | bytes 294920 | tf_op jit(solution)/shard_map/ppermute | solution.py:634
  28.5 3.1 %collective-permute-done.18.refs_5_ = bf16[64,768]{1,0:T(8,128)(2,1)S(1)} collective-permute-done((bf16[64,768]{1,0:T(8,128)(2,1)S(1)}, bf16[64,768]{1,0:T(8,128)(2,1)S(1)}, u32[]{:S(2)}, u32[]{:S(2)}) %collective-permute-start.18) | collective-permute-done | bytes 98336 | tf_op jit(solution)/shard_map/ppermute | solution.py:634
  31.6 0.0 collective-permute-done.9.refs_2_
  31.6 0.3 shard_map.59
  32.0 1.4 %collective-permute-start.19 = (bf16[2,128,256]{2,1,0:T(8,128)(2,1)S(1)}, bf16[2,128,256]{2,1,0:T(8,128)(2,1)S(1)}, u32[]{:S(2)}, u32[]{:S(2)}) collective-permute-start(bf16[2,128,256]{2,1,0:T(8,128)(2,1)S(1)} %get-tuple-element.92), channel_id=1, source_target_pairs={{0,2},{1,3},{2,0},{3,1},{4,6},{5,7},{6,4},{7,5},{8,9},{9,8},{10,11... | collective-permute-start | bytes 393224 | tf_op jit(solution)/shard_map/ppermute | solution.py:634
  33.4 0.3 shard_map.56
  33.7 0.8 %collective-permute-start.16 = (bf16[2,128,256]{2,1,0:T(8,128)(2,1)S(1)}, bf16[2,128,256]{2,1,0:T(8,128)(2,1)S(1)}, u32[]{:S(2)}, u32[]{:S(2)}) collective-permute-start(bf16[2,128,256]{2,1,0:T(8,128)(2,1)S(1)} %get-tuple-element.83), channel_id=1, source_target_pairs={{0,2},{1,3},{2,0},{3,1},{4,6},{5,7},{6,4},{7,5},{8,9},{9,8},{10,11... | collective-permute-start | bytes 393224 | tf_op jit(solution)/shard_map/ppermute | solution.py:634
  34.5 2.5 %collective-permute-done.19.came = bf16[2,128,256]{2,1,0:T(8,128)(2,1)S(1)} collective-permute-done((bf16[2,128,256]{2,1,0:T(8,128)(2,1)S(1)}, bf16[2,128,256]{2,1,0:T(8,128)(2,1)S(1)}, u32[]{:S(2)}, u32[]{:S(2)}) %collective-permute-start.19) | collective-permute-done | bytes 131104 | tf_op jit(solution)/shard_map/ppermute | solution.py:634
  37.0 2.4 %collective-permute-start.20 = (bf16[1,128,256]{2,1,0:T(8,128)(2,1)S(1)}, bf16[1,128,256]{2,1,0:T(8,128)(2,1)S(1)}, u32[]{:S(2)}, u32[]{:S(2)}) collective-permute-start(bf16[1,128,256]{2,1,0:T(8,128)(2,1)S(1)} %get-tuple-element.94), channel_id=1, source_target_pairs={{0,4},{1,5},{2,6},{3,7},{4,0},{5,1},{6,2},{7,3},{8,12},{9,13},{10,... | collective-permute-start | bytes 196616 | tf_op jit(solution)/shard_map/ppermute | solution.py:634
  39.5 2.6 %collective-permute-start.17 = (bf16[1,128,256]{2,1,0:T(8,128)(2,1)S(1)}, bf16[1,128,256]{2,1,0:T(8,128)(2,1)S(1)}, u32[]{:S(2)}, u32[]{:S(2)}) collective-permute-start(bf16[1,128,256]{2,1,0:T(8,128)(2,1)S(1)} %get-tuple-element.85), channel_id=1, source_target_pairs={{0,4},{1,5},{2,6},{3,7},{4,0},{5,1},{6,2},{7,3},{8,12},{9,13},{10,... | collective-permute-start | bytes 196616 | tf_op jit(solution)/shard_map/ppermute | solution.py:634
  42.1 2.3 %collective-permute-done.20.came_expand = bf16[1,128,256]{2,1,0:T(8,128)(2,1)S(1)} collective-permute-done((bf16[1,128,256]{2,1,0:T(8,128)(2,1)S(1)}, bf16[1,128,256]{2,1,0:T(8,128)(2,1)S(1)}, u32[]{:S(2)}, u32[]{:S(2)}) %collective-permute-start.20) | collective-permute-done | bytes 65568 | tf_op jit(solution)/shard_map/ppermute | solution.py:634
  44.3 0.7 %collective-permute-done.17.came_reduce = bf16[1,128,256]{2,1,0:T(8,128)(2,1)S(1)} collective-permute-done((bf16[1,128,256]{2,1,0:T(8,128)(2,1)S(1)}, bf16[1,128,256]{2,1,0:T(8,128)(2,1)S(1)}, u32[]{:S(2)}, u32[]{:S(2)}) %collective-permute-start.17) | collective-permute-done | bytes 65568 | tf_op jit(solution)/shard_map/ppermute | solution.py:634
  45.0 0.7 %shard_map.61 = f32[1,2,128,256]{3,2,1,0:T(8,128)} custom-call(f32[1,128,256]{2,1,0:T(8,128)S(1)} %get-tuple-element.84.keep_reduce, bf16[1,128,256]{2,1,0:T(8,128)(2,1)S(1)} %collective-permute-done.17.came_reduce, f32[1,128,256]{2,1,0:T(8,128)S(1)} %get-tuple-element.93.keep_expand, bf16[1,128,256]{2,1,0:T(8,128)(2,1)S(1)} %collective-permute-done.20.came_expand), custom_call_target="tpu_custom_call" | custom-call | tf_op jit(solution)/shard_map/pallas_call | solution.py:609
  (29 shorter events, 0.3 us)
Async XLA Ops:
  1.2 2.4 %collective-permute-start = (bf16[1024,256]{1,0:T(8,128)(2,1)S(1)}, bf16[1024,256]{1,0:T(8,128)(2,1)S(1)}, u32[]{:S(2)}, u32[]{:S(2)}) collective-permute-start(bf16[1024,256]{1,0:T(8,128)(2,1)S(1)} %get-tuple-element.51.own.refs_0_), channel_id=1, source_target_pairs={{0,8},{8,0},{16,24},{24,16},{1,9},{9,1},{17,25},{25,17},{2,10},{10... | collective-permute-start | bytes 1572872 | tf_op jit(solution)/shard_map/ppermute | solution.py:486
  1.8 2.3 %collective-permute-start.1 = (bf16[1024,256]{1,0:T(8,128)(2,1)S(1)}, bf16[1024,256]{1,0:T(8,128)(2,1)S(1)}, u32[]{:S(2)}, u32[]{:S(2)}) collective-permute-start(bf16[1024,256]{1,0:T(8,128)(2,1)S(1)} %get-tuple-element.52.refs_1_.own), channel_id=1, source_target_pairs={{0,8},{8,0},{16,24},{24,16},{1,9},{9,1},{17,25},{25,17},{2,10},{10... | collective-permute-start | bytes 1572872 | tf_op jit(solution)/shard_map/ppermute | solution.py:486
  3.1 4.7 %collective-permute-start.3 = (bf16[1024,256]{1,0:T(8,128)(2,1)S(1)}, bf16[1024,256]{1,0:T(8,128)(2,1)S(1)}, u32[]{:S(2)}, u32[]{:S(2)}) collective-permute-start(bf16[1024,256]{1,0:T(8,128)(2,1)S(1)} %get-tuple-element.59.expand_own.refs_1_), channel_id=1, source_target_pairs={{0,8},{8,0},{16,24},{24,16},{1,9},{9,1},{17,25},{25,17},{2,10},{10... | collective-permute-start | bytes 1572872 | tf_op jit(solution)/shard_map/ppermute | solution.py:486
  3.6 5.4 %collective-permute-start.2 = (bf16[1024,256]{1,0:T(8,128)(2,1)S(1)}, bf16[1024,256]{1,0:T(8,128)(2,1)S(1)}, u32[]{:S(2)}, u32[]{:S(2)}) collective-permute-start(bf16[1024,256]{1,0:T(8,128)(2,1)S(1)} %get-tuple-element.58.refs_0_), channel_id=1, source_target_pairs={{0,8},{8,0},{16,24},{24,16},{1,9},{9,1},{17,25},{25,17},{2,10},{10... | collective-permute-start | bytes 1572872 | tf_op jit(solution)/shard_map/ppermute | solution.py:486
  4.9 5.3 %collective-permute-start.4 = (bf16[32,1024]{1,0:T(8,128)(2,1)S(1)}, bf16[32,1024]{1,0:T(8,128)(2,1)S(1)}, u32[]{:S(2)}, u32[]{:S(2)}) collective-permute-start(bf16[32,1024]{1,0:T(8,128)(2,1)S(1)} %get-tuple-element.60.leave), channel_id=1, source_target_pairs={{0,16},{16,0},{8,24},{24,8},{1,17},{17,1},{9,25},{25,9},{2,18},{18... | collective-permute-start | bytes 196616 | tf_op jit(solution)/shard_map/ppermute | solution.py:483
  12.0 4.4 %collective-permute-start.6 = (bf16[32,1024]{1,0:T(8,128)(2,1)S(1)}, bf16[32,1024]{1,0:T(8,128)(2,1)S(1)}, u32[]{:S(2)}, u32[]{:S(2)}) collective-permute-start(bf16[32,1024]{1,0:T(8,128)(2,1)S(1)} %get-tuple-element.65), channel_id=1, source_target_pairs={{0,16},{16,0},{8,24},{24,8},{1,17},{17,1},{9,25},{25,9},{2,18},{18... | collective-permute-start | bytes 196616 | tf_op jit(solution)/shard_map/ppermute | solution.py:483
  14.0 10.7 %collective-permute-start.5 = (bf16[32,1280]{1,0:T(8,128)(2,1)S(1)}, bf16[32,1280]{1,0:T(8,128)(2,1)S(1)}, u32[]{:S(2)}, u32[]{:S(2)}) collective-permute-start(bf16[32,1280]{1,0:T(8,128)(2,1)S(1)} %fusion), channel_id=1, source_target_pairs={{0,8},{8,0},{16,24},{24,16},{1,9},{9,1},{17,25},{25,17},{2,10},{10... | collective-permute-start | bytes 245768 | tf_op jit(solution)/shard_map/ppermute | solution.py:486
  14.2 6.0 %collective-permute-start.10 = (bf16[32,1536]{1,0:T(8,128)(2,1)S(1)}, bf16[32,1536]{1,0:T(8,128)(2,1)S(1)}, u32[]{:S(2)}, u32[]{:S(2)}) collective-permute-start(bf16[32,1536]{1,0:T(8,128)(2,1)S(1)} %pad_maximum_fusion), channel_id=1, source_target_pairs={{0,16},{8,24},{16,0},{24,8},{1,17},{9,25},{17,1},{25,9},{2,18},{10... | collective-permute-start | bytes 294920 | tf_op jit(solution)/shard_map/ppermute | solution.py:489
  17.3 7.3 %collective-permute-start.8 = (bf16[32,256]{1,0:T(8,128)(2,1)S(1)}, bf16[32,256]{1,0:T(8,128)(2,1)S(1)}, u32[]{:S(2)}, u32[]{:S(2)}) collective-permute-start(bf16[32,256]{1,0:T(8,128)(2,1)S(1)} %fusion.4), channel_id=1, source_target_pairs={{0,8},{8,0},{16,24},{24,16},{1,9},{9,1},{17,25},{25,17},{2,10},{10... | collective-permute-start | bytes 49160 | tf_op jit(solution)/shard_map/ppermute | solution.py:486
  17.4 4.5 %collective-permute-start.12 = (bf16[2,32,256]{2,1,0:T(8,128)(2,1)S(1)}, bf16[2,32,256]{2,1,0:T(8,128)(2,1)S(1)}, u32[]{:S(2)}, u32[]{:S(2)}) collective-permute-start(bf16[2,32,256]{2,1,0:T(8,128)(2,1)S(1)} %broadcast_select_fusion.7), channel_id=1, source_target_pairs={{0,16},{8,24},{16,0},{24,8},{1,17},{9,25},{17,1},{25,9},{2,18},{10... | collective-permute-start | bytes 98312 | tf_op jit(solution)/shard_map/ppermute | solution.py:489
  20.0 4.7 %collective-permute-start.7 = (bf16[32,1024]{1,0:T(8,128)(2,1)S(1)}, bf16[32,1024]{1,0:T(8,128)(2,1)S(1)}, u32[]{:S(2)}, u32[]{:S(2)}) collective-permute-start(bf16[32,1024]{1,0:T(8,128)(2,1)S(1)} %fusion.3), channel_id=1, source_target_pairs={{0,8},{8,0},{16,24},{24,16},{1,9},{9,1},{17,25},{25,17},{2,10},{10... | collective-permute-start | bytes 196616 | tf_op jit(solution)/shard_map/ppermute | solution.py:486
  20.1 4.4 %collective-permute-start.13 = (bf16[32,1024]{1,0:T(8,128)(2,1)S(1)}, bf16[32,1024]{1,0:T(8,128)(2,1)S(1)}, u32[]{:S(2)}, u32[]{:S(2)}) collective-permute-start(bf16[32,1024]{1,0:T(8,128)(2,1)S(1)} %fusion.1), channel_id=1, source_target_pairs={{0,16},{8,24},{16,0},{24,8},{1,17},{9,25},{17,1},{25,9},{2,18},{10... | collective-permute-start | bytes 196616 | tf_op jit(solution)/shard_map/ppermute | solution.py:489
  21.9 4.3 %collective-permute-start.11 = (bf16[32,1280]{1,0:T(8,128)(2,1)S(1)}, bf16[32,1280]{1,0:T(8,128)(2,1)S(1)}, u32[]{:S(2)}, u32[]{:S(2)}) collective-permute-start(bf16[32,1280]{1,0:T(8,128)(2,1)S(1)} %pad_maximum_fusion.2), channel_id=1, source_target_pairs={{0,8},{8,0},{16,24},{24,16},{1,9},{9,1},{17,25},{25,17},{2,10},{10... | collective-permute-start | bytes 245768 | tf_op jit(solution)/shard_map/ppermute | solution.py:486
  24.6 1.6 %collective-permute-start.14 = (bf16[32,1280]{1,0:T(8,128)(2,1)S(1)}, bf16[32,1280]{1,0:T(8,128)(2,1)S(1)}, u32[]{:S(2)}, u32[]{:S(2)}) collective-permute-start(bf16[32,1280]{1,0:T(8,128)(2,1)S(1)} %pad_maximum_fusion.3), channel_id=1, source_target_pairs={{0,8},{8,0},{16,24},{24,16},{1,9},{9,1},{17,25},{25,17},{2,10},{10... | collective-permute-start | bytes 245768 | tf_op jit(solution)/shard_map/ppermute | solution.py:486
  24.8 6.8 %collective-permute-start.9 = (bf16[64,1536]{1,0:T(8,128)(2,1)S(1)}, bf16[64,1536]{1,0:T(8,128)(2,1)S(1)}, u32[]{:S(2)}, u32[]{:S(2)}) collective-permute-start(bf16[64,1536]{1,0:T(8,128)(2,1)S(1)} %get-tuple-element.74), channel_id=1, source_target_pairs={{0,1},{1,0},{2,3},{3,2},{4,5},{5,4},{6,7},{7,6},{8,10},{9,11},{10,... | collective-permute-start | bytes 589832 | tf_op jit(solution)/shard_map/ppermute | solution.py:634
  26.3 5.4 %collective-permute-start.18 = (bf16[64,768]{1,0:T(8,128)(2,1)S(1)}, bf16[64,768]{1,0:T(8,128)(2,1)S(1)}, u32[]{:S(2)}, u32[]{:S(2)}) collective-permute-start(bf16[64,768]{1,0:T(8,128)(2,1)S(1)} %get-tuple-element.90), channel_id=1, source_target_pairs={{0,1},{1,0},{2,3},{3,2},{4,5},{5,4},{6,7},{7,6},{8,10},{9,11},{10,... | collective-permute-start | bytes 294920 | tf_op jit(solution)/shard_map/ppermute | solution.py:634
  27.4 6.0 %collective-permute-start.15 = (bf16[64,768]{1,0:T(8,128)(2,1)S(1)}, bf16[64,768]{1,0:T(8,128)(2,1)S(1)}, u32[]{:S(2)}, u32[]{:S(2)}) collective-permute-start(bf16[64,768]{1,0:T(8,128)(2,1)S(1)} %get-tuple-element.81), channel_id=1, source_target_pairs={{0,1},{1,0},{2,3},{3,2},{4,5},{5,4},{6,7},{7,6},{8,10},{9,11},{10,... | collective-permute-start | bytes 294920 | tf_op jit(solution)/shard_map/ppermute | solution.py:634
  32.0 5.0 %collective-permute-start.19 = (bf16[2,128,256]{2,1,0:T(8,128)(2,1)S(1)}, bf16[2,128,256]{2,1,0:T(8,128)(2,1)S(1)}, u32[]{:S(2)}, u32[]{:S(2)}) collective-permute-start(bf16[2,128,256]{2,1,0:T(8,128)(2,1)S(1)} %get-tuple-element.92), channel_id=1, source_target_pairs={{0,2},{1,3},{2,0},{3,1},{4,6},{5,7},{6,4},{7,5},{8,9},{9,8},{10,11... | collective-permute-start | bytes 393224 | tf_op jit(solution)/shard_map/ppermute | solution.py:634
  33.7 5.7 %collective-permute-start.16 = (bf16[2,128,256]{2,1,0:T(8,128)(2,1)S(1)}, bf16[2,128,256]{2,1,0:T(8,128)(2,1)S(1)}, u32[]{:S(2)}, u32[]{:S(2)}) collective-permute-start(bf16[2,128,256]{2,1,0:T(8,128)(2,1)S(1)} %get-tuple-element.83), channel_id=1, source_target_pairs={{0,2},{1,3},{2,0},{3,1},{4,6},{5,7},{6,4},{7,5},{8,9},{9,8},{10,11... | collective-permute-start | bytes 393224 | tf_op jit(solution)/shard_map/ppermute | solution.py:634
  37.0 7.3 %collective-permute-start.20 = (bf16[1,128,256]{2,1,0:T(8,128)(2,1)S(1)}, bf16[1,128,256]{2,1,0:T(8,128)(2,1)S(1)}, u32[]{:S(2)}, u32[]{:S(2)}) collective-permute-start(bf16[1,128,256]{2,1,0:T(8,128)(2,1)S(1)} %get-tuple-element.94), channel_id=1, source_target_pairs={{0,4},{1,5},{2,6},{3,7},{4,0},{5,1},{6,2},{7,3},{8,12},{9,13},{10,... | collective-permute-start | bytes 196616 | tf_op jit(solution)/shard_map/ppermute | solution.py:634
  39.5 5.6 %collective-permute-start.17 = (bf16[1,128,256]{2,1,0:T(8,128)(2,1)S(1)}, bf16[1,128,256]{2,1,0:T(8,128)(2,1)S(1)}, u32[]{:S(2)}, u32[]{:S(2)}) collective-permute-start(bf16[1,128,256]{2,1,0:T(8,128)(2,1)S(1)} %get-tuple-element.85), channel_id=1, source_target_pairs={{0,4},{1,5},{2,6},{3,7},{4,0},{5,1},{6,2},{7,3},{8,12},{9,13},{10,... | collective-permute-start | bytes 196616 | tf_op jit(solution)/shard_map/ppermute | solution.py:634
